TPU v7x, 256 devices: a whole 4x4x8 slice. The times are simulated.
256 devices in a mesh: dp: 16 (over z_hi, y, core), tensor: 16 (over x, z_lo).
Axes of the slice: x: 4, y: 4, z: 8 (z_hi: 2, z_lo: 4; z = z_hi * 4 + z_lo), core: 2. Of those that a mesh axis runs over, the one named last changes fastest.
Arguments:
- tokens: bfloat16 [2048, 1024], P('dp', 'tensor'), may hold values from -6 to 6
- init_noise: float32 [2048, 1024], P('dp', 'tensor'), may hold values from -1 to 1
- segment_ids: int32 [2048], P('dp'), may hold values from 0 to 31, never falling along the last dimension, each value on 1 to 256 neighbouring positions
- target: float32 [2048, 1024], P('dp', 'tensor'), may hold values from -6 to 6
- norm_gain: float32 [1024], replicated, may hold values from 0.1 to 1.9
- weight_in: bfloat16 [1024, 32768], P(None, 'tensor'), may hold values from -0.1875 to 0.1875
- weight_out: bfloat16 [32768, 1024], P('tensor'), may hold values from -0.03125 to 0.03125
- moment_in: float32 [1024, 32768], P('dp', 'tensor'), may hold values from -1.5 to 1.5
- moment_out: float32 [32768, 1024], P('tensor', 'dp'), may hold values from -1.5 to 1.5
Outputs:
- new_weight_in: bfloat16 [1024, 32768], P('dp', 'tensor')
- new_weight_out: bfloat16 [32768, 1024], P('tensor', 'dp')
- new_moment_in: float32 [1024, 32768], P('dp', 'tensor')
- new_moment_out: float32 [32768, 1024], P('tensor', 'dp')
- perturbation: float32 [2048, 1024], P('dp', 'tensor')
Inputs may be any that keep to these rules, and one draw needn't show every extreme that they name: `segment_ids`: example ids never fall along the tokens; every example holds 1 to 256 tokens.
All inputs are finite; a program needn't handle non-finite values.
Results may differ from a plain program's by a relative error of at most 0.0051.
Values may be sent and summed in bfloat16 or wider, within the bound.
No kernel may reach another device: no remote copies, remote signals or barrier semaphores. Data moves between devices by JAX's collectives and lax.ppermute only.
A program may use at most 128 MiB of HBM per device.

v0:
```python
import functools

import jax
import jax.numpy as jnp
from jax import lax
from jax.sharding import Mesh
from jax.sharding import PartitionSpec as P

D = 1024
ASCENTS = 2
DP = ("dp_0", "dp_1", "dp_2")
TENSOR = ("tensor_0", "tensor_1")
DP_TENSOR = ("dp_0", "dp_1", "dp_2", "tensor_0", "tensor_1")


coeff = 0.7978845608
adv_init = 0.5
adv_step = 0.5
decay = 0.9
learn_rate = 0.01


def from_everyone(array, axis):
    copies = jnp.broadcast_to(array, (lax.axis_size(axis), *array.shape))
    return lax.all_to_all(copies, axis, split_axis=0, concat_axis=0, tiled=True)


def over_copies(array, axis):
    everything = from_everyone(array, axis)
    return jnp.sum(everything, axis=0)


def in_order(blocks, dim):
    lengths = list(blocks.shape[1:])
    lengths[dim] *= blocks.shape[0]
    return jnp.moveaxis(blocks, 0, dim).reshape(lengths)


def gather_directly(array, axis, dim):
    blocks = from_everyone(array, axis)
    return in_order(blocks, dim)


def in_blocks(array, dim, peers):
    before, after = (array.shape[:dim], array.shape[dim + 1 :])
    return jnp.moveaxis(array.reshape(*before, peers, -1, *after), dim, 0)


def summed_on_arrival(array, axis, dim):
    peers = lax.axis_size(axis)
    blocks = lax.all_to_all(in_blocks(array, dim, peers), axis, 0, 0, tiled=True)
    return jnp.sum(blocks, axis=0)


def one_axis_at_a_time(array, axes):
    return functools.reduce(lax.psum, axes, array)


def gelu_value(values):
    tangent = jnp.tanh(coeff * (values + 0.044715 * values * values * values))
    return 0.5 * values * (1.0 + tangent)


def gelu_slope(values):
    tangent = jnp.tanh(coeff * (values + 0.044715 * values * values * values))
    return 0.5 * (1.0 + tangent) + 0.5 * values * (1.0 - tangent * tangent) * coeff * (
        1.0 + 3.0 * 0.044715 * values * values
    )


def shards(
    tokens, init_noise, segment_ids, target, norm_gain, weight_in, weight_out, moment_in, moment_out
):
    dp_count = lax.axis_size(DP)
    local_tokens = tokens.shape[0]
    width_local = tokens.shape[1]
    loss_scale = (local_tokens * dp_count) ** (-0.5)
    column = lax.axis_index(TENSOR)
    gain_local = lax.dynamic_slice_in_dim(norm_gain, column * width_local, width_local)
    labels = jnp.arange(2 * dp_count, dtype=jnp.int32)
    onehot = (segment_ids[:, None] == labels[None, :]).astype(jnp.float32)
    counts = over_copies(jnp.sum(onehot, axis=0), DP)
    perturb = adv_init * init_noise
    local_in = jnp.zeros(weight_in.shape, jnp.float32)
    local_out = jnp.zeros(weight_out.shape, jnp.float32)
    for ascent in range(ASCENTS):
        embedded = tokens.astype(jnp.float32) + perturb
        emb_bf = lax.optimization_barrier(embedded.astype(jnp.bfloat16))
        emb_local = emb_bf.astype(jnp.float32)
        gathered = gather_directly(emb_bf, TENSOR, 1).astype(jnp.float32)
        inv_rms = lax.rsqrt(jnp.mean(gathered * gathered, axis=1, keepdims=True) + 1e-06)
        normed = (gathered * inv_rms * norm_gain).astype(jnp.bfloat16)
        preact = jnp.dot(normed, weight_in, preferred_element_type=jnp.float32)
        hidden = gelu_value(preact).astype(jnp.bfloat16)
        partial_value = jnp.dot(hidden, weight_out, preferred_element_type=jnp.float32)
        mixed = summed_on_arrival(partial_value, TENSOR, 1)
        out_grad = (embedded + mixed - target) * loss_scale
        grad_whole = gather_directly(out_grad.astype(jnp.bfloat16), TENSOR, 1)
        hidden_grad = (
            jnp.dot(grad_whole, weight_out.T, preferred_element_type=jnp.float32)
            * gelu_slope(preact)
        ).astype(jnp.bfloat16)
        part_in = jnp.dot(normed.T, hidden_grad, preferred_element_type=jnp.float32)
        part_out = jnp.dot(hidden.T, grad_whole, preferred_element_type=jnp.float32)
        local_in = local_in + part_in
        local_out = local_out + part_out
        if ascent + 1 < ASCENTS:
            normed_partial = jnp.dot(hidden_grad, weight_in.T, preferred_element_type=jnp.float32)
            normed_grad = summed_on_arrival(normed_partial, TENSOR, 1)
            scaled = normed_grad * gain_local
            row_dot = over_copies(jnp.sum(scaled * emb_local, axis=1), TENSOR)[:, None]
            delta_grad = (
                out_grad + inv_rms * scaled - emb_local * inv_rms * inv_rms * inv_rms * row_dot / D
            )
            row_squares = jnp.sum(delta_grad * delta_grad, axis=1)
            square_sums = one_axis_at_a_time(
                jnp.sum(onehot * row_squares[:, None], axis=0), DP_TENSOR
            )
            root_mean = jnp.sqrt(square_sums / (counts * D) + 1e-06)
            token_scale = jnp.sum(onehot * (adv_step / root_mean)[None, :], axis=1)
            perturb = perturb + delta_grad * token_scale[:, None]
    summed_in, summed_out = (
        lax.psum_scatter(local_in, DP, scatter_dimension=0, tiled=True),
        lax.psum_scatter(local_out, DP, scatter_dimension=1, tiled=True),
    )
    dp_rows = moment_in.shape[0]
    offset = lax.axis_index(DP) * dp_rows
    own_in = lax.dynamic_slice_in_dim(weight_in, offset, dp_rows, 0)
    own_out = lax.dynamic_slice_in_dim(weight_out, offset, dp_rows, 1)
    new_moment_in = decay * moment_in + summed_in / ASCENTS
    new_moment_out = decay * moment_out + summed_out / ASCENTS
    new_weight_in = (own_in.astype(jnp.float32) - learn_rate * new_moment_in).astype(jnp.bfloat16)
    new_weight_out = (own_out.astype(jnp.float32) - learn_rate * new_moment_out).astype(
        jnp.bfloat16
    )
    return (new_weight_in, new_weight_out, new_moment_in, new_moment_out, perturb)


def solution(mesh):
    torus = Mesh(
        mesh.devices.reshape(2, 4, 2, 4, 4), ("dp_0", "dp_1", "dp_2", "tensor_0", "tensor_1")
    )
    in_specs = (
        P(DP, TENSOR),
        P(DP, TENSOR),
        P(DP),
        P(DP, TENSOR),
        P(),
        P(None, TENSOR),
        P(TENSOR, None),
        P(DP, TENSOR),
        P(TENSOR, DP),
    )
    out_specs = (P(DP, TENSOR), P(TENSOR, DP), P(DP, TENSOR), P(TENSOR, DP), P(DP, TENSOR))
    return jax.shard_map(
        shards, mesh=torus, in_specs=in_specs, out_specs=out_specs, check_vma=False
    )
```

profile of v0, /device:TPU:33, one launch (start us, length us, event | category | flops | bytes accessed | tf_op | source)
XLA Modules:
  0.0 501.5 jit_solution(4870087113546831471)
XLA Ops:
  7.2 0.0 copy-start.1
  7.2 0.9 fusion.37
  8.2 15.9 %all_to_all.47 = bf16[16,128,64]{1,2,0:T(8,128)(2,1)S(1)} all-to-all(bf16[16,128,64]{1,2,0:T(8,128)(2,1)S(1)} %broadcast_in_dim.12), channel_id=1, replica_groups=mesh['dp_0'=2,'dp_1'=4,'dp_2'=2,'tensor_0'=4,'tensor_1'=4] {'tensor_0','..., dimensions={0} | all-to-all | bytes 524288 | tf_op jit(solution)/shard_map/all_to_all | solution.py:25
  24.1 0.2 multiply_reduce_fusion.1
  24.3 0.9 fusion.24
  25.1 2.9 fusion.48
  28.1 0.0 copy-done.1
  28.1 0.0 copy-start.7
  28.1 0.0 copy-start.8
  28.1 0.0 copy-start.9
  28.1 1.9 fusion.44
  30.0 17.5 %all_to_all.48 = f32[16,128,64]{1,2,0:T(8,128)S(1)} all-to-all(f32[16,128,64]{1,2,0:T(8,128)S(1)} %bitcast.54), channel_id=1, replica_groups=mesh['dp_0'=2,'dp_1'=4,'dp_2'=2,'tensor_0'=4,'tensor_1'=4] {'tensor_0','..., dimensions={0} | all-to-all | bytes 1048576 | tf_op jit(solution)/shard_map/all_to_all | solution.py:51
  47.5 0.0 copy-done.7
  47.5 0.0 copy-done.8
  47.5 0.0 copy-done.9
  47.6 14.9 %all_to_all.49 = bf16[16,128,64]{1,2,0:T(8,128)(2,1)S(1)} all-to-all(bf16[16,128,64]{1,2,0:T(8,128)(2,1)S(1)} %broadcast_in_dim.13), channel_id=1, replica_groups=mesh['dp_0'=2,'dp_1'=4,'dp_2'=2,'tensor_0'=4,'tensor_1'=4] {'tensor_0','..., dimensions={0} | all-to-all | bytes 524288 | tf_op jit(solution)/shard_map/all_to_all | solution.py:25
  62.5 4.2 fusion
  66.7 0.0 copy-done.3
  66.7 0.0 copy-done
  66.7 0.0 copy-start.11
  66.7 0.0 copy-start.12
  66.7 2.1 fusion.50
  68.8 5.6 %all-to-all-start.3 = ((f32[16,128,64]{1,2,0:T(8,128)}), f32[16,128,64]{1,2,0:T(8,128)S(1)}, u32[]{:S(2)}, u32[]{:S(2)}) async-start(f32[16,128,64]{1,2,0:T(8,128)} %bitcast.7), calls=%async_computation.3 | async-start | bytes 1048576 | tf_op jit(solution)/shard_map/all_to_all | solution.py:51
  74.4 0.1 dynamic_slice.10
  74.5 11.7 %all-to-all-done.3 = f32[16,128,64]{1,2,0:T(8,128)S(1)} async-done(((f32[16,128,64]{1,2,0:T(8,128)}), f32[16,128,64]{1,2,0:T(8,128)S(1)}, u32[]{:S(2)}, u32[]{:S(2)}) %all-to-all-start.3) | async-done | bytes 524320 | tf_op jit(solution)/shard_map/all_to_all | solution.py:51
  86.2 0.1 fusion.35
  86.3 12.5 %all_to_all.50 = f32[16,1,128]{2,1,0:T(1,128)S(1)} all-to-all(f32[16,1,128]{2,1,0:T(1,128)S(1)} %broadcast_in_dim.14), channel_id=1, replica_groups=mesh['dp_0'=2,'dp_1'=4,'dp_2'=2,'tensor_0'=4,'tensor_1'=4] {'tensor_0','..., dimensions={0} | all-to-all | bytes 16384 | tf_op jit(solution)/shard_map/all_to_all | solution.py:25
  98.9 0.1 multiply_reduce_fusion.2
  99.0 0.1 convert_reduce_fusion
  99.1 0.6 broadcast_in_dim.15
  99.7 11.3 %all-to-all-start.5 = ((f32[16,1,32]{2,1,0:T(1,128)}), f32[16,1,32]{2,1,0:T(1,128)S(1)}, u32[]{:S(2)}, u32[]{:S(2)}) async-start(f32[16,1,32]{2,1,0:T(1,128)} %broadcast_in_dim.15), calls=%async_computation.5 | async-start | bytes 16384 | tf_op jit(solution)/shard_map/all_to_all | solution.py:25
  111.0 8.0 %psum.35 = f32[32]{0:T(128)S(1)} all-reduce(f32[32]{0:T(128)S(1)} %get-tuple-element.6), channel_id=1, replica_groups=mesh['dp_0'=2,'dp_1'=4,'dp_2'=2,'tensor_0'=4,'tensor_1'=4] {'dp_0'}, use_global_device_ids=true, to_apply=%region_7.0 | all-reduce | flops 32 | bytes 256 | tf_op jit(solution)/shard_map/psum | solution.py:56
  119.0 8.5 %psum.36 = f32[32]{0:T(128)S(1)} all-reduce(f32[32]{0:T(128)S(1)} %psum.35), channel_id=1, replica_groups=mesh['dp_0'=2,'dp_1'=4,'dp_2'=2,'tensor_0'=4,'tensor_1'=4] {'dp_1'}, use_global_device_ids=true, to_apply=%region_8.0 | all-reduce | flops 32 | bytes 256 | tf_op jit(solution)/shard_map/psum | solution.py:56
  127.5 5.4 %psum.37 = f32[32]{0:T(128)S(1)} all-reduce(f32[32]{0:T(128)S(1)} %psum.36), channel_id=1, replica_groups=mesh['dp_0'=2,'dp_1'=4,'dp_2'=2,'tensor_0'=4,'tensor_1'=4] {'dp_2'}, use_global_device_ids=true, to_apply=%region_9.0 | all-reduce | flops 32 | bytes 256 | tf_op jit(solution)/shard_map/psum | solution.py:56
  132.9 6.8 %psum.38 = f32[32]{0:T(128)S(1)} all-reduce(f32[32]{0:T(128)S(1)} %psum.37), channel_id=1, replica_groups=mesh['dp_0'=2,'dp_1'=4,'dp_2'=2,'tensor_0'=4,'tensor_1'=4] {'tensor_0'}, use_global_device_ids=true, to_apply=%region_10.0 | all-reduce | flops 32 | bytes 256 | tf_op jit(solution)/shard_map/psum | solution.py:56
  139.7 7.8 %psum.39 = f32[32]{0:T(128)S(1)} all-reduce(f32[32]{0:T(128)S(1)} %psum.38), channel_id=1, replica_groups=mesh['dp_0'=2,'dp_1'=4,'dp_2'=2,'tensor_0'=4,'tensor_1'=4] {'tensor_1'}, use_global_device_ids=true, to_apply=%region_11.0 | all-reduce | flops 32 | bytes 256 | tf_op jit(solution)/shard_map/psum | solution.py:56
  147.5 0.0 all-to-all-done.5
  147.5 0.1 select_reduce_fusion
  147.7 0.0 copy-start.10
  147.7 10.9 %all_to_all.51 = bf16[16,128,64]{1,2,0:T(8,128)(2,1)S(1)} all-to-all(bf16[16,128,64]{1,2,0:T(8,128)(2,1)S(1)} %broadcast_in_dim.16), channel_id=1, replica_groups=mesh['dp_0'=2,'dp_1'=4,'dp_2'=2,'tensor_0'=4,'tensor_1'=4] {'tensor_0','..., dimensions={0} | all-to-all | bytes 524288 | tf_op jit(solution)/shard_map/all_to_all | solution.py:25
  158.6 0.2 multiply_reduce_fusion
  158.8 0.2 fusion.22
  159.0 2.9 fusion.51
  161.9 1.9 fusion.45
  163.8 13.5 %all_to_all.52 = f32[16,128,64]{1,2,0:T(8,128)} all-to-all(f32[16,128,64]{1,2,0:T(8,128)S(1)} %bitcast.55), channel_id=1, replica_groups=mesh['dp_0'=2,'dp_1'=4,'dp_2'=2,'tensor_0'=4,'tensor_1'=4] {'tensor_0','..., dimensions={0} | all-to-all | bytes 1048576 | tf_op jit(solution)/shard_map/all_to_all | solution.py:51
  177.3 1.1 reduce_sum.119
  178.4 0.8 broadcast_in_dim.34
  179.1 5.1 %all-to-all-start.8 = ((bf16[16,128,64]{1,2,0:T(8,128)(2,1)}), bf16[16,128,64]{1,2,0:T(8,128)(2,1)S(1)}, u32[]{:S(2)}, u32[]{:S(2)}) async-start(bf16[16,128,64]{1,2,0:T(8,128)(2,1)} %broadcast_in_dim.34), calls=%async_computation.8 | async-start | bytes 524288 | tf_op jit(solution)/shard_map/all_to_all | solution.py:25
  184.2 0.2 reduce-scatter.3.cloned.1.call-start
  184.5 4.4 fusion.49
  188.9 2.9 all-to-all-done.8
  191.8 10.7 %convolution_add_fusion.1 = f32[1024,2048]{1,0:T(8,128)} fusion(f32[1024,2048]{1,0:T(8,128)} %fusion.49, bf16[128,1024]{0,1:T(8,128)(2,1)S(1)} %fusion.22, bf16[128,1024]{0,1:T(8,128)(2,1)S(1)} %bitcast.50, bf16[2048,1024]{1,0:T(8,128)(2,1)} %param.15, f32[128,2048]{1,0:T(8,128)S(1)} %fusion.51), kind=kOutput, calls=%fused_computation.1 | convolution fusion | flops 1080819712 | bytes 22544384 | tf_op jit(solution)/shard_map/dot_general | solution.py:103
  202.5 0.0 reduce-scatter.3.cloned.1.call-update
  202.5 0.0 reduce-scatter.5.cloned.1.call-start
  202.6 0.9 copy-done.4
  203.5 1.3 fusion.43
  204.8 4.5 convolution_add_fusion
  209.3 0.0 reduce-scatter.5.cloned.1.call-update
  209.4 1.3 constant_dynamic-slice_fusion
  210.7 0.2 copy.36
  210.9 138.0 %reduce-scatter.3.cloned.1.call-done = f32[64,2048]{1,0:T(8,128)} async-done(((f32[1024,2048]{1,0:T(8,128)}), f32[64,2048]{1,0:T(8,128)}) %reduce-scatter.3.cloned.1.call-update) | async-done | bytes 524304 | tf_op jit(solution)/shard_map/reduce_scatter | solution.py:123
  348.9 2.1 subtract_convert_fusion.1
  351.0 141.6 %reduce-scatter.5.cloned.1.call-done = f32[2048,64]{0,1:T(8,128)} async-done(((f32[2048,1024]{0,1:T(8,128)}), f32[2048,64]{0,1:T(8,128)}) %reduce-scatter.5.cloned.1.call-update) | async-done | bytes 524304 | tf_op jit(solution)/shard_map/reduce_scatter | solution.py:124
  492.6 2.0 subtract_convert_fusion
  (26 shorter events, 0.3 us)
Async XLA Ops:
  7.2 20.9 %copy-start.1 = (bf16[2048,1024]{1,0:T(8,128)(2,1)S(1)}, bf16[2048,1024]{1,0:T(8,128)(2,1)}, u32[]{:S(2)}) copy-start(bf16[2048,1024]{1,0:T(8,128)(2,1)} %param.15) | copy-start | bytes 12582916
  28.1 19.4 %copy-start.7 = (f32[128,64]{0,1:T(8,128)S(1)}, f32[128,64]{0,1:T(8,128)}, u32[]{:S(2)}) copy-start(f32[128,64]{0,1:T(8,128)} %param.10) | copy-start | bytes 98308
  28.1 19.4 %copy-start.8 = (bf16[128,64]{0,1:T(8,128)(2,1)S(1)}, bf16[128,64]{0,1:T(8,128)(2,1)}, u32[]{:S(2)}) copy-start(bf16[128,64]{0,1:T(8,128)(2,1)} %param.9) | copy-start | bytes 49156
  28.1 19.4 %copy-start.9 = (f32[128,64]{0,1:T(8,128)S(1)}, f32[128,64]{0,1:T(8,128)}, u32[]{:S(2)}) copy-start(f32[128,64]{0,1:T(8,128)} %param.12) | copy-start | bytes 98308
  62.5 4.2 copy-start.3
  62.5 4.2 copy-start
  66.7 7.7 %copy-start.11 = (f32[1024]{0:T(1024)S(1)}, f32[1024]{0:T(1024)}, u32[]{:S(2)}) copy-start(f32[1024]{0:T(1024)} %param.13) | copy-start | bytes 12292
  66.7 32.3 %copy-start.12 = (s32[128]{0:T(128)S(1)}, s32[128]{0:T(128)}, u32[]{:S(2)}) copy-start(s32[128]{0:T(128)} %param.11) | copy-start | bytes 1540
  68.8 17.4 %all-to-all-start.3 = ((f32[16,128,64]{1,2,0:T(8,128)}), f32[16,128,64]{1,2,0:T(8,128)S(1)}, u32[]{:S(2)}, u32[]{:S(2)}) async-start(f32[16,128,64]{1,2,0:T(8,128)} %bitcast.7), calls=%async_computation.3 | async-start | bytes 1048576 | tf_op jit(solution)/shard_map/all_to_all | solution.py:51
  99.7 47.8 %all-to-all-start.5 = ((f32[16,1,32]{2,1,0:T(1,128)}), f32[16,1,32]{2,1,0:T(1,128)S(1)}, u32[]{:S(2)}, u32[]{:S(2)}) async-start(f32[16,1,32]{2,1,0:T(1,128)} %broadcast_in_dim.15), calls=%async_computation.5 | async-start | bytes 16384 | tf_op jit(solution)/shard_map/all_to_all | solution.py:25
  147.5 14.4 %copy-start.2 = (bf16[2048,1024]{1,0:T(8,128)(2,1)S(1)}, bf16[2048,1024]{1,0:T(8,128)(2,1)}, u32[]{:S(2)}) copy-start(bf16[2048,1024]{1,0:T(8,128)(2,1)} %param.15) | copy-start | bytes 12582916
  147.7 30.7 %copy-start.10 = (f32[128,64]{0,1:T(8,128)}, f32[128,64]{0,1:T(8,128)S(1)}, u32[]{:S(2)}) copy-start(f32[128,64]{0,1:T(8,128)S(1)} %get-tuple-element.12) | copy-start | bytes 98308
  179.1 12.7 %all-to-all-start.8 = ((bf16[16,128,64]{1,2,0:T(8,128)(2,1)}), bf16[16,128,64]{1,2,0:T(8,128)(2,1)S(1)}, u32[]{:S(2)}, u32[]{:S(2)}) async-start(bf16[16,128,64]{1,2,0:T(8,128)(2,1)} %broadcast_in_dim.34), calls=%async_computation.8 | async-start | bytes 524288 | tf_op jit(solution)/shard_map/all_to_all | solution.py:25
  184.2 164.7 %reduce-scatter.3.cloned.1.call-start = ((), (), s32[]{:S(2)}) async-start(), calls=%async_computation.11 | async-start | bytes 8912896 | tf_op jit(solution)/shard_map/reduce_scatter | solution.py:123
  202.5 0.9 copy-start.4
  202.5 290.1 %reduce-scatter.5.cloned.1.call-start = ((), (), s32[]{:S(2)}) async-start(), calls=%async_computation.12 | async-start | bytes 8912896 | tf_op jit(solution)/shard_map/reduce_scatter | solution.py:124
  209.3 139.6 %copy-start.5 = (f32[64,2048]{1,0:T(8,128)S(1)}, f32[64,2048]{1,0:T(8,128)}, u32[]{:S(2)}) copy-start(f32[64,2048]{1,0:T(8,128)} %param.16) | copy-start | bytes 1572868
  209.3 283.3 %copy-start.6 = (f32[2048,64]{0,1:T(8,128)S(1)}, f32[2048,64]{0,1:T(8,128)}, u32[]{:S(2)}) copy-start(f32[2048,64]{0,1:T(8,128)} %param.17) | copy-start | bytes 1572868
Sparse Core Ops, SparseCore 0:
  202.7 146.2 reduce-scatter.2
  353.5 139.0 reduce-scatter.4
where the time goes:
time: 505 us; the launch traced here: 501 us
  waiting for transfers between devices  294 us (58%)
  blocking collectives  122 us (24%)
  matrix products  36.9 us (7%)
  starting transfers between devices  22.3 us (4%)
  between operations  14.3 us (3%)
  other arithmetic  8.11 us (2%)
    reduce_scatter x1, waiting for transfers between devices, shards(): lax.psum_scatter(local_out, DP, scatter_dimension=1, tiled=True)  142 us
    reduce_scatter x1, waiting for transfers between devices, shards(): lax.psum_scatter(local_in, DP, scatter_dimension=0, tiled=True)  138 us
    all_to_all x4, blocking collectives, from_everyone(): return lax.all_to_all(copies, axis, split_axis=0, concat_axis=0, tiled=True)  54.2 us
    psum x5, blocking collectives, one_axis_at_a_time(): return functools.reduce(lax.psum, axes, array)  36.5 us
    all_to_all x2, blocking collectives, summed_on_arrival(): lax.all_to_all(in_blocks(array, dim, peers), axis, 0, 0, tiled=True)  31 us
    all_to_all x2, starting transfers between devices, from_everyone(): return lax.all_to_all(copies, axis, split_axis=0, concat_axis=0, tiled=True)  16.4 us
    dot_general x2, matrix products, shards(): part_in = jnp.dot(normed.T, hidden_grad, preferred_element_type=jnp.float32)  15.2 us
    all_to_all x1, waiting for transfers between devices, summed_on_arrival(): lax.all_to_all(in_blocks(array, dim, peers), axis, 0, 0, tiled=True)  11.7 us
  transfers between devices with their start and end apart: 5, of which 4 were waited for; matrix products, arithmetic and copies ran while one was open for 3% of the time, Pallas kernels for 0%

commit v1 on v0

v1 whole, which is shorter than its diff:
```python
import jax
import jax.numpy as jnp
from jax import lax
from jax.sharding import Mesh
from jax.sharding import PartitionSpec as P

D = 1024
ASCENTS = 2
EXAMPLES = 32
DP = ("z_hi", "y", "core")
BLOCKS = ("z_hi", "y")
TENSOR = ("x", "z_lo")

coeff = 0.7978845608
adv_init = 0.5
adv_step = 0.5
decay = 0.9
learn_rate = 0.01


def to_peers(blocks, axis):
    return lax.all_to_all(blocks, axis, 0, 0, tiled=True)


def gathered_features(array):
    copies = jnp.broadcast_to(array, (lax.axis_size(TENSOR), *array.shape))
    blocks = to_peers(copies, TENSOR)
    return jnp.moveaxis(blocks, 0, 1).reshape(array.shape[0], -1)


def feature_blocks(array):
    return jnp.moveaxis(array.reshape(array.shape[0], lax.axis_size(TENSOR), -1), 1, 0)


def from_partner(array, axis):
    return lax.ppermute(array, axis, [(0, 1), (1, 0)])


def gelu_value(values):
    tangent = jnp.tanh(coeff * (values + 0.044715 * values * values * values))
    return 0.5 * values * (1.0 + tangent)


def gelu_slope(values):
    tangent = jnp.tanh(coeff * (values + 0.044715 * values * values * values))
    return 0.5 * (1.0 + tangent) + 0.5 * values * (1.0 - tangent * tangent) * coeff * (
        1.0 + 3.0 * 0.044715 * values * values
    )


def over_neighbours(sums):
    count = lax.axis_size(BLOCKS)
    sums = sums + from_partner(sums, "core")
    before = lax.ppermute(sums, BLOCKS, [(i, i + 1) for i in range(count - 1)])
    after = lax.ppermute(sums, BLOCKS, [(i + 1, i) for i in range(count - 1)])
    return sums + before + after


def halves(array, core):
    width = array.shape[1] // 2
    own = lax.dynamic_slice_in_dim(array, core * width, width, 1)
    other = lax.dynamic_slice_in_dim(array, (1 - core) * width, width, 1)
    return own, other


def summed_over_dp(left, right):
    core, z_hi = lax.axis_index("core"), lax.axis_index("z_hi")
    n_z, n_y = lax.axis_size("z_hi"), lax.axis_size("y")
    half = right.shape[1]
    partial = lax.dot_general(
        left, right, (((0,), (0,)), ((), ())), preferred_element_type=jnp.float32
    ).astype(jnp.bfloat16)
    blocks = jnp.moveaxis(partial.reshape(n_z, n_y, -1, half), 1, 0)
    blocks = to_peers(blocks, "y").astype(jnp.float32)
    sums = jnp.sum(blocks, axis=0)
    own = lax.dynamic_index_in_dim(sums, z_hi, 0, keepdims=False)
    other = lax.dynamic_index_in_dim(sums, 1 - z_hi, 0, keepdims=False)
    rows = own + from_partner(other.astype(jnp.bfloat16), "z_hi").astype(jnp.float32)
    few = rows.shape[0] // 2
    mine = lax.dynamic_slice_in_dim(rows, core * few, few, 0)
    theirs = from_partner(lax.dynamic_slice_in_dim(rows, (1 - core) * few, few, 0), "core")
    return jnp.where(
        core == 0, jnp.concatenate([mine, theirs], 1), jnp.concatenate([theirs, mine], 1)
    )


def shards(
    tokens, init_noise, segment_ids, target, norm_gain, weight_in, weight_out, moment_in, moment_out
):
    dp_count = lax.axis_size(DP)
    local_tokens, width_local = tokens.shape
    loss_scale = (local_tokens * dp_count) ** (-0.5)
    column = lax.axis_index(TENSOR)
    core = lax.axis_index("core")
    gain_local = lax.dynamic_slice_in_dim(norm_gain, column * width_local, width_local)
    labels = jnp.arange(EXAMPLES, dtype=jnp.int32)
    onehot = (segment_ids[:, None] == labels[None, :]).astype(jnp.float32)
    perturb = adv_init * init_noise
    embedded = tokens.astype(jnp.float32) + perturb
    whole = gathered_features(embedded)
    lefts_in, rights_in, lefts_out, rights_out = [], [], [], []
    for ascent in range(ASCENTS):
        emb = lax.optimization_barrier(whole.astype(jnp.bfloat16)).astype(jnp.float32)
        inv_rms = lax.rsqrt(jnp.mean(emb * emb, axis=1, keepdims=True) + 1e-06)
        normed = (emb * inv_rms * norm_gain).astype(jnp.bfloat16)
        preact = jnp.dot(normed, weight_in, preferred_element_type=jnp.float32)
        hidden = gelu_value(preact).astype(jnp.bfloat16)
        partial_value = jnp.dot(hidden, weight_out, preferred_element_type=jnp.float32)
        mixed = jnp.sum(to_peers(feature_blocks(partial_value), TENSOR), axis=0)
        out_grad = (embedded + mixed - target) * loss_scale
        grad_whole = gathered_features(out_grad.astype(jnp.bfloat16))
        hidden_grad = (
            jnp.dot(grad_whole, weight_out.T, preferred_element_type=jnp.float32)
            * gelu_slope(preact)
        ).astype(jnp.bfloat16)
        hidden_own, hidden_other = halves(hidden, core)
        slope_own, slope_other = halves(hidden_grad, core)
        lefts_in += [normed, from_partner(normed, "core")]
        rights_in += [slope_own, from_partner(slope_other, "core")]
        lefts_out += [grad_whole, from_partner(grad_whole, "core")]
        rights_out += [hidden_own, from_partner(hidden_other, "core")]
        if ascent + 1 < ASCENTS:
            normed_partial = jnp.dot(hidden_grad, weight_in.T, preferred_element_type=jnp.float32)
            dot_partial = jnp.sum(normed_partial * norm_gain * emb, axis=1)
            blocks = jnp.concatenate(
                [
                    feature_blocks(normed_partial),
                    jnp.broadcast_to(
                        dot_partial[None, :, None], (lax.axis_size(TENSOR), local_tokens, 1)
                    ),
                ],
                axis=2,
            )
            arrived = jnp.sum(to_peers(blocks, TENSOR), axis=0)
            scaled = arrived[:, :width_local] * gain_local
            row_dot = arrived[:, width_local:]
            emb_local = embedded.astype(jnp.bfloat16).astype(jnp.float32)
            delta_grad = (
                out_grad + inv_rms * scaled - emb_local * inv_rms * inv_rms * inv_rms * row_dot / D
            )
            delta_whole = gathered_features(delta_grad)
            row_squares = jnp.sum(delta_whole * delta_whole, axis=1)
            sums = jnp.stack(
                [jnp.sum(onehot * row_squares[:, None], axis=0), jnp.sum(onehot, axis=0)]
            )
            square_sums, counts = over_neighbours(sums)
            root_mean = jnp.sqrt(square_sums / (jnp.maximum(counts, 1.0) * D) + 1e-06)
            token_scale = jnp.sum(onehot * (adv_step / root_mean)[None, :], axis=1)[:, None]
            perturb = perturb + delta_grad * token_scale
            embedded = tokens.astype(jnp.float32) + perturb
            whole = whole + delta_whole * token_scale
    summed_out = summed_over_dp(
        jnp.concatenate(lefts_out, 0), jnp.concatenate(rights_out, 0)
    ).T
    summed_in = summed_over_dp(jnp.concatenate(lefts_in, 0), jnp.concatenate(rights_in, 0))
    dp_rows = moment_in.shape[0]
    offset = lax.axis_index(DP) * dp_rows
    own_in = lax.dynamic_slice_in_dim(weight_in, offset, dp_rows, 0)
    own_out = lax.dynamic_slice_in_dim(weight_out, offset, dp_rows, 1)
    new_moment_in = decay * moment_in + summed_in / ASCENTS
    new_moment_out = decay * moment_out + summed_out / ASCENTS
    new_weight_in = (own_in.astype(jnp.float32) - learn_rate * new_moment_in).astype(jnp.bfloat16)
    new_weight_out = (own_out.astype(jnp.float32) - learn_rate * new_moment_out).astype(
        jnp.bfloat16
    )
    return (new_weight_in, new_weight_out, new_moment_in, new_moment_out, perturb)


def solution(mesh):
    torus = Mesh(mesh.devices.reshape(2, 4, 2, 4, 4), DP + TENSOR)
    in_specs = (
        P(DP, TENSOR),
        P(DP, TENSOR),
        P(DP),
        P(DP, TENSOR),
        P(),
        P(None, TENSOR),
        P(TENSOR, None),
        P(DP, TENSOR),
        P(TENSOR, DP),
    )
    out_specs = (P(DP, TENSOR), P(TENSOR, DP), P(DP, TENSOR), P(TENSOR, DP), P(DP, TENSOR))
    return jax.shard_map(
        shards, mesh=torus, in_specs=in_specs, out_specs=out_specs, check_vma=False
    )
```

time: 505 us -> 264 us (0.52)
  waiting for transfers between devices: 294 us -> 66.4 us
  starting transfers between devices: 22.3 us -> 63.7 us
  blocking collectives: 122 us -> 88.7 us
  between operations: 14.3 us -> 1.02 us
  matrix products: 36.9 us -> 25.9 us
    reduce_scatter x2 -> x0, waiting for transfers between devices: 280 us -> none  [the longest x1 142 us: shards(): lax.psum_scatter(local_out, DP, scatter_dimension=1, tiled=True)]
    all_to_all x3 -> x4, waiting for transfers between devices: 14.6 us -> 53.1 us  [to_peers(): return lax.all_to_all(blocks, axis, 0, 0, tiled=True)]
    psum x5 -> x0, blocking collectives: 36.5 us -> none  [one_axis_at_a_time(): return functools.reduce(lax.psum, axes, array)]
    ppermute x0 -> x15, starting transfers between devices: none -> 36 us  [the longest x13 30.7 us: from_partner(): return lax.ppermute(array, axis, [(0, 1), (1, 0)])]
    dot_general x4 -> x2, matrix products: 21 us -> 3.5 us  [summed_over_dp(): lax.dot_general(left, right, (((0,), (0,)), ((), ())), preferred_element_...]
    ppermute x0 -> x15, waiting for transfers between devices: none -> 13.3 us  [the longest x13 12.8 us: from_partner(): return lax.ppermute(array, axis, [(0, 1), (1, 0)])]
    all_to_all x3 -> x4, starting transfers between devices: 22 us -> 27.7 us  [to_peers(): return lax.all_to_all(blocks, axis, 0, 0, tiled=True)]
    all_to_all x6 -> x5, blocking collectives: 85.2 us -> 88.7 us  [to_peers(): return lax.all_to_all(blocks, axis, 0, 0, tiled=True)]
  transfers between devices with their start and end apart: 5 -> 19, of which waited for: 4 -> 12; matrix products, arithmetic and copies ran while one was open for 3% -> 5% of each run, Pallas kernels for 0% -> 0%
where the time goes in v1:
time: 264 us; the launch traced here: 263 us
  blocking collectives  88.7 us (34%)
  waiting for transfers between devices  66.4 us (25%)
  starting transfers between devices  63.7 us (24%)
  matrix products  25.9 us (10%)
  other arithmetic  9.19 us (3%)
  local copies, waits for them, and re-layouts  7.86 us (3%)
    all_to_all x5, blocking collectives, to_peers(): return lax.all_to_all(blocks, axis, 0, 0, tiled=True)  88.7 us
    all_to_all x4, waiting for transfers between devices, to_peers(): return lax.all_to_all(blocks, axis, 0, 0, tiled=True)  53.1 us
    ppermute x13, starting transfers between devices, from_partner(): return lax.ppermute(array, axis, [(0, 1), (1, 0)])  30.7 us
    all_to_all x4, starting transfers between devices, to_peers(): return lax.all_to_all(blocks, axis, 0, 0, tiled=True)  27.7 us
    ppermute x13, waiting for transfers between devices, from_partner(): return lax.ppermute(array, axis, [(0, 1), (1, 0)])  12.8 us
    dot_general x2, matrix products, shards(): jnp.dot(grad_whole, weight_out.T, preferred_element_type=jnp.float32)  8.76 us
    dot_general x2, matrix products, shards(): preact = jnp.dot(normed, weight_in, preferred_element_type=jnp.float32)  8.42 us
  transfers between devices with their start and end apart: 19, of which 12 were waited for; matrix products, arithmetic and copies ran while one was open for 5% of the time, Pallas kernels for 0%

profile of v1, /device:TPU:33, one launch (start us, length us, event | category | flops | bytes accessed | tf_op | source)
XLA Modules:
  0.0 262.8 jit_solution(18353719513217070673)
XLA Ops:
  0.6 0.8 convert_add_fusion.1
  1.5 20.2 %all_to_all.45 = f32[16,128,64]{1,2,0:T(8,128)S(1)} all-to-all(f32[16,128,64]{1,2,0:T(8,128)S(1)} %broadcast_in_dim.10), channel_id=1, replica_groups=mesh['z_hi'=2,'y'=4,'core'=2,'x'=4,'z_lo'=4] {'x','z_lo'}, dimensions={0} | all-to-all | bytes 1048576 | tf_op jit(solution)/shard_map/all_to_all | solution.py:22
  21.7 0.2 copy.35
  21.9 0.1 fusion.43
  22.2 4.2 %multiply_convert_fusion.1 = (bf16[128,2048]{1,0:T(8,128)(2,1)S(1)}, f32[128,2048]{1,0:T(8,128)}) fusion(bf16[128,1024]{1,0:T(8,128)(2,1)S(1)} %fusion.45, bf16[1024,2048]{1,0:T(8,128)(2,1)} %param.14), kind=kOutput, calls=%fused_computation.53 | convolution fusion | flops 539230208 | bytes 6029312 | tf_op jit(solution)/shard_map/dot_general | solution.py:106
  26.4 1.8 fusion.68
  28.2 18.5 %all_to_all.46 = f32[16,128,64]{1,2,0:T(8,128)S(1)} all-to-all(f32[16,128,64]{1,2,0:T(8,128)S(1)} %bitcast.68), channel_id=1, replica_groups=mesh['z_hi'=2,'y'=4,'core'=2,'x'=4,'z_lo'=4] {'x','z_lo'}, dimensions={0} | all-to-all | bytes 1048576 | tf_op jit(solution)/shard_map/all_to_all | solution.py:22
  46.8 14.8 %all_to_all.47 = bf16[16,128,64]{1,2,0:T(8,128)(2,1)S(1)} all-to-all(bf16[16,128,64]{1,2,0:T(8,128)(2,1)S(1)} %broadcast_in_dim.11), channel_id=1, replica_groups=mesh['z_hi'=2,'y'=4,'core'=2,'x'=4,'z_lo'=4] {'x','z_lo'}, dimensions={0} | all-to-all | bytes 524288 | tf_op jit(solution)/shard_map/all_to_all | solution.py:22
  61.7 0.7 copy-done.6
  62.4 4.5 %fusion = bf16[128,2048]{1,0:T(8,128)(2,1)S(1)} fusion(bf16[128,1024]{0,1:T(8,128)(2,1)S(1)} %bitcast.74, bf16[2048,1024]{1,0:T(8,128)(2,1)} %param.15, f32[128,2048]{1,0:T(8,128)} %get-tuple-element.26), kind=kOutput, calls=%fused_computation.4 | convolution fusion | flops 541851648 | bytes 6029312 | tf_op jit(solution)/shard_map/dot_general | solution.py:113
  66.8 1.6 fusion.46
  68.5 0.2 copy.37
  68.7 0.9 pad_maximum_fusion
  69.5 5.8 %all-to-all-start.3 = ((f32[16,128,65]{1,2,0:T(8,128)}), f32[16,128,65]{1,2,0:T(8,128)S(1)}, u32[]{:S(2)}, u32[]{:S(2)}) async-start(f32[16,128,65]{1,2,0:T(8,128)} %pad_maximum_fusion), calls=%async_computation.3 | async-start | bytes 1179648 | tf_op jit(solution)/shard_map/all_to_all | solution.py:22
  75.4 13.1 %all-to-all-done.3 = f32[16,128,65]{1,2,0:T(8,128)S(1)} async-done(((f32[16,128,65]{1,2,0:T(8,128)}), f32[16,128,65]{1,2,0:T(8,128)S(1)}, u32[]{:S(2)}, u32[]{:S(2)}) %all-to-all-start.3) | async-done | bytes 532512 | tf_op jit(solution)/shard_map/all_to_all | solution.py:22
  88.7 18.8 %all_to_all.48 = f32[16,128,64]{1,2,0:T(8,128)S(1)} all-to-all(f32[16,128,64]{1,2,0:T(8,128)S(1)} %broadcast_in_dim.13), channel_id=1, replica_groups=mesh['z_hi'=2,'y'=4,'core'=2,'x'=4,'z_lo'=4] {'x','z_lo'}, dimensions={0} | all-to-all | bytes 1048576 | tf_op jit(solution)/shard_map/all_to_all | solution.py:22
  107.5 0.2 fusion.52
  107.8 3.9 %collective-permute-start.1 = (f32[2,32]{1,0:T(2,128)S(1)}, f32[2,32]{1,0:T(2,128)S(1)}, u32[]{:S(2)}, u32[]{:S(2)}) collective-permute-start(f32[2,32]{1,0:T(2,128)S(1)} %pad_maximum_fusion.1), channel_id=1, source_target_pairs={{0,16},{16,0},{1,17},{17,1},{2,18},{18,2},{3,19},{19,3},{4,20},{20... | collective-permute-start | bytes 776 | tf_op jit(solution)/shard_map/ppermute | solution.py:36
  111.6 0.8 collective-permute-done.1
  112.5 1.3 collective-permute-start.3
  113.8 4.0 %collective-permute-start.2 = (f32[2,32]{1,0:T(2,128)S(1)}, f32[2,32]{1,0:T(2,128)S(1)}, u32[]{:S(2)}, u32[]{:S(2)}) collective-permute-start(f32[2,32]{1,0:T(2,128)S(1)} %fusion.65), channel_id=1, source_target_pairs={{0,32},{32,64},{64,96},{96,128},{128,160},{160,192},{192,224},{1,3... | collective-permute-start | bytes 776 | tf_op jit(solution)/shard_map/ppermute | solution.py:54
  117.8 0.2 copy.38
  118.0 0.5 collective-permute-done.2
  118.7 0.1 fusion.40
  118.9 0.1 fusion.42
  119.0 4.2 %multiply_convert_fusion = (bf16[128,2048]{1,0:T(8,128)(2,1)S(1)}, f32[128,2048]{1,0:T(8,128)}) fusion(bf16[128,1024]{1,0:T(8,128)(2,1)S(1)} %fusion.42, bf16[1024,2048]{1,0:T(8,128)(2,1)} %param.14), kind=kOutput, calls=%fused_computation.52 | convolution fusion | flops 539230208 | bytes 6029312 | tf_op jit(solution)/shard_map/dot_general | solution.py:106
  123.2 1.8 fusion.69
  125.0 16.4 %all_to_all.49 = f32[16,128,64]{1,2,0:T(8,128)S(1)} all-to-all(f32[16,128,64]{1,2,0:T(8,128)S(1)} %bitcast.69), channel_id=1, replica_groups=mesh['z_hi'=2,'y'=4,'core'=2,'x'=4,'z_lo'=4] {'x','z_lo'}, dimensions={0} | all-to-all | bytes 1048576 | tf_op jit(solution)/shard_map/all_to_all | solution.py:22
  141.4 0.6 fusion.58
  142.1 0.8 broadcast_in_dim.14
  142.8 7.3 %all-to-all-start.6 = ((bf16[16,128,64]{1,2,0:T(8,128)(2,1)}), bf16[16,128,64]{1,2,0:T(8,128)(2,1)S(1)}, u32[]{:S(2)}, u32[]{:S(2)}) async-start(bf16[16,128,64]{1,2,0:T(8,128)(2,1)} %broadcast_in_dim.14), calls=%async_computation.6 | async-start | bytes 524288 | tf_op jit(solution)/shard_map/all_to_all | solution.py:22
  150.1 2.0 collective-permute-start
  152.3 0.5 collective-permute-start.4
  152.8 5.1 %all-to-all-done.6 = bf16[16,128,64]{1,2,0:T(8,128)(2,1)S(1)} async-done(((bf16[16,128,64]{1,2,0:T(8,128)(2,1)}), bf16[16,128,64]{1,2,0:T(8,128)(2,1)S(1)}, u32[]{:S(2)}, u32[]{:S(2)}) %all-to-all-start.6) | async-done | bytes 262176 | tf_op jit(solution)/shard_map/all_to_all | solution.py:22
  158.0 0.7 copy-done.8
  158.7 4.3 %fusion.1 = bf16[128,2048]{1,0:T(8,128)(2,1)S(1)} fusion(bf16[128,1024]{0,1:T(8,128)(2,1)S(1)} %bitcast.77, bf16[2048,1024]{1,0:T(8,128)(2,1)} %param.15, f32[128,2048]{1,0:T(8,128)} %get-tuple-element.30), kind=kOutput, calls=%fused_computation.5 | convolution fusion | flops 541851648 | bytes 6029312 | tf_op jit(solution)/shard_map/dot_general | solution.py:113
  163.0 2.8 %collective-permute-start.6 = (bf16[128,1024]{1,0:T(8,128)(2,1)S(1)}, bf16[128,1024]{1,0:T(8,128)(2,1)S(1)}, u32[]{:S(2)}, u32[]{:S(2)}) collective-permute-start(bf16[128,1024]{1,0:T(8,128)(2,1)S(1)} %get-tuple-element.24), channel_id=1, source_target_pairs={{0,16},{16,0},{1,17},{17,1},{2,18},{18,2},{3,19},{19,3},{4,20},{20... | collective-permute-start | bytes 786440 | tf_op jit(solution)/shard_map/ppermute | solution.py:36
  165.8 1.1 collective-permute-done.6
  167.0 2.2 convolution_convert_fusion.1
  169.2 1.6 copy.50
  170.8 10.2 %all-to-all-start.7 = ((bf16[4,2,128,1024]{3,2,1,0:T(8,128)(2,1)}), bf16[4,2,128,1024]{3,2,1,0:T(8,128)(2,1)S(1)}, u32[]{:S(2)}, u32[]{:S(2)}) async-start(bf16[4,2,128,1024]{3,2,1,0:T(8,128)(2,1)} %bitcast.66), calls=%async_computation.7 | async-start | bytes 4194304 | tf_op jit(solution)/shard_map/all_to_all | solution.py:22
  181.0 0.7 collective-permute-start.11
  181.8 0.5 collective-permute-start.12
  182.3 0.2 collective-permute-start.10
  182.5 0.3 collective-permute-done.11
  182.9 0.4 collective-permute-done.9
  183.2 0.4 collective-permute-done.12
  183.6 0.4 collective-permute-done.10
  184.0 1.3 convolution_convert_fusion
  185.2 1.5 copy.49
  186.8 19.9 %all-to-all-done.7 = bf16[4,2,128,1024]{3,2,1,0:T(8,128)(2,1)S(1)} async-done(((bf16[4,2,128,1024]{3,2,1,0:T(8,128)(2,1)}), bf16[4,2,128,1024]{3,2,1,0:T(8,128)(2,1)S(1)}, u32[]{:S(2)}, u32[]{:S(2)}) %all-to-all-start.7) | async-done | bytes 2097184 | tf_op jit(solution)/shard_map/all_to_all | solution.py:22
  206.7 4.4 %all-to-all-start.8 = ((bf16[4,2,128,1024]{3,2,1,0:T(8,128)(2,1)}), bf16[4,2,128,1024]{3,2,1,0:T(8,128)(2,1)}, u32[]{:S(2)}, u32[]{:S(2)}) async-start(bf16[4,2,128,1024]{3,2,1,0:T(8,128)(2,1)} %bitcast.65), calls=%async_computation.8 | async-start | bytes 4194304 | tf_op jit(solution)/shard_map/all_to_all | solution.py:22
  211.1 1.3 constant_dynamic-slice_fusion.6
  212.4 0.2 copy.46
  212.6 0.4 convert_reduce_fusion.1
  213.0 8.0 %collective-permute-start.7 = (bf16[128,1024]{1,0:T(8,128)(2,1)S(1)}, bf16[128,1024]{1,0:T(8,128)(2,1)S(1)}, u32[]{:S(2)}, u32[]{:S(2)}) collective-permute-start(bf16[128,1024]{1,0:T(8,128)(2,1)S(1)} %fusion.53), channel_id=1, source_target_pairs={{0,128},{128,0},{1,129},{129,1},{2,130},{130,2},{3,131},{131,3},{4... | collective-permute-start | bytes 786440 | tf_op jit(solution)/shard_map/ppermute | solution.py:36
  221.0 15.0 %all-to-all-done.8 = bf16[4,2,128,1024]{3,2,1,0:T(8,128)(2,1)} async-done(((bf16[4,2,128,1024]{3,2,1,0:T(8,128)(2,1)}), bf16[4,2,128,1024]{3,2,1,0:T(8,128)(2,1)}, u32[]{:S(2)}, u32[]{:S(2)}) %all-to-all-start.8) | async-done | bytes 2097184 | tf_op jit(solution)/shard_map/all_to_all | solution.py:22
  236.0 2.1 convert_reduce_fusion
  238.2 8.3 %collective-permute-start.13 = (bf16[128,1024]{1,0:T(8,128)(2,1)S(1)}, bf16[128,1024]{1,0:T(8,128)(2,1)S(1)}, u32[]{:S(2)}, u32[]{:S(2)}) collective-permute-start(bf16[128,1024]{1,0:T(8,128)(2,1)S(1)} %fusion.54), channel_id=1, source_target_pairs={{0,128},{128,0},{1,129},{129,1},{2,130},{130,2},{3,131},{131,3},{4... | collective-permute-start | bytes 786440 | tf_op jit(solution)/shard_map/ppermute | solution.py:36
  246.7 2.5 collective-permute-start.8
  249.2 9.4 %collective-permute-done.13 = bf16[128,1024]{1,0:T(8,128)(2,1)S(1)} collective-permute-done((bf16[128,1024]{1,0:T(8,128)(2,1)S(1)}, bf16[128,1024]{1,0:T(8,128)(2,1)S(1)}, u32[]{:S(2)}, u32[]{:S(2)}) %collective-permute-start.13) | collective-permute-done | bytes 262176 | tf_op jit(solution)/shard_map/ppermute | solution.py:36
  258.7 1.1 collective-permute-start.14
  259.8 2.0 subtract_convert_fusion.1
  261.8 1.0 subtract_convert_fusion
  (67 shorter events, 1.7 us)
Async XLA Ops:
  0.6 21.4 %copy-start.12 = (f32[1024]{0:T(1024)S(1)}, f32[1024]{0:T(1024)}, u32[]{:S(2)}) copy-start(f32[1024]{0:T(1024)} %param.13) | copy-start | bytes 12292
  22.2 4.2 %copy-start = (bf16[2048,1024]{1,0:T(8,128)(2,1)S(1)}, bf16[2048,1024]{1,0:T(8,128)(2,1)}, u32[]{:S(2)}) copy-start(bf16[2048,1024]{1,0:T(8,128)(2,1)} %param.15) | copy-start | bytes 12582916
  26.4 20.3 %copy-start.5 = (f32[128,64]{0,1:T(8,128)S(1)}, f32[128,64]{0,1:T(8,128)}, u32[]{:S(2)}) copy-start(f32[128,64]{0,1:T(8,128)} %param.12) | copy-start | bytes 98308
  61.7 0.7 copy-start.6
  62.4 4.5 %copy-start.2 = (bf16[1024,2048]{1,0:T(8,128)(2,1)S(1)}, bf16[1024,2048]{1,0:T(8,128)(2,1)}, u32[]{:S(2)}) copy-start(bf16[1024,2048]{1,0:T(8,128)(2,1)} %param.14) | copy-start | bytes 12582916
  69.5 38.1 %copy-start.13 = (s32[128]{0:T(128)S(1)}, s32[128]{0:T(128)}, u32[]{:S(2)}) copy-start(s32[128]{0:T(128)} %param.11) | copy-start | bytes 1540
  69.5 19.0 %all-to-all-start.3 = ((f32[16,128,65]{1,2,0:T(8,128)}), f32[16,128,65]{1,2,0:T(8,128)S(1)}, u32[]{:S(2)}, u32[]{:S(2)}) async-start(f32[16,128,65]{1,2,0:T(8,128)} %pad_maximum_fusion), calls=%async_computation.3 | async-start | bytes 1179648 | tf_op jit(solution)/shard_map/all_to_all | solution.py:22
  107.8 4.7 %collective-permute-start.1 = (f32[2,32]{1,0:T(2,128)S(1)}, f32[2,32]{1,0:T(2,128)S(1)}, u32[]{:S(2)}, u32[]{:S(2)}) collective-permute-start(f32[2,32]{1,0:T(2,128)S(1)} %pad_maximum_fusion.1), channel_id=1, source_target_pairs={{0,16},{16,0},{1,17},{17,1},{2,18},{18,2},{3,19},{19,3},{4,20},{20... | collective-permute-start | bytes 776 | tf_op jit(solution)/shard_map/ppermute | solution.py:36
  112.5 5.5 %collective-permute-start.3 = (f32[2,32]{1,0:T(2,128)S(1)}, f32[2,32]{1,0:T(2,128)S(1)}, u32[]{:S(2)}, u32[]{:S(2)}) collective-permute-start(f32[2,32]{1,0:T(2,128)S(1)} %fusion.65), channel_id=1, source_target_pairs={{32,0},{64,32},{96,64},{128,96},{160,128},{192,160},{224,192},{33,... | collective-permute-start | bytes 776 | tf_op jit(solution)/shard_map/ppermute | solution.py:55
  113.8 4.7 %collective-permute-start.2 = (f32[2,32]{1,0:T(2,128)S(1)}, f32[2,32]{1,0:T(2,128)S(1)}, u32[]{:S(2)}, u32[]{:S(2)}) collective-permute-start(f32[2,32]{1,0:T(2,128)S(1)} %fusion.65), channel_id=1, source_target_pairs={{0,32},{32,64},{64,96},{96,128},{128,160},{160,192},{192,224},{1,3... | collective-permute-start | bytes 776 | tf_op jit(solution)/shard_map/ppermute | solution.py:54
  119.0 4.2 %copy-start.1 = (bf16[2048,1024]{1,0:T(8,128)(2,1)S(1)}, bf16[2048,1024]{1,0:T(8,128)(2,1)}, u32[]{:S(2)}) copy-start(bf16[2048,1024]{1,0:T(8,128)(2,1)} %param.15) | copy-start | bytes 12582916
  123.2 18.2 %copy-start.10 = (f32[128,64]{0,1:T(8,128)S(1)}, f32[128,64]{0,1:T(8,128)}, u32[]{:S(2)}) copy-start(f32[128,64]{0,1:T(8,128)} %param.10) | copy-start | bytes 98308
  123.2 18.2 %copy-start.11 = (bf16[128,64]{0,1:T(8,128)(2,1)S(1)}, bf16[128,64]{0,1:T(8,128)(2,1)}, u32[]{:S(2)}) copy-start(bf16[128,64]{0,1:T(8,128)(2,1)} %param.9) | copy-start | bytes 49156
  142.8 15.1 %all-to-all-start.6 = ((bf16[16,128,64]{1,2,0:T(8,128)(2,1)}), bf16[16,128,64]{1,2,0:T(8,128)(2,1)S(1)}, u32[]{:S(2)}, u32[]{:S(2)}) async-start(bf16[16,128,64]{1,2,0:T(8,128)(2,1)} %broadcast_in_dim.14), calls=%async_computation.6 | async-start | bytes 524288 | tf_op jit(solution)/shard_map/all_to_all | solution.py:22
  150.1 15.6 %collective-permute-start = (bf16[128,1024]{1,0:T(8,128)(2,1)S(1)}, bf16[128,1024]{1,0:T(8,128)(2,1)}, u32[]{:S(2)}, u32[]{:S(2)}) collective-permute-start(bf16[128,1024]{1,0:T(8,128)(2,1)S(1)} %fusion.45), channel_id=1, source_target_pairs={{0,16},{16,0},{1,17},{17,1},{2,18},{18,2},{3,19},{19,3},{4,20},{20... | collective-permute-start | bytes 786440 | tf_op jit(solution)/shard_map/ppermute | solution.py:36
  152.2 13.6 %collective-permute-start.5 = (bf16[128,1024]{1,0:T(8,128)(2,1)S(1)}, bf16[128,1024]{1,0:T(8,128)(2,1)S(1)}, u32[]{:S(2)}, u32[]{:S(2)}) collective-permute-start(bf16[128,1024]{1,0:T(8,128)(2,1)S(1)} %get-tuple-element.22), channel_id=1, source_target_pairs={{0,16},{16,0},{1,17},{17,1},{2,18},{18,2},{3,19},{19,3},{4,20},{20... | collective-permute-start | bytes 786440 | tf_op jit(solution)/shard_map/ppermute | solution.py:36
  152.3 13.5 %collective-permute-start.4 = (bf16[128,1024]{1,0:T(8,128)(2,1)S(1)}, bf16[128,1024]{1,0:T(8,128)(2,1)S(1)}, u32[]{:S(2)}, u32[]{:S(2)}) collective-permute-start(bf16[128,1024]{1,0:T(8,128)(2,1)S(1)} %fusion.42), channel_id=1, source_target_pairs={{0,16},{16,0},{1,17},{17,1},{2,18},{18,2},{3,19},{19,3},{4,20},{20... | collective-permute-start | bytes 786440 | tf_op jit(solution)/shard_map/ppermute | solution.py:36
  157.9 0.7 copy-start.8
  163.0 3.9 %collective-permute-start.6 = (bf16[128,1024]{1,0:T(8,128)(2,1)S(1)}, bf16[128,1024]{1,0:T(8,128)(2,1)S(1)}, u32[]{:S(2)}, u32[]{:S(2)}) collective-permute-start(bf16[128,1024]{1,0:T(8,128)(2,1)S(1)} %get-tuple-element.24), channel_id=1, source_target_pairs={{0,16},{16,0},{1,17},{17,1},{2,18},{18,2},{3,19},{19,3},{4,20},{20... | collective-permute-start | bytes 786440 | tf_op jit(solution)/shard_map/ppermute | solution.py:36
  170.8 10.9 %copy-start.7 = (bf16[16,128,64]{1,2,0:T(8,128)(2,1)S(1)}, bf16[16,128,64]{1,2,0:T(8,128)(2,1)}, u32[]{:S(2)}) copy-start(bf16[16,128,64]{1,2,0:T(8,128)(2,1)} %copy-done.6) | copy-start | bytes 786436
  170.8 35.9 %all-to-all-start.7 = ((bf16[4,2,128,1024]{3,2,1,0:T(8,128)(2,1)}), bf16[4,2,128,1024]{3,2,1,0:T(8,128)(2,1)S(1)}, u32[]{:S(2)}, u32[]{:S(2)}) async-start(bf16[4,2,128,1024]{3,2,1,0:T(8,128)(2,1)} %bitcast.66), calls=%async_computation.7 | async-start | bytes 4194304 | tf_op jit(solution)/shard_map/all_to_all | solution.py:22
  180.9 1.4 copy-start.9
  181.0 1.9 collective-permute-start.11
  181.7 1.5 collective-permute-start.9
  181.8 1.8 collective-permute-start.12
  182.3 1.6 collective-permute-start.10
  206.7 29.4 %all-to-all-start.8 = ((bf16[4,2,128,1024]{3,2,1,0:T(8,128)(2,1)}), bf16[4,2,128,1024]{3,2,1,0:T(8,128)(2,1)}, u32[]{:S(2)}, u32[]{:S(2)}) async-start(bf16[4,2,128,1024]{3,2,1,0:T(8,128)(2,1)} %bitcast.65), calls=%async_computation.8 | async-start | bytes 4194304 | tf_op jit(solution)/shard_map/all_to_all | solution.py:22
  213.0 33.5 %collective-permute-start.7 = (bf16[128,1024]{1,0:T(8,128)(2,1)S(1)}, bf16[128,1024]{1,0:T(8,128)(2,1)S(1)}, u32[]{:S(2)}, u32[]{:S(2)}) collective-permute-start(bf16[128,1024]{1,0:T(8,128)(2,1)S(1)} %fusion.53), channel_id=1, source_target_pairs={{0,128},{128,0},{1,129},{129,1},{2,130},{130,2},{3,131},{131,3},{4... | collective-permute-start | bytes 786440 | tf_op jit(solution)/shard_map/ppermute | solution.py:36
  238.2 21.6 %copy-start.4 = (f32[64,2048]{1,0:T(8,128)S(1)}, f32[64,2048]{1,0:T(8,128)}, u32[]{:S(2)}) copy-start(f32[64,2048]{1,0:T(8,128)} %param.16) | copy-start | bytes 1572868
  238.2 20.4 %collective-permute-start.13 = (bf16[128,1024]{1,0:T(8,128)(2,1)S(1)}, bf16[128,1024]{1,0:T(8,128)(2,1)S(1)}, u32[]{:S(2)}, u32[]{:S(2)}) collective-permute-start(bf16[128,1024]{1,0:T(8,128)(2,1)S(1)} %fusion.54), channel_id=1, source_target_pairs={{0,128},{128,0},{1,129},{129,1},{2,130},{130,2},{3,131},{131,3},{4... | collective-permute-start | bytes 786440 | tf_op jit(solution)/shard_map/ppermute | solution.py:36
  246.7 15.1 %copy-start.3 = (f32[2048,64]{0,1:T(8,128)S(1)}, f32[2048,64]{0,1:T(8,128)}, u32[]{:S(2)}) copy-start(f32[2048,64]{0,1:T(8,128)} %param.17) | copy-start | bytes 1572868
  246.7 13.1 %collective-permute-start.8 = (f32[64,1024]{1,0:T(8,128)S(1)}, f32[64,1024]{1,0:T(8,128)S(1)}, u32[]{:S(2)}, u32[]{:S(2)}) collective-permute-start(f32[64,1024]{1,0:T(8,128)S(1)} %get-tuple-element.19), channel_id=1, source_target_pairs={{0,16},{16,0},{1,17},{17,1},{2,18},{18,2},{3,19},{19,3},{4,20},{20... | collective-permute-start | bytes 786440 | tf_op jit(solution)/shard_map/ppermute | solution.py:36
  258.7 3.1 %collective-permute-start.14 = (f32[64,1024]{1,0:T(8,128)S(1)}, f32[64,1024]{1,0:T(8,128)S(1)}, u32[]{:S(2)}, u32[]{:S(2)}) collective-permute-start(f32[64,1024]{1,0:T(8,128)S(1)} %get-tuple-element.13), channel_id=1, source_target_pairs={{0,16},{16,0},{1,17},{17,1},{2,18},{18,2},{3,19},{19,3},{4,20},{20... | collective-permute-start | bytes 786440 | tf_op jit(solution)/shard_map/ppermute | solution.py:36

commit v2 on v1

--- a/solution.py
+++ b/solution.py
@@ -28,24 +28,38 @@
     return jnp.moveaxis(blocks, 0, 1).reshape(array.shape[0], -1)
 
 
+def gathered_for_both(array):
+    axes = ("z_hi", *TENSOR)
+    copies = jnp.broadcast_to(array, (lax.axis_size(axes), *array.shape))
+    blocks = to_peers(copies, axes).reshape(2, -1, *array.shape)
+    z_hi = lax.axis_index("z_hi")
+
+    def whole(index):
+        some = lax.dynamic_index_in_dim(blocks, index, 0, keepdims=False)
+        return jnp.moveaxis(some, 0, 1).reshape(array.shape[0], -1)
+
+    return whole(z_hi), whole(1 - z_hi)
+
+
 def feature_blocks(array):
     return jnp.moveaxis(array.reshape(array.shape[0], lax.axis_size(TENSOR), -1), 1, 0)
 
 
+def over_tensor(blocks):
+    return jnp.sum(to_peers(blocks, TENSOR).astype(jnp.float32), axis=0)
+
+
 def from_partner(array, axis):
     return lax.ppermute(array, axis, [(0, 1), (1, 0)])
 
 
-def gelu_value(values):
+def gelu_and_slope(values):
     tangent = jnp.tanh(coeff * (values + 0.044715 * values * values * values))
-    return 0.5 * values * (1.0 + tangent)
-
-
-def gelu_slope(values):
-    tangent = jnp.tanh(coeff * (values + 0.044715 * values * values * values))
-    return 0.5 * (1.0 + tangent) + 0.5 * values * (1.0 - tangent * tangent) * coeff * (
+    value = 0.5 * values * (1.0 + tangent)
+    slope = 0.5 * (1.0 + tangent) + 0.5 * values * (1.0 - tangent * tangent) * coeff * (
         1.0 + 3.0 * 0.044715 * values * values
     )
+    return lax.optimization_barrier((value.astype(jnp.bfloat16), slope))
 
 
 def over_neighbours(sums):
@@ -56,29 +70,25 @@
     return sums + before + after
 
 
-def halves(array, core):
-    width = array.shape[1] // 2
-    own = lax.dynamic_slice_in_dim(array, core * width, width, 1)
-    other = lax.dynamic_slice_in_dim(array, (1 - core) * width, width, 1)
-    return own, other
+def half_of(array, index, dim):
+    width = array.shape[dim] // 2
+    return lax.dynamic_slice_in_dim(array, index * width, width, dim)
 
 
 def summed_over_dp(left, right):
-    core, z_hi = lax.axis_index("core"), lax.axis_index("z_hi")
-    n_z, n_y = lax.axis_size("z_hi"), lax.axis_size("y")
-    half = right.shape[1]
+    core, y = lax.axis_index("core"), lax.axis_index("y")
+    n_y = lax.axis_size("y")
     partial = lax.dot_general(
         left, right, (((0,), (0,)), ((), ())), preferred_element_type=jnp.float32
     ).astype(jnp.bfloat16)
-    blocks = jnp.moveaxis(partial.reshape(n_z, n_y, -1, half), 1, 0)
-    blocks = to_peers(blocks, "y").astype(jnp.float32)
-    sums = jnp.sum(blocks, axis=0)
-    own = lax.dynamic_index_in_dim(sums, z_hi, 0, keepdims=False)
-    other = lax.dynamic_index_in_dim(sums, 1 - z_hi, 0, keepdims=False)
-    rows = own + from_partner(other.astype(jnp.bfloat16), "z_hi").astype(jnp.float32)
-    few = rows.shape[0] // 2
-    mine = lax.dynamic_slice_in_dim(rows, core * few, few, 0)
-    theirs = from_partner(lax.dynamic_slice_in_dim(rows, (1 - core) * few, few, 0), "core")
+    blocks = partial.reshape(n_y, -1, right.shape[1])
+    rows = lax.dynamic_index_in_dim(blocks, y, 0, keepdims=False).astype(jnp.float32)
+    for shift in range(1, n_y):
+        sent = lax.dynamic_index_in_dim(blocks, lax.rem(y + shift, n_y), 0, keepdims=False)
+        ring = [(i, (i + shift) % n_y) for i in range(n_y)]
+        rows = rows + lax.ppermute(sent, "y", ring).astype(jnp.float32)
+    mine = half_of(rows, core, 0)
+    theirs = from_partner(half_of(rows, 1 - core, 0), "core")
     return jnp.where(
         core == 0, jnp.concatenate([mine, theirs], 1), jnp.concatenate([theirs, mine], 1)
     )
@@ -91,54 +101,73 @@
     local_tokens, width_local = tokens.shape
     loss_scale = (local_tokens * dp_count) ** (-0.5)
     column = lax.axis_index(TENSOR)
-    core = lax.axis_index("core")
+    core, z_hi = lax.axis_index("core"), lax.axis_index("z_hi")
     gain_local = lax.dynamic_slice_in_dim(norm_gain, column * width_local, width_local)
     labels = jnp.arange(EXAMPLES, dtype=jnp.int32)
     onehot = (segment_ids[:, None] == labels[None, :]).astype(jnp.float32)
     perturb = adv_init * init_noise
     embedded = tokens.astype(jnp.float32) + perturb
     whole = gathered_features(embedded)
+    half_in, half_out = half_of(weight_in, core, 1), half_of(weight_out, core, 0)
     lefts_in, rights_in, lefts_out, rights_out = [], [], [], []
     for ascent in range(ASCENTS):
+        last = ascent + 1 == ASCENTS
         emb = lax.optimization_barrier(whole.astype(jnp.bfloat16)).astype(jnp.float32)
         inv_rms = lax.rsqrt(jnp.mean(emb * emb, axis=1, keepdims=True) + 1e-06)
         normed = (emb * inv_rms * norm_gain).astype(jnp.bfloat16)
         preact = jnp.dot(normed, weight_in, preferred_element_type=jnp.float32)
-        hidden = gelu_value(preact).astype(jnp.bfloat16)
+        hidden, slope = gelu_and_slope(preact)
         partial_value = jnp.dot(hidden, weight_out, preferred_element_type=jnp.float32)
-        mixed = jnp.sum(to_peers(feature_blocks(partial_value), TENSOR), axis=0)
+        mixed = over_tensor(feature_blocks(partial_value.astype(jnp.bfloat16)))
+        far_normed = from_partner(normed, "z_hi")
+        far_normed = jnp.concatenate([far_normed, from_partner(far_normed, "core")], 0)
+        far_preact = jnp.dot(far_normed, half_in, preferred_element_type=jnp.float32)
+        far_hidden, far_slope = gelu_and_slope(far_preact)
+        near_hidden = [half_of(hidden, core, 1), from_partner(half_of(hidden, 1 - core, 1), "core")]
+        rights_out += [*near_hidden, far_hidden]
+        some_normed = half_of(normed, z_hi, 1)
+        lefts_in += [some_normed, from_partner(some_normed, "core"), half_of(far_normed, z_hi, 1)]
         out_grad = (embedded + mixed - target) * loss_scale
-        grad_whole = gathered_features(out_grad.astype(jnp.bfloat16))
+        if last:
+            grad, far_grad = gathered_for_both(out_grad.astype(jnp.bfloat16))
+        else:
+            grad = gathered_features(out_grad.astype(jnp.bfloat16))
+            far_grad = from_partner(grad, "z_hi")
+        some_grad = half_of(grad, z_hi, 1)
+        far_grad = jnp.concatenate([far_grad, from_partner(far_grad, "core")], 0)
+        lefts_out += [some_grad, from_partner(some_grad, "core"), half_of(far_grad, z_hi, 1)]
         hidden_grad = (
-            jnp.dot(grad_whole, weight_out.T, preferred_element_type=jnp.float32)
-            * gelu_slope(preact)
+            jnp.dot(grad, weight_out.T, preferred_element_type=jnp.float32) * slope
         ).astype(jnp.bfloat16)
-        hidden_own, hidden_other = halves(hidden, core)
-        slope_own, slope_other = halves(hidden_grad, core)
-        lefts_in += [normed, from_partner(normed, "core")]
-        rights_in += [slope_own, from_partner(slope_other, "core")]
-        lefts_out += [grad_whole, from_partner(grad_whole, "core")]
-        rights_out += [hidden_own, from_partner(hidden_other, "core")]
-        if ascent + 1 < ASCENTS:
+        far_hidden_grad = (
+            jnp.dot(far_grad, half_out.T, preferred_element_type=jnp.float32) * far_slope
+        ).astype(jnp.bfloat16)
+        rights_in += [
+            half_of(hidden_grad, core, 1),
+            from_partner(half_of(hidden_grad, 1 - core, 1), "core"),
+            far_hidden_grad,
+        ]
+        if not last:
             normed_partial = jnp.dot(hidden_grad, weight_in.T, preferred_element_type=jnp.float32)
             dot_partial = jnp.sum(normed_partial * norm_gain * emb, axis=1)
+            dot_head = dot_partial.astype(jnp.bfloat16)
+            dot_rest = (dot_partial - dot_head.astype(jnp.float32)).astype(jnp.bfloat16)
+            dots = jnp.stack([dot_head, dot_rest], 1)[None]
             blocks = jnp.concatenate(
                 [
-                    feature_blocks(normed_partial),
-                    jnp.broadcast_to(
-                        dot_partial[None, :, None], (lax.axis_size(TENSOR), local_tokens, 1)
-                    ),
+                    feature_blocks(normed_partial.astype(jnp.bfloat16)),
+                    jnp.broadcast_to(dots, (lax.axis_size(TENSOR), local_tokens, 2)),
                 ],
                 axis=2,
             )
-            arrived = jnp.sum(to_peers(blocks, TENSOR), axis=0)
+            arrived = over_tensor(blocks)
             scaled = arrived[:, :width_local] * gain_local
-            row_dot = arrived[:, width_local:]
+            row_dot = jnp.sum(arrived[:, width_local:], axis=1, keepdims=True)
             emb_local = embedded.astype(jnp.bfloat16).astype(jnp.float32)
             delta_grad = (
                 out_grad + inv_rms * scaled - emb_local * inv_rms * inv_rms * inv_rms * row_dot / D
             )
-            delta_whole = gathered_features(delta_grad)
+            delta_whole = gathered_features(delta_grad.astype(jnp.bfloat16)).astype(jnp.float32)
             row_squares = jnp.sum(delta_whole * delta_whole, axis=1)
             sums = jnp.stack(
                 [jnp.sum(onehot * row_squares[:, None], axis=0), jnp.sum(onehot, axis=0)]

time: 264 us -> 245 us (0.928); the launches traced: 263 us -> 241 us
  blocking collectives: 88.7 us -> 34.7 us
  waiting for transfers between devices: 66.4 us -> 33.4 us
  starting transfers between devices: 63.7 us -> 94.1 us
  local copies, waits for them, and re-layouts: 7.86 us -> 30.3 us
  matrix products: 25.9 us -> 36 us
    all_to_all x5 -> x2, blocking collectives: 88.7 us -> 34.7 us  [to_peers(): return lax.all_to_all(blocks, axis, 0, 0, tiled=True)]
    all_to_all x4 -> x5, waiting for transfers between devices: 53.1 us -> 2.65 us  [to_peers(): return lax.all_to_all(blocks, axis, 0, 0, tiled=True)]
    unnamed x29 -> x63, local copies, waits for them, and re-layouts: 1.65 us -> 17.6 us
    ppermute x0 -> x6, waiting for transfers between devices: none -> 15.9 us  [summed_over_dp(): rows = rows + lax.ppermute(sent, 'y', ring).astype(jnp.float32)]
    all_to_all x4 -> x5, starting transfers between devices: 27.7 us -> 42.1 us  [to_peers(): return lax.all_to_all(blocks, axis, 0, 0, tiled=True)]
    dot_general x2 -> x6, matrix products: 8.76 us -> 19.5 us  [the longest x2 8.32 us: shards(): jnp.dot(far_normed, half_in, preferred_element_type=jnp.float32)]
    ppermute x13 -> x18, starting transfers between devices: 30.7 us -> 39.3 us  [from_partner(): return lax.ppermute(array, axis, [(0, 1), (1, 0)])]
    ppermute x0 -> x6, starting transfers between devices: none -> 8.23 us  [summed_over_dp(): rows = rows + lax.ppermute(sent, 'y', ring).astype(jnp.float32)]
  transfers between devices with their start and end apart: 19 -> 31, of which waited for: 12 -> 9; matrix products, arithmetic and copies ran while one was open for 5% -> 24% of each run, Pallas kernels for 0% -> 0%
where the time goes in v2:
time: 245 us; the launch traced here: 241 us
  starting transfers between devices  94.1 us (38%)
  matrix products  36 us (15%)
  blocking collectives  34.7 us (14%)
  waiting for transfers between devices  33.4 us (14%)
  local copies, waits for them, and re-layouts  30.3 us (12%)
  other arithmetic  11.1 us (5%)
    all_to_all x5, starting transfers between devices, to_peers(): return lax.all_to_all(blocks, axis, 0, 0, tiled=True)  42.1 us
    ppermute x18, starting transfers between devices, from_partner(): return lax.ppermute(array, axis, [(0, 1), (1, 0)])  39.3 us
    all_to_all x2, blocking collectives, to_peers(): return lax.all_to_all(blocks, axis, 0, 0, tiled=True)  34.7 us
    unnamed x63, local copies, waits for them, and re-layouts  17.6 us
    ppermute x6, waiting for transfers between devices, summed_over_dp(): rows = rows + lax.ppermute(sent, 'y', ring).astype(jnp.float32)  15.9 us
    ppermute x18, waiting for transfers between devices, from_partner(): return lax.ppermute(array, axis, [(0, 1), (1, 0)])  14 us
    dot_general x2, matrix products, shards(): preact = jnp.dot(normed, weight_in, preferred_element_type=jnp.float32)  8.43 us
    dot_general x2, matrix products, shards(): jnp.dot(far_normed, half_in, preferred_element_type=jnp.float32)  8.32 us
  transfers between devices with their start and end apart: 31, of which 9 were waited for; matrix products, arithmetic and copies ran while one was open for 24% of the time, Pallas kernels for 0%

profile of v2, /device:TPU:33, one launch (start us, length us, event | category | flops | bytes accessed | tf_op | source)
XLA Modules:
  0.0 240.9 jit_solution(8895126447351813577)
XLA Ops:
  0.6 0.8 convert_add_fusion.3
  1.5 20.2 %all_to_all.35 = f32[16,128,64]{1,2,0:T(8,128)S(1)} all-to-all(f32[16,128,64]{1,2,0:T(8,128)S(1)} %broadcast_in_dim.10), channel_id=1, replica_groups=mesh['z_hi'=2,'y'=4,'core'=2,'x'=4,'z_lo'=4] {'x','z_lo'}, dimensions={0} | all-to-all | bytes 1048576 | tf_op jit(solution)/shard_map/all_to_all | solution.py:22
  22.2 3.7 %fusion.32 = (f32[128,2048]{1,0:T(8,128)S(1)}, bf16[128,2048]{1,0:T(8,128)(2,1)S(1)}) fusion(bf16[128,1024]{1,0:T(8,128)(2,1)S(1)} %fusion.53, bf16[1024,2048]{1,0:T(8,128)(2,1)} %param.14), kind=kOutput, calls=%fused_computation.34 | convolution fusion | flops 541851648 | bytes 6029312 | tf_op jit(solution)/shard_map/dot_general | solution.py:118
  26.9 14.5 %all_to_all.36 = bf16[16,128,64]{1,2,0:T(8,128)(2,1)S(1)} all-to-all(bf16[16,128,64]{1,2,0:T(8,128)(2,1)S(1)} %bitcast.97), channel_id=1, replica_groups=mesh['z_hi'=2,'y'=4,'core'=2,'x'=4,'z_lo'=4] {'x','z_lo'}, dimensions={0} | all-to-all | bytes 524288 | tf_op jit(solution)/shard_map/all_to_all | solution.py:22
  42.2 5.7 %all-to-all-start.2 = ((bf16[16,128,64]{1,2,0:T(8,128)(2,1)}), bf16[16,128,64]{1,2,0:T(8,128)(2,1)}, u32[]{:S(2)}, u32[]{:S(2)}) async-start(bf16[16,128,64]{1,2,0:T(8,128)(2,1)} %broadcast_in_dim.11), calls=%async_computation.2 | async-start | bytes 524288 | tf_op jit(solution)/shard_map/all_to_all | solution.py:22
  47.9 4.2 %collective-permute-start.1 = (bf16[128,1024]{1,0:T(8,128)(2,1)S(1)}, bf16[128,1024]{1,0:T(8,128)(2,1)}, u32[]{:S(2)}, u32[]{:S(2)}) collective-permute-start(bf16[128,1024]{1,0:T(8,128)(2,1)S(1)} %fusion.53), channel_id=1, source_target_pairs={{0,128},{128,0},{1,129},{129,1},{2,130},{130,2},{3,131},{131,3},{4... | collective-permute-start | bytes 786440 | tf_op jit(solution)/shard_map/ppermute | solution.py:53
  52.7 2.8 %collective-permute-start = (bf16[128,512]{1,0:T(8,128)(2,1)S(1)}, bf16[128,512]{1,0:T(8,128)(2,1)S(1)}, u32[]{:S(2)}, u32[]{:S(2)}) collective-permute-start(bf16[128,512]{1,0:T(8,128)(2,1)S(1)} %get-tuple-element.38), channel_id=1, source_target_pairs={{0,16},{16,0},{1,17},{17,1},{2,18},{18,2},{3,19},{19,3},{4,20},{20... | collective-permute-start | bytes 393224 | tf_op jit(solution)/shard_map/ppermute | solution.py:53
  57.2 6.3 %collective-permute-done.1 = bf16[128,1024]{1,0:T(8,128)(2,1)} collective-permute-done((bf16[128,1024]{1,0:T(8,128)(2,1)S(1)}, bf16[128,1024]{1,0:T(8,128)(2,1)}, u32[]{:S(2)}, u32[]{:S(2)}) %collective-permute-start.1) | collective-permute-done | bytes 262176 | tf_op jit(solution)/shard_map/ppermute | solution.py:53
  63.5 2.8 %collective-permute-start.2 = (bf16[128,1024]{1,0:T(8,128)(2,1)}, bf16[128,1024]{1,0:T(8,128)(2,1)}, u32[]{:S(2)}, u32[]{:S(2)}) collective-permute-start(bf16[128,1024]{1,0:T(8,128)(2,1)} %collective-permute-done.1), channel_id=1, source_target_pairs={{0,16},{16,0},{1,17},{17,1},{2,18},{18,2},{3,19},{19,3},{4,20},{20... | collective-permute-start | bytes 786440 | tf_op jit(solution)/shard_map/ppermute | solution.py:53
  66.3 1.0 constant_dynamic-update-slice_fusion.1
  67.3 3.9 %fusion = bf16[128,2048]{1,0:T(8,128)(2,1)S(1)} fusion(f32[128,2048]{1,0:T(8,128)S(1)} %get-tuple-element.14, bf16[128,1024]{0,1:T(8,128)(2,1)} %bitcast.6, bf16[2048,1024]{1,0:T(8,128)(2,1)} %param.15), kind=kOutput, calls=%fused_computation.2 | convolution fusion | flops 537395200 | bytes 6029312 | tf_op jit(solution)/shard_map/dot_general | solution.py:140
  71.3 1.6 fusion.85
  73.8 10.2 %all-to-all-start.3 = ((bf16[16,128,66]{1,2,0:T(8,128)(2,1)}), bf16[16,128,66]{1,2,0:T(8,128)(2,1)S(1)}, u32[]{:S(2)}, u32[]{:S(2)}) async-start(bf16[16,128,66]{1,2,0:T(8,128)(2,1)} %pad_maximum_fusion.2), calls=%async_computation.3 | async-start | bytes 589824 | tf_op jit(solution)/shard_map/all_to_all | solution.py:22
  84.0 1.7 constant_dynamic-update-slice_fusion.19
  85.7 1.0 constant_dynamic-update-slice_fusion
  86.7 4.1 %fusion.37 = (f32[256,1024]{1,0:T(8,128)}, bf16[256,1024]{1,0:T(8,128)(2,1)S(1)}) fusion(bf16[256,1024]{1,0:T(8,128)(2,1)S(1)} %constant_dynamic-update-slice_fusion, bf16[1024,2048]{1,0:T(8,128)(2,1)} %param.14, s32[]{:T(128)S(6)} %select_n.79), kind=kOutput, calls=%fused_computation.39 | convolution fusion | flops 541851648 | bytes 4194308 | tf_op jit(solution)/shard_map/dot_general | solution.py:124
  90.7 2.6 %all-to-all-done.3 = bf16[16,128,66]{1,2,0:T(8,128)(2,1)S(1)} async-done(((bf16[16,128,66]{1,2,0:T(8,128)(2,1)}), bf16[16,128,66]{1,2,0:T(8,128)(2,1)S(1)}, u32[]{:S(2)}, u32[]{:S(2)}) %all-to-all-start.3) | async-done | bytes 270368 | tf_op jit(solution)/shard_map/all_to_all | solution.py:22
  94.3 5.6 %all-to-all-start.4 = ((bf16[16,128,64]{1,2,0:T(8,128)(2,1)}), bf16[16,128,64]{1,2,0:T(8,128)(2,1)S(1)}, u32[]{:S(2)}, u32[]{:S(2)}) async-start(bf16[16,128,64]{1,2,0:T(8,128)(2,1)} %broadcast_in_dim.13), calls=%async_computation.4 | async-start | bytes 524288 | tf_op jit(solution)/shard_map/all_to_all | solution.py:22
  99.9 0.9 constant_dynamic-update-slice_fusion.18
  100.7 1.6 constant_dynamic-update-slice_fusion.15
  102.4 1.4 collective-permute-start.18
  104.5 1.8 collective-permute-start.10
  108.2 2.6 %collective-permute-start.3 = (f32[2,32]{1,0:T(2,128)S(1)}, f32[2,32]{1,0:T(2,128)S(1)}, u32[]{:S(2)}, u32[]{:S(2)}) collective-permute-start(f32[2,32]{1,0:T(2,128)S(1)} %pad_maximum_fusion.3), channel_id=1, source_target_pairs={{0,16},{16,0},{1,17},{17,1},{2,18},{18,2},{3,19},{19,3},{4,20},{20... | collective-permute-start | bytes 776 | tf_op jit(solution)/shard_map/ppermute | solution.py:53
  110.8 7.5 %collective-permute-done.10 = bf16[128,1024]{0,1:T(8,128)(2,1)} collective-permute-done((bf16[128,1024]{0,1:T(8,128)(2,1)}, bf16[128,1024]{0,1:T(8,128)(2,1)}, u32[]{:S(2)}, u32[]{:S(2)}) %collective-permute-start.10) | collective-permute-done | bytes 262176 | tf_op jit(solution)/shard_map/ppermute | solution.py:53
  118.4 1.7 constant_dynamic-update-slice_fusion.9
  120.0 0.9 collective-permute-start.11
  121.0 3.2 %collective-permute-start.4 = (f32[2,32]{1,0:T(2,128)S(1)}, f32[2,32]{1,0:T(2,128)S(1)}, u32[]{:S(2)}, u32[]{:S(2)}) collective-permute-start(f32[2,32]{1,0:T(2,128)S(1)} %fusion.80), channel_id=1, source_target_pairs={{0,32},{32,64},{64,96},{96,128},{128,160},{160,192},{192,224},{1,3... | collective-permute-start | bytes 776 | tf_op jit(solution)/shard_map/ppermute | solution.py:68
  124.2 1.3 collective-permute-start.5
  125.5 0.8 convert_element_type.230
  126.4 1.2 copy.30
  127.6 0.9 collective-permute-done.5
  128.9 0.8 fusion.50
  129.8 4.7 %fusion.42 = (f32[128,2048]{1,0:T(8,128)}, bf16[128,2048]{1,0:T(8,128)(2,1)S(1)}) fusion(bf16[128,1024]{1,0:T(8,128)(2,1)} %fusion.50, bf16[1024,2048]{1,0:T(8,128)(2,1)} %param.14), kind=kOutput, calls=%fused_computation.44 | convolution fusion | flops 541851648 | bytes 6029312 | tf_op jit(solution)/shard_map/dot_general | solution.py:118
  135.3 0.8 copy.32
  136.1 10.6 %all-to-all-start.5 = ((bf16[16,128,64]{1,2,0:T(8,128)(2,1)}), bf16[16,128,64]{1,2,0:T(8,128)(2,1)S(1)}, u32[]{:S(2)}, u32[]{:S(2)}) async-start(bf16[16,128,64]{1,2,0:T(8,128)(2,1)} %bitcast.95), calls=%async_computation.5 | async-start | bytes 524288 | tf_op jit(solution)/shard_map/all_to_all | solution.py:22
  146.7 1.0 constant_dynamic-update-slice_fusion.8
  147.7 2.6 %fusion.25 = bf16[1024,1024]{1,0:T(8,128)(2,1)S(1)} fusion(bf16[1024,1024]{1,0:T(8,128)(2,1)S(1)} %constant_dynamic-update-slice_fusion.11, f32[256,1024]{1,0:T(8,128)} %get-tuple-element.15, bf16[256,1024]{0,1:T(8,128)(2,1)S(1)} %constant_dynamic-update-slice_fusion.8, bf16[2048,1024]{1,0:T(8,128)(2,1)} %param.15, s32[]{:T(128)S(6)} %select_n.79), kind=kOutput, calls=%fused_computation.27 | convolution fusion | flops 537395200 | bytes 4194308 | tf_op jit(solution)/shard_map/dot_general | solution.py:143
  150.4 8.0 %collective-permute-start.7 = (bf16[128,1024]{1,0:T(8,128)(2,1)}, bf16[128,1024]{1,0:T(8,128)(2,1)}, u32[]{:S(2)}, u32[]{:S(2)}) collective-permute-start(bf16[128,1024]{1,0:T(8,128)(2,1)} %fusion.50), channel_id=1, source_target_pairs={{0,128},{128,0},{1,129},{129,1},{2,130},{130,2},{3,131},{131,3},{4... | collective-permute-start | bytes 786440 | tf_op jit(solution)/shard_map/ppermute | solution.py:53
  158.4 1.6 constant_dynamic-update-slice_fusion.5
  160.0 1.4 collective-permute-start.6
  161.5 1.3 fusion.69
  162.8 0.9 broadcast_in_dim.14
  163.7 10.1 %all-to-all-start.6 = ((bf16[32,128,64]{1,2,0:T(8,128)(2,1)}), bf16[32,128,64]{1,2,0:T(8,128)(2,1)}, u32[]{:S(2)}, u32[]{:S(2)}) async-start(bf16[32,128,64]{1,2,0:T(8,128)(2,1)} %broadcast_in_dim.14), calls=%async_computation.6 | async-start | bytes 1048576 | tf_op jit(solution)/shard_map/all_to_all | solution.py:22
  174.5 7.3 %collective-permute-start.21 = (bf16[128,1024]{1,0:T(8,128)(2,1)S(1)}, bf16[128,1024]{1,0:T(8,128)(2,1)S(1)}, u32[]{:S(2)}, u32[]{:S(2)}) collective-permute-start(bf16[128,1024]{1,0:T(8,128)(2,1)S(1)} %get-tuple-element.55), channel_id=1, source_target_pairs={{0,16},{16,0},{1,17},{17,1},{2,18},{18,2},{3,19},{19,3},{4,20},{20... | collective-permute-start | bytes 786440 | tf_op jit(solution)/shard_map/ppermute | solution.py:53
  182.6 1.6 constant_dynamic-update-slice_fusion.4
  184.2 1.0 constant_dynamic-update-slice_fusion.3
  185.9 4.3 %fusion.47 = (f32[256,1024]{1,0:T(8,128)}, bf16[256,1024]{1,0:T(8,128)(2,1)}) fusion(bf16[256,1024]{1,0:T(8,128)(2,1)S(1)} %constant_dynamic-update-slice_fusion.2, bf16[1024,2048]{1,0:T(8,128)(2,1)} %param.14, s32[]{:T(128)S(6)} %select_n.79), kind=kOutput, calls=%fused_computation.49 | convolution fusion | flops 541851648 | bytes 4194308 | tf_op jit(solution)/shard_map/dot_general | solution.py:124
  190.2 1.1 constant_dynamic-slice_fusion.9
  191.3 3.9 %fusion.1 = bf16[128,2048]{1,0:T(8,128)(2,1)S(1)} fusion(f32[128,2048]{1,0:T(8,128)S(1)} %copy-done.5, bf16[128,1024]{0,1:T(8,128)(2,1)S(1)} %bitcast.90, bf16[2048,1024]{1,0:T(8,128)(2,1)} %param.15), kind=kOutput, calls=%fused_computation.3 | convolution fusion | flops 537395200 | bytes 6029312 | tf_op jit(solution)/shard_map/dot_general | solution.py:140
  195.3 3.8 %collective-permute-start.12 = (bf16[128,1024]{1,0:T(8,128)(2,1)S(1)}, bf16[128,1024]{1,0:T(8,128)(2,1)S(1)}, u32[]{:S(2)}, u32[]{:S(2)}) collective-permute-start(bf16[128,1024]{1,0:T(8,128)(2,1)S(1)} %get-tuple-element.63), channel_id=1, source_target_pairs={{0,16},{16,0},{1,17},{17,1},{2,18},{18,2},{3,19},{19,3},{4,20},{20... | collective-permute-start | bytes 786440 | tf_op jit(solution)/shard_map/ppermute | solution.py:53
  199.8 0.8 collective-permute-start.13
  202.9 2.5 %convolution_convert_fusion.1 = bf16[512,1024]{1,0:T(8,128)(2,1)S(1)} fusion(bf16[1024,512]{1,0:T(8,128)(2,1)} %dynamic-slice_dynamic-update-slice_fusion.5, bf16[1024,1024]{1,0:T(8,128)(2,1)S(1)} %fusion.19), kind=kOutput, calls=%fused_computation.21 | convolution fusion | flops 1074266112 | bytes 4194304 | tf_op jit(solution)/shard_map/dot_general | solution.py:81
  205.5 4.7 %collective-permute-start.15 = (bf16[128,1024]{1,0:T(8,128)(2,1)S(1)}, bf16[128,1024]{1,0:T(8,128)(2,1)}, u32[]{:S(2)}, u32[]{:S(2)}) collective-permute-start(bf16[128,1024]{1,0:T(8,128)(2,1)S(1)} %get-tuple-element.44), channel_id=1, source_target_pairs={{0,64},{32,96},{64,0},{96,32},{1,65},{33,97},{65,1},{97,33},{2,66}... | collective-permute-start | bytes 786440 | tf_op jit(solution)/shard_map/ppermute | solution.py:89
  211.0 2.5 %convolution_convert_fusion = bf16[512,1024]{1,0:T(8,128)(2,1)S(1)} fusion(bf16[1024,512]{0,1:T(8,128)(2,1)} %fusion.65, bf16[1024,1024]{1,0:T(8,128)(2,1)S(1)} %constant_dynamic-update-slice_fusion.16), kind=kOutput, calls=%fused_computation.20 | convolution fusion | flops 1074266112 | bytes 4194304 | tf_op jit(solution)/shard_map/dot_general | solution.py:81
  213.5 1.5 collective-permute-start.22
  216.3 1.9 collective-permute-start.24
  218.3 4.1 %collective-permute-done.15 = bf16[128,1024]{1,0:T(8,128)(2,1)} collective-permute-done((bf16[128,1024]{1,0:T(8,128)(2,1)S(1)}, bf16[128,1024]{1,0:T(8,128)(2,1)}, u32[]{:S(2)}, u32[]{:S(2)}) %collective-permute-start.15) | collective-permute-done | bytes 262176 | tf_op jit(solution)/shard_map/ppermute | solution.py:89
  222.4 6.2 %collective-permute-done.22 = bf16[128,1024]{1,0:T(8,128)(2,1)} collective-permute-done((bf16[128,1024]{1,0:T(8,128)(2,1)S(1)}, bf16[128,1024]{1,0:T(8,128)(2,1)}, u32[]{:S(2)}, u32[]{:S(2)}) %collective-permute-start.22) | collective-permute-done | bytes 262176 | tf_op jit(solution)/shard_map/ppermute | solution.py:89
  228.6 5.0 %collective-permute-done.23 = bf16[128,1024]{1,0:T(8,128)(2,1)} collective-permute-done((bf16[128,1024]{1,0:T(8,128)(2,1)S(1)}, bf16[128,1024]{1,0:T(8,128)(2,1)}, u32[]{:S(2)}, u32[]{:S(2)}) %collective-permute-start.23) | collective-permute-done | bytes 262176 | tf_op jit(solution)/shard_map/ppermute | solution.py:89
  233.6 1.7 fusion.61
  235.4 0.9 collective-permute-start.17
  236.3 1.2 constant_dynamic-slice_fusion.6
  237.9 2.0 subtract_convert_fusion.1
  239.9 1.0 subtract_convert_fusion
  (134 shorter events, 18.3 us)
Async XLA Ops:
  0.6 21.4 %copy-start.17 = (f32[1024]{0:T(1024)S(1)}, f32[1024]{0:T(1024)}, u32[]{:S(2)}) copy-start(f32[1024]{0:T(1024)} %param.13) | copy-start | bytes 12292
  22.2 3.7 %copy-start = (bf16[2048,1024]{1,0:T(8,128)(2,1)S(1)}, bf16[2048,1024]{1,0:T(8,128)(2,1)}, u32[]{:S(2)}) copy-start(bf16[2048,1024]{1,0:T(8,128)(2,1)} %param.15) | copy-start | bytes 12582916
  25.9 15.5 %copy-start.13 = (f32[128,64]{0,1:T(8,128)S(1)}, f32[128,64]{0,1:T(8,128)}, u32[]{:S(2)}) copy-start(f32[128,64]{0,1:T(8,128)} %param.12) | copy-start | bytes 98308
  42.2 25.1 %all-to-all-start.2 = ((bf16[16,128,64]{1,2,0:T(8,128)(2,1)}), bf16[16,128,64]{1,2,0:T(8,128)(2,1)}, u32[]{:S(2)}, u32[]{:S(2)}) async-start(bf16[16,128,64]{1,2,0:T(8,128)(2,1)} %broadcast_in_dim.11), calls=%async_computation.2 | async-start | bytes 524288 | tf_op jit(solution)/shard_map/all_to_all | solution.py:22
  47.9 15.6 %collective-permute-start.1 = (bf16[128,1024]{1,0:T(8,128)(2,1)S(1)}, bf16[128,1024]{1,0:T(8,128)(2,1)}, u32[]{:S(2)}, u32[]{:S(2)}) collective-permute-start(bf16[128,1024]{1,0:T(8,128)(2,1)S(1)} %fusion.53), channel_id=1, source_target_pairs={{0,128},{128,0},{1,129},{129,1},{2,130},{130,2},{3,131},{131,3},{4... | collective-permute-start | bytes 786440 | tf_op jit(solution)/shard_map/ppermute | solution.py:53
  52.7 3.8 %collective-permute-start = (bf16[128,512]{1,0:T(8,128)(2,1)S(1)}, bf16[128,512]{1,0:T(8,128)(2,1)S(1)}, u32[]{:S(2)}, u32[]{:S(2)}) collective-permute-start(bf16[128,512]{1,0:T(8,128)(2,1)S(1)} %get-tuple-element.38), channel_id=1, source_target_pairs={{0,16},{16,0},{1,17},{17,1},{2,18},{18,2},{3,19},{19,3},{4,20},{20... | collective-permute-start | bytes 393224 | tf_op jit(solution)/shard_map/ppermute | solution.py:53
  56.4 27.6 %collective-permute-start.20 = (bf16[128,1024]{1,0:T(8,128)(2,1)S(1)}, bf16[128,1024]{1,0:T(8,128)(2,1)}, u32[]{:S(2)}, u32[]{:S(2)}) collective-permute-start(bf16[128,1024]{1,0:T(8,128)(2,1)S(1)} %get-tuple-element.57), channel_id=1, source_target_pairs={{0,16},{16,0},{1,17},{17,1},{2,18},{18,2},{3,19},{19,3},{4,20},{20... | collective-permute-start | bytes 786440 | tf_op jit(solution)/shard_map/ppermute | solution.py:53
  63.5 22.2 %collective-permute-start.2 = (bf16[128,1024]{1,0:T(8,128)(2,1)}, bf16[128,1024]{1,0:T(8,128)(2,1)}, u32[]{:S(2)}, u32[]{:S(2)}) collective-permute-start(bf16[128,1024]{1,0:T(8,128)(2,1)} %collective-permute-done.1), channel_id=1, source_target_pairs={{0,16},{16,0},{1,17},{17,1},{2,18},{18,2},{3,19},{19,3},{4,20},{20... | collective-permute-start | bytes 786440 | tf_op jit(solution)/shard_map/ppermute | solution.py:53
  67.3 4.0 %copy-start.3 = (bf16[1024,2048]{1,0:T(8,128)(2,1)S(1)}, bf16[1024,2048]{1,0:T(8,128)(2,1)}, u32[]{:S(2)}) copy-start(bf16[1024,2048]{1,0:T(8,128)(2,1)} %param.14) | copy-start | bytes 12582916
  73.8 19.5 %all-to-all-start.3 = ((bf16[16,128,66]{1,2,0:T(8,128)(2,1)}), bf16[16,128,66]{1,2,0:T(8,128)(2,1)S(1)}, u32[]{:S(2)}, u32[]{:S(2)}) async-start(bf16[16,128,66]{1,2,0:T(8,128)(2,1)} %pad_maximum_fusion.2), calls=%async_computation.3 | async-start | bytes 589824 | tf_op jit(solution)/shard_map/all_to_all | solution.py:22
  86.7 4.1 %copy-start.7 = (bf16[256,1024]{1,0:T(8,128)(2,1)}, bf16[256,1024]{1,0:T(8,128)(2,1)S(1)}, u32[]{:S(2)}) copy-start(bf16[256,1024]{1,0:T(8,128)(2,1)S(1)} %constant_dynamic-update-slice_fusion) | copy-start | bytes 1572868
  90.7 13.0 %copy-start.8 = (bf16[256,1024]{1,0:T(8,128)(2,1)S(1)}, bf16[256,1024]{1,0:T(8,128)(2,1)}, u32[]{:S(2)}) copy-start(bf16[256,1024]{1,0:T(8,128)(2,1)} %copy-done.7) | copy-start | bytes 1572868
  94.3 13.8 %copy-start.20 = (s32[128]{0:T(128)S(1)}, s32[128]{0:T(128)}, u32[]{:S(2)}) copy-start(s32[128]{0:T(128)} %param.11) | copy-start | bytes 1540
  94.3 13.7 %all-to-all-start.4 = ((bf16[16,128,64]{1,2,0:T(8,128)(2,1)}), bf16[16,128,64]{1,2,0:T(8,128)(2,1)S(1)}, u32[]{:S(2)}, u32[]{:S(2)}) async-start(bf16[16,128,64]{1,2,0:T(8,128)(2,1)} %broadcast_in_dim.13), calls=%async_computation.4 | async-start | bytes 524288 | tf_op jit(solution)/shard_map/all_to_all | solution.py:22
  102.4 4.9 %collective-permute-start.18 = (bf16[128,512]{0,1:T(8,128)(2,1)S(1)}, bf16[128,512]{0,1:T(8,128)(2,1)S(1)}, u32[]{:S(2)}, u32[]{:S(2)}) collective-permute-start(bf16[128,512]{0,1:T(8,128)(2,1)S(1)} %get-tuple-element.28), channel_id=1, source_target_pairs={{0,16},{16,0},{1,17},{17,1},{2,18},{18,2},{3,19},{19,3},{4,20},{20... | collective-permute-start | bytes 393224 | tf_op jit(solution)/shard_map/ppermute | solution.py:53
  104.5 13.9 %collective-permute-start.10 = (bf16[128,1024]{0,1:T(8,128)(2,1)}, bf16[128,1024]{0,1:T(8,128)(2,1)}, u32[]{:S(2)}, u32[]{:S(2)}) collective-permute-start(bf16[128,1024]{0,1:T(8,128)(2,1)} %bitcast.6), channel_id=1, source_target_pairs={{0,128},{128,0},{1,129},{129,1},{2,130},{130,2},{3,131},{131,3},{4... | collective-permute-start | bytes 786440 | tf_op jit(solution)/shard_map/ppermute | solution.py:53
  107.0 18.5 %collective-permute-start.9 = (bf16[128,1024]{1,0:T(8,128)(2,1)}, bf16[128,1024]{1,0:T(8,128)(2,1)S(1)}, u32[]{:S(2)}, u32[]{:S(2)}) collective-permute-start(bf16[128,1024]{1,0:T(8,128)(2,1)} %get-tuple-element.65), channel_id=1, source_target_pairs={{0,16},{16,0},{1,17},{17,1},{2,18},{18,2},{3,19},{19,3},{4,20},{20... | collective-permute-start | bytes 786440 | tf_op jit(solution)/shard_map/ppermute | solution.py:53
  108.2 12.8 %collective-permute-start.3 = (f32[2,32]{1,0:T(2,128)S(1)}, f32[2,32]{1,0:T(2,128)S(1)}, u32[]{:S(2)}, u32[]{:S(2)}) collective-permute-start(f32[2,32]{1,0:T(2,128)S(1)} %pad_maximum_fusion.3), channel_id=1, source_target_pairs={{0,16},{16,0},{1,17},{17,1},{2,18},{18,2},{3,19},{19,3},{4,20},{20... | collective-permute-start | bytes 776 | tf_op jit(solution)/shard_map/ppermute | solution.py:53
  120.0 26.6 %collective-permute-start.11 = (bf16[128,1024]{0,1:T(8,128)(2,1)}, bf16[128,1024]{0,1:T(8,128)(2,1)}, u32[]{:S(2)}, u32[]{:S(2)}) collective-permute-start(bf16[128,1024]{0,1:T(8,128)(2,1)} %collective-permute-done.10), channel_id=1, source_target_pairs={{0,16},{16,0},{1,17},{17,1},{2,18},{18,2},{3,19},{19,3},{4,20},{20... | collective-permute-start | bytes 786440 | tf_op jit(solution)/shard_map/ppermute | solution.py:53
  121.0 6.6 %collective-permute-start.4 = (f32[2,32]{1,0:T(2,128)S(1)}, f32[2,32]{1,0:T(2,128)S(1)}, u32[]{:S(2)}, u32[]{:S(2)}) collective-permute-start(f32[2,32]{1,0:T(2,128)S(1)} %fusion.80), channel_id=1, source_target_pairs={{0,32},{32,64},{64,96},{96,128},{128,160},{160,192},{192,224},{1,3... | collective-permute-start | bytes 776 | tf_op jit(solution)/shard_map/ppermute | solution.py:68
  124.2 4.3 %collective-permute-start.5 = (f32[2,32]{1,0:T(2,128)S(1)}, f32[2,32]{1,0:T(2,128)S(1)}, u32[]{:S(2)}, u32[]{:S(2)}) collective-permute-start(f32[2,32]{1,0:T(2,128)S(1)} %fusion.80), channel_id=1, source_target_pairs={{32,0},{64,32},{96,64},{128,96},{160,128},{192,160},{224,192},{33,... | collective-permute-start | bytes 776 | tf_op jit(solution)/shard_map/ppermute | solution.py:69
  128.6 5.9 %copy-start.19 = (f32[128]{0:T(128)}, f32[128]{0:T(128)S(1)}, u32[]{:S(2)}) copy-start(f32[128]{0:T(128)S(1)} %select_reduce_fusion) | copy-start | bytes 1540
  129.8 4.7 %copy-start.1 = (bf16[2048,1024]{1,0:T(8,128)(2,1)S(1)}, bf16[2048,1024]{1,0:T(8,128)(2,1)}, u32[]{:S(2)}) copy-start(bf16[2048,1024]{1,0:T(8,128)(2,1)} %param.15) | copy-start | bytes 12582916
  134.5 12.2 %copy-start.4 = (bf16[256,1024]{0,1:T(8,128)(2,1)S(1)}, bf16[256,1024]{0,1:T(8,128)(2,1)}, u32[]{:S(2)}) copy-start(bf16[256,1024]{0,1:T(8,128)(2,1)} %constant_dynamic-update-slice_fusion.9) | copy-start | bytes 1572868
  136.1 25.3 %all-to-all-start.5 = ((bf16[16,128,64]{1,2,0:T(8,128)(2,1)}), bf16[16,128,64]{1,2,0:T(8,128)(2,1)S(1)}, u32[]{:S(2)}, u32[]{:S(2)}) async-start(bf16[16,128,64]{1,2,0:T(8,128)(2,1)} %bitcast.95), calls=%async_computation.5 | async-start | bytes 524288 | tf_op jit(solution)/shard_map/all_to_all | solution.py:22
  147.7 13.8 %copy-start.15 = (f32[128,64]{0,1:T(8,128)S(1)}, f32[128,64]{0,1:T(8,128)}, u32[]{:S(2)}) copy-start(f32[128,64]{0,1:T(8,128)} %param.10) | copy-start | bytes 98308
  147.7 13.8 %copy-start.16 = (bf16[128,64]{0,1:T(8,128)(2,1)S(1)}, bf16[128,64]{0,1:T(8,128)(2,1)}, u32[]{:S(2)}) copy-start(bf16[128,64]{0,1:T(8,128)(2,1)} %param.9) | copy-start | bytes 49156
  150.4 32.2 %collective-permute-start.7 = (bf16[128,1024]{1,0:T(8,128)(2,1)}, bf16[128,1024]{1,0:T(8,128)(2,1)}, u32[]{:S(2)}, u32[]{:S(2)}) collective-permute-start(bf16[128,1024]{1,0:T(8,128)(2,1)} %fusion.50), channel_id=1, source_target_pairs={{0,128},{128,0},{1,129},{129,1},{2,130},{130,2},{3,131},{131,3},{4... | collective-permute-start | bytes 786440 | tf_op jit(solution)/shard_map/ppermute | solution.py:53
  160.0 22.6 %collective-permute-start.6 = (bf16[128,512]{1,0:T(8,128)(2,1)}, bf16[128,512]{1,0:T(8,128)(2,1)}, u32[]{:S(2)}, u32[]{:S(2)}) collective-permute-start(bf16[128,512]{1,0:T(8,128)(2,1)} %get-tuple-element.34), channel_id=1, source_target_pairs={{0,16},{16,0},{1,17},{17,1},{2,18},{18,2},{3,19},{19,3},{4,20},{20... | collective-permute-start | bytes 393224 | tf_op jit(solution)/shard_map/ppermute | solution.py:53
  163.7 26.6 %all-to-all-start.6 = ((bf16[32,128,64]{1,2,0:T(8,128)(2,1)}), bf16[32,128,64]{1,2,0:T(8,128)(2,1)}, u32[]{:S(2)}, u32[]{:S(2)}) async-start(bf16[32,128,64]{1,2,0:T(8,128)(2,1)} %broadcast_in_dim.14), calls=%async_computation.6 | async-start | bytes 1048576 | tf_op jit(solution)/shard_map/all_to_all | solution.py:22
  174.5 10.6 %collective-permute-start.21 = (bf16[128,1024]{1,0:T(8,128)(2,1)S(1)}, bf16[128,1024]{1,0:T(8,128)(2,1)S(1)}, u32[]{:S(2)}, u32[]{:S(2)}) collective-permute-start(bf16[128,1024]{1,0:T(8,128)(2,1)S(1)} %get-tuple-element.55), channel_id=1, source_target_pairs={{0,16},{16,0},{1,17},{17,1},{2,18},{18,2},{3,19},{19,3},{4,20},{20... | collective-permute-start | bytes 786440 | tf_op jit(solution)/shard_map/ppermute | solution.py:53
  182.6 3.3 %collective-permute-start.8 = (bf16[128,1024]{1,0:T(8,128)(2,1)}, bf16[128,1024]{1,0:T(8,128)(2,1)S(1)}, u32[]{:S(2)}, u32[]{:S(2)}) collective-permute-start(bf16[128,1024]{1,0:T(8,128)(2,1)} %collective-permute-done.7), channel_id=1, source_target_pairs={{0,16},{16,0},{1,17},{17,1},{2,18},{18,2},{3,19},{19,3},{4,20},{20... | collective-permute-start | bytes 786440 | tf_op jit(solution)/shard_map/ppermute | solution.py:53
  185.9 4.3 %copy-start.9 = (bf16[256,1024]{1,0:T(8,128)(2,1)}, bf16[256,1024]{1,0:T(8,128)(2,1)S(1)}, u32[]{:S(2)}) copy-start(bf16[256,1024]{1,0:T(8,128)(2,1)S(1)} %constant_dynamic-update-slice_fusion.2) | copy-start | bytes 1572868
  185.9 5.4 %copy-start.5 = (f32[128,2048]{1,0:T(8,128)S(1)}, f32[128,2048]{1,0:T(8,128)}, u32[]{:S(2)}) copy-start(f32[128,2048]{1,0:T(8,128)} %get-tuple-element.17) | copy-start | bytes 3145732
  191.3 8.5 %copy-start.11 = (bf16[256,1024]{1,0:T(8,128)(2,1)S(1)}, bf16[256,1024]{1,0:T(8,128)(2,1)}, u32[]{:S(2)}) copy-start(bf16[256,1024]{1,0:T(8,128)(2,1)} %get-tuple-element.20) | copy-start | bytes 1572868
  191.3 8.5 %copy-start.18 = (bf16[1024,1024]{1,0:T(8,128)(2,1)S(1)}, bf16[1024,1024]{1,0:T(8,128)(2,1)}, u32[]{:S(2)}) copy-start(bf16[1024,1024]{1,0:T(8,128)(2,1)} %constant_dynamic-update-slice_fusion.17) | copy-start | bytes 6291460
  191.3 10.8 %copy-start.2 = (bf16[2048,1024]{1,0:T(8,128)(2,1)S(1)}, bf16[2048,1024]{1,0:T(8,128)(2,1)}, u32[]{:S(2)}) copy-start(bf16[2048,1024]{1,0:T(8,128)(2,1)} %param.15) | copy-start | bytes 12582916
  195.2 5.4 %copy-start.10 = (bf16[256,1024]{1,0:T(8,128)(2,1)S(1)}, bf16[256,1024]{1,0:T(8,128)(2,1)}, u32[]{:S(2)}) copy-start(bf16[256,1024]{1,0:T(8,128)(2,1)} %copy-done.9) | copy-start | bytes 1572868
  195.2 6.9 %copy-start.21 = (f32[256,1024]{1,0:T(8,128)S(1)}, f32[256,1024]{1,0:T(8,128)}, u32[]{:S(2)}) copy-start(f32[256,1024]{1,0:T(8,128)} %get-tuple-element.18) | copy-start | bytes 3145732
  195.3 6.8 %collective-permute-start.12 = (bf16[128,1024]{1,0:T(8,128)(2,1)S(1)}, bf16[128,1024]{1,0:T(8,128)(2,1)S(1)}, u32[]{:S(2)}, u32[]{:S(2)}) collective-permute-start(bf16[128,1024]{1,0:T(8,128)(2,1)S(1)} %get-tuple-element.63), channel_id=1, source_target_pairs={{0,16},{16,0},{1,17},{17,1},{2,18},{18,2},{3,19},{19,3},{4,20},{20... | collective-permute-start | bytes 786440 | tf_op jit(solution)/shard_map/ppermute | solution.py:53
  199.8 1.6 collective-permute-start.19
  199.8 2.2 collective-permute-start.13
  205.5 10.2 %collective-permute-start.14 = (bf16[128,1024]{1,0:T(8,128)(2,1)S(1)}, bf16[128,1024]{1,0:T(8,128)(2,1)S(1)}, u32[]{:S(2)}, u32[]{:S(2)}) collective-permute-start(bf16[128,1024]{1,0:T(8,128)(2,1)S(1)} %get-tuple-element.42), channel_id=1, source_target_pairs={{0,32},{32,64},{64,96},{96,0},{1,33},{33,65},{65,97},{97,1},{2,34}... | collective-permute-start | bytes 786440 | tf_op jit(solution)/shard_map/ppermute | solution.py:89
  205.5 16.8 %collective-permute-start.15 = (bf16[128,1024]{1,0:T(8,128)(2,1)S(1)}, bf16[128,1024]{1,0:T(8,128)(2,1)}, u32[]{:S(2)}, u32[]{:S(2)}) collective-permute-start(bf16[128,1024]{1,0:T(8,128)(2,1)S(1)} %get-tuple-element.44), channel_id=1, source_target_pairs={{0,64},{32,96},{64,0},{96,32},{1,65},{33,97},{65,1},{97,33},{2,66}... | collective-permute-start | bytes 786440 | tf_op jit(solution)/shard_map/ppermute | solution.py:89
  210.2 12.2 %collective-permute-start.16 = (bf16[128,1024]{1,0:T(8,128)(2,1)S(1)}, bf16[128,1024]{1,0:T(8,128)(2,1)}, u32[]{:S(2)}, u32[]{:S(2)}) collective-permute-start(bf16[128,1024]{1,0:T(8,128)(2,1)S(1)} %get-tuple-element.43), channel_id=1, source_target_pairs={{0,96},{32,0},{64,32},{96,64},{1,97},{33,1},{65,33},{97,65},{2,98}... | collective-permute-start | bytes 786440 | tf_op jit(solution)/shard_map/ppermute | solution.py:89
  213.5 15.1 %collective-permute-start.22 = (bf16[128,1024]{1,0:T(8,128)(2,1)S(1)}, bf16[128,1024]{1,0:T(8,128)(2,1)}, u32[]{:S(2)}, u32[]{:S(2)}) collective-permute-start(bf16[128,1024]{1,0:T(8,128)(2,1)S(1)} %get-tuple-element.39), channel_id=1, source_target_pairs={{0,32},{32,64},{64,96},{96,0},{1,33},{33,65},{65,97},{97,1},{2,34}... | collective-permute-start | bytes 786440 | tf_op jit(solution)/shard_map/ppermute | solution.py:89
  215.1 18.5 %collective-permute-start.23 = (bf16[128,1024]{1,0:T(8,128)(2,1)S(1)}, bf16[128,1024]{1,0:T(8,128)(2,1)}, u32[]{:S(2)}, u32[]{:S(2)}) collective-permute-start(bf16[128,1024]{1,0:T(8,128)(2,1)S(1)} %get-tuple-element.41), channel_id=1, source_target_pairs={{0,64},{32,96},{64,0},{96,32},{1,65},{33,97},{65,1},{97,33},{2,66}... | collective-permute-start | bytes 786440 | tf_op jit(solution)/shard_map/ppermute | solution.py:89
  215.6 0.7 copy-start.14
  216.3 17.3 %collective-permute-start.24 = (bf16[128,1024]{1,0:T(8,128)(2,1)S(1)}, bf16[128,1024]{1,0:T(8,128)(2,1)}, u32[]{:S(2)}, u32[]{:S(2)}) collective-permute-start(bf16[128,1024]{1,0:T(8,128)(2,1)S(1)} %get-tuple-element.40), channel_id=1, source_target_pairs={{0,96},{32,0},{64,32},{96,64},{1,97},{33,1},{65,33},{97,65},{2,98}... | collective-permute-start | bytes 786440 | tf_op jit(solution)/shard_map/ppermute | solution.py:89
  235.3 2.6 %copy-start.12 = (f32[64,2048]{1,0:T(8,128)S(1)}, f32[64,2048]{1,0:T(8,128)}, u32[]{:S(2)}) copy-start(f32[64,2048]{1,0:T(8,128)} %param.16) | copy-start | bytes 1572868
  235.4 2.6 %collective-permute-start.17 = (f32[64,1024]{1,0:T(8,128)S(1)}, f32[64,1024]{1,0:T(8,128)S(1)}, u32[]{:S(2)}, u32[]{:S(2)}) collective-permute-start(f32[64,1024]{1,0:T(8,128)S(1)} %get-tuple-element.59), channel_id=1, source_target_pairs={{0,16},{16,0},{1,17},{17,1},{2,18},{18,2},{3,19},{19,3},{4,20},{20... | collective-permute-start | bytes 786440 | tf_op jit(solution)/shard_map/ppermute | solution.py:53
  237.5 2.4 copy-start.6
  237.8 2.1 collective-permute-start.25

commit v3 on v2

--- a/solution.py
+++ b/solution.py
@@ -26,19 +26,6 @@
     copies = jnp.broadcast_to(array, (lax.axis_size(TENSOR), *array.shape))
     blocks = to_peers(copies, TENSOR)
     return jnp.moveaxis(blocks, 0, 1).reshape(array.shape[0], -1)
-
-
-def gathered_for_both(array):
-    axes = ("z_hi", *TENSOR)
-    copies = jnp.broadcast_to(array, (lax.axis_size(axes), *array.shape))
-    blocks = to_peers(copies, axes).reshape(2, -1, *array.shape)
-    z_hi = lax.axis_index("z_hi")
-
-    def whole(index):
-        some = lax.dynamic_index_in_dim(blocks, index, 0, keepdims=False)
-        return jnp.moveaxis(some, 0, 1).reshape(array.shape[0], -1)
-
-    return whole(z_hi), whole(1 - z_hi)
 
 
 def feature_blocks(array):
@@ -70,28 +57,45 @@
     return sums + before + after
 
 
-def half_of(array, index, dim):
-    width = array.shape[dim] // 2
-    return lax.dynamic_slice_in_dim(array, index * width, width, dim)
+def rows_of_core(array, core):
+    tokens, features = array.shape
+    blocks = array.reshape(tokens, lax.axis_size(BLOCKS), 2, -1)
+    return lax.dynamic_index_in_dim(blocks, core, 2, keepdims=False).reshape(tokens, features // 2)
 
 
-def summed_over_dp(left, right):
-    core, y = lax.axis_index("core"), lax.axis_index("y")
-    n_y = lax.axis_size("y")
+def for_both_cores(array, core):
+    return [rows_of_core(array, core), from_partner(rows_of_core(array, 1 - core), "core")]
+
+
+def picked(blocks, index, dim):
+    return lax.dynamic_index_in_dim(blocks, index, dim, keepdims=False)
+
+
+def over_y(blocks, dim):
+    y, n_y = lax.axis_index("y"), lax.axis_size("y")
+    total = picked(blocks, y, dim).astype(jnp.float32)
+    for shift in range(1, n_y):
+        ring = [(i, (i + shift) % n_y) for i in range(n_y)]
+        sent = picked(blocks, lax.rem(y + shift, n_y), dim).astype(jnp.bfloat16)
+        total = total + lax.ppermute(sent, "y", ring).astype(jnp.float32)
+    return total
+
+
+def over_z(blocks):
+    z_hi = lax.axis_index("z_hi")
+    sent = picked(blocks, 1 - z_hi, 0).astype(jnp.bfloat16)
+    return picked(blocks, z_hi, 0).astype(jnp.float32) + from_partner(sent, "z_hi").astype(
+        jnp.float32
+    )
+
+
+def summed_over_dp(lefts, rights):
+    left, right = jnp.concatenate(lefts, 0), jnp.concatenate(rights, 0)
     partial = lax.dot_general(
         left, right, (((0,), (0,)), ((), ())), preferred_element_type=jnp.float32
     ).astype(jnp.bfloat16)
-    blocks = partial.reshape(n_y, -1, right.shape[1])
-    rows = lax.dynamic_index_in_dim(blocks, y, 0, keepdims=False).astype(jnp.float32)
-    for shift in range(1, n_y):
-        sent = lax.dynamic_index_in_dim(blocks, lax.rem(y + shift, n_y), 0, keepdims=False)
-        ring = [(i, (i + shift) % n_y) for i in range(n_y)]
-        rows = rows + lax.ppermute(sent, "y", ring).astype(jnp.float32)
-    mine = half_of(rows, core, 0)
-    theirs = from_partner(half_of(rows, 1 - core, 0), "core")
-    return jnp.where(
-        core == 0, jnp.concatenate([mine, theirs], 1), jnp.concatenate([theirs, mine], 1)
-    )
+    blocks = partial.reshape(lax.axis_size("z_hi"), lax.axis_size("y"), -1, right.shape[1])
+    return over_z(over_y(blocks, 1))
 
 
 def shards(
@@ -101,14 +105,13 @@
     local_tokens, width_local = tokens.shape
     loss_scale = (local_tokens * dp_count) ** (-0.5)
     column = lax.axis_index(TENSOR)
-    core, z_hi = lax.axis_index("core"), lax.axis_index("z_hi")
+    core = lax.axis_index("core")
     gain_local = lax.dynamic_slice_in_dim(norm_gain, column * width_local, width_local)
     labels = jnp.arange(EXAMPLES, dtype=jnp.int32)
     onehot = (segment_ids[:, None] == labels[None, :]).astype(jnp.float32)
     perturb = adv_init * init_noise
     embedded = tokens.astype(jnp.float32) + perturb
     whole = gathered_features(embedded)
-    half_in, half_out = half_of(weight_in, core, 1), half_of(weight_out, core, 0)
     lefts_in, rights_in, lefts_out, rights_out = [], [], [], []
     for ascent in range(ASCENTS):
         last = ascent + 1 == ASCENTS
@@ -119,34 +122,17 @@
         hidden, slope = gelu_and_slope(preact)
         partial_value = jnp.dot(hidden, weight_out, preferred_element_type=jnp.float32)
         mixed = over_tensor(feature_blocks(partial_value.astype(jnp.bfloat16)))
-        far_normed = from_partner(normed, "z_hi")
-        far_normed = jnp.concatenate([far_normed, from_partner(far_normed, "core")], 0)
-        far_preact = jnp.dot(far_normed, half_in, preferred_element_type=jnp.float32)
-        far_hidden, far_slope = gelu_and_slope(far_preact)
-        near_hidden = [half_of(hidden, core, 1), from_partner(half_of(hidden, 1 - core, 1), "core")]
-        rights_out += [*near_hidden, far_hidden]
-        some_normed = half_of(normed, z_hi, 1)
-        lefts_in += [some_normed, from_partner(some_normed, "core"), half_of(far_normed, z_hi, 1)]
+        rights_out += [hidden, from_partner(hidden, "core")]
+        lefts_in += for_both_cores(normed, core)
         out_grad = (embedded + mixed - target) * loss_scale
+        grad = gathered_features(out_grad.astype(jnp.bfloat16))
+        lefts_out += for_both_cores(grad, core)
         if last:
-            grad, far_grad = gathered_for_both(out_grad.astype(jnp.bfloat16))
-        else:
-            grad = gathered_features(out_grad.astype(jnp.bfloat16))
-            far_grad = from_partner(grad, "z_hi")
-        some_grad = half_of(grad, z_hi, 1)
-        far_grad = jnp.concatenate([far_grad, from_partner(far_grad, "core")], 0)
-        lefts_out += [some_grad, from_partner(some_grad, "core"), half_of(far_grad, z_hi, 1)]
+            summed_out = summed_over_dp(lefts_out, rights_out).T
         hidden_grad = (
             jnp.dot(grad, weight_out.T, preferred_element_type=jnp.float32) * slope
         ).astype(jnp.bfloat16)
-        far_hidden_grad = (
-            jnp.dot(far_grad, half_out.T, preferred_element_type=jnp.float32) * far_slope
-        ).astype(jnp.bfloat16)
-        rights_in += [
-            half_of(hidden_grad, core, 1),
-            from_partner(half_of(hidden_grad, 1 - core, 1), "core"),
-            far_hidden_grad,
-        ]
+        rights_in += [hidden_grad, from_partner(hidden_grad, "core")]
         if not last:
             normed_partial = jnp.dot(hidden_grad, weight_in.T, preferred_element_type=jnp.float32)
             dot_partial = jnp.sum(normed_partial * norm_gain * emb, axis=1)
@@ -178,10 +164,7 @@
             perturb = perturb + delta_grad * token_scale
             embedded = tokens.astype(jnp.float32) + perturb
             whole = whole + delta_whole * token_scale
-    summed_out = summed_over_dp(
-        jnp.concatenate(lefts_out, 0), jnp.concatenate(rights_out, 0)
-    ).T
-    summed_in = summed_over_dp(jnp.concatenate(lefts_in, 0), jnp.concatenate(rights_in, 0))
+    summed_in = summed_over_dp(lefts_in, rights_in)
     dp_rows = moment_in.shape[0]
     offset = lax.axis_index(DP) * dp_rows
     own_in = lax.dynamic_slice_in_dim(weight_in, offset, dp_rows, 0)

time: 245 us -> 222 us (0.906); the launches traced: 241 us -> 221 us
  starting transfers between devices: 94.1 us -> 51.2 us
  blocking collectives: 34.7 us -> 73.7 us
  waiting for transfers between devices: 33.4 us -> 57.9 us
  local copies, waits for them, and re-layouts: 30.3 us -> 6.33 us
  matrix products: 36 us -> 23 us
  other arithmetic: 11.1 us -> 7.93 us
    all_to_all x2 -> x5, blocking collectives: 34.7 us -> 73.7 us  [to_peers(): return lax.all_to_all(blocks, axis, 0, 0, tiled=True)]
    all_to_all x5 -> x2, starting transfers between devices: 42.1 us -> 11.3 us  [to_peers(): return lax.all_to_all(blocks, axis, 0, 0, tiled=True)]
    ppermute x6, waiting for transfers between devices: 15.9 us -> 35.1 us  [over_y(): total = total + lax.ppermute(sent, 'y', ring).astype(jnp.float32)]
    ppermute x18 -> x11, starting transfers between devices: 39.3 us -> 21.3 us  [from_partner(): return lax.ppermute(array, axis, [(0, 1), (1, 0)])]
    unnamed x63 -> x25, local copies, waits for them, and re-layouts: 17.6 us -> 1.8 us
    dot_general x4 -> x0, matrix products: 11.7 us -> none  [the longest x2 8.32 us: shards(): jnp.dot(far_normed, half_in, preferred_element_type=jnp.float32)]
    all_to_all x5 -> x2, waiting for transfers between devices: 2.65 us -> 10.3 us  [to_peers(): return lax.all_to_all(blocks, axis, 0, 0, tiled=True)]
    ppermute x6, starting transfers between devices: 8.23 us -> 13.3 us  [over_y(): total = total + lax.ppermute(sent, 'y', ring).astype(jnp.float32)]
  transfers between devices with their start and end apart: 31 -> 21, of which waited for: 9 -> 9; matrix products, arithmetic and copies ran while one was open for 24% -> 6% of each run, Pallas kernels for 0% -> 0%
where the time goes in v3:
time: 222 us; the launch traced here: 221 us
  blocking collectives  73.7 us (33%)
  waiting for transfers between devices  57.9 us (26%)
  starting transfers between devices  51.2 us (23%)
  matrix products  23 us (10%)
  other arithmetic  7.93 us (4%)
  local copies, waits for them, and re-layouts  6.33 us (3%)
    all_to_all x5, blocking collectives, to_peers(): return lax.all_to_all(blocks, axis, 0, 0, tiled=True)  73.7 us
    ppermute x6, waiting for transfers between devices, over_y(): total = total + lax.ppermute(sent, 'y', ring).astype(jnp.float32)  35.1 us
    ppermute x11, starting transfers between devices, from_partner(): return lax.ppermute(array, axis, [(0, 1), (1, 0)])  21.3 us
    ppermute x6, starting transfers between devices, over_y(): total = total + lax.ppermute(sent, 'y', ring).astype(jnp.float32)  13.3 us
    ppermute x11, waiting for transfers between devices, from_partner(): return lax.ppermute(array, axis, [(0, 1), (1, 0)])  12 us
    all_to_all x2, starting transfers between devices, to_peers(): return lax.all_to_all(blocks, axis, 0, 0, tiled=True)  11.3 us
    all_to_all x2, waiting for transfers between devices, to_peers(): return lax.all_to_all(blocks, axis, 0, 0, tiled=True)  10.3 us
    dot_general x2, matrix products, shards(): jnp.dot(grad, weight_out.T, preferred_element_type=jnp.float32) * slope  7.41 us
  transfers between devices with their start and end apart: 21, of which 9 were waited for; matrix products, arithmetic and copies ran while one was open for 6% of the time, Pallas kernels for 0%

profile of v3, /device:TPU:33, one launch (start us, length us, event | category | flops | bytes accessed | tf_op | source)
XLA Modules:
  0.0 221.2 jit_solution(17742077034225047811)
XLA Ops:
  0.6 0.8 convert_add_fusion.3
  1.5 20.2 %all_to_all.35 = f32[16,128,64]{1,2,0:T(8,128)S(1)} all-to-all(f32[16,128,64]{1,2,0:T(8,128)S(1)} %broadcast_in_dim.10), channel_id=1, replica_groups=mesh['z_hi'=2,'y'=4,'core'=2,'x'=4,'z_lo'=4] {'x','z_lo'}, dimensions={0} | all-to-all | bytes 1048576 | tf_op jit(solution)/shard_map/all_to_all | solution.py:22
  21.7 0.2 copy.37
  21.9 0.1 fusion.33
  22.1 0.8 fusion.35
  22.9 3.7 %fusion.20 = (f32[128,2048]{1,0:T(8,128)S(1)}, bf16[128,2048]{1,0:T(8,128)(2,1)S(1)}) fusion(bf16[128,1024]{1,0:T(8,128)(2,1)S(1)} %fusion.35, bf16[1024,2048]{1,0:T(8,128)(2,1)} %param.14), kind=kOutput, calls=%fused_computation.30 | convolution fusion | flops 541851648 | bytes 6029312 | tf_op jit(solution)/shard_map/dot_general | solution.py:121
  26.6 0.8 copy-done.4
  27.4 0.7 convolution_convert_fusion.3
  28.1 0.2 copy.39
  28.3 14.7 %all_to_all.36 = bf16[16,128,64]{1,2,0:T(8,128)(2,1)S(1)} all-to-all(bf16[16,128,64]{1,2,0:T(8,128)(2,1)S(1)} %bitcast.126), channel_id=1, replica_groups=mesh['z_hi'=2,'y'=4,'core'=2,'x'=4,'z_lo'=4] {'x','z_lo'}, dimensions={0} | all-to-all | bytes 524288 | tf_op jit(solution)/shard_map/all_to_all | solution.py:22
  43.2 13.3 %all_to_all.37 = bf16[16,128,64]{1,2,0:T(8,128)(2,1)S(1)} all-to-all(bf16[16,128,64]{1,2,0:T(8,128)(2,1)S(1)} %broadcast_in_dim.11), channel_id=1, replica_groups=mesh['z_hi'=2,'y'=4,'core'=2,'x'=4,'z_lo'=4] {'x','z_lo'}, dimensions={0} | all-to-all | bytes 524288 | tf_op jit(solution)/shard_map/all_to_all | solution.py:22
  56.5 3.7 %fusion = bf16[128,2048]{1,0:T(8,128)(2,1)S(1)} fusion(f32[128,2048]{1,0:T(8,128)S(1)} %get-tuple-element.10, bf16[128,1024]{0,1:T(8,128)(2,1)S(1)} %bitcast.113, bf16[2048,1024]{1,0:T(8,128)(2,1)} %param.15), kind=kOutput, calls=%fused_computation.4 | convolution fusion | flops 537395200 | bytes 6029312 | tf_op jit(solution)/shard_map/dot_general | solution.py:133
  60.2 1.6 fusion.71
  61.8 0.2 copy.40
  62.0 0.7 pad_maximum_fusion
  62.8 5.6 %all-to-all-start.3 = ((bf16[16,128,66]{1,2,0:T(8,128)(2,1)}), bf16[16,128,66]{1,2,0:T(8,128)(2,1)S(1)}, u32[]{:S(2)}, u32[]{:S(2)}) async-start(bf16[16,128,66]{1,2,0:T(8,128)(2,1)} %pad_maximum_fusion), calls=%async_computation.3 | async-start | bytes 589824 | tf_op jit(solution)/shard_map/all_to_all | solution.py:22
  68.5 8.0 %all-to-all-done.3 = bf16[16,128,66]{1,2,0:T(8,128)(2,1)S(1)} async-done(((bf16[16,128,66]{1,2,0:T(8,128)(2,1)}), bf16[16,128,66]{1,2,0:T(8,128)(2,1)S(1)}, u32[]{:S(2)}, u32[]{:S(2)}) %all-to-all-start.3) | async-done | bytes 270368 | tf_op jit(solution)/shard_map/all_to_all | solution.py:22
  76.7 13.7 %all_to_all.38 = bf16[16,128,64]{1,2,0:T(8,128)(2,1)S(1)} all-to-all(bf16[16,128,64]{1,2,0:T(8,128)(2,1)S(1)} %broadcast_in_dim.13), channel_id=1, replica_groups=mesh['z_hi'=2,'y'=4,'core'=2,'x'=4,'z_lo'=4] {'x','z_lo'}, dimensions={0} | all-to-all | bytes 524288 | tf_op jit(solution)/shard_map/all_to_all | solution.py:22
  90.4 0.2 multiply_reduce_fusion
  90.6 2.7 %collective-permute-start.1 = (f32[2,32]{1,0:T(2,128)S(1)}, f32[2,32]{1,0:T(2,128)S(1)}, u32[]{:S(2)}, u32[]{:S(2)}) collective-permute-start(f32[2,32]{1,0:T(2,128)S(1)} %pad_maximum_fusion.1), channel_id=1, source_target_pairs={{0,16},{16,0},{1,17},{17,1},{2,18},{18,2},{3,19},{19,3},{4,20},{20... | collective-permute-start | bytes 776 | tf_op jit(solution)/shard_map/ppermute | solution.py:40
  93.3 0.8 collective-permute-done.1
  94.2 1.3 collective-permute-start.3
  95.5 4.0 %collective-permute-start.2 = (f32[2,32]{1,0:T(2,128)S(1)}, f32[2,32]{1,0:T(2,128)S(1)}, u32[]{:S(2)}, u32[]{:S(2)}) collective-permute-start(f32[2,32]{1,0:T(2,128)S(1)} %fusion.67), channel_id=1, source_target_pairs={{0,32},{32,64},{64,96},{96,128},{128,160},{160,192},{192,224},{1,3... | collective-permute-start | bytes 776 | tf_op jit(solution)/shard_map/ppermute | solution.py:55
  99.5 0.2 copy.41
  99.7 0.4 collective-permute-done.2
  100.6 0.1 fusion.32
  100.7 3.7 %fusion.25 = (f32[128,2048]{1,0:T(8,128)S(1)}, bf16[128,2048]{1,0:T(8,128)(2,1)S(1)}) fusion(bf16[128,1024]{1,0:T(8,128)(2,1)S(1)} %fusion.32, bf16[1024,2048]{1,0:T(8,128)(2,1)} %param.14), kind=kOutput, calls=%fused_computation.35 | convolution fusion | flops 541851648 | bytes 6029312 | tf_op jit(solution)/shard_map/dot_general | solution.py:121
  104.4 0.8 copy-done.5
  105.2 0.7 convolution_convert_fusion.2
  105.9 0.2 copy.44
  106.1 11.8 %all_to_all.39 = bf16[16,128,64]{1,2,0:T(8,128)(2,1)S(1)} all-to-all(bf16[16,128,64]{1,2,0:T(8,128)(2,1)S(1)} %bitcast.127), channel_id=1, replica_groups=mesh['z_hi'=2,'y'=4,'core'=2,'x'=4,'z_lo'=4] {'x','z_lo'}, dimensions={0} | all-to-all | bytes 524288 | tf_op jit(solution)/shard_map/all_to_all | solution.py:22
  118.0 0.6 fusion.59
  118.6 0.8 broadcast_in_dim.14
  119.4 5.7 %all-to-all-start.6 = ((bf16[16,128,64]{1,2,0:T(8,128)(2,1)}), bf16[16,128,64]{1,2,0:T(8,128)(2,1)S(1)}, u32[]{:S(2)}, u32[]{:S(2)}) async-start(bf16[16,128,64]{1,2,0:T(8,128)(2,1)} %broadcast_in_dim.14), calls=%async_computation.6 | async-start | bytes 524288 | tf_op jit(solution)/shard_map/all_to_all | solution.py:22
  125.1 1.2 constant_dynamic-slice_fusion.4
  126.3 0.2 copy.53
  126.5 0.2 copy.38
  126.7 2.2 collective-permute-start.13
  129.0 0.7 constant_dynamic-slice_fusion.3
  129.7 0.4 collective-permute-start.11
  130.1 0.2 copy.43
  130.3 0.2 collective-permute-start.14
  130.5 2.3 %all-to-all-done.6 = bf16[16,128,64]{1,2,0:T(8,128)(2,1)S(1)} async-done(((bf16[16,128,64]{1,2,0:T(8,128)(2,1)}), bf16[16,128,64]{1,2,0:T(8,128)(2,1)S(1)}, u32[]{:S(2)}, u32[]{:S(2)}) %all-to-all-start.6) | async-done | bytes 262176 | tf_op jit(solution)/shard_map/all_to_all | solution.py:22
  132.9 2.9 %collective-permute-start.12 = (bf16[128,512]{0,1:T(8,128)(2,1)S(1)}, bf16[128,512]{0,1:T(8,128)(2,1)S(1)}, u32[]{:S(2)}, u32[]{:S(2)}) collective-permute-start(bf16[128,512]{0,1:T(8,128)(2,1)S(1)} %bitcast.134), channel_id=1, source_target_pairs={{0,16},{16,0},{1,17},{17,1},{2,18},{18,2},{3,19},{19,3},{4,20},{20... | collective-permute-start | bytes 393224 | tf_op jit(solution)/shard_map/ppermute | solution.py:40
  135.7 3.7 %fusion.1 = bf16[128,2048]{1,0:T(8,128)(2,1)S(1)} fusion(f32[128,2048]{1,0:T(8,128)S(1)} %get-tuple-element.12, bf16[128,1024]{0,1:T(8,128)(2,1)S(1)} %bitcast.116, bf16[2048,1024]{1,0:T(8,128)(2,1)} %param.15), kind=kOutput, calls=%fused_computation.5 | convolution fusion | flops 537395200 | bytes 6029312 | tf_op jit(solution)/shard_map/dot_general | solution.py:133
  139.6 0.5 collective-permute-start
  140.2 2.9 %convolution_convert_fusion = bf16[512,2048]{1,0:T(8,128)(2,1)S(1)} fusion(bf16[128,2048]{1,0:T(8,128)(2,1)} %collective-permute-done.14, bf16[128,2048]{1,0:T(8,128)(2,1)} %copy-done.5, bf16[128,2048]{1,0:T(8,128)(2,1)} %collective-permute-done.13, bf16[128,2048]{1,0:T(8,128)(2,1)} %copy-done.4, bf16[128,512]{0,1:T(8,128)(2,1)S(1)} %collective-permute-done.12, ...), kind=kOutput, calls=%fused_computation | convolution fusion | flops 1085276160 | bytes 4718592 | tf_op jit(solution)/shard_map/dot_general | solution.py:94
  143.0 0.2 dynamic-slice_bitcast_fusion.2
  143.2 8.8 %collective-permute-start.17 = (bf16[2,64,2048]{2,1,0:T(8,128)(2,1)S(1)}, bf16[2,64,2048]{2,1,0:T(8,128)(2,1)S(1)}, u32[]{:S(2)}, u32[]{:S(2)}) collective-permute-start(bf16[2,64,2048]{2,1,0:T(8,128)(2,1)S(1)} %get-tuple-element.24), channel_id=1, source_target_pairs={{0,96},{32,0},{64,32},{96,64},{1,97},{33,1},{65,33},{97,65},{2,98}... | collective-permute-start | bytes 1572872 | tf_op jit(solution)/shard_map/ppermute | solution.py:80
  152.1 0.7 collective-permute-start.15
  152.8 2.3 %convolution_convert_fusion.1 = bf16[512,2048]{1,0:T(8,128)(2,1)S(1)} fusion(bf16[128,2048]{1,0:T(8,128)(2,1)S(1)} %collective-permute-done.6, bf16[128,2048]{1,0:T(8,128)(2,1)S(1)} %fusion.1, bf16[128,2048]{1,0:T(8,128)(2,1)} %collective-permute-done.5, bf16[128,2048]{1,0:T(8,128)(2,1)S(1)} %fusion, bf16[128,512]{0,1:T(8,128)(2,1)S(1)} %collective-permute-done.4, ...), kind=kOutput, calls=%fused_computation.1 | convolution fusion | flops 1085276160 | bytes 4718592 | tf_op jit(solution)/shard_map/dot_general | solution.py:94
  155.2 2.2 collective-permute-start.9
  157.4 1.7 collective-permute-start.8
  159.0 15.2 %collective-permute-done.17 = bf16[2,64,2048]{2,1,0:T(8,128)(2,1)S(1)} collective-permute-done((bf16[2,64,2048]{2,1,0:T(8,128)(2,1)S(1)}, bf16[2,64,2048]{2,1,0:T(8,128)(2,1)S(1)}, u32[]{:S(2)}, u32[]{:S(2)}) %collective-permute-start.17) | collective-permute-done | bytes 524320 | tf_op jit(solution)/shard_map/ppermute | solution.py:80
  174.2 4.6 %collective-permute-done.15 = bf16[2,64,2048]{2,1,0:T(8,128)(2,1)S(1)} collective-permute-done((bf16[2,64,2048]{2,1,0:T(8,128)(2,1)S(1)}, bf16[2,64,2048]{2,1,0:T(8,128)(2,1)S(1)}, u32[]{:S(2)}, u32[]{:S(2)}) %collective-permute-start.15) | collective-permute-done | bytes 524320 | tf_op jit(solution)/shard_map/ppermute | solution.py:80
  178.8 0.3 fusion.27
  179.2 6.1 %collective-permute-start.18 = (bf16[64,2048]{1,0:T(8,128)(2,1)S(1)}, bf16[64,2048]{1,0:T(8,128)(2,1)S(1)}, u32[]{:S(2)}, u32[]{:S(2)}) collective-permute-start(bf16[64,2048]{1,0:T(8,128)(2,1)S(1)} %fusion.55), channel_id=1, source_target_pairs={{0,128},{128,0},{1,129},{129,1},{2,130},{130,2},{3,131},{131,3},{4... | collective-permute-start | bytes 786440 | tf_op jit(solution)/shard_map/ppermute | solution.py:40
  185.2 11.4 %collective-permute-done.9 = bf16[2,64,2048]{2,1,0:T(8,128)(2,1)S(1)} collective-permute-done((bf16[2,64,2048]{2,1,0:T(8,128)(2,1)S(1)}, bf16[2,64,2048]{2,1,0:T(8,128)(2,1)S(1)}, u32[]{:S(2)}, u32[]{:S(2)}) %collective-permute-start.9) | collective-permute-done | bytes 524320 | tf_op jit(solution)/shard_map/ppermute | solution.py:80
  196.7 3.9 %collective-permute-done.7 = bf16[2,64,2048]{2,1,0:T(8,128)(2,1)S(1)} collective-permute-done((bf16[2,64,2048]{2,1,0:T(8,128)(2,1)S(1)}, bf16[2,64,2048]{2,1,0:T(8,128)(2,1)S(1)}, u32[]{:S(2)}, u32[]{:S(2)}) %collective-permute-start.7) | collective-permute-done | bytes 524320 | tf_op jit(solution)/shard_map/ppermute | solution.py:80
  200.6 0.3 fusion.29
  200.9 6.0 %collective-permute-start.10 = (bf16[64,2048]{1,0:T(8,128)(2,1)S(1)}, bf16[64,2048]{1,0:T(8,128)(2,1)S(1)}, u32[]{:S(2)}, u32[]{:S(2)}) collective-permute-start(bf16[64,2048]{1,0:T(8,128)(2,1)S(1)} %fusion.54), channel_id=1, source_target_pairs={{0,128},{128,0},{1,129},{129,1},{2,130},{130,2},{3,131},{131,3},{4... | collective-permute-start | bytes 786440 | tf_op jit(solution)/shard_map/ppermute | solution.py:40
  207.0 1.0 subtract_convert_fusion
  208.0 11.2 %collective-permute-done.10 = bf16[64,2048]{1,0:T(8,128)(2,1)S(1)} collective-permute-done((bf16[64,2048]{1,0:T(8,128)(2,1)S(1)}, bf16[64,2048]{1,0:T(8,128)(2,1)S(1)}, u32[]{:S(2)}, u32[]{:S(2)}) %collective-permute-start.10) | collective-permute-done | bytes 262176 | tf_op jit(solution)/shard_map/ppermute | solution.py:40
  219.2 2.0 subtract_convert_fusion.1
  (70 shorter events, 1.7 us)
Async XLA Ops:
  22.9 4.5 %copy-start = (bf16[2048,1024]{1,0:T(8,128)(2,1)S(1)}, bf16[2048,1024]{1,0:T(8,128)(2,1)}, u32[]{:S(2)}) copy-start(bf16[2048,1024]{1,0:T(8,128)(2,1)} %param.15) | copy-start | bytes 12582916
  26.6 0.8 copy-start.4
  26.6 16.5 %copy-start.7 = (f32[128,64]{0,1:T(8,128)S(1)}, f32[128,64]{0,1:T(8,128)}, u32[]{:S(2)}) copy-start(f32[128,64]{0,1:T(8,128)} %param.12) | copy-start | bytes 98308
  28.1 32.0 %copy-start.10 = (f32[1024]{0:T(1024)S(1)}, f32[1024]{0:T(1024)}, u32[]{:S(2)}) copy-start(f32[1024]{0:T(1024)} %param.13) | copy-start | bytes 12292
  28.3 31.9 %copy-start.2 = (bf16[1024,2048]{1,0:T(8,128)(2,1)S(1)}, bf16[1024,2048]{1,0:T(8,128)(2,1)}, u32[]{:S(2)}) copy-start(bf16[1024,2048]{1,0:T(8,128)(2,1)} %param.14) | copy-start | bytes 12582916
  60.2 30.3 %copy-start.11 = (s32[128]{0:T(128)S(1)}, s32[128]{0:T(128)}, u32[]{:S(2)}) copy-start(s32[128]{0:T(128)} %param.11) | copy-start | bytes 1540
  62.8 13.7 %all-to-all-start.3 = ((bf16[16,128,66]{1,2,0:T(8,128)(2,1)}), bf16[16,128,66]{1,2,0:T(8,128)(2,1)S(1)}, u32[]{:S(2)}, u32[]{:S(2)}) async-start(bf16[16,128,66]{1,2,0:T(8,128)(2,1)} %pad_maximum_fusion), calls=%async_computation.3 | async-start | bytes 589824 | tf_op jit(solution)/shard_map/all_to_all | solution.py:22
  90.6 3.5 %collective-permute-start.1 = (f32[2,32]{1,0:T(2,128)S(1)}, f32[2,32]{1,0:T(2,128)S(1)}, u32[]{:S(2)}, u32[]{:S(2)}) collective-permute-start(f32[2,32]{1,0:T(2,128)S(1)} %pad_maximum_fusion.1), channel_id=1, source_target_pairs={{0,16},{16,0},{1,17},{17,1},{2,18},{18,2},{3,19},{19,3},{4,20},{20... | collective-permute-start | bytes 776 | tf_op jit(solution)/shard_map/ppermute | solution.py:40
  94.2 5.5 %collective-permute-start.3 = (f32[2,32]{1,0:T(2,128)S(1)}, f32[2,32]{1,0:T(2,128)S(1)}, u32[]{:S(2)}, u32[]{:S(2)}) collective-permute-start(f32[2,32]{1,0:T(2,128)S(1)} %fusion.67), channel_id=1, source_target_pairs={{32,0},{64,32},{96,64},{128,96},{160,128},{192,160},{224,192},{33,... | collective-permute-start | bytes 776 | tf_op jit(solution)/shard_map/ppermute | solution.py:56
  95.5 4.7 %collective-permute-start.2 = (f32[2,32]{1,0:T(2,128)S(1)}, f32[2,32]{1,0:T(2,128)S(1)}, u32[]{:S(2)}, u32[]{:S(2)}) collective-permute-start(f32[2,32]{1,0:T(2,128)S(1)} %fusion.67), channel_id=1, source_target_pairs={{0,32},{32,64},{64,96},{96,128},{128,160},{160,192},{192,224},{1,3... | collective-permute-start | bytes 776 | tf_op jit(solution)/shard_map/ppermute | solution.py:55
  100.7 4.5 %copy-start.1 = (bf16[2048,1024]{1,0:T(8,128)(2,1)S(1)}, bf16[2048,1024]{1,0:T(8,128)(2,1)}, u32[]{:S(2)}) copy-start(bf16[2048,1024]{1,0:T(8,128)(2,1)} %param.15) | copy-start | bytes 12582916
  104.4 0.8 copy-start.5
  104.4 13.6 %copy-start.8 = (f32[128,64]{0,1:T(8,128)S(1)}, f32[128,64]{0,1:T(8,128)}, u32[]{:S(2)}) copy-start(f32[128,64]{0,1:T(8,128)} %param.10) | copy-start | bytes 98308
  104.4 13.6 %copy-start.9 = (bf16[128,64]{0,1:T(8,128)(2,1)S(1)}, bf16[128,64]{0,1:T(8,128)(2,1)}, u32[]{:S(2)}) copy-start(bf16[128,64]{0,1:T(8,128)(2,1)} %param.9) | copy-start | bytes 49156
  119.4 13.4 %all-to-all-start.6 = ((bf16[16,128,64]{1,2,0:T(8,128)(2,1)}), bf16[16,128,64]{1,2,0:T(8,128)(2,1)S(1)}, u32[]{:S(2)}, u32[]{:S(2)}) async-start(bf16[16,128,64]{1,2,0:T(8,128)(2,1)} %broadcast_in_dim.14), calls=%async_computation.6 | async-start | bytes 524288 | tf_op jit(solution)/shard_map/all_to_all | solution.py:22
  126.7 12.7 %collective-permute-start.13 = (bf16[128,2048]{1,0:T(8,128)(2,1)}, bf16[128,2048]{1,0:T(8,128)(2,1)}, u32[]{:S(2)}, u32[]{:S(2)}) collective-permute-start(bf16[128,2048]{1,0:T(8,128)(2,1)} %copy-done.4), channel_id=1, source_target_pairs={{0,16},{16,0},{1,17},{17,1},{2,18},{18,2},{3,19},{19,3},{4,20},{20... | collective-permute-start | bytes 1572872 | tf_op jit(solution)/shard_map/ppermute | solution.py:40
  128.9 23.1 %collective-permute-start.5 = (bf16[128,2048]{1,0:T(8,128)(2,1)S(1)}, bf16[128,2048]{1,0:T(8,128)(2,1)}, u32[]{:S(2)}, u32[]{:S(2)}) collective-permute-start(bf16[128,2048]{1,0:T(8,128)(2,1)S(1)} %fusion), channel_id=1, source_target_pairs={{0,16},{16,0},{1,17},{17,1},{2,18},{18,2},{3,19},{19,3},{4,20},{20... | collective-permute-start | bytes 1572872 | tf_op jit(solution)/shard_map/ppermute | solution.py:40
  129.7 9.9 %collective-permute-start.11 = (bf16[128,512]{0,1:T(8,128)(2,1)}, bf16[128,512]{0,1:T(8,128)(2,1)}, u32[]{:S(2)}, u32[]{:S(2)}) collective-permute-start(bf16[128,512]{0,1:T(8,128)(2,1)} %bitcast.35), channel_id=1, source_target_pairs={{0,16},{16,0},{1,17},{17,1},{2,18},{18,2},{3,19},{19,3},{4,20},{20... | collective-permute-start | bytes 393224 | tf_op jit(solution)/shard_map/ppermute | solution.py:40
  130.3 9.8 %collective-permute-start.14 = (bf16[128,2048]{1,0:T(8,128)(2,1)}, bf16[128,2048]{1,0:T(8,128)(2,1)}, u32[]{:S(2)}, u32[]{:S(2)}) collective-permute-start(bf16[128,2048]{1,0:T(8,128)(2,1)} %copy-done.5), channel_id=1, source_target_pairs={{0,16},{16,0},{1,17},{17,1},{2,18},{18,2},{3,19},{19,3},{4,20},{20... | collective-permute-start | bytes 1572872 | tf_op jit(solution)/shard_map/ppermute | solution.py:40
  132.9 7.3 %collective-permute-start.12 = (bf16[128,512]{0,1:T(8,128)(2,1)S(1)}, bf16[128,512]{0,1:T(8,128)(2,1)S(1)}, u32[]{:S(2)}, u32[]{:S(2)}) collective-permute-start(bf16[128,512]{0,1:T(8,128)(2,1)S(1)} %bitcast.134), channel_id=1, source_target_pairs={{0,16},{16,0},{1,17},{17,1},{2,18},{18,2},{3,19},{19,3},{4,20},{20... | collective-permute-start | bytes 393224 | tf_op jit(solution)/shard_map/ppermute | solution.py:40
  139.5 12.6 %collective-permute-start.4 = (bf16[128,512]{0,1:T(8,128)(2,1)S(1)}, bf16[128,512]{0,1:T(8,128)(2,1)S(1)}, u32[]{:S(2)}, u32[]{:S(2)}) collective-permute-start(bf16[128,512]{0,1:T(8,128)(2,1)S(1)} %bitcast.131), channel_id=1, source_target_pairs={{0,16},{16,0},{1,17},{17,1},{2,18},{18,2},{3,19},{19,3},{4,20},{20... | collective-permute-start | bytes 393224 | tf_op jit(solution)/shard_map/ppermute | solution.py:40
  139.6 13.2 %collective-permute-start = (bf16[128,512]{0,1:T(8,128)(2,1)S(1)}, bf16[128,512]{0,1:T(8,128)(2,1)S(1)}, u32[]{:S(2)}, u32[]{:S(2)}) collective-permute-start(bf16[128,512]{0,1:T(8,128)(2,1)S(1)} %bitcast.130), channel_id=1, source_target_pairs={{0,16},{16,0},{1,17},{17,1},{2,18},{18,2},{3,19},{19,3},{4,20},{20... | collective-permute-start | bytes 393224 | tf_op jit(solution)/shard_map/ppermute | solution.py:40
  140.1 12.7 %collective-permute-start.6 = (bf16[128,2048]{1,0:T(8,128)(2,1)S(1)}, bf16[128,2048]{1,0:T(8,128)(2,1)S(1)}, u32[]{:S(2)}, u32[]{:S(2)}) collective-permute-start(bf16[128,2048]{1,0:T(8,128)(2,1)S(1)} %fusion.1), channel_id=1, source_target_pairs={{0,16},{16,0},{1,17},{17,1},{2,18},{18,2},{3,19},{19,3},{4,20},{20... | collective-permute-start | bytes 1572872 | tf_op jit(solution)/shard_map/ppermute | solution.py:40
  143.2 31.0 %collective-permute-start.17 = (bf16[2,64,2048]{2,1,0:T(8,128)(2,1)S(1)}, bf16[2,64,2048]{2,1,0:T(8,128)(2,1)S(1)}, u32[]{:S(2)}, u32[]{:S(2)}) collective-permute-start(bf16[2,64,2048]{2,1,0:T(8,128)(2,1)S(1)} %get-tuple-element.24), channel_id=1, source_target_pairs={{0,96},{32,0},{64,32},{96,64},{1,97},{33,1},{65,33},{97,65},{2,98}... | collective-permute-start | bytes 1572872 | tf_op jit(solution)/shard_map/ppermute | solution.py:80
  152.1 22.1 %collective-permute-start.16 = (bf16[2,64,2048]{2,1,0:T(8,128)(2,1)S(1)}, bf16[2,64,2048]{2,1,0:T(8,128)(2,1)S(1)}, u32[]{:S(2)}, u32[]{:S(2)}) collective-permute-start(bf16[2,64,2048]{2,1,0:T(8,128)(2,1)S(1)} %get-tuple-element.25), channel_id=1, source_target_pairs={{0,64},{32,96},{64,0},{96,32},{1,65},{33,97},{65,1},{97,33},{2,66}... | collective-permute-start | bytes 1572872 | tf_op jit(solution)/shard_map/ppermute | solution.py:80
  152.1 26.7 %collective-permute-start.15 = (bf16[2,64,2048]{2,1,0:T(8,128)(2,1)S(1)}, bf16[2,64,2048]{2,1,0:T(8,128)(2,1)S(1)}, u32[]{:S(2)}, u32[]{:S(2)}) collective-permute-start(bf16[2,64,2048]{2,1,0:T(8,128)(2,1)S(1)} %get-tuple-element.23), channel_id=1, source_target_pairs={{0,32},{32,64},{64,96},{96,0},{1,33},{33,65},{65,97},{97,1},{2,34}... | collective-permute-start | bytes 1572872 | tf_op jit(solution)/shard_map/ppermute | solution.py:80
  155.2 51.8 %copy-start.3 = (f32[2048,64]{0,1:T(8,128)S(1)}, f32[2048,64]{0,1:T(8,128)}, u32[]{:S(2)}) copy-start(f32[2048,64]{0,1:T(8,128)} %param.17) | copy-start | bytes 1572868
  155.2 41.5 %collective-permute-start.9 = (bf16[2,64,2048]{2,1,0:T(8,128)(2,1)S(1)}, bf16[2,64,2048]{2,1,0:T(8,128)(2,1)S(1)}, u32[]{:S(2)}, u32[]{:S(2)}) collective-permute-start(bf16[2,64,2048]{2,1,0:T(8,128)(2,1)S(1)} %get-tuple-element.27), channel_id=1, source_target_pairs={{0,96},{32,0},{64,32},{96,64},{1,97},{33,1},{65,33},{97,65},{2,98}... | collective-permute-start | bytes 1572872 | tf_op jit(solution)/shard_map/ppermute | solution.py:80
  157.4 39.3 %collective-permute-start.8 = (bf16[2,64,2048]{2,1,0:T(8,128)(2,1)S(1)}, bf16[2,64,2048]{2,1,0:T(8,128)(2,1)S(1)}, u32[]{:S(2)}, u32[]{:S(2)}) collective-permute-start(bf16[2,64,2048]{2,1,0:T(8,128)(2,1)S(1)} %get-tuple-element.28), channel_id=1, source_target_pairs={{0,64},{32,96},{64,0},{96,32},{1,65},{33,97},{65,1},{97,33},{2,66}... | collective-permute-start | bytes 1572872 | tf_op jit(solution)/shard_map/ppermute | solution.py:80
  174.2 45.0 %copy-start.6 = (f32[64,2048]{1,0:T(8,128)S(1)}, f32[64,2048]{1,0:T(8,128)}, u32[]{:S(2)}) copy-start(f32[64,2048]{1,0:T(8,128)} %param.16) | copy-start | bytes 1572868
  174.2 26.4 %collective-permute-start.7 = (bf16[2,64,2048]{2,1,0:T(8,128)(2,1)S(1)}, bf16[2,64,2048]{2,1,0:T(8,128)(2,1)S(1)}, u32[]{:S(2)}, u32[]{:S(2)}) collective-permute-start(bf16[2,64,2048]{2,1,0:T(8,128)(2,1)S(1)} %get-tuple-element.26), channel_id=1, source_target_pairs={{0,32},{32,64},{64,96},{96,0},{1,33},{33,65},{65,97},{97,1},{2,34}... | collective-permute-start | bytes 1572872 | tf_op jit(solution)/shard_map/ppermute | solution.py:80
  179.2 27.8 %collective-permute-start.18 = (bf16[64,2048]{1,0:T(8,128)(2,1)S(1)}, bf16[64,2048]{1,0:T(8,128)(2,1)S(1)}, u32[]{:S(2)}, u32[]{:S(2)}) collective-permute-start(bf16[64,2048]{1,0:T(8,128)(2,1)S(1)} %fusion.55), channel_id=1, source_target_pairs={{0,128},{128,0},{1,129},{129,1},{2,130},{130,2},{3,131},{131,3},{4... | collective-permute-start | bytes 786440 | tf_op jit(solution)/shard_map/ppermute | solution.py:40
  200.9 18.3 %collective-permute-start.10 = (bf16[64,2048]{1,0:T(8,128)(2,1)S(1)}, bf16[64,2048]{1,0:T(8,128)(2,1)S(1)}, u32[]{:S(2)}, u32[]{:S(2)}) collective-permute-start(bf16[64,2048]{1,0:T(8,128)(2,1)S(1)} %fusion.54), channel_id=1, source_target_pairs={{0,128},{128,0},{1,129},{129,1},{2,130},{130,2},{3,131},{131,3},{4... | collective-permute-start | bytes 786440 | tf_op jit(solution)/shard_map/ppermute | solution.py:40

commit v4 on v3

--- a/solution.py
+++ b/solution.py
@@ -71,31 +71,46 @@
     return lax.dynamic_index_in_dim(blocks, index, dim, keepdims=False)
 
 
-def over_y(blocks, dim):
+def over_y(blocks):
     y, n_y = lax.axis_index("y"), lax.axis_size("y")
-    total = picked(blocks, y, dim).astype(jnp.float32)
-    for shift in range(1, n_y):
-        ring = [(i, (i + shift) % n_y) for i in range(n_y)]
-        sent = picked(blocks, lax.rem(y + shift, n_y), dim).astype(jnp.bfloat16)
-        total = total + lax.ppermute(sent, "y", ring).astype(jnp.float32)
+    up = [(i, (i + 1) % n_y) for i in range(n_y)]
+    down = [(i, (i - 1) % n_y) for i in range(n_y)]
+    at = lambda shift: lax.rem(y + shift, n_y)
+    across = picked(blocks, at(2), 1)
+    from_below = lax.ppermute(across[0], "y", up).astype(jnp.float32)
+    from_above = lax.ppermute(across[1], "y", down).astype(jnp.float32)
+    above = picked(blocks, at(1), 1).astype(jnp.float32)
+    below = picked(blocks, at(n_y - 1), 1).astype(jnp.float32)
+    above = jnp.stack([above[0] + from_below, above[1]]).astype(jnp.bfloat16)
+    below = jnp.stack([below[0], below[1] + from_above]).astype(jnp.bfloat16)
+    above, below = lax.optimization_barrier((above, below))
+    arrived = lax.ppermute(above, "y", up).astype(jnp.float32) + lax.ppermute(
+        below, "y", down
+    ).astype(jnp.float32)
+    return picked(blocks, y, 1).astype(jnp.float32) + arrived
+
+
+def nothing(value):
+    return jnp.minimum(jnp.abs(value.astype(jnp.float32)), 0.0)
+
+
+def over_z(blocks, earlier):
+    z_hi = lax.axis_index("z_hi")
+    sent = (picked(blocks, 1 - z_hi, 0) + nothing(earlier)).astype(jnp.bfloat16)
+    total = picked(blocks, z_hi, 0) + from_partner(sent, "z_hi").astype(jnp.float32)
     return total
 
 
-def over_z(blocks):
-    z_hi = lax.axis_index("z_hi")
-    sent = picked(blocks, 1 - z_hi, 0).astype(jnp.bfloat16)
-    return picked(blocks, z_hi, 0).astype(jnp.float32) + from_partner(sent, "z_hi").astype(
-        jnp.float32
-    )
-
-
-def summed_over_dp(lefts, rights):
+def partial_over_chip(lefts, rights):
     left, right = jnp.concatenate(lefts, 0), jnp.concatenate(rights, 0)
-    partial = lax.dot_general(
+    return lax.dot_general(
         left, right, (((0,), (0,)), ((), ())), preferred_element_type=jnp.float32
     ).astype(jnp.bfloat16)
-    blocks = partial.reshape(lax.axis_size("z_hi"), lax.axis_size("y"), -1, right.shape[1])
-    return over_z(over_y(blocks, 1))
+
+
+def summed_over_dp(partial, earlier):
+    blocks = partial.reshape(lax.axis_size("z_hi"), lax.axis_size("y"), -1, partial.shape[1])
+    return over_z(over_y(blocks), earlier)
 
 
 def shards(
@@ -128,7 +143,9 @@
         grad = gathered_features(out_grad.astype(jnp.bfloat16))
         lefts_out += for_both_cores(grad, core)
         if last:
-            summed_out = summed_over_dp(lefts_out, rights_out).T
+            partial_out = partial_over_chip(lefts_out, rights_out)
+            summed_out = summed_over_dp(partial_out, partial_out[0, 0])
+            slope = slope + nothing(partial_out[0, 0])
         hidden_grad = (
             jnp.dot(grad, weight_out.T, preferred_element_type=jnp.float32) * slope
         ).astype(jnp.bfloat16)
@@ -164,7 +181,8 @@
             perturb = perturb + delta_grad * token_scale
             embedded = tokens.astype(jnp.float32) + perturb
             whole = whole + delta_whole * token_scale
-    summed_in = summed_over_dp(lefts_in, rights_in)
+    partial_in = partial_over_chip(lefts_in, rights_in)
+    summed_in, summed_out = summed_over_dp(partial_in, summed_out[0, 0]), summed_out.T
     dp_rows = moment_in.shape[0]
     offset = lax.axis_index(DP) * dp_rows
     own_in = lax.dynamic_slice_in_dim(weight_in, offset, dp_rows, 0)

time: 222 us -> 217 us (0.977)
  starting transfers between devices: 51.2 us -> 47.1 us
  other arithmetic: 7.93 us -> 11.3 us
  matrix products: 23 us -> 20.6 us
    ppermute x6 -> x8, waiting for transfers between devices: 35.1 us -> 16.6 us  [the longest x2 8.68 us: over_y(): from_below = lax.ppermute(across[0], 'y', up).astype(jnp.float32)]
    ppermute x11, waiting for transfers between devices: 12 us -> 26 us  [from_partner(): return lax.ppermute(array, axis, [(0, 1), (1, 0)])]
    ppermute x11, starting transfers between devices: 21.3 us -> 11.6 us  [from_partner(): return lax.ppermute(array, axis, [(0, 1), (1, 0)])]
    ppermute x6 -> x8, starting transfers between devices: 13.3 us -> 19.9 us  [the longest x2 12.8 us: over_y(): from_above = lax.ppermute(across[1], 'y', down).astype(jnp.float32)]
    ppermute x1, waiting for transfers between devices: 0.01 us -> 2.75 us  [over_neighbours(): after = lax.ppermute(sums, BLOCKS, [(i + 1, i) for i in range(count - 1)])]
  transfers between devices with their start and end apart: 21 -> 23, of which waited for: 9 -> 10; matrix products, arithmetic and copies ran while one was open for 6% -> 5% of each run, Pallas kernels for 0% -> 0%
where the time goes in v4:
time: 217 us
  blocking collectives  73.5 us (34%)
  waiting for transfers between devices  57 us (26%)
  starting transfers between devices  47.1 us (22%)
  matrix products  20.6 us (9%)
  other arithmetic  11.3 us (5%)
  local copies, waits for them, and re-layouts  4.61 us (2%)
  between operations  2.51 us (1%)
    all_to_all x5, blocking collectives, to_peers(): return lax.all_to_all(blocks, axis, 0, 0, tiled=True)  73.5 us
    ppermute x11, waiting for transfers between devices, from_partner(): return lax.ppermute(array, axis, [(0, 1), (1, 0)])  26 us
    ppermute x2, starting transfers between devices, over_y(): from_above = lax.ppermute(across[1], 'y', down).astype(jnp.float32)  12.8 us
    all_to_all x2, waiting for transfers between devices, to_peers(): return lax.all_to_all(blocks, axis, 0, 0, tiled=True)  11.7 us
    ppermute x11, starting transfers between devices, from_partner(): return lax.ppermute(array, axis, [(0, 1), (1, 0)])  11.6 us
    all_to_all x2, starting transfers between devices, to_peers(): return lax.all_to_all(blocks, axis, 0, 0, tiled=True)  11 us
    ppermute x2, waiting for transfers between devices, over_y(): from_below = lax.ppermute(across[0], 'y', up).astype(jnp.float32)  8.68 us
    dot_general x2, matrix products, shards(): preact = jnp.dot(normed, weight_in, preferred_element_type=jnp.float32)  8.38 us
  transfers between devices with their start and end apart: 23, of which 10 were waited for; matrix products, arithmetic and copies ran while one was open for 5% of the time, Pallas kernels for 0%

profile of v4, /device:TPU:33, one launch (start us, length us, event | category | flops | bytes accessed | tf_op | source)
XLA Modules:
  0.0 216.5 jit_solution(7293596139586698031)
XLA Ops:
  0.6 0.8 convert_add_fusion.7
  1.5 20.2 %all_to_all.35 = f32[16,128,64]{1,2,0:T(8,128)S(1)} all-to-all(f32[16,128,64]{1,2,0:T(8,128)S(1)} %broadcast_in_dim.10), channel_id=1, replica_groups=mesh['z_hi'=2,'y'=4,'core'=2,'x'=4,'z_lo'=4] {'x','z_lo'}, dimensions={0} | all-to-all | bytes 1048576 | tf_op jit(solution)/shard_map/all_to_all | solution.py:22
  21.7 0.2 copy.33
  21.9 0.1 fusion.29
  22.1 0.8 fusion.31
  22.9 3.7 %fusion.20 = (f32[128,2048]{1,0:T(8,128)S(1)}, bf16[128,2048]{1,0:T(8,128)(2,1)S(1)}) fusion(bf16[128,1024]{1,0:T(8,128)(2,1)S(1)} %fusion.31, bf16[1024,2048]{1,0:T(8,128)(2,1)} %param.14), kind=kOutput, calls=%fused_computation.30 | convolution fusion | flops 541851648 | bytes 6029312 | tf_op jit(solution)/shard_map/dot_general | solution.py:136
  26.6 0.7 convolution_convert_fusion.3
  27.4 0.2 copy.35
  27.6 14.7 %all_to_all.36 = bf16[16,128,64]{1,2,0:T(8,128)(2,1)S(1)} all-to-all(bf16[16,128,64]{1,2,0:T(8,128)(2,1)S(1)} %bitcast.154), channel_id=1, replica_groups=mesh['z_hi'=2,'y'=4,'core'=2,'x'=4,'z_lo'=4] {'x','z_lo'}, dimensions={0} | all-to-all | bytes 524288 | tf_op jit(solution)/shard_map/all_to_all | solution.py:22
  42.4 13.3 %all_to_all.37 = bf16[16,128,64]{1,2,0:T(8,128)(2,1)S(1)} all-to-all(bf16[16,128,64]{1,2,0:T(8,128)(2,1)S(1)} %broadcast_in_dim.11), channel_id=1, replica_groups=mesh['z_hi'=2,'y'=4,'core'=2,'x'=4,'z_lo'=4] {'x','z_lo'}, dimensions={0} | all-to-all | bytes 524288 | tf_op jit(solution)/shard_map/all_to_all | solution.py:22
  55.7 3.7 %fusion = bf16[128,2048]{1,0:T(8,128)(2,1)S(1)} fusion(f32[128,2048]{1,0:T(8,128)S(1)} %get-tuple-element.14, bf16[128,1024]{0,1:T(8,128)(2,1)S(1)} %bitcast.141, bf16[2048,1024]{1,0:T(8,128)(2,1)} %param.15), kind=kOutput, calls=%fused_computation.4 | convolution fusion | flops 537395200 | bytes 6029312 | tf_op jit(solution)/shard_map/dot_general | solution.py:150
  59.4 1.6 fusion.74
  61.1 0.2 copy.36
  61.3 0.7 pad_maximum_fusion.4
  62.0 5.6 %all-to-all-start.3 = ((bf16[16,128,66]{1,2,0:T(8,128)(2,1)}), bf16[16,128,66]{1,2,0:T(8,128)(2,1)S(1)}, u32[]{:S(2)}, u32[]{:S(2)}) async-start(bf16[16,128,66]{1,2,0:T(8,128)(2,1)} %pad_maximum_fusion.4), calls=%async_computation.3 | async-start | bytes 589824 | tf_op jit(solution)/shard_map/all_to_all | solution.py:22
  67.7 8.0 %all-to-all-done.3 = bf16[16,128,66]{1,2,0:T(8,128)(2,1)S(1)} async-done(((bf16[16,128,66]{1,2,0:T(8,128)(2,1)}), bf16[16,128,66]{1,2,0:T(8,128)(2,1)S(1)}, u32[]{:S(2)}, u32[]{:S(2)}) %all-to-all-start.3) | async-done | bytes 270368 | tf_op jit(solution)/shard_map/all_to_all | solution.py:22
  75.9 13.7 %all_to_all.38 = bf16[16,128,64]{1,2,0:T(8,128)(2,1)S(1)} all-to-all(bf16[16,128,64]{1,2,0:T(8,128)(2,1)S(1)} %broadcast_in_dim.13), channel_id=1, replica_groups=mesh['z_hi'=2,'y'=4,'core'=2,'x'=4,'z_lo'=4] {'x','z_lo'}, dimensions={0} | all-to-all | bytes 524288 | tf_op jit(solution)/shard_map/all_to_all | solution.py:22
  89.6 0.2 multiply_reduce_fusion
  89.9 2.7 %collective-permute-start.1 = (f32[2,32]{1,0:T(2,128)S(1)}, f32[2,32]{1,0:T(2,128)S(1)}, u32[]{:S(2)}, u32[]{:S(2)}) collective-permute-start(f32[2,32]{1,0:T(2,128)S(1)} %pad_maximum_fusion.5), channel_id=1, source_target_pairs={{0,16},{16,0},{1,17},{17,1},{2,18},{18,2},{3,19},{19,3},{4,20},{20... | collective-permute-start | bytes 776 | tf_op jit(solution)/shard_map/ppermute | solution.py:40
  92.6 0.8 collective-permute-done.1
  93.4 3.2 %collective-permute-start.2 = (f32[2,32]{1,0:T(2,128)S(1)}, f32[2,32]{1,0:T(2,128)S(1)}, u32[]{:S(2)}, u32[]{:S(2)}) collective-permute-start(f32[2,32]{1,0:T(2,128)S(1)} %fusion.70), channel_id=1, source_target_pairs={{0,32},{32,64},{64,96},{96,128},{128,160},{160,192},{192,224},{1,3... | collective-permute-start | bytes 776 | tf_op jit(solution)/shard_map/ppermute | solution.py:55
  96.6 1.3 collective-permute-start.3
  98.0 0.2 copy.37
  98.2 2.7 %collective-permute-done.3 = f32[2,32]{1,0:T(2,128)S(1)} collective-permute-done((f32[2,32]{1,0:T(2,128)S(1)}, f32[2,32]{1,0:T(2,128)S(1)}, u32[]{:S(2)}, u32[]{:S(2)}) %collective-permute-start.3) | collective-permute-done | bytes 288 | tf_op jit(solution)/shard_map/ppermute | solution.py:56
  101.3 0.1 fusion.28
  101.5 4.7 %fusion.25 = (f32[128,2048]{1,0:T(8,128)}, bf16[128,2048]{1,0:T(8,128)(2,1)S(1)}) fusion(bf16[128,1024]{1,0:T(8,128)(2,1)S(1)} %fusion.28, bf16[1024,2048]{1,0:T(8,128)(2,1)} %param.14), kind=kOutput, calls=%fused_computation.35 | convolution fusion | flops 541851648 | bytes 6029312 | tf_op jit(solution)/shard_map/dot_general | solution.py:136
  106.2 0.7 convolution_convert_fusion.2
  106.9 0.2 copy.40
  107.1 11.5 %all_to_all.39 = bf16[16,128,64]{1,2,0:T(8,128)(2,1)S(1)} all-to-all(bf16[16,128,64]{1,2,0:T(8,128)(2,1)S(1)} %bitcast.155), channel_id=1, replica_groups=mesh['z_hi'=2,'y'=4,'core'=2,'x'=4,'z_lo'=4] {'x','z_lo'}, dimensions={0} | all-to-all | bytes 524288 | tf_op jit(solution)/shard_map/all_to_all | solution.py:22
  118.7 0.6 fusion.62
  119.3 0.8 broadcast_in_dim.14
  120.1 5.3 %all-to-all-start.6 = ((bf16[16,128,64]{1,2,0:T(8,128)(2,1)}), bf16[16,128,64]{1,2,0:T(8,128)(2,1)S(1)}, u32[]{:S(2)}, u32[]{:S(2)}) async-start(bf16[16,128,64]{1,2,0:T(8,128)(2,1)} %broadcast_in_dim.14), calls=%async_computation.6 | async-start | bytes 524288 | tf_op jit(solution)/shard_map/all_to_all | solution.py:22
  125.4 2.8 %collective-permute-start.8 = (bf16[128,2048]{1,0:T(8,128)(2,1)S(1)}, bf16[128,2048]{1,0:T(8,128)(2,1)}, u32[]{:S(2)}, u32[]{:S(2)}) collective-permute-start(bf16[128,2048]{1,0:T(8,128)(2,1)S(1)} %get-tuple-element.13), channel_id=1, source_target_pairs={{0,16},{16,0},{1,17},{17,1},{2,18},{18,2},{3,19},{19,3},{4,20},{20... | collective-permute-start | bytes 1572872 | tf_op jit(solution)/shard_map/ppermute | solution.py:40
  128.3 0.7 collective-permute-start.6
  129.0 0.2 copy.39
  129.2 3.7 %all-to-all-done.6 = bf16[16,128,64]{1,2,0:T(8,128)(2,1)S(1)} async-done(((bf16[16,128,64]{1,2,0:T(8,128)(2,1)}), bf16[16,128,64]{1,2,0:T(8,128)(2,1)S(1)}, u32[]{:S(2)}, u32[]{:S(2)}) %all-to-all-start.6) | async-done | bytes 262176 | tf_op jit(solution)/shard_map/all_to_all | solution.py:22
  132.9 0.7 constant_dynamic-slice_fusion.2
  133.6 3.7 %collective-permute-start.7 = (bf16[128,512]{0,1:T(8,128)(2,1)S(1)}, bf16[128,512]{0,1:T(8,128)(2,1)S(1)}, u32[]{:S(2)}, u32[]{:S(2)}) collective-permute-start(bf16[128,512]{0,1:T(8,128)(2,1)S(1)} %bitcast.158), channel_id=1, source_target_pairs={{0,16},{16,0},{1,17},{17,1},{2,18},{18,2},{3,19},{19,3},{4,20},{20... | collective-permute-start | bytes 393224 | tf_op jit(solution)/shard_map/ppermute | solution.py:40
  137.3 0.2 copy.34
  137.6 0.5 collective-permute-start.5
  138.3 2.6 %convolution_convert_fusion.1 = bf16[512,2048]{1,0:T(8,128)(2,1)S(1)} fusion(bf16[128,2048]{1,0:T(8,128)(2,1)} %collective-permute-done.9, bf16[128,2048]{1,0:T(8,128)(2,1)S(1)} %get-tuple-element.15, bf16[128,2048]{1,0:T(8,128)(2,1)} %collective-permute-done.8, bf16[128,2048]{1,0:T(8,128)(2,1)S(1)} %get-tuple-element.13, ...), kind=kOutput, calls=%fused_computation.1 | convolution fusion | flops 1085276160 | bytes 4718592 | tf_op jit(solution)/shard_map/dot_general | solution.py:106
  140.9 0.5 slice.99
  141.5 1.4 collective-permute-start.15
  142.9 10.1 %collective-permute-start.16 = (bf16[64,2048]{1,0:T(8,128)(2,1)S(1)}, bf16[64,2048]{1,0:T(8,128)(2,1)S(1)}, u32[]{:S(2)}, u32[]{:S(2)}) collective-permute-start(bf16[64,2048]{1,0:T(8,128)(2,1)S(1)} %get-tuple-element.34), channel_id=1, source_target_pairs={{0,96},{32,0},{64,32},{96,64},{1,97},{33,1},{65,33},{97,65},{2,98}... | collective-permute-start | bytes 786440 | tf_op jit(solution)/shard_map/ppermute | solution.py:81
  153.7 1.5 fusion.1
  155.2 4.1 %collective-permute-done.15 = bf16[64,2048]{1,0:T(8,128)(2,1)S(1)} collective-permute-done((bf16[64,2048]{1,0:T(8,128)(2,1)S(1)}, bf16[64,2048]{1,0:T(8,128)(2,1)S(1)}, u32[]{:S(2)}, u32[]{:S(2)}) %collective-permute-start.15) | collective-permute-done | bytes 262176 | tf_op jit(solution)/shard_map/ppermute | solution.py:80
  159.3 0.9 collective-permute-start.10
  160.5 2.7 %collective-permute-start.18 = (bf16[2,64,2048]{2,1,0:T(8,128)(2,1)S(1)}, bf16[2,64,2048]{2,1,0:T(8,128)(2,1)S(1)}, u32[]{:S(2)}, u32[]{:S(2)}) collective-permute-start(bf16[2,64,2048]{2,1,0:T(8,128)(2,1)S(1)} %pad_maximum_fusion.3), channel_id=1, source_target_pairs={{0,96},{32,0},{64,32},{96,64},{1,97},{33,1},{65,33},{97,65},{2,98}... | collective-permute-start | bytes 1572872 | tf_op jit(solution)/shard_map/ppermute | solution.py:87
  163.2 1.3 convolution_convert_fusion
  164.7 2.7 %collective-permute-start.12 = (bf16[64,2048]{1,0:T(8,128)(2,1)S(1)}, bf16[64,2048]{1,0:T(8,128)(2,1)S(1)}, u32[]{:S(2)}, u32[]{:S(2)}) collective-permute-start(bf16[64,2048]{1,0:T(8,128)(2,1)S(1)} %get-tuple-element.40), channel_id=1, source_target_pairs={{0,96},{32,0},{64,32},{96,64},{1,97},{33,1},{65,33},{97,65},{2,98}... | collective-permute-start | bytes 786440 | tf_op jit(solution)/shard_map/ppermute | solution.py:81
  167.3 7.9 %collective-permute-done.17 = bf16[2,64,2048]{2,1,0:T(8,128)(2,1)S(1)} collective-permute-done((bf16[2,64,2048]{2,1,0:T(8,128)(2,1)S(1)}, bf16[2,64,2048]{2,1,0:T(8,128)(2,1)S(1)}, u32[]{:S(2)}, u32[]{:S(2)}) %collective-permute-start.17) | collective-permute-done | bytes 524320 | tf_op jit(solution)/shard_map/ppermute | solution.py:87
  175.3 0.2 convert_add_fusion
  175.5 0.7 fusion.53
  176.3 4.6 %collective-permute-done.11 = bf16[64,2048]{1,0:T(8,128)(2,1)S(1)} collective-permute-done((bf16[64,2048]{1,0:T(8,128)(2,1)S(1)}, bf16[64,2048]{1,0:T(8,128)(2,1)S(1)}, u32[]{:S(2)}, u32[]{:S(2)}) %collective-permute-start.11) | collective-permute-done | bytes 262176 | tf_op jit(solution)/shard_map/ppermute | solution.py:80
  181.2 0.3 collective-permute-start.13
  181.5 2.7 %collective-permute-start.14 = (bf16[2,64,2048]{2,1,0:T(8,128)(2,1)S(1)}, bf16[2,64,2048]{2,1,0:T(8,128)(2,1)}, u32[]{:S(2)}, u32[]{:S(2)}) collective-permute-start(bf16[2,64,2048]{2,1,0:T(8,128)(2,1)S(1)} %pad_maximum_fusion.1), channel_id=1, source_target_pairs={{0,96},{32,0},{64,32},{96,64},{1,97},{33,1},{65,33},{97,65},{2,98}... | collective-permute-start | bytes 1572872 | tf_op jit(solution)/shard_map/ppermute | solution.py:87
  184.1 0.2 constant_dynamic-slice_fusion
  184.4 0.2 copy.50
  184.6 9.5 %collective-permute-done.19 = bf16[64,2048]{1,0:T(8,128)(2,1)} collective-permute-done((bf16[64,2048]{1,0:T(8,128)(2,1)}, bf16[64,2048]{1,0:T(8,128)(2,1)}, u32[]{:S(2)}, u32[]{:S(2)}) %collective-permute-start.19) | collective-permute-done | bytes 262176 | tf_op jit(solution)/shard_map/ppermute | solution.py:40
  194.1 2.0 subtract_convert_fusion
  196.1 0.5 slice.100
  197.3 1.6 convert_add_fusion.1
  199.0 15.5 %collective-permute-done.20 = bf16[64,2048]{1,0:T(8,128)(2,1)S(1)} collective-permute-done((bf16[64,2048]{1,0:T(8,128)(2,1)S(1)}, bf16[64,2048]{1,0:T(8,128)(2,1)S(1)}, u32[]{:S(2)}, u32[]{:S(2)}) %collective-permute-start.20) | collective-permute-done | bytes 262176 | tf_op jit(solution)/shard_map/ppermute | solution.py:40
  214.6 2.0 subtract_convert_fusion.1
  (84 shorter events, 2.6 us)
Async XLA Ops:
  22.9 3.7 %copy-start = (bf16[2048,1024]{1,0:T(8,128)(2,1)S(1)}, bf16[2048,1024]{1,0:T(8,128)(2,1)}, u32[]{:S(2)}) copy-start(bf16[2048,1024]{1,0:T(8,128)(2,1)} %param.15) | copy-start | bytes 12582916
  26.6 15.8 %copy-start.8 = (f32[128,64]{0,1:T(8,128)S(1)}, f32[128,64]{0,1:T(8,128)}, u32[]{:S(2)}) copy-start(f32[128,64]{0,1:T(8,128)} %param.12) | copy-start | bytes 98308
  27.4 32.0 %copy-start.11 = (f32[1024]{0:T(1024)S(1)}, f32[1024]{0:T(1024)}, u32[]{:S(2)}) copy-start(f32[1024]{0:T(1024)} %param.13) | copy-start | bytes 12292
  27.6 31.9 %copy-start.3 = (bf16[1024,2048]{1,0:T(8,128)(2,1)S(1)}, bf16[1024,2048]{1,0:T(8,128)(2,1)}, u32[]{:S(2)}) copy-start(bf16[1024,2048]{1,0:T(8,128)(2,1)} %param.14) | copy-start | bytes 12582916
  59.4 30.3 %copy-start.12 = (s32[128]{0:T(128)S(1)}, s32[128]{0:T(128)}, u32[]{:S(2)}) copy-start(s32[128]{0:T(128)} %param.11) | copy-start | bytes 1540
  62.0 13.7 %all-to-all-start.3 = ((bf16[16,128,66]{1,2,0:T(8,128)(2,1)}), bf16[16,128,66]{1,2,0:T(8,128)(2,1)S(1)}, u32[]{:S(2)}, u32[]{:S(2)}) async-start(bf16[16,128,66]{1,2,0:T(8,128)(2,1)} %pad_maximum_fusion.4), calls=%async_computation.3 | async-start | bytes 589824 | tf_op jit(solution)/shard_map/all_to_all | solution.py:22
  89.9 3.5 %collective-permute-start.1 = (f32[2,32]{1,0:T(2,128)S(1)}, f32[2,32]{1,0:T(2,128)S(1)}, u32[]{:S(2)}, u32[]{:S(2)}) collective-permute-start(f32[2,32]{1,0:T(2,128)S(1)} %pad_maximum_fusion.5), channel_id=1, source_target_pairs={{0,16},{16,0},{1,17},{17,1},{2,18},{18,2},{3,19},{19,3},{4,20},{20... | collective-permute-start | bytes 776 | tf_op jit(solution)/shard_map/ppermute | solution.py:40
  93.4 4.8 %collective-permute-start.2 = (f32[2,32]{1,0:T(2,128)S(1)}, f32[2,32]{1,0:T(2,128)S(1)}, u32[]{:S(2)}, u32[]{:S(2)}) collective-permute-start(f32[2,32]{1,0:T(2,128)S(1)} %fusion.70), channel_id=1, source_target_pairs={{0,32},{32,64},{64,96},{96,128},{128,160},{160,192},{192,224},{1,3... | collective-permute-start | bytes 776 | tf_op jit(solution)/shard_map/ppermute | solution.py:55
  96.6 4.3 %collective-permute-start.3 = (f32[2,32]{1,0:T(2,128)S(1)}, f32[2,32]{1,0:T(2,128)S(1)}, u32[]{:S(2)}, u32[]{:S(2)}) collective-permute-start(f32[2,32]{1,0:T(2,128)S(1)} %fusion.70), channel_id=1, source_target_pairs={{32,0},{64,32},{96,64},{128,96},{160,128},{192,160},{224,192},{33,... | collective-permute-start | bytes 776 | tf_op jit(solution)/shard_map/ppermute | solution.py:56
  101.5 4.7 %copy-start.1 = (bf16[2048,1024]{1,0:T(8,128)(2,1)S(1)}, bf16[2048,1024]{1,0:T(8,128)(2,1)}, u32[]{:S(2)}) copy-start(bf16[2048,1024]{1,0:T(8,128)(2,1)} %param.15) | copy-start | bytes 12582916
  106.2 12.5 %copy-start.9 = (f32[128,64]{0,1:T(8,128)S(1)}, f32[128,64]{0,1:T(8,128)}, u32[]{:S(2)}) copy-start(f32[128,64]{0,1:T(8,128)} %param.10) | copy-start | bytes 98308
  106.2 12.5 %copy-start.10 = (bf16[128,64]{0,1:T(8,128)(2,1)S(1)}, bf16[128,64]{0,1:T(8,128)(2,1)}, u32[]{:S(2)}) copy-start(bf16[128,64]{0,1:T(8,128)(2,1)} %param.9) | copy-start | bytes 49156
  120.1 12.8 %all-to-all-start.6 = ((bf16[16,128,64]{1,2,0:T(8,128)(2,1)}), bf16[16,128,64]{1,2,0:T(8,128)(2,1)S(1)}, u32[]{:S(2)}, u32[]{:S(2)}) async-start(bf16[16,128,64]{1,2,0:T(8,128)(2,1)} %broadcast_in_dim.14), calls=%async_computation.6 | async-start | bytes 524288 | tf_op jit(solution)/shard_map/all_to_all | solution.py:22
  125.4 12.2 %collective-permute-start.8 = (bf16[128,2048]{1,0:T(8,128)(2,1)S(1)}, bf16[128,2048]{1,0:T(8,128)(2,1)}, u32[]{:S(2)}, u32[]{:S(2)}) collective-permute-start(bf16[128,2048]{1,0:T(8,128)(2,1)S(1)} %get-tuple-element.13), channel_id=1, source_target_pairs={{0,16},{16,0},{1,17},{17,1},{2,18},{18,2},{3,19},{19,3},{4,20},{20... | collective-permute-start | bytes 1572872 | tf_op jit(solution)/shard_map/ppermute | solution.py:40
  128.2 10.0 %collective-permute-start.9 = (bf16[128,2048]{1,0:T(8,128)(2,1)S(1)}, bf16[128,2048]{1,0:T(8,128)(2,1)}, u32[]{:S(2)}, u32[]{:S(2)}) collective-permute-start(bf16[128,2048]{1,0:T(8,128)(2,1)S(1)} %get-tuple-element.15), channel_id=1, source_target_pairs={{0,16},{16,0},{1,17},{17,1},{2,18},{18,2},{3,19},{19,3},{4,20},{20... | collective-permute-start | bytes 1572872 | tf_op jit(solution)/shard_map/ppermute | solution.py:40
  128.3 9.8 %collective-permute-start.6 = (bf16[128,512]{0,1:T(8,128)(2,1)S(1)}, bf16[128,512]{0,1:T(8,128)(2,1)S(1)}, u32[]{:S(2)}, u32[]{:S(2)}) collective-permute-start(bf16[128,512]{0,1:T(8,128)(2,1)S(1)} %bitcast.160), channel_id=1, source_target_pairs={{0,16},{16,0},{1,17},{17,1},{2,18},{18,2},{3,19},{19,3},{4,20},{20... | collective-permute-start | bytes 393224 | tf_op jit(solution)/shard_map/ppermute | solution.py:40
  133.6 4.7 %collective-permute-start.7 = (bf16[128,512]{0,1:T(8,128)(2,1)S(1)}, bf16[128,512]{0,1:T(8,128)(2,1)S(1)}, u32[]{:S(2)}, u32[]{:S(2)}) collective-permute-start(bf16[128,512]{0,1:T(8,128)(2,1)S(1)} %bitcast.158), channel_id=1, source_target_pairs={{0,16},{16,0},{1,17},{17,1},{2,18},{18,2},{3,19},{19,3},{4,20},{20... | collective-permute-start | bytes 393224 | tf_op jit(solution)/shard_map/ppermute | solution.py:40
  137.5 23.0 %collective-permute-start = (bf16[128,512]{0,1:T(8,128)(2,1)S(1)}, bf16[128,512]{0,1:T(8,128)(2,1)S(1)}, u32[]{:S(2)}, u32[]{:S(2)}) collective-permute-start(bf16[128,512]{0,1:T(8,128)(2,1)S(1)} %bitcast.162), channel_id=1, source_target_pairs={{0,16},{16,0},{1,17},{17,1},{2,18},{18,2},{3,19},{19,3},{4,20},{20... | collective-permute-start | bytes 393224 | tf_op jit(solution)/shard_map/ppermute | solution.py:40
  137.6 25.6 %collective-permute-start.5 = (bf16[128,2048]{1,0:T(8,128)(2,1)S(1)}, bf16[128,2048]{1,0:T(8,128)(2,1)S(1)}, u32[]{:S(2)}, u32[]{:S(2)}) collective-permute-start(bf16[128,2048]{1,0:T(8,128)(2,1)S(1)} %fusion), channel_id=1, source_target_pairs={{0,16},{16,0},{1,17},{17,1},{2,18},{18,2},{3,19},{19,3},{4,20},{20... | collective-permute-start | bytes 1572872 | tf_op jit(solution)/shard_map/ppermute | solution.py:40
  138.1 25.1 %collective-permute-start.4 = (bf16[128,512]{0,1:T(8,128)(2,1)}, bf16[128,512]{0,1:T(8,128)(2,1)S(1)}, u32[]{:S(2)}, u32[]{:S(2)}) collective-permute-start(bf16[128,512]{0,1:T(8,128)(2,1)} %bitcast.20), channel_id=1, source_target_pairs={{0,16},{16,0},{1,17},{17,1},{2,18},{18,2},{3,19},{19,3},{4,20},{20... | collective-permute-start | bytes 393224 | tf_op jit(solution)/shard_map/ppermute | solution.py:40
  138.3 15.4 %copy-start.2 = (bf16[2048,1024]{1,0:T(8,128)(2,1)S(1)}, bf16[2048,1024]{1,0:T(8,128)(2,1)}, u32[]{:S(2)}) copy-start(bf16[2048,1024]{1,0:T(8,128)(2,1)} %param.15) | copy-start | bytes 12582916
  138.3 15.4 %copy-start.5 = (f32[128,2048]{1,0:T(8,128)S(1)}, f32[128,2048]{1,0:T(8,128)}, u32[]{:S(2)}) copy-start(f32[128,2048]{1,0:T(8,128)} %get-tuple-element.16) | copy-start | bytes 3145732
  141.5 17.8 %collective-permute-start.15 = (bf16[64,2048]{1,0:T(8,128)(2,1)S(1)}, bf16[64,2048]{1,0:T(8,128)(2,1)S(1)}, u32[]{:S(2)}, u32[]{:S(2)}) collective-permute-start(bf16[64,2048]{1,0:T(8,128)(2,1)S(1)} %get-tuple-element.33), channel_id=1, source_target_pairs={{0,32},{32,64},{64,96},{96,0},{1,33},{33,65},{65,97},{97,1},{2,34}... | collective-permute-start | bytes 786440 | tf_op jit(solution)/shard_map/ppermute | solution.py:80
  142.9 17.3 %collective-permute-start.16 = (bf16[64,2048]{1,0:T(8,128)(2,1)S(1)}, bf16[64,2048]{1,0:T(8,128)(2,1)S(1)}, u32[]{:S(2)}, u32[]{:S(2)}) collective-permute-start(bf16[64,2048]{1,0:T(8,128)(2,1)S(1)} %get-tuple-element.34), channel_id=1, source_target_pairs={{0,96},{32,0},{64,32},{96,64},{1,97},{33,1},{65,33},{97,65},{2,98}... | collective-permute-start | bytes 786440 | tf_op jit(solution)/shard_map/ppermute | solution.py:81
  159.3 3.9 %collective-permute-start.10 = (bf16[128,2048]{1,0:T(8,128)(2,1)S(1)}, bf16[128,2048]{1,0:T(8,128)(2,1)S(1)}, u32[]{:S(2)}, u32[]{:S(2)}) collective-permute-start(bf16[128,2048]{1,0:T(8,128)(2,1)S(1)} %fusion.1), channel_id=1, source_target_pairs={{0,16},{16,0},{1,17},{17,1},{2,18},{18,2},{3,19},{19,3},{4,20},{20... | collective-permute-start | bytes 1572872 | tf_op jit(solution)/shard_map/ppermute | solution.py:40
  160.4 14.8 %collective-permute-start.17 = (bf16[2,64,2048]{2,1,0:T(8,128)(2,1)S(1)}, bf16[2,64,2048]{2,1,0:T(8,128)(2,1)S(1)}, u32[]{:S(2)}, u32[]{:S(2)}) collective-permute-start(bf16[2,64,2048]{2,1,0:T(8,128)(2,1)S(1)} %pad_maximum_fusion.2), channel_id=1, source_target_pairs={{0,32},{32,64},{64,96},{96,0},{1,33},{33,65},{65,97},{97,1},{2,34}... | collective-permute-start | bytes 1572872 | tf_op jit(solution)/shard_map/ppermute | solution.py:87
  160.5 14.7 %collective-permute-start.18 = (bf16[2,64,2048]{2,1,0:T(8,128)(2,1)S(1)}, bf16[2,64,2048]{2,1,0:T(8,128)(2,1)S(1)}, u32[]{:S(2)}, u32[]{:S(2)}) collective-permute-start(bf16[2,64,2048]{2,1,0:T(8,128)(2,1)S(1)} %pad_maximum_fusion.3), channel_id=1, source_target_pairs={{0,96},{32,0},{64,32},{96,64},{1,97},{33,1},{65,33},{97,65},{2,98}... | collective-permute-start | bytes 1572872 | tf_op jit(solution)/shard_map/ppermute | solution.py:87
  164.5 16.7 %copy-start.4 = (bf16[512,2048]{1,0:T(8,128)(2,1)}, bf16[512,2048]{1,0:T(8,128)(2,1)S(1)}, u32[]{:S(2)}) copy-start(bf16[512,2048]{1,0:T(8,128)(2,1)S(1)} %convolution_convert_fusion) | copy-start | bytes 6291460
  164.6 16.3 %collective-permute-start.11 = (bf16[64,2048]{1,0:T(8,128)(2,1)S(1)}, bf16[64,2048]{1,0:T(8,128)(2,1)S(1)}, u32[]{:S(2)}, u32[]{:S(2)}) collective-permute-start(bf16[64,2048]{1,0:T(8,128)(2,1)S(1)} %get-tuple-element.39), channel_id=1, source_target_pairs={{0,32},{32,64},{64,96},{96,0},{1,33},{33,65},{65,97},{97,1},{2,34}... | collective-permute-start | bytes 786440 | tf_op jit(solution)/shard_map/ppermute | solution.py:80
  164.7 29.4 %copy-start.6 = (f32[2048,64]{0,1:T(8,128)S(1)}, f32[2048,64]{0,1:T(8,128)}, u32[]{:S(2)}) copy-start(f32[2048,64]{0,1:T(8,128)} %param.17) | copy-start | bytes 1572868
  164.7 16.2 %collective-permute-start.12 = (bf16[64,2048]{1,0:T(8,128)(2,1)S(1)}, bf16[64,2048]{1,0:T(8,128)(2,1)S(1)}, u32[]{:S(2)}, u32[]{:S(2)}) collective-permute-start(bf16[64,2048]{1,0:T(8,128)(2,1)S(1)} %get-tuple-element.40), channel_id=1, source_target_pairs={{0,96},{32,0},{64,32},{96,64},{1,97},{33,1},{65,33},{97,65},{2,98}... | collective-permute-start | bytes 786440 | tf_op jit(solution)/shard_map/ppermute | solution.py:81
  176.2 17.9 %collective-permute-start.19 = (bf16[64,2048]{1,0:T(8,128)(2,1)}, bf16[64,2048]{1,0:T(8,128)(2,1)}, u32[]{:S(2)}, u32[]{:S(2)}) collective-permute-start(bf16[64,2048]{1,0:T(8,128)(2,1)} %fusion.53), channel_id=1, source_target_pairs={{0,128},{128,0},{1,129},{129,1},{2,130},{130,2},{3,131},{131,3},{4... | collective-permute-start | bytes 786440 | tf_op jit(solution)/shard_map/ppermute | solution.py:40
  181.2 16.1 %collective-permute-start.13 = (bf16[2,64,2048]{2,1,0:T(8,128)(2,1)S(1)}, bf16[2,64,2048]{2,1,0:T(8,128)(2,1)}, u32[]{:S(2)}, u32[]{:S(2)}) collective-permute-start(bf16[2,64,2048]{2,1,0:T(8,128)(2,1)S(1)} %pad_maximum_fusion), channel_id=1, source_target_pairs={{0,32},{32,64},{64,96},{96,0},{1,33},{33,65},{65,97},{97,1},{2,34}... | collective-permute-start | bytes 1572872 | tf_op jit(solution)/shard_map/ppermute | solution.py:87
  181.5 15.8 %collective-permute-start.14 = (bf16[2,64,2048]{2,1,0:T(8,128)(2,1)S(1)}, bf16[2,64,2048]{2,1,0:T(8,128)(2,1)}, u32[]{:S(2)}, u32[]{:S(2)}) collective-permute-start(bf16[2,64,2048]{2,1,0:T(8,128)(2,1)S(1)} %pad_maximum_fusion.1), channel_id=1, source_target_pairs={{0,96},{32,0},{64,32},{96,64},{1,97},{33,1},{65,33},{97,65},{2,98}... | collective-permute-start | bytes 1572872 | tf_op jit(solution)/shard_map/ppermute | solution.py:87
  184.6 30.0 %copy-start.7 = (f32[64,2048]{1,0:T(8,128)S(1)}, f32[64,2048]{1,0:T(8,128)}, u32[]{:S(2)}) copy-start(f32[64,2048]{1,0:T(8,128)} %param.16) | copy-start | bytes 1572868
  198.9 15.6 %collective-permute-start.20 = (bf16[64,2048]{1,0:T(8,128)(2,1)S(1)}, bf16[64,2048]{1,0:T(8,128)(2,1)S(1)}, u32[]{:S(2)}, u32[]{:S(2)}) collective-permute-start(bf16[64,2048]{1,0:T(8,128)(2,1)S(1)} %fusion.54), channel_id=1, source_target_pairs={{0,128},{128,0},{1,129},{129,1},{2,130},{130,2},{3,131},{131,3},{4... | collective-permute-start | bytes 786440 | tf_op jit(solution)/shard_map/ppermute | solution.py:40

commit v5 on v4

--- a/solution.py
+++ b/solution.py
@@ -71,34 +71,36 @@
     return lax.dynamic_index_in_dim(blocks, index, dim, keepdims=False)
 
 
-def over_y(blocks):
+def over_y(blocks, late):
     y, n_y = lax.axis_index("y"), lax.axis_size("y")
     up = [(i, (i + 1) % n_y) for i in range(n_y)]
     down = [(i, (i - 1) % n_y) for i in range(n_y)]
-    at = lambda shift: lax.rem(y + shift, n_y)
-    across = picked(blocks, at(2), 1)
-    from_below = lax.ppermute(across[0], "y", up).astype(jnp.float32)
-    from_above = lax.ppermute(across[1], "y", down).astype(jnp.float32)
-    above = picked(blocks, at(1), 1).astype(jnp.float32)
-    below = picked(blocks, at(n_y - 1), 1).astype(jnp.float32)
-    above = jnp.stack([above[0] + from_below, above[1]]).astype(jnp.bfloat16)
-    below = jnp.stack([below[0], below[1] + from_above]).astype(jnp.bfloat16)
-    above, below = lax.optimization_barrier((above, below))
-    arrived = lax.ppermute(above, "y", up).astype(jnp.float32) + lax.ppermute(
-        below, "y", down
-    ).astype(jnp.float32)
-    return picked(blocks, y, 1).astype(jnp.float32) + arrived
+
+    def block(z_hi, shift):
+        return picked(blocks, z_hi * n_y + lax.rem(y + shift, n_y), 0)
+
+    def with_own(own, arrived):
+        return own.astype(jnp.float32) + arrived.astype(jnp.float32)
+
+    risen = lax.ppermute(jnp.stack([block(0, 2), block(1, 1)]), "y", up)
+    sunk = lax.ppermute(jnp.stack([block(1, 2), block(0, n_y - 1)]), "y", down)
+    on_up = (with_own(block(0, 1), risen[0]) + late).astype(jnp.bfloat16)
+    on_down = (with_own(block(1, n_y - 1), sunk[0]) + late).astype(jnp.bfloat16)
+    on_up, on_down = lax.optimization_barrier((on_up, on_down))
+    first = with_own(with_own(block(0, 0), sunk[1]), lax.ppermute(on_up, "y", up))
+    second = with_own(with_own(block(1, 0), risen[1]), lax.ppermute(on_down, "y", down))
+    return first, second
 
 
 def nothing(value):
     return jnp.minimum(jnp.abs(value.astype(jnp.float32)), 0.0)
 
 
-def over_z(blocks, earlier):
-    z_hi = lax.axis_index("z_hi")
-    sent = (picked(blocks, 1 - z_hi, 0) + nothing(earlier)).astype(jnp.bfloat16)
-    total = picked(blocks, z_hi, 0) + from_partner(sent, "z_hi").astype(jnp.float32)
-    return total
+def over_z(totals, late):
+    first, second = totals
+    low = lax.axis_index("z_hi") == 0
+    sent = (jnp.where(low, second, first) + late).astype(jnp.bfloat16)
+    return jnp.where(low, first, second) + from_partner(sent, "z_hi").astype(jnp.float32)
 
 
 def partial_over_chip(lefts, rights):
@@ -108,9 +110,9 @@
     ).astype(jnp.bfloat16)
 
 
-def summed_over_dp(partial, earlier):
-    blocks = partial.reshape(lax.axis_size("z_hi"), lax.axis_size("y"), -1, partial.shape[1])
-    return over_z(over_y(blocks), earlier)
+def summed_over_dp(partial, late_y, late_z):
+    blocks = partial.reshape(lax.axis_size(BLOCKS), -1, partial.shape[1])
+    return over_z(over_y(blocks, late_y), late_z)
 
 
 def shards(
@@ -126,11 +128,12 @@
     onehot = (segment_ids[:, None] == labels[None, :]).astype(jnp.float32)
     perturb = adv_init * init_noise
     embedded = tokens.astype(jnp.float32) + perturb
-    whole = gathered_features(embedded)
+    emb_local = embedded.astype(jnp.bfloat16)
+    emb_bf = gathered_features(emb_local)
     lefts_in, rights_in, lefts_out, rights_out = [], [], [], []
     for ascent in range(ASCENTS):
         last = ascent + 1 == ASCENTS
-        emb = lax.optimization_barrier(whole.astype(jnp.bfloat16)).astype(jnp.float32)
+        emb = lax.optimization_barrier(emb_bf).astype(jnp.float32)
         inv_rms = lax.rsqrt(jnp.mean(emb * emb, axis=1, keepdims=True) + 1e-06)
         normed = (emb * inv_rms * norm_gain).astype(jnp.bfloat16)
         preact = jnp.dot(normed, weight_in, preferred_element_type=jnp.float32)
@@ -144,7 +147,6 @@
         lefts_out += for_both_cores(grad, core)
         if last:
             partial_out = partial_over_chip(lefts_out, rights_out)
-            summed_out = summed_over_dp(partial_out, partial_out[0, 0])
             slope = slope + nothing(partial_out[0, 0])
         hidden_grad = (
             jnp.dot(grad, weight_out.T, preferred_element_type=jnp.float32) * slope
@@ -166,7 +168,7 @@
             arrived = over_tensor(blocks)
             scaled = arrived[:, :width_local] * gain_local
             row_dot = jnp.sum(arrived[:, width_local:], axis=1, keepdims=True)
-            emb_local = embedded.astype(jnp.bfloat16).astype(jnp.float32)
+            emb_local = emb_local.astype(jnp.float32)
             delta_grad = (
                 out_grad + inv_rms * scaled - emb_local * inv_rms * inv_rms * inv_rms * row_dot / D
             )
@@ -180,9 +182,12 @@
             token_scale = jnp.sum(onehot * (adv_step / root_mean)[None, :], axis=1)[:, None]
             perturb = perturb + delta_grad * token_scale
             embedded = tokens.astype(jnp.float32) + perturb
-            whole = whole + delta_whole * token_scale
+            emb_bf = (emb + delta_whole * token_scale).astype(jnp.bfloat16)
     partial_in = partial_over_chip(lefts_in, rights_in)
-    summed_in, summed_out = summed_over_dp(partial_in, summed_out[0, 0]), summed_out.T
+    there = nothing(partial_in[0, 0])
+    summed_out = summed_over_dp(partial_out, there, there)
+    summed_in = summed_over_dp(partial_in, there, nothing(summed_out[0, 0]))
+    summed_out = summed_out.T
     dp_rows = moment_in.shape[0]
     offset = lax.axis_index(DP) * dp_rows
     own_in = lax.dynamic_slice_in_dim(weight_in, offset, dp_rows, 0)

time: 217 us -> 219 us (level)
  waiting for transfers between devices: 57 us -> 47.5 us
  other arithmetic: 11.3 us -> 18.6 us
  blocking collectives: 73.5 us -> 68 us
  local copies, waits for them, and re-layouts: 4.61 us -> 8.79 us
  matrix products: 20.6 us -> 24.6 us
    ppermute x11, waiting for transfers between devices: 26 us -> 19.8 us  [from_partner(): return lax.ppermute(array, axis, [(0, 1), (1, 0)])]
    convert_element_type x4 -> x6, other arithmetic: 0.94 us -> 6.93 us  [the longest x2 3.24 us: over_y(): on_down = (with_own(block(1, n_y - 1), sunk[0]) + late).astype(jnp.bfloat16)]
    all_to_all x5, blocking collectives: 73.5 us -> 68 us  [to_peers(): return lax.all_to_all(blocks, axis, 0, 0, tiled=True)]
    ppermute x8, waiting for transfers between devices: 16.6 us -> 13.6 us  [the longest x2 13.6 us: over_y(): risen = lax.ppermute(jnp.stack([block(0, 2), block(1, 1)]), 'y', up)]
    another operation x6 -> x4, other arithmetic: 0.46 us -> 3.36 us  [the longest x2 1.68 us: over_y(): risen = lax.ppermute(jnp.stack([block(0, 2), block(1, 1)]), 'y', up)]
    add x3 -> x0, other arithmetic: 2.57 us -> none  [the longest x2 1.78 us: over_y(): return picked(blocks, y, 1).astype(jnp.float32) + arrived]
  transfers between devices with their start and end apart: 23 -> 23, of which waited for: 10 -> 9; matrix products, arithmetic and copies ran while one was open for 5% -> 10% of each run, Pallas kernels for 0% -> 0%
where the time goes in v5:
time: 219 us; the launch traced here: 218 us
  blocking collectives  68 us (31%)
  starting transfers between devices  47.5 us (22%)
  waiting for transfers between devices  47.5 us (22%)
  matrix products  24.6 us (11%)
  other arithmetic  18.6 us (8%)
  local copies, waits for them, and re-layouts  8.79 us (4%)
  between operations  3.12 us (1%)
    all_to_all x5, blocking collectives, to_peers(): return lax.all_to_all(blocks, axis, 0, 0, tiled=True)  68 us
    ppermute x11, waiting for transfers between devices, from_partner(): return lax.ppermute(array, axis, [(0, 1), (1, 0)])  19.8 us
    ppermute x2, waiting for transfers between devices, over_y(): risen = lax.ppermute(jnp.stack([block(0, 2), block(1, 1)]), 'y', up)  13.6 us
    ppermute x2, starting transfers between devices, over_y(): sunk = lax.ppermute(jnp.stack([block(1, 2), block(0, n_y - 1)]), 'y', down)  12.7 us
    ppermute x11, starting transfers between devices, from_partner(): return lax.ppermute(array, axis, [(0, 1), (1, 0)])  11.6 us
    all_to_all x2, waiting for transfers between devices, to_peers(): return lax.all_to_all(blocks, axis, 0, 0, tiled=True)  11.3 us
    all_to_all x2, starting transfers between devices, to_peers(): return lax.all_to_all(blocks, axis, 0, 0, tiled=True)  11 us
    dot_general x2, matrix products, shards(): preact = jnp.dot(normed, weight_in, preferred_element_type=jnp.float32)  9.4 us
  transfers between devices with their start and end apart: 23, of which 9 were waited for; matrix products, arithmetic and copies ran while one was open for 10% of the time, Pallas kernels for 0%

profile of v5, /device:TPU:33, one launch (start us, length us, event | category | flops | bytes accessed | tf_op | source)
XLA Modules:
  0.0 218.1 jit_solution(2360379349422255816)
XLA Ops:
  0.6 0.8 fusion.59
  1.5 15.8 %all_to_all.35 = bf16[16,128,64]{1,2,0:T(8,128)(2,1)S(1)} all-to-all(bf16[16,128,64]{1,2,0:T(8,128)(2,1)S(1)} %broadcast_in_dim.10), channel_id=1, replica_groups=mesh['z_hi'=2,'y'=4,'core'=2,'x'=4,'z_lo'=4] {'x','z_lo'}, dimensions={0} | all-to-all | bytes 524288 | tf_op jit(solution)/shard_map/all_to_all | solution.py:22
  17.6 0.8 fusion.31
  18.4 4.7 %fusion.20 = (f32[128,2048]{1,0:T(8,128)}, bf16[128,2048]{1,0:T(8,128)(2,1)S(1)}) fusion(bf16[128,1024]{1,0:T(8,128)(2,1)S(1)} %fusion.31, bf16[1024,2048]{1,0:T(8,128)(2,1)} %param.14), kind=kOutput, calls=%fused_computation.30 | convolution fusion | flops 541851648 | bytes 6029312 | tf_op jit(solution)/shard_map/dot_general | solution.py:139
  23.1 0.7 convolution_convert_fusion.3
  24.1 13.8 %all_to_all.36 = bf16[16,128,64]{1,2,0:T(8,128)(2,1)S(1)} all-to-all(bf16[16,128,64]{1,2,0:T(8,128)(2,1)S(1)} %bitcast.129), channel_id=1, replica_groups=mesh['z_hi'=2,'y'=4,'core'=2,'x'=4,'z_lo'=4] {'x','z_lo'}, dimensions={0} | all-to-all | bytes 524288 | tf_op jit(solution)/shard_map/all_to_all | solution.py:22
  38.0 13.2 %all_to_all.37 = bf16[16,128,64]{1,2,0:T(8,128)(2,1)S(1)} all-to-all(bf16[16,128,64]{1,2,0:T(8,128)(2,1)S(1)} %broadcast_in_dim.11), channel_id=1, replica_groups=mesh['z_hi'=2,'y'=4,'core'=2,'x'=4,'z_lo'=4] {'x','z_lo'}, dimensions={0} | all-to-all | bytes 524288 | tf_op jit(solution)/shard_map/all_to_all | solution.py:22
  51.2 4.0 %fusion = bf16[128,2048]{1,0:T(8,128)(2,1)S(1)} fusion(f32[128,2048]{1,0:T(8,128)} %get-tuple-element.14, bf16[128,1024]{0,1:T(8,128)(2,1)S(1)} %bitcast.122, bf16[2048,1024]{1,0:T(8,128)(2,1)} %param.15), kind=kOutput, calls=%fused_computation.4 | convolution fusion | flops 537395200 | bytes 6029312 | tf_op jit(solution)/shard_map/dot_general | solution.py:152
  55.2 1.6 fusion.66
  57.0 0.7 pad_maximum_fusion.4
  57.8 5.6 %all-to-all-start.3 = ((bf16[16,128,66]{1,2,0:T(8,128)(2,1)}), bf16[16,128,66]{1,2,0:T(8,128)(2,1)S(1)}, u32[]{:S(2)}, u32[]{:S(2)}) async-start(bf16[16,128,66]{1,2,0:T(8,128)(2,1)} %pad_maximum_fusion.4), calls=%async_computation.3 | async-start | bytes 589824 | tf_op jit(solution)/shard_map/all_to_all | solution.py:22
  63.5 8.0 %all-to-all-done.3 = bf16[16,128,66]{1,2,0:T(8,128)(2,1)S(1)} async-done(((bf16[16,128,66]{1,2,0:T(8,128)(2,1)}), bf16[16,128,66]{1,2,0:T(8,128)(2,1)S(1)}, u32[]{:S(2)}, u32[]{:S(2)}) %all-to-all-start.3) | async-done | bytes 270368 | tf_op jit(solution)/shard_map/all_to_all | solution.py:22
  71.6 13.7 %all_to_all.38 = bf16[16,128,64]{1,2,0:T(8,128)(2,1)S(1)} all-to-all(bf16[16,128,64]{1,2,0:T(8,128)(2,1)S(1)} %broadcast_in_dim.13), channel_id=1, replica_groups=mesh['z_hi'=2,'y'=4,'core'=2,'x'=4,'z_lo'=4] {'x','z_lo'}, dimensions={0} | all-to-all | bytes 524288 | tf_op jit(solution)/shard_map/all_to_all | solution.py:22
  85.6 2.7 %collective-permute-start.1 = (f32[2,32]{1,0:T(2,128)S(1)}, f32[2,32]{1,0:T(2,128)S(1)}, u32[]{:S(2)}, u32[]{:S(2)}) collective-permute-start(f32[2,32]{1,0:T(2,128)S(1)} %pad_maximum_fusion.5), channel_id=1, source_target_pairs={{0,16},{16,0},{1,17},{17,1},{2,18},{18,2},{3,19},{19,3},{4,20},{20... | collective-permute-start | bytes 776 | tf_op jit(solution)/shard_map/ppermute | solution.py:40
  88.3 0.8 collective-permute-done.1
  89.2 3.2 %collective-permute-start.2 = (f32[2,32]{1,0:T(2,128)S(1)}, f32[2,32]{1,0:T(2,128)S(1)}, u32[]{:S(2)}, u32[]{:S(2)}) collective-permute-start(f32[2,32]{1,0:T(2,128)S(1)} %fusion.64), channel_id=1, source_target_pairs={{0,32},{32,64},{64,96},{96,128},{128,160},{160,192},{192,224},{1,3... | collective-permute-start | bytes 776 | tf_op jit(solution)/shard_map/ppermute | solution.py:55
  92.4 1.3 collective-permute-start.3
  93.9 2.7 %collective-permute-done.3 = f32[2,32]{1,0:T(2,128)S(1)} collective-permute-done((f32[2,32]{1,0:T(2,128)S(1)}, f32[2,32]{1,0:T(2,128)S(1)}, u32[]{:S(2)}, u32[]{:S(2)}) %collective-permute-start.3) | collective-permute-done | bytes 288 | tf_op jit(solution)/shard_map/ppermute | solution.py:56
  97.2 4.7 %fusion.25 = (f32[128,2048]{1,0:T(8,128)}, bf16[128,2048]{1,0:T(8,128)(2,1)S(1)}) fusion(bf16[128,1024]{1,0:T(8,128)(2,1)S(1)} %fusion.28, bf16[1024,2048]{1,0:T(8,128)(2,1)} %param.14), kind=kOutput, calls=%fused_computation.35 | convolution fusion | flops 541851648 | bytes 6029312 | tf_op jit(solution)/shard_map/dot_general | solution.py:139
  102.0 0.7 convolution_convert_fusion.2
  102.9 11.5 %all_to_all.39 = bf16[16,128,64]{1,2,0:T(8,128)(2,1)S(1)} all-to-all(bf16[16,128,64]{1,2,0:T(8,128)(2,1)S(1)} %bitcast.130), channel_id=1, replica_groups=mesh['z_hi'=2,'y'=4,'core'=2,'x'=4,'z_lo'=4] {'x','z_lo'}, dimensions={0} | all-to-all | bytes 524288 | tf_op jit(solution)/shard_map/all_to_all | solution.py:22
  114.5 0.7 fusion.55
  115.2 0.8 broadcast_in_dim.14
  115.9 5.3 %all-to-all-start.6 = ((bf16[16,128,64]{1,2,0:T(8,128)(2,1)}), bf16[16,128,64]{1,2,0:T(8,128)(2,1)S(1)}, u32[]{:S(2)}, u32[]{:S(2)}) async-start(bf16[16,128,64]{1,2,0:T(8,128)(2,1)} %broadcast_in_dim.14), calls=%async_computation.6 | async-start | bytes 524288 | tf_op jit(solution)/shard_map/all_to_all | solution.py:22
  121.3 2.8 %collective-permute-start.8 = (bf16[128,2048]{1,0:T(8,128)(2,1)S(1)}, bf16[128,2048]{1,0:T(8,128)(2,1)}, u32[]{:S(2)}, u32[]{:S(2)}) collective-permute-start(bf16[128,2048]{1,0:T(8,128)(2,1)S(1)} %get-tuple-element.13), channel_id=1, source_target_pairs={{0,16},{16,0},{1,17},{17,1},{2,18},{18,2},{3,19},{19,3},{4,20},{20... | collective-permute-start | bytes 1572872 | tf_op jit(solution)/shard_map/ppermute | solution.py:40
  124.1 0.7 constant_dynamic-slice_fusion.12
  124.8 0.4 collective-permute-start.6
  125.4 3.3 %all-to-all-done.6 = bf16[16,128,64]{1,2,0:T(8,128)(2,1)S(1)} async-done(((bf16[16,128,64]{1,2,0:T(8,128)(2,1)}), bf16[16,128,64]{1,2,0:T(8,128)(2,1)S(1)}, u32[]{:S(2)}, u32[]{:S(2)}) %all-to-all-start.6) | async-done | bytes 262176 | tf_op jit(solution)/shard_map/all_to_all | solution.py:22
  128.7 0.7 constant_dynamic-slice_fusion.10
  129.5 3.7 %collective-permute-start.7 = (bf16[128,512]{0,1:T(8,128)(2,1)S(1)}, bf16[128,512]{0,1:T(8,128)(2,1)S(1)}, u32[]{:S(2)}, u32[]{:S(2)}) collective-permute-start(bf16[128,512]{0,1:T(8,128)(2,1)S(1)} %bitcast.133), channel_id=1, source_target_pairs={{0,16},{16,0},{1,17},{17,1},{2,18},{18,2},{3,19},{19,3},{4,20},{20... | collective-permute-start | bytes 393224 | tf_op jit(solution)/shard_map/ppermute | solution.py:40
  133.4 0.7 constant_dynamic-slice_fusion.16
  134.0 0.5 collective-permute-start.5
  134.6 0.6 copy-done.15
  135.2 3.0 %convolution_convert_fusion.1 = bf16[512,2048]{1,0:T(8,128)(2,1)S(1)} fusion(bf16[128,2048]{1,0:T(8,128)(2,1)} %collective-permute-done.9, bf16[128,2048]{1,0:T(8,128)(2,1)} %copy-done.7, bf16[128,2048]{1,0:T(8,128)(2,1)} %collective-permute-done.8, bf16[128,2048]{1,0:T(8,128)(2,1)S(1)} %get-tuple-element.13, bf16[128,512]{0,1:T(8,128)(2,1)} %copy-done.17, ...), kind=kOutput, calls=%fused_computation.1 | convolution fusion | flops 1085276160 | bytes 4718592 | tf_op jit(solution)/shard_map/dot_general | solution.py:108
  138.3 0.5 slice.54
  139.5 2.3 %fusion.1 = bf16[128,2048]{1,0:T(8,128)(2,1)} fusion(bf16[128,1024]{0,1:T(8,128)(2,1)S(1)} %bitcast.121, bf16[2048,1024]{1,0:T(8,128)(2,1)S(1)} %copy-done.2, f32[128,2048]{1,0:T(8,128)S(1)} %copy-done.6, f32[]{:T(128)} %bitcast.32), kind=kOutput, calls=%fused_computation.5 | convolution fusion | flops 537657344 | bytes 6029316 | tf_op jit(solution)/shard_map/dot_general | solution.py:152
  141.9 0.8 pad_maximum_fusion.3
  142.7 1.3 collective-permute-start.16
  144.0 0.8 pad_maximum_fusion.2
  144.9 10.0 %collective-permute-start.15 = (bf16[2,64,2048]{2,1,0:T(8,128)(2,1)}, bf16[2,64,2048]{2,1,0:T(8,128)(2,1)}, u32[]{:S(2)}, u32[]{:S(2)}) collective-permute-start(bf16[2,64,2048]{2,1,0:T(8,128)(2,1)} %pad_maximum_fusion.2), channel_id=1, source_target_pairs={{0,96},{32,0},{64,32},{96,64},{1,97},{33,1},{65,33},{97,65},{2,98}... | collective-permute-start | bytes 1572872 | tf_op jit(solution)/shard_map/ppermute | solution.py:86
  154.9 0.7 copy-done.16
  155.6 0.8 collective-permute-start.4
  156.3 1.2 collective-permute-done.4
  157.5 2.8 %convolution_convert_fusion = bf16[512,2048]{1,0:T(8,128)(2,1)S(1)} fusion(bf16[128,2048]{1,0:T(8,128)(2,1)} %collective-permute-done.10, bf16[128,2048]{1,0:T(8,128)(2,1)} %fusion.1, bf16[128,2048]{1,0:T(8,128)(2,1)} %collective-permute-done.5, bf16[128,2048]{1,0:T(8,128)(2,1)S(1)} %fusion, bf16[128,512]{0,1:T(8,128)(2,1)S(1)} %collective-permute-done.4, ...), kind=kOutput, calls=%fused_computation | convolution fusion | flops 1085276160 | bytes 4718592 | tf_op jit(solution)/shard_map/dot_general | solution.py:108
  160.3 0.6 slice.57
  161.5 4.5 %collective-permute-done.16 = bf16[2,64,2048]{2,1,0:T(8,128)(2,1)S(1)} collective-permute-done((bf16[2,64,2048]{2,1,0:T(8,128)(2,1)}, bf16[2,64,2048]{2,1,0:T(8,128)(2,1)S(1)}, u32[]{:S(2)}, u32[]{:S(2)}) %collective-permute-start.16) | collective-permute-done | bytes 524320 | tf_op jit(solution)/shard_map/ppermute | solution.py:85
  166.1 1.9 fusion.51
  168.0 1.5 collective-permute-start.17
  169.5 1.8 collective-permute-start.18
  171.4 0.8 pad_maximum_fusion.1
  172.2 0.8 pad_maximum_fusion
  173.1 2.7 %collective-permute-start.11 = (bf16[2,64,2048]{2,1,0:T(8,128)(2,1)}, bf16[2,64,2048]{2,1,0:T(8,128)(2,1)}, u32[]{:S(2)}, u32[]{:S(2)}) collective-permute-start(bf16[2,64,2048]{2,1,0:T(8,128)(2,1)} %pad_maximum_fusion), channel_id=1, source_target_pairs={{0,96},{32,0},{64,32},{96,64},{1,97},{33,1},{65,33},{97,65},{2,98}... | collective-permute-start | bytes 1572872 | tf_op jit(solution)/shard_map/ppermute | solution.py:86
  175.7 1.2 constant_dynamic-slice_fusion
  177.3 1.5 add_convert_fusion.1
  179.1 9.0 %collective-permute-done.12 = bf16[2,64,2048]{2,1,0:T(8,128)(2,1)} collective-permute-done((bf16[2,64,2048]{2,1,0:T(8,128)(2,1)}, bf16[2,64,2048]{2,1,0:T(8,128)(2,1)}, u32[]{:S(2)}, u32[]{:S(2)}) %collective-permute-start.12) | collective-permute-done | bytes 524320 | tf_op jit(solution)/shard_map/ppermute | solution.py:85
  188.1 1.3 fusion.49
  189.6 3.0 %collective-permute-start.14 = (bf16[64,2048]{1,0:T(8,128)(2,1)S(1)}, bf16[64,2048]{1,0:T(8,128)(2,1)S(1)}, u32[]{:S(2)}, u32[]{:S(2)}) collective-permute-start(bf16[64,2048]{1,0:T(8,128)(2,1)S(1)} %get-tuple-element.18), channel_id=1, source_target_pairs={{0,96},{32,0},{64,32},{96,64},{1,97},{33,1},{65,33},{97,65},{2,98}... | collective-permute-start | bytes 786440 | tf_op jit(solution)/shard_map/ppermute | solution.py:91
  192.6 3.2 %collective-permute-done.19 = bf16[64,2048]{1,0:T(8,128)(2,1)S(1)} collective-permute-done((bf16[64,2048]{1,0:T(8,128)(2,1)S(1)}, bf16[64,2048]{1,0:T(8,128)(2,1)S(1)}, u32[]{:S(2)}, u32[]{:S(2)}) %collective-permute-start.19) | collective-permute-done | bytes 262176 | tf_op jit(solution)/shard_map/ppermute | solution.py:40
  195.9 2.5 %subtract_convert_fusion = (bf16[2048,64]{0,1:T(8,128)(2,1)}, f32[2048,64]{0,1:T(8,128)}, f32[64,2048]{1,0:T(8,128)S(1)}) fusion(bf16[2048,64]{0,1:T(8,128)(2,1)S(1)} %copy.48, f32[2048,64]{0,1:T(8,128)} %param.17, bf16[64,2048]{1,0:T(8,128)(2,1)S(1)} %collective-permute-done.19, bf16[64,2048]{1,0:T(8,128)(2,1)} %collective-permute-done.18, ...), kind=kLoop, calls=%fused_computation.76 | loop fusion | flops 2621440 | bytes 3932169 | tf_op jit(solution)/shard_map/convert_element_type | solution.py:198
  198.4 0.5 slice.64
  199.6 1.3 add_convert_fusion
  200.9 0.3 collective-permute-start.20
  201.2 14.6 %collective-permute-done.20 = bf16[64,2048]{1,0:T(8,128)(2,1)S(1)} collective-permute-done((bf16[64,2048]{1,0:T(8,128)(2,1)S(1)}, bf16[64,2048]{1,0:T(8,128)(2,1)S(1)}, u32[]{:S(2)}, u32[]{:S(2)}) %collective-permute-start.20) | collective-permute-done | bytes 262176 | tf_op jit(solution)/shard_map/ppermute | solution.py:40
  215.7 2.4 %subtract_convert_fusion.1 = (bf16[64,2048]{1,0:T(8,128)(2,1)}, f32[64,2048]{1,0:T(8,128)}) fusion(bf16[1024,2048]{1,0:T(8,128)(2,1)} %param.14, s32[]{:T(128)S(6)} %select_n.73, bf16[64,2048]{1,0:T(8,128)(2,1)S(1)} %collective-permute-done.20, bf16[64,2048]{1,0:T(8,128)(2,1)S(1)} %collective-permute-done.14, ...), kind=kLoop, calls=%fused_computation.77 | loop fusion | flops 2621440 | bytes 3407885 | tf_op jit(solution)/shard_map/convert_element_type | solution.py:197
  (92 shorter events, 3.7 us)
Async XLA Ops:
  18.4 4.7 %copy-start = (bf16[2048,1024]{1,0:T(8,128)(2,1)S(1)}, bf16[2048,1024]{1,0:T(8,128)(2,1)}, u32[]{:S(2)}) copy-start(bf16[2048,1024]{1,0:T(8,128)(2,1)} %param.15) | copy-start | bytes 12582916
  23.1 14.8 %copy-start.9 = (f32[128,64]{0,1:T(8,128)S(1)}, f32[128,64]{0,1:T(8,128)}, u32[]{:S(2)}) copy-start(f32[128,64]{0,1:T(8,128)} %param.10) | copy-start | bytes 98308
  23.1 14.8 %copy-start.10 = (bf16[128,64]{0,1:T(8,128)(2,1)S(1)}, bf16[128,64]{0,1:T(8,128)(2,1)}, u32[]{:S(2)}) copy-start(bf16[128,64]{0,1:T(8,128)(2,1)} %param.9) | copy-start | bytes 49156
  23.1 14.8 %copy-start.11 = (f32[128,64]{0,1:T(8,128)S(1)}, f32[128,64]{0,1:T(8,128)}, u32[]{:S(2)}) copy-start(f32[128,64]{0,1:T(8,128)} %param.12) | copy-start | bytes 98308
  23.9 31.3 %copy-start.13 = (f32[1024]{0:T(1024)S(1)}, f32[1024]{0:T(1024)}, u32[]{:S(2)}) copy-start(f32[1024]{0:T(1024)} %param.13) | copy-start | bytes 12292
  24.1 31.2 %copy-start.3 = (bf16[1024,2048]{1,0:T(8,128)(2,1)S(1)}, bf16[1024,2048]{1,0:T(8,128)(2,1)}, u32[]{:S(2)}) copy-start(bf16[1024,2048]{1,0:T(8,128)(2,1)} %param.14) | copy-start | bytes 12582916
  55.2 30.3 %copy-start.14 = (s32[128]{0:T(128)S(1)}, s32[128]{0:T(128)}, u32[]{:S(2)}) copy-start(s32[128]{0:T(128)} %param.11) | copy-start | bytes 1540
  57.8 13.7 %all-to-all-start.3 = ((bf16[16,128,66]{1,2,0:T(8,128)(2,1)}), bf16[16,128,66]{1,2,0:T(8,128)(2,1)S(1)}, u32[]{:S(2)}, u32[]{:S(2)}) async-start(bf16[16,128,66]{1,2,0:T(8,128)(2,1)} %pad_maximum_fusion.4), calls=%async_computation.3 | async-start | bytes 589824 | tf_op jit(solution)/shard_map/all_to_all | solution.py:22
  85.6 3.5 %collective-permute-start.1 = (f32[2,32]{1,0:T(2,128)S(1)}, f32[2,32]{1,0:T(2,128)S(1)}, u32[]{:S(2)}, u32[]{:S(2)}) collective-permute-start(f32[2,32]{1,0:T(2,128)S(1)} %pad_maximum_fusion.5), channel_id=1, source_target_pairs={{0,16},{16,0},{1,17},{17,1},{2,18},{18,2},{3,19},{19,3},{4,20},{20... | collective-permute-start | bytes 776 | tf_op jit(solution)/shard_map/ppermute | solution.py:40
  89.2 4.8 %collective-permute-start.2 = (f32[2,32]{1,0:T(2,128)S(1)}, f32[2,32]{1,0:T(2,128)S(1)}, u32[]{:S(2)}, u32[]{:S(2)}) collective-permute-start(f32[2,32]{1,0:T(2,128)S(1)} %fusion.64), channel_id=1, source_target_pairs={{0,32},{32,64},{64,96},{96,128},{128,160},{160,192},{192,224},{1,3... | collective-permute-start | bytes 776 | tf_op jit(solution)/shard_map/ppermute | solution.py:55
  92.4 4.3 %collective-permute-start.3 = (f32[2,32]{1,0:T(2,128)S(1)}, f32[2,32]{1,0:T(2,128)S(1)}, u32[]{:S(2)}, u32[]{:S(2)}) collective-permute-start(f32[2,32]{1,0:T(2,128)S(1)} %fusion.64), channel_id=1, source_target_pairs={{32,0},{64,32},{96,64},{128,96},{160,128},{192,160},{224,192},{33,... | collective-permute-start | bytes 776 | tf_op jit(solution)/shard_map/ppermute | solution.py:56
  97.2 4.7 %copy-start.1 = (bf16[2048,1024]{1,0:T(8,128)(2,1)S(1)}, bf16[2048,1024]{1,0:T(8,128)(2,1)}, u32[]{:S(2)}) copy-start(bf16[2048,1024]{1,0:T(8,128)(2,1)} %param.15) | copy-start | bytes 12582916
  101.9 23.4 %copy-start.7 = (bf16[128,2048]{1,0:T(8,128)(2,1)}, bf16[128,2048]{1,0:T(8,128)(2,1)S(1)}, u32[]{:S(2)}) copy-start(bf16[128,2048]{1,0:T(8,128)(2,1)S(1)} %get-tuple-element.15) | copy-start | bytes 1572868
  101.9 12.5 %copy-start.12 = (f32[128,64]{0,1:T(8,128)S(1)}, f32[128,64]{0,1:T(8,128)}, u32[]{:S(2)}) copy-start(f32[128,64]{0,1:T(8,128)} %param.12) | copy-start | bytes 98308
  115.9 12.8 %all-to-all-start.6 = ((bf16[16,128,64]{1,2,0:T(8,128)(2,1)}), bf16[16,128,64]{1,2,0:T(8,128)(2,1)S(1)}, u32[]{:S(2)}, u32[]{:S(2)}) async-start(bf16[16,128,64]{1,2,0:T(8,128)(2,1)} %broadcast_in_dim.14), calls=%async_computation.6 | async-start | bytes 524288 | tf_op jit(solution)/shard_map/all_to_all | solution.py:22
  121.3 12.8 %collective-permute-start.8 = (bf16[128,2048]{1,0:T(8,128)(2,1)S(1)}, bf16[128,2048]{1,0:T(8,128)(2,1)}, u32[]{:S(2)}, u32[]{:S(2)}) collective-permute-start(bf16[128,2048]{1,0:T(8,128)(2,1)S(1)} %get-tuple-element.13), channel_id=1, source_target_pairs={{0,16},{16,0},{1,17},{17,1},{2,18},{18,2},{3,19},{19,3},{4,20},{20... | collective-permute-start | bytes 1572872 | tf_op jit(solution)/shard_map/ppermute | solution.py:40
  124.0 10.5 %collective-permute-start.9 = (bf16[128,2048]{1,0:T(8,128)(2,1)S(1)}, bf16[128,2048]{1,0:T(8,128)(2,1)}, u32[]{:S(2)}, u32[]{:S(2)}) collective-permute-start(bf16[128,2048]{1,0:T(8,128)(2,1)S(1)} %get-tuple-element.15), channel_id=1, source_target_pairs={{0,16},{16,0},{1,17},{17,1},{2,18},{18,2},{3,19},{19,3},{4,20},{20... | collective-permute-start | bytes 1572872 | tf_op jit(solution)/shard_map/ppermute | solution.py:40
  124.8 9.7 %collective-permute-start.6 = (bf16[128,512]{0,1:T(8,128)(2,1)S(1)}, bf16[128,512]{0,1:T(8,128)(2,1)S(1)}, u32[]{:S(2)}, u32[]{:S(2)}) collective-permute-start(bf16[128,512]{0,1:T(8,128)(2,1)S(1)} %bitcast.136), channel_id=1, source_target_pairs={{0,16},{16,0},{1,17},{17,1},{2,18},{18,2},{3,19},{19,3},{4,20},{20... | collective-permute-start | bytes 393224 | tf_op jit(solution)/shard_map/ppermute | solution.py:40
  129.5 5.1 %collective-permute-start.7 = (bf16[128,512]{0,1:T(8,128)(2,1)S(1)}, bf16[128,512]{0,1:T(8,128)(2,1)S(1)}, u32[]{:S(2)}, u32[]{:S(2)}) collective-permute-start(bf16[128,512]{0,1:T(8,128)(2,1)S(1)} %bitcast.133), channel_id=1, source_target_pairs={{0,16},{16,0},{1,17},{17,1},{2,18},{18,2},{3,19},{19,3},{4,20},{20... | collective-permute-start | bytes 393224 | tf_op jit(solution)/shard_map/ppermute | solution.py:40
  134.0 20.9 %collective-permute-start = (bf16[128,512]{0,1:T(8,128)(2,1)S(1)}, bf16[128,512]{0,1:T(8,128)(2,1)S(1)}, u32[]{:S(2)}, u32[]{:S(2)}) collective-permute-start(bf16[128,512]{0,1:T(8,128)(2,1)S(1)} %bitcast.137), channel_id=1, source_target_pairs={{0,16},{16,0},{1,17},{17,1},{2,18},{18,2},{3,19},{19,3},{4,20},{20... | collective-permute-start | bytes 393224 | tf_op jit(solution)/shard_map/ppermute | solution.py:40
  134.0 22.3 %collective-permute-start.5 = (bf16[128,2048]{1,0:T(8,128)(2,1)S(1)}, bf16[128,2048]{1,0:T(8,128)(2,1)}, u32[]{:S(2)}, u32[]{:S(2)}) collective-permute-start(bf16[128,2048]{1,0:T(8,128)(2,1)S(1)} %fusion), channel_id=1, source_target_pairs={{0,16},{16,0},{1,17},{17,1},{2,18},{18,2},{3,19},{19,3},{4,20},{20... | collective-permute-start | bytes 1572872 | tf_op jit(solution)/shard_map/ppermute | solution.py:40
  134.5 0.6 copy-start.15
  134.6 0.7 copy-start.17
  135.2 4.2 %copy-start.2 = (bf16[2048,1024]{1,0:T(8,128)(2,1)S(1)}, bf16[2048,1024]{1,0:T(8,128)(2,1)}, u32[]{:S(2)}) copy-start(bf16[2048,1024]{1,0:T(8,128)(2,1)} %param.15) | copy-start | bytes 12582916
  135.2 4.2 %copy-start.6 = (f32[128,2048]{1,0:T(8,128)S(1)}, f32[128,2048]{1,0:T(8,128)}, u32[]{:S(2)}) copy-start(f32[128,2048]{1,0:T(8,128)} %get-tuple-element.16) | copy-start | bytes 3145732
  141.8 15.7 %collective-permute-start.10 = (bf16[128,2048]{1,0:T(8,128)(2,1)}, bf16[128,2048]{1,0:T(8,128)(2,1)}, u32[]{:S(2)}, u32[]{:S(2)}) collective-permute-start(bf16[128,2048]{1,0:T(8,128)(2,1)} %fusion.1), channel_id=1, source_target_pairs={{0,16},{16,0},{1,17},{17,1},{2,18},{18,2},{3,19},{19,3},{4,20},{20... | collective-permute-start | bytes 1572872 | tf_op jit(solution)/shard_map/ppermute | solution.py:40
  142.7 23.4 %collective-permute-start.16 = (bf16[2,64,2048]{2,1,0:T(8,128)(2,1)}, bf16[2,64,2048]{2,1,0:T(8,128)(2,1)S(1)}, u32[]{:S(2)}, u32[]{:S(2)}) collective-permute-start(bf16[2,64,2048]{2,1,0:T(8,128)(2,1)} %pad_maximum_fusion.3), channel_id=1, source_target_pairs={{0,32},{32,64},{64,96},{96,0},{1,33},{33,65},{65,97},{97,1},{2,34}... | collective-permute-start | bytes 1572872 | tf_op jit(solution)/shard_map/ppermute | solution.py:85
  144.9 21.2 %collective-permute-start.15 = (bf16[2,64,2048]{2,1,0:T(8,128)(2,1)}, bf16[2,64,2048]{2,1,0:T(8,128)(2,1)}, u32[]{:S(2)}, u32[]{:S(2)}) collective-permute-start(bf16[2,64,2048]{2,1,0:T(8,128)(2,1)} %pad_maximum_fusion.2), channel_id=1, source_target_pairs={{0,96},{32,0},{64,32},{96,64},{1,97},{33,1},{65,33},{97,65},{2,98}... | collective-permute-start | bytes 1572872 | tf_op jit(solution)/shard_map/ppermute | solution.py:86
  154.9 0.7 copy-start.16
  155.6 2.0 collective-permute-start.4
  160.3 11.0 %copy-start.4 = (bf16[512,2048]{1,0:T(8,128)(2,1)}, bf16[512,2048]{1,0:T(8,128)(2,1)S(1)}, u32[]{:S(2)}) copy-start(bf16[512,2048]{1,0:T(8,128)(2,1)S(1)} %convolution_convert_fusion) | copy-start | bytes 6291460
  168.0 9.2 %collective-permute-start.17 = (bf16[64,2048]{1,0:T(8,128)(2,1)}, bf16[64,2048]{1,0:T(8,128)(2,1)}, u32[]{:S(2)}, u32[]{:S(2)}) collective-permute-start(bf16[64,2048]{1,0:T(8,128)(2,1)} %get-tuple-element.19), channel_id=1, source_target_pairs={{0,32},{32,64},{64,96},{96,0},{1,33},{33,65},{65,97},{97,1},{2,34}... | collective-permute-start | bytes 786440 | tf_op jit(solution)/shard_map/ppermute | solution.py:90
  169.5 7.8 %collective-permute-start.18 = (bf16[64,2048]{1,0:T(8,128)(2,1)}, bf16[64,2048]{1,0:T(8,128)(2,1)}, u32[]{:S(2)}, u32[]{:S(2)}) collective-permute-start(bf16[64,2048]{1,0:T(8,128)(2,1)} %get-tuple-element.20), channel_id=1, source_target_pairs={{0,96},{32,0},{64,32},{96,64},{1,97},{33,1},{65,33},{97,65},{2,98}... | collective-permute-start | bytes 786440 | tf_op jit(solution)/shard_map/ppermute | solution.py:91
  172.2 15.9 %collective-permute-start.12 = (bf16[2,64,2048]{2,1,0:T(8,128)(2,1)}, bf16[2,64,2048]{2,1,0:T(8,128)(2,1)}, u32[]{:S(2)}, u32[]{:S(2)}) collective-permute-start(bf16[2,64,2048]{2,1,0:T(8,128)(2,1)} %pad_maximum_fusion.1), channel_id=1, source_target_pairs={{0,32},{32,64},{64,96},{96,0},{1,33},{33,65},{65,97},{97,1},{2,34}... | collective-permute-start | bytes 1572872 | tf_op jit(solution)/shard_map/ppermute | solution.py:85
  173.1 15.0 %collective-permute-start.11 = (bf16[2,64,2048]{2,1,0:T(8,128)(2,1)}, bf16[2,64,2048]{2,1,0:T(8,128)(2,1)}, u32[]{:S(2)}, u32[]{:S(2)}) collective-permute-start(bf16[2,64,2048]{2,1,0:T(8,128)(2,1)} %pad_maximum_fusion), channel_id=1, source_target_pairs={{0,96},{32,0},{64,32},{96,64},{1,97},{33,1},{65,33},{97,65},{2,98}... | collective-permute-start | bytes 1572872 | tf_op jit(solution)/shard_map/ppermute | solution.py:86
  177.2 22.4 %copy-start.5 = (bf16[512,2048]{1,0:T(8,128)(2,1)S(1)}, bf16[512,2048]{1,0:T(8,128)(2,1)}, u32[]{:S(2)}) copy-start(bf16[512,2048]{1,0:T(8,128)(2,1)} %copy-done.4) | copy-start | bytes 6291460
  177.2 38.5 %copy-start.8 = (f32[64,2048]{1,0:T(8,128)S(1)}, f32[64,2048]{1,0:T(8,128)}, u32[]{:S(2)}) copy-start(f32[64,2048]{1,0:T(8,128)} %param.16) | copy-start | bytes 1572868
  178.8 17.1 %collective-permute-start.19 = (bf16[64,2048]{1,0:T(8,128)(2,1)S(1)}, bf16[64,2048]{1,0:T(8,128)(2,1)S(1)}, u32[]{:S(2)}, u32[]{:S(2)}) collective-permute-start(bf16[64,2048]{1,0:T(8,128)(2,1)S(1)} %add_convert_fusion.1), channel_id=1, source_target_pairs={{0,128},{128,0},{1,129},{129,1},{2,130},{130,2},{3,131},{131,3},{4... | collective-permute-start | bytes 786440 | tf_op jit(solution)/shard_map/ppermute | solution.py:40
  189.5 10.1 %collective-permute-start.13 = (bf16[64,2048]{1,0:T(8,128)(2,1)S(1)}, bf16[64,2048]{1,0:T(8,128)(2,1)S(1)}, u32[]{:S(2)}, u32[]{:S(2)}) collective-permute-start(bf16[64,2048]{1,0:T(8,128)(2,1)S(1)} %get-tuple-element.17), channel_id=1, source_target_pairs={{0,32},{32,64},{64,96},{96,0},{1,33},{33,65},{65,97},{97,1},{2,34}... | collective-permute-start | bytes 786440 | tf_op jit(solution)/shard_map/ppermute | solution.py:90
  189.6 10.0 %collective-permute-start.14 = (bf16[64,2048]{1,0:T(8,128)(2,1)S(1)}, bf16[64,2048]{1,0:T(8,128)(2,1)S(1)}, u32[]{:S(2)}, u32[]{:S(2)}) collective-permute-start(bf16[64,2048]{1,0:T(8,128)(2,1)S(1)} %get-tuple-element.18), channel_id=1, source_target_pairs={{0,96},{32,0},{64,32},{96,64},{1,97},{33,1},{65,33},{97,65},{2,98}... | collective-permute-start | bytes 786440 | tf_op jit(solution)/shard_map/ppermute | solution.py:91
  200.9 14.9 %collective-permute-start.20 = (bf16[64,2048]{1,0:T(8,128)(2,1)S(1)}, bf16[64,2048]{1,0:T(8,128)(2,1)S(1)}, u32[]{:S(2)}, u32[]{:S(2)}) collective-permute-start(bf16[64,2048]{1,0:T(8,128)(2,1)S(1)} %add_convert_fusion), channel_id=1, source_target_pairs={{0,128},{128,0},{1,129},{129,1},{2,130},{130,2},{3,131},{131,3},{4... | collective-permute-start | bytes 786440 | tf_op jit(solution)/shard_map/ppermute | solution.py:40

commit v6 on v5

--- a/solution.py
+++ b/solution.py
@@ -57,50 +57,52 @@
     return sums + before + after
 
 
-def rows_of_core(array, core):
-    tokens, features = array.shape
-    blocks = array.reshape(tokens, lax.axis_size(BLOCKS), 2, -1)
-    return lax.dynamic_index_in_dim(blocks, core, 2, keepdims=False).reshape(tokens, features // 2)
-
-
-def for_both_cores(array, core):
-    return [rows_of_core(array, core), from_partner(rows_of_core(array, 1 - core), "core")]
-
-
-def picked(blocks, index, dim):
-    return lax.dynamic_index_in_dim(blocks, index, dim, keepdims=False)
-
-
-def over_y(blocks, late):
-    y, n_y = lax.axis_index("y"), lax.axis_size("y")
+LEAVING = ((0, 2), (1, 1), (1, 2), (0, 3), (0, 0), (1, 0), (0, 1), (1, 3))
+
+
+def leaving_order(features, flip):
+    z_hi, y, core = (lax.axis_index(name) for name in DP)
+    n_y = lax.axis_size("y")
+    width = features // (2 * len(LEAVING))
+    blocks = [
+        ((z_hi ^ far) * n_y + lax.rem(y + steps, n_y)) * 2 + (core ^ flip) for far, steps in LEAVING
+    ]
+    column = jnp.arange(features // 2, dtype=jnp.int32)
+    source = column % width
+    for place, block in enumerate(blocks):
+        source = source + jnp.where(column // width == place, block * width, 0)
+    return (jnp.arange(features, dtype=jnp.int32)[:, None] == source[None, :]).astype(jnp.bfloat16)
+
+
+def for_both_cores(array, orders):
+    own, other = [
+        jnp.dot(array, order, preferred_element_type=jnp.float32).astype(jnp.bfloat16)
+        for order in orders
+    ]
+    return [own, from_partner(other, "core")]
+
+
+def over_y(partial, late):
+    n_y = lax.axis_size("y")
     up = [(i, (i + 1) % n_y) for i in range(n_y)]
     down = [(i, (i - 1) % n_y) for i in range(n_y)]
-
-    def block(z_hi, shift):
-        return picked(blocks, z_hi * n_y + lax.rem(y + shift, n_y), 0)
-
-    def with_own(own, arrived):
-        return own.astype(jnp.float32) + arrived.astype(jnp.float32)
-
-    risen = lax.ppermute(jnp.stack([block(0, 2), block(1, 1)]), "y", up)
-    sunk = lax.ppermute(jnp.stack([block(1, 2), block(0, n_y - 1)]), "y", down)
-    on_up = (with_own(block(0, 1), risen[0]) + late).astype(jnp.bfloat16)
-    on_down = (with_own(block(1, n_y - 1), sunk[0]) + late).astype(jnp.bfloat16)
+    few = partial.shape[0] // len(LEAVING)
+
+    def wide(array, place):
+        return array[place * few : (place + 1) * few].astype(jnp.float32)
+
+    risen = lax.ppermute(partial[: 2 * few], "y", up)
+    sunk = lax.ppermute(partial[2 * few : 4 * few], "y", down)
+    on_up = (wide(partial, 6) + wide(risen, 0) + late).astype(jnp.bfloat16)
+    on_down = (wide(partial, 7) + wide(sunk, 0) + late).astype(jnp.bfloat16)
     on_up, on_down = lax.optimization_barrier((on_up, on_down))
-    first = with_own(with_own(block(0, 0), sunk[1]), lax.ppermute(on_up, "y", up))
-    second = with_own(with_own(block(1, 0), risen[1]), lax.ppermute(on_down, "y", down))
-    return first, second
+    kept = wide(partial, 4) + wide(sunk, 1) + wide(lax.ppermute(on_up, "y", up), 0)
+    other = wide(partial, 5) + wide(risen, 1) + wide(lax.ppermute(on_down, "y", down), 0)
+    return kept, other
 
 
 def nothing(value):
     return jnp.minimum(jnp.abs(value.astype(jnp.float32)), 0.0)
-
-
-def over_z(totals, late):
-    first, second = totals
-    low = lax.axis_index("z_hi") == 0
-    sent = (jnp.where(low, second, first) + late).astype(jnp.bfloat16)
-    return jnp.where(low, first, second) + from_partner(sent, "z_hi").astype(jnp.float32)
 
 
 def partial_over_chip(lefts, rights):
@@ -111,8 +113,9 @@
 
 
 def summed_over_dp(partial, late_y, late_z):
-    blocks = partial.reshape(lax.axis_size(BLOCKS), -1, partial.shape[1])
-    return over_z(over_y(blocks, late_y), late_z)
+    kept, other = over_y(partial, late_y)
+    sent = (other + late_z).astype(jnp.bfloat16)
+    return kept + from_partner(sent, "z_hi").astype(jnp.float32)
 
 
 def shards(
@@ -122,7 +125,7 @@
     local_tokens, width_local = tokens.shape
     loss_scale = (local_tokens * dp_count) ** (-0.5)
     column = lax.axis_index(TENSOR)
-    core = lax.axis_index("core")
+    orders = [leaving_order(D, flip) for flip in (0, 1)]
     gain_local = lax.dynamic_slice_in_dim(norm_gain, column * width_local, width_local)
     labels = jnp.arange(EXAMPLES, dtype=jnp.int32)
     onehot = (segment_ids[:, None] == labels[None, :]).astype(jnp.float32)
@@ -141,10 +144,10 @@
         partial_value = jnp.dot(hidden, weight_out, preferred_element_type=jnp.float32)
         mixed = over_tensor(feature_blocks(partial_value.astype(jnp.bfloat16)))
         rights_out += [hidden, from_partner(hidden, "core")]
-        lefts_in += for_both_cores(normed, core)
+        lefts_in += for_both_cores(normed, orders)
         out_grad = (embedded + mixed - target) * loss_scale
         grad = gathered_features(out_grad.astype(jnp.bfloat16))
-        lefts_out += for_both_cores(grad, core)
+        lefts_out += for_both_cores(grad, orders)
         if last:
             partial_out = partial_over_chip(lefts_out, rights_out)
             slope = slope + nothing(partial_out[0, 0])
@@ -186,7 +189,7 @@
     partial_in = partial_over_chip(lefts_in, rights_in)
     there = nothing(partial_in[0, 0])
     summed_out = summed_over_dp(partial_out, there, there)
-    summed_in = summed_over_dp(partial_in, there, nothing(summed_out[0, 0]))
+    summed_in = summed_over_dp(partial_in, 0.0, nothing(summed_out[0, 0]))
     summed_out = summed_out.T
     dp_rows = moment_in.shape[0]
     offset = lax.axis_index(DP) * dp_rows

time: 219 us -> 216 us (0.986); the launches traced: 218 us -> 213 us
  blocking collectives: 68 us -> 42.8 us
  waiting for transfers between devices: 47.5 us -> 64 us
  starting transfers between devices: 47.5 us -> 55.3 us
  other arithmetic: 18.6 us -> 12.3 us
  matrix products: 24.6 us -> 28.4 us
  local copies, waits for them, and re-layouts: 8.79 us -> 6.58 us
    all_to_all x5 -> x3, blocking collectives: 68 us -> 42.8 us  [to_peers(): return lax.all_to_all(blocks, axis, 0, 0, tiled=True)]
    all_to_all x2 -> x4, starting transfers between devices: 11 us -> 22.1 us  [to_peers(): return lax.all_to_all(blocks, axis, 0, 0, tiled=True)]
    all_to_all x2 -> x4, waiting for transfers between devices: 11.3 us -> 21.2 us  [to_peers(): return lax.all_to_all(blocks, axis, 0, 0, tiled=True)]
    ppermute x4, waiting for transfers between devices: 13.6 us -> 21.1 us  [the longest x2 18 us: over_y(): sunk = lax.ppermute(partial[2 * few:4 * few], 'y', down)]
    dot_general x0 -> x8, matrix products: none -> 6.88 us  [for_both_cores(): jnp.dot(array, order, preferred_element_type=jnp.float32)]
    another operation x4 -> x0, other arithmetic: 3.36 us -> none  [the longest x2 1.68 us: over_y(): risen = lax.ppermute(jnp.stack([block(0, 2), block(1, 1)]), 'y', up)]
    ppermute x11, waiting for transfers between devices: 19.8 us -> 16.5 us  [from_partner(): return lax.ppermute(array, axis, [(0, 1), (1, 0)])]
    ppermute x2, starting transfers between devices: 4.85 us -> 2.25 us  [over_y(): lax.ppermute(on_down, 'y', down)]
  transfers between devices with their start and end apart: 23 -> 25, of which waited for: 9 -> 12; matrix products, arithmetic and copies ran while one was open for 10% -> 11% of each run, Pallas kernels for 0% -> 0%
where the time goes in v6:
time: 216 us; the launch traced here: 213 us
  waiting for transfers between devices  64 us (30%)
  starting transfers between devices  55.3 us (26%)
  blocking collectives  42.8 us (20%)
  matrix products  28.4 us (13%)
  other arithmetic  12.3 us (6%)
  local copies, waits for them, and re-layouts  6.58 us (3%)
  between operations  3.16 us (1%)
    all_to_all x3, blocking collectives, to_peers(): return lax.all_to_all(blocks, axis, 0, 0, tiled=True)  42.8 us
    all_to_all x4, starting transfers between devices, to_peers(): return lax.all_to_all(blocks, axis, 0, 0, tiled=True)  22.1 us
    all_to_all x4, waiting for transfers between devices, to_peers(): return lax.all_to_all(blocks, axis, 0, 0, tiled=True)  21.2 us
    ppermute x2, waiting for transfers between devices, over_y(): sunk = lax.ppermute(partial[2 * few:4 * few], 'y', down)  18 us
    ppermute x11, waiting for transfers between devices, from_partner(): return lax.ppermute(array, axis, [(0, 1), (1, 0)])  16.5 us
    ppermute x11, starting transfers between devices, from_partner(): return lax.ppermute(array, axis, [(0, 1), (1, 0)])  12.4 us
    ppermute x2, starting transfers between devices, over_y(): sunk = lax.ppermute(partial[2 * few:4 * few], 'y', down)  11.4 us
    dot_general x2, matrix products, shards(): preact = jnp.dot(normed, weight_in, preferred_element_type=jnp.float32)  8.56 us
  transfers between devices with their start and end apart: 25, of which 12 were waited for; matrix products, arithmetic and copies ran while one was open for 11% of the time, Pallas kernels for 0%

profile of v6, /device:TPU:33, one launch (start us, length us, event | category | flops | bytes accessed | tf_op | source)
XLA Modules:
  0.0 212.6 jit_solution(3964151637376105839)
XLA Ops:
  0.6 0.8 fusion.79
  1.5 15.8 %all_to_all.35 = bf16[16,128,64]{1,2,0:T(8,128)(2,1)S(1)} all-to-all(bf16[16,128,64]{1,2,0:T(8,128)(2,1)S(1)} %broadcast_in_dim.100), channel_id=1, replica_groups=mesh['z_hi'=2,'y'=4,'core'=2,'x'=4,'z_lo'=4] {'x','z_lo'}, dimensions={0} | all-to-all | bytes 524288 | tf_op jit(solution)/shard_map/all_to_all | solution.py:22
  17.6 3.8 %fusion.36 = (f32[128,2048]{1,0:T(8,128)S(1)}, bf16[128,2048]{1,0:T(8,128)(2,1)S(1)}) fusion(bf16[1024,2048]{1,0:T(8,128)(2,1)} %param.14, bf16[128,1024]{1,0:T(8,128)(2,1)S(1)} %copy.26, f32[1024]{0:T(1024)} %param.13, f32[128]{0:T(128)S(1)} %add_rsqrt_fusion.1), kind=kOutput, calls=%fused_computation.48 | convolution fusion | flops 542375936 | bytes 6033920 | tf_op jit(solution)/shard_map/dot_general | solution.py:142
  21.4 0.7 convolution_convert_fusion.3
  22.4 13.7 %all_to_all.36 = bf16[16,128,64]{1,2,0:T(8,128)(2,1)S(1)} all-to-all(bf16[16,128,64]{1,2,0:T(8,128)(2,1)S(1)} %bitcast.63), channel_id=1, replica_groups=mesh['z_hi'=2,'y'=4,'core'=2,'x'=4,'z_lo'=4] {'x','z_lo'}, dimensions={0} | all-to-all | bytes 524288 | tf_op jit(solution)/shard_map/all_to_all | solution.py:22
  36.3 13.3 %all_to_all.37 = bf16[16,128,64]{1,2,0:T(8,128)(2,1)S(1)} all-to-all(bf16[16,128,64]{1,2,0:T(8,128)(2,1)S(1)} %broadcast_in_dim.117), channel_id=1, replica_groups=mesh['z_hi'=2,'y'=4,'core'=2,'x'=4,'z_lo'=4] {'x','z_lo'}, dimensions={0} | all-to-all | bytes 524288 | tf_op jit(solution)/shard_map/all_to_all | solution.py:22
  49.5 3.7 %fusion = bf16[128,2048]{1,0:T(8,128)(2,1)S(1)} fusion(f32[128,2048]{1,0:T(8,128)S(1)} %get-tuple-element.14, bf16[128,1024]{0,1:T(8,128)(2,1)S(1)} %bitcast.55, bf16[2048,1024]{1,0:T(8,128)(2,1)} %param.15), kind=kOutput, calls=%fused_computation.4 | convolution fusion | flops 537395200 | bytes 6029312 | tf_op jit(solution)/shard_map/dot_general | solution.py:155
  53.3 1.6 fusion.109
  55.1 0.7 pad_maximum_fusion
  55.8 5.6 %all-to-all-start.3 = ((bf16[16,128,66]{1,2,0:T(8,128)(2,1)}), bf16[16,128,66]{1,2,0:T(8,128)(2,1)S(1)}, u32[]{:S(2)}, u32[]{:S(2)}) async-start(bf16[16,128,66]{1,2,0:T(8,128)(2,1)} %pad_maximum_fusion), calls=%async_computation.3 | async-start | bytes 589824 | tf_op jit(solution)/shard_map/all_to_all | solution.py:22
  61.5 8.0 %all-to-all-done.3 = bf16[16,128,66]{1,2,0:T(8,128)(2,1)S(1)} async-done(((bf16[16,128,66]{1,2,0:T(8,128)(2,1)}), bf16[16,128,66]{1,2,0:T(8,128)(2,1)S(1)}, u32[]{:S(2)}, u32[]{:S(2)}) %all-to-all-start.3) | async-done | bytes 270368 | tf_op jit(solution)/shard_map/all_to_all | solution.py:22
  69.6 0.8 broadcast_in_dim.119
  70.4 6.1 %all-to-all-start.4 = ((bf16[16,128,64]{1,2,0:T(8,128)(2,1)}), bf16[16,128,64]{1,2,0:T(8,128)(2,1)S(1)}, u32[]{:S(2)}, u32[]{:S(2)}) async-start(bf16[16,128,64]{1,2,0:T(8,128)(2,1)} %broadcast_in_dim.119), calls=%async_computation.4 | async-start | bytes 524288 | tf_op jit(solution)/shard_map/all_to_all | solution.py:22
  76.5 7.7 %all-to-all-done.4 = bf16[16,128,64]{1,2,0:T(8,128)(2,1)S(1)} async-done(((bf16[16,128,64]{1,2,0:T(8,128)(2,1)}), bf16[16,128,64]{1,2,0:T(8,128)(2,1)S(1)}, u32[]{:S(2)}, u32[]{:S(2)}) %all-to-all-start.4) | async-done | bytes 262176 | tf_op jit(solution)/shard_map/all_to_all | solution.py:22
  84.5 2.9 %collective-permute-start.1 = (f32[2,32]{1,0:T(2,128)S(1)}, f32[2,32]{1,0:T(2,128)S(1)}, u32[]{:S(2)}, u32[]{:S(2)}) collective-permute-start(f32[2,32]{1,0:T(2,128)S(1)} %pad_maximum_fusion.1), channel_id=1, source_target_pairs={{0,16},{16,0},{1,17},{17,1},{2,18},{18,2},{3,19},{19,3},{4,20},{20... | collective-permute-start | bytes 776 | tf_op jit(solution)/shard_map/ppermute | solution.py:40
  87.4 0.8 collective-permute-done.1
  88.2 3.2 %collective-permute-start.2 = (f32[2,32]{1,0:T(2,128)S(1)}, f32[2,32]{1,0:T(2,128)S(1)}, u32[]{:S(2)}, u32[]{:S(2)}) collective-permute-start(f32[2,32]{1,0:T(2,128)S(1)} %fusion.97), channel_id=1, source_target_pairs={{0,32},{32,64},{64,96},{96,128},{128,160},{160,192},{192,224},{1,3... | collective-permute-start | bytes 776 | tf_op jit(solution)/shard_map/ppermute | solution.py:55
  91.4 1.3 collective-permute-start.3
  93.0 2.7 %collective-permute-done.3 = f32[2,32]{1,0:T(2,128)S(1)} collective-permute-done((f32[2,32]{1,0:T(2,128)S(1)}, f32[2,32]{1,0:T(2,128)S(1)}, u32[]{:S(2)}, u32[]{:S(2)}) %collective-permute-start.3) | collective-permute-done | bytes 288 | tf_op jit(solution)/shard_map/ppermute | solution.py:56
  96.1 4.8 %fusion.41 = (f32[128,2048]{1,0:T(8,128)}, bf16[128,2048]{1,0:T(8,128)(2,1)S(1)}) fusion(bf16[1024,2048]{1,0:T(8,128)(2,1)} %param.14, bf16[128,1024]{1,0:T(8,128)(2,1)S(1)} %fusion.57, f32[128]{0:T(128)S(1)} %add_rsqrt_fusion, f32[1024]{0:T(1024)S(1)} %copy-done.13), kind=kOutput, calls=%fused_computation.53 | convolution fusion | flops 542375936 | bytes 6033920 | tf_op jit(solution)/shard_map/dot_general | solution.py:142
  100.9 0.7 convolution_convert_fusion.2
  101.7 0.8 copy.30
  102.5 4.7 %all-to-all-start.5 = ((bf16[16,128,64]{1,2,0:T(8,128)(2,1)}), bf16[16,128,64]{1,2,0:T(8,128)(2,1)S(1)}, u32[]{:S(2)}, u32[]{:S(2)}) async-start(bf16[16,128,64]{1,2,0:T(8,128)(2,1)} %bitcast.15), calls=%async_computation.5 | async-start | bytes 524288 | tf_op jit(solution)/shard_map/all_to_all | solution.py:22
  107.3 2.1 %collective-permute-start.8 = (bf16[128,2048]{1,0:T(8,128)(2,1)S(1)}, bf16[128,2048]{1,0:T(8,128)(2,1)}, u32[]{:S(2)}, u32[]{:S(2)}) collective-permute-start(bf16[128,2048]{1,0:T(8,128)(2,1)S(1)} %get-tuple-element.13), channel_id=1, source_target_pairs={{0,16},{16,0},{1,17},{17,1},{2,18},{18,2},{3,19},{19,3},{4,20},{20... | collective-permute-start | bytes 1572872 | tf_op jit(solution)/shard_map/ppermute | solution.py:40
  109.4 1.2 fusion.28
  110.6 1.2 fusion.24
  111.8 3.3 %all-to-all-done.5 = bf16[16,128,64]{1,2,0:T(8,128)(2,1)S(1)} async-done(((bf16[16,128,64]{1,2,0:T(8,128)(2,1)}), bf16[16,128,64]{1,2,0:T(8,128)(2,1)S(1)}, u32[]{:S(2)}, u32[]{:S(2)}) %all-to-all-start.5) | async-done | bytes 262176 | tf_op jit(solution)/shard_map/all_to_all | solution.py:22
  115.1 0.7 fusion.75
  115.8 0.8 broadcast_in_dim.120
  116.5 5.6 %all-to-all-start.6 = ((bf16[16,128,64]{1,2,0:T(8,128)(2,1)}), bf16[16,128,64]{1,2,0:T(8,128)(2,1)S(1)}, u32[]{:S(2)}, u32[]{:S(2)}) async-start(bf16[16,128,64]{1,2,0:T(8,128)(2,1)} %broadcast_in_dim.120), calls=%async_computation.6 | async-start | bytes 524288 | tf_op jit(solution)/shard_map/all_to_all | solution.py:22
  122.2 0.5 fusion.30
  122.7 2.3 %collective-permute-start.6 = (bf16[128,512]{1,0:T(8,128)(2,1)S(1)}, bf16[128,512]{1,0:T(8,128)(2,1)S(1)}, u32[]{:S(2)}, u32[]{:S(2)}) collective-permute-start(bf16[128,512]{1,0:T(8,128)(2,1)S(1)} %fusion.30), channel_id=1, source_target_pairs={{0,16},{16,0},{1,17},{17,1},{2,18},{18,2},{3,19},{19,3},{4,20},{20... | collective-permute-start | bytes 393224 | tf_op jit(solution)/shard_map/ppermute | solution.py:40
  125.0 1.2 fusion.26
  126.2 1.2 fusion.29
  127.4 2.3 %all-to-all-done.6 = bf16[16,128,64]{1,2,0:T(8,128)(2,1)S(1)} async-done(((bf16[16,128,64]{1,2,0:T(8,128)(2,1)}), bf16[16,128,64]{1,2,0:T(8,128)(2,1)S(1)}, u32[]{:S(2)}, u32[]{:S(2)}) %all-to-all-start.6) | async-done | bytes 262176 | tf_op jit(solution)/shard_map/all_to_all | solution.py:22
  129.6 0.5 fusion.31
  130.2 3.2 %collective-permute-start.7 = (bf16[128,512]{1,0:T(8,128)(2,1)S(1)}, bf16[128,512]{1,0:T(8,128)(2,1)S(1)}, u32[]{:S(2)}, u32[]{:S(2)}) collective-permute-start(bf16[128,512]{1,0:T(8,128)(2,1)S(1)} %fusion.31), channel_id=1, source_target_pairs={{0,16},{16,0},{1,17},{17,1},{2,18},{18,2},{3,19},{19,3},{4,20},{20... | collective-permute-start | bytes 393224 | tf_op jit(solution)/shard_map/ppermute | solution.py:40
  133.4 0.5 fusion.27
  134.1 0.5 collective-permute-start.4
  134.7 3.4 %convolution_convert_fusion.1 = bf16[512,2048]{1,0:T(8,128)(2,1)S(1)} fusion(bf16[128,2048]{1,0:T(8,128)(2,1)} %collective-permute-done.9, bf16[128,2048]{1,0:T(8,128)(2,1)} %copy-done.7, bf16[128,2048]{1,0:T(8,128)(2,1)} %collective-permute-done.8, bf16[128,2048]{1,0:T(8,128)(2,1)} %copy-done.6, bf16[128,512]{1,0:T(8,128)(2,1)S(1)} %collective-permute-done.7, ...), kind=kOutput, calls=%fused_computation.1 | convolution fusion | flops 1085276160 | bytes 4718592 | tf_op jit(solution)/shard_map/dot_general | solution.py:110
  138.1 0.5 slice.102
  139.3 1.5 fusion.1
  141.4 11.4 %collective-permute-start.15 = (bf16[128,2048]{1,0:T(8,128)(2,1)S(1)}, bf16[128,2048]{1,0:T(8,128)(2,1)S(1)}, u32[]{:S(2)}, u32[]{:S(2)}) collective-permute-start(bf16[128,2048]{1,0:T(8,128)(2,1)S(1)} %get-tuple-element.34), channel_id=1, source_target_pairs={{0,96},{32,0},{64,32},{96,64},{1,97},{33,1},{65,33},{97,65},{2,98}... | collective-permute-start | bytes 1572872 | tf_op jit(solution)/shard_map/ppermute | solution.py:95
  152.8 0.5 fusion.25
  153.4 1.3 convolution_convert_fusion
  154.7 0.6 slice.119
  155.9 8.1 %collective-permute-done.15 = bf16[128,2048]{1,0:T(8,128)(2,1)S(1)} collective-permute-done((bf16[128,2048]{1,0:T(8,128)(2,1)S(1)}, bf16[128,2048]{1,0:T(8,128)(2,1)S(1)}, u32[]{:S(2)}, u32[]{:S(2)}) %collective-permute-start.15) | collective-permute-done | bytes 524320 | tf_op jit(solution)/shard_map/ppermute | solution.py:95
  164.0 3.1 %collective-permute-done.16 = bf16[128,2048]{1,0:T(8,128)(2,1)S(1)} collective-permute-done((bf16[128,2048]{1,0:T(8,128)(2,1)S(1)}, bf16[128,2048]{1,0:T(8,128)(2,1)S(1)}, u32[]{:S(2)}, u32[]{:S(2)}) %collective-permute-start.16) | collective-permute-done | bytes 524320 | tf_op jit(solution)/shard_map/ppermute | solution.py:94
  167.1 1.0 add_convert_fusion.2
  168.4 1.1 fusion.108
  169.4 1.5 collective-permute-start.12
  171.4 1.2 collective-permute-start.17
  172.6 2.3 %collective-permute-done.18 = bf16[64,2048]{1,0:T(8,128)(2,1)} collective-permute-done((bf16[64,2048]{1,0:T(8,128)(2,1)}, bf16[64,2048]{1,0:T(8,128)(2,1)}, u32[]{:S(2)}, u32[]{:S(2)}) %collective-permute-start.18) | collective-permute-done | bytes 262176 | tf_op jit(solution)/shard_map/ppermute | solution.py:100
  174.9 1.1 add_convert_fusion.1
  176.1 10.0 %collective-permute-done.11 = bf16[128,2048]{1,0:T(8,128)(2,1)} collective-permute-done((bf16[128,2048]{1,0:T(8,128)(2,1)}, bf16[128,2048]{1,0:T(8,128)(2,1)}, u32[]{:S(2)}, u32[]{:S(2)}) %collective-permute-start.11) | collective-permute-done | bytes 524320 | tf_op jit(solution)/shard_map/ppermute | solution.py:95
  186.1 1.3 add_convert_fusion.4
  187.5 1.9 collective-permute-start.14
  189.4 2.5 %collective-permute-done.19 = bf16[64,2048]{1,0:T(8,128)(2,1)S(1)} collective-permute-done((bf16[64,2048]{1,0:T(8,128)(2,1)S(1)}, bf16[64,2048]{1,0:T(8,128)(2,1)S(1)}, u32[]{:S(2)}, u32[]{:S(2)}) %collective-permute-start.19) | collective-permute-done | bytes 262176 | tf_op jit(solution)/shard_map/ppermute | solution.py:40
  191.9 2.2 %subtract_convert_fusion = (bf16[2048,64]{0,1:T(8,128)(2,1)}, f32[2048,64]{0,1:T(8,128)}, f32[64,2048]{1,0:T(8,128)S(1)}) fusion(bf16[2048,64]{0,1:T(8,128)(2,1)S(1)} %copy.32, f32[2048,64]{0,1:T(8,128)} %param.17, bf16[64,2048]{1,0:T(8,128)(2,1)S(1)} %collective-permute-done.19, bf16[64,2048]{1,0:T(8,128)(2,1)S(1)} %collective-permute-done.17, ...), kind=kLoop, calls=%fused_computation.94 | loop fusion | flops 1835008 | bytes 3145728 | tf_op jit(solution)/shard_map/convert_element_type | solution.py:201
  194.0 0.5 slice.124
  195.2 1.1 add_convert_fusion
  196.3 0.8 collective-permute-start.20
  197.1 13.2 %collective-permute-done.20 = bf16[64,2048]{1,0:T(8,128)(2,1)S(1)} collective-permute-done((bf16[64,2048]{1,0:T(8,128)(2,1)S(1)}, bf16[64,2048]{1,0:T(8,128)(2,1)S(1)}, u32[]{:S(2)}, u32[]{:S(2)}) %collective-permute-start.20) | collective-permute-done | bytes 262176 | tf_op jit(solution)/shard_map/ppermute | solution.py:40
  210.4 2.2 %subtract_convert_fusion.1 = (bf16[64,2048]{1,0:T(8,128)(2,1)}, f32[64,2048]{1,0:T(8,128)}) fusion(bf16[1024,2048]{1,0:T(8,128)(2,1)} %param.14, s32[]{:T(128)S(6)} %select_n.195, bf16[64,2048]{1,0:T(8,128)(2,1)S(1)} %collective-permute-done.20, bf16[64,2048]{1,0:T(8,128)(2,1)S(1)} %collective-permute-done.13, bf16[128,2048]{1,0:T(8,128)(2,1)} %collective-permute-done.11, ...), kind=kLoop, calls=%fused_computation.95 | loop fusion | flops 1835008 | bytes 2621444 | tf_op jit(solution)/shard_map/convert_element_type | solution.py:200
  (91 shorter events, 3.8 us)
Async XLA Ops:
  17.6 3.8 %copy-start = (bf16[2048,1024]{1,0:T(8,128)(2,1)S(1)}, bf16[2048,1024]{1,0:T(8,128)(2,1)}, u32[]{:S(2)}) copy-start(bf16[2048,1024]{1,0:T(8,128)(2,1)} %param.15) | copy-start | bytes 12582916
  21.4 85.9 %copy-start.6 = (bf16[128,2048]{1,0:T(8,128)(2,1)}, bf16[128,2048]{1,0:T(8,128)(2,1)S(1)}, u32[]{:S(2)}) copy-start(bf16[128,2048]{1,0:T(8,128)(2,1)S(1)} %get-tuple-element.13) | copy-start | bytes 1572868
  21.4 14.8 %copy-start.10 = (f32[128,64]{0,1:T(8,128)S(1)}, f32[128,64]{0,1:T(8,128)}, u32[]{:S(2)}) copy-start(f32[128,64]{0,1:T(8,128)} %param.10) | copy-start | bytes 98308
  21.4 14.8 %copy-start.11 = (bf16[128,64]{0,1:T(8,128)(2,1)S(1)}, bf16[128,64]{0,1:T(8,128)(2,1)}, u32[]{:S(2)}) copy-start(bf16[128,64]{0,1:T(8,128)(2,1)} %param.9) | copy-start | bytes 49156
  21.4 14.8 %copy-start.12 = (f32[128,64]{0,1:T(8,128)S(1)}, f32[128,64]{0,1:T(8,128)}, u32[]{:S(2)}) copy-start(f32[128,64]{0,1:T(8,128)} %param.12) | copy-start | bytes 98308
  22.2 31.1 %copy-start.13 = (f32[1024]{0:T(1024)S(1)}, f32[1024]{0:T(1024)}, u32[]{:S(2)}) copy-start(f32[1024]{0:T(1024)} %param.13) | copy-start | bytes 12292
  22.4 30.9 %copy-start.3 = (bf16[1024,2048]{1,0:T(8,128)(2,1)S(1)}, bf16[1024,2048]{1,0:T(8,128)(2,1)}, u32[]{:S(2)}) copy-start(bf16[1024,2048]{1,0:T(8,128)(2,1)} %param.14) | copy-start | bytes 12582916
  53.3 31.1 %copy-start.14 = (s32[128]{0:T(128)S(1)}, s32[128]{0:T(128)}, u32[]{:S(2)}) copy-start(s32[128]{0:T(128)} %param.11) | copy-start | bytes 1540
  55.8 13.6 %all-to-all-start.3 = ((bf16[16,128,66]{1,2,0:T(8,128)(2,1)}), bf16[16,128,66]{1,2,0:T(8,128)(2,1)S(1)}, u32[]{:S(2)}, u32[]{:S(2)}) async-start(bf16[16,128,66]{1,2,0:T(8,128)(2,1)} %pad_maximum_fusion), calls=%async_computation.3 | async-start | bytes 589824 | tf_op jit(solution)/shard_map/all_to_all | solution.py:22
  70.4 13.9 %all-to-all-start.4 = ((bf16[16,128,64]{1,2,0:T(8,128)(2,1)}), bf16[16,128,64]{1,2,0:T(8,128)(2,1)S(1)}, u32[]{:S(2)}, u32[]{:S(2)}) async-start(bf16[16,128,64]{1,2,0:T(8,128)(2,1)} %broadcast_in_dim.119), calls=%async_computation.4 | async-start | bytes 524288 | tf_op jit(solution)/shard_map/all_to_all | solution.py:22
  84.5 3.7 %collective-permute-start.1 = (f32[2,32]{1,0:T(2,128)S(1)}, f32[2,32]{1,0:T(2,128)S(1)}, u32[]{:S(2)}, u32[]{:S(2)}) collective-permute-start(f32[2,32]{1,0:T(2,128)S(1)} %pad_maximum_fusion.1), channel_id=1, source_target_pairs={{0,16},{16,0},{1,17},{17,1},{2,18},{18,2},{3,19},{19,3},{4,20},{20... | collective-permute-start | bytes 776 | tf_op jit(solution)/shard_map/ppermute | solution.py:40
  88.2 4.7 %collective-permute-start.2 = (f32[2,32]{1,0:T(2,128)S(1)}, f32[2,32]{1,0:T(2,128)S(1)}, u32[]{:S(2)}, u32[]{:S(2)}) collective-permute-start(f32[2,32]{1,0:T(2,128)S(1)} %fusion.97), channel_id=1, source_target_pairs={{0,32},{32,64},{64,96},{96,128},{128,160},{160,192},{192,224},{1,3... | collective-permute-start | bytes 776 | tf_op jit(solution)/shard_map/ppermute | solution.py:55
  91.4 4.3 %collective-permute-start.3 = (f32[2,32]{1,0:T(2,128)S(1)}, f32[2,32]{1,0:T(2,128)S(1)}, u32[]{:S(2)}, u32[]{:S(2)}) collective-permute-start(f32[2,32]{1,0:T(2,128)S(1)} %fusion.97), channel_id=1, source_target_pairs={{32,0},{64,32},{96,64},{128,96},{160,128},{192,160},{224,192},{33,... | collective-permute-start | bytes 776 | tf_op jit(solution)/shard_map/ppermute | solution.py:56
  96.1 4.8 %copy-start.1 = (bf16[2048,1024]{1,0:T(8,128)(2,1)S(1)}, bf16[2048,1024]{1,0:T(8,128)(2,1)}, u32[]{:S(2)}) copy-start(bf16[2048,1024]{1,0:T(8,128)(2,1)} %param.15) | copy-start | bytes 12582916
  100.9 25.3 %copy-start.7 = (bf16[128,2048]{1,0:T(8,128)(2,1)}, bf16[128,2048]{1,0:T(8,128)(2,1)S(1)}, u32[]{:S(2)}) copy-start(bf16[128,2048]{1,0:T(8,128)(2,1)S(1)} %get-tuple-element.15) | copy-start | bytes 1572868
  102.5 12.5 %all-to-all-start.5 = ((bf16[16,128,64]{1,2,0:T(8,128)(2,1)}), bf16[16,128,64]{1,2,0:T(8,128)(2,1)S(1)}, u32[]{:S(2)}, u32[]{:S(2)}) async-start(bf16[16,128,64]{1,2,0:T(8,128)(2,1)} %bitcast.15), calls=%async_computation.5 | async-start | bytes 524288 | tf_op jit(solution)/shard_map/all_to_all | solution.py:22
  107.3 26.7 %collective-permute-start.8 = (bf16[128,2048]{1,0:T(8,128)(2,1)S(1)}, bf16[128,2048]{1,0:T(8,128)(2,1)}, u32[]{:S(2)}, u32[]{:S(2)}) collective-permute-start(bf16[128,2048]{1,0:T(8,128)(2,1)S(1)} %get-tuple-element.13), channel_id=1, source_target_pairs={{0,16},{16,0},{1,17},{17,1},{2,18},{18,2},{3,19},{19,3},{4,20},{20... | collective-permute-start | bytes 1572872 | tf_op jit(solution)/shard_map/ppermute | solution.py:40
  110.6 42.2 %collective-permute-start = (bf16[128,512]{1,0:T(8,128)(2,1)}, bf16[128,512]{1,0:T(8,128)(2,1)S(1)}, u32[]{:S(2)}, u32[]{:S(2)}) collective-permute-start(bf16[128,512]{1,0:T(8,128)(2,1)} %fusion.28), channel_id=1, source_target_pairs={{0,16},{16,0},{1,17},{17,1},{2,18},{18,2},{3,19},{19,3},{4,20},{20... | collective-permute-start | bytes 393224 | tf_op jit(solution)/shard_map/ppermute | solution.py:40
  116.5 13.1 %all-to-all-start.6 = ((bf16[16,128,64]{1,2,0:T(8,128)(2,1)}), bf16[16,128,64]{1,2,0:T(8,128)(2,1)S(1)}, u32[]{:S(2)}, u32[]{:S(2)}) async-start(bf16[16,128,64]{1,2,0:T(8,128)(2,1)} %broadcast_in_dim.120), calls=%async_computation.6 | async-start | bytes 524288 | tf_op jit(solution)/shard_map/all_to_all | solution.py:22
  122.7 11.4 %collective-permute-start.6 = (bf16[128,512]{1,0:T(8,128)(2,1)S(1)}, bf16[128,512]{1,0:T(8,128)(2,1)S(1)}, u32[]{:S(2)}, u32[]{:S(2)}) collective-permute-start(bf16[128,512]{1,0:T(8,128)(2,1)S(1)} %fusion.30), channel_id=1, source_target_pairs={{0,16},{16,0},{1,17},{17,1},{2,18},{18,2},{3,19},{19,3},{4,20},{20... | collective-permute-start | bytes 393224 | tf_op jit(solution)/shard_map/ppermute | solution.py:40
  126.2 8.4 %collective-permute-start.9 = (bf16[128,2048]{1,0:T(8,128)(2,1)S(1)}, bf16[128,2048]{1,0:T(8,128)(2,1)}, u32[]{:S(2)}, u32[]{:S(2)}) collective-permute-start(bf16[128,2048]{1,0:T(8,128)(2,1)S(1)} %get-tuple-element.15), channel_id=1, source_target_pairs={{0,16},{16,0},{1,17},{17,1},{2,18},{18,2},{3,19},{19,3},{4,20},{20... | collective-permute-start | bytes 1572872 | tf_op jit(solution)/shard_map/ppermute | solution.py:40
  130.2 4.6 %collective-permute-start.7 = (bf16[128,512]{1,0:T(8,128)(2,1)S(1)}, bf16[128,512]{1,0:T(8,128)(2,1)S(1)}, u32[]{:S(2)}, u32[]{:S(2)}) collective-permute-start(bf16[128,512]{1,0:T(8,128)(2,1)S(1)} %fusion.31), channel_id=1, source_target_pairs={{0,16},{16,0},{1,17},{17,1},{2,18},{18,2},{3,19},{19,3},{4,20},{20... | collective-permute-start | bytes 393224 | tf_op jit(solution)/shard_map/ppermute | solution.py:40
  133.9 5.3 %copy-start.2 = (bf16[2048,1024]{1,0:T(8,128)(2,1)S(1)}, bf16[2048,1024]{1,0:T(8,128)(2,1)}, u32[]{:S(2)}) copy-start(bf16[2048,1024]{1,0:T(8,128)(2,1)} %param.15) | copy-start | bytes 12582916
  134.0 5.3 %copy-start.5 = (f32[128,2048]{1,0:T(8,128)S(1)}, f32[128,2048]{1,0:T(8,128)}, u32[]{:S(2)}) copy-start(f32[128,2048]{1,0:T(8,128)} %get-tuple-element.16) | copy-start | bytes 3145732
  134.0 19.4 %collective-permute-start.5 = (bf16[128,2048]{1,0:T(8,128)(2,1)S(1)}, bf16[128,2048]{1,0:T(8,128)(2,1)S(1)}, u32[]{:S(2)}, u32[]{:S(2)}) collective-permute-start(bf16[128,2048]{1,0:T(8,128)(2,1)S(1)} %fusion), channel_id=1, source_target_pairs={{0,16},{16,0},{1,17},{17,1},{2,18},{18,2},{3,19},{19,3},{4,20},{20... | collective-permute-start | bytes 1572872 | tf_op jit(solution)/shard_map/ppermute | solution.py:40
  134.1 0.7 copy-start.15
  134.1 19.3 %collective-permute-start.4 = (bf16[128,512]{1,0:T(8,128)(2,1)}, bf16[128,512]{1,0:T(8,128)(2,1)S(1)}, u32[]{:S(2)}, u32[]{:S(2)}) collective-permute-start(bf16[128,512]{1,0:T(8,128)(2,1)} %fusion.29), channel_id=1, source_target_pairs={{0,16},{16,0},{1,17},{17,1},{2,18},{18,2},{3,19},{19,3},{4,20},{20... | collective-permute-start | bytes 393224 | tf_op jit(solution)/shard_map/ppermute | solution.py:40
  139.3 14.1 %copy-start.16 = (bf16[128,512]{1,0:T(8,128)(2,1)S(1)}, bf16[128,512]{1,0:T(8,128)(2,1)}, u32[]{:S(2)}) copy-start(bf16[128,512]{1,0:T(8,128)(2,1)} %fusion.24) | copy-start | bytes 393220
  140.9 12.5 %collective-permute-start.10 = (bf16[128,2048]{1,0:T(8,128)(2,1)S(1)}, bf16[128,2048]{1,0:T(8,128)(2,1)S(1)}, u32[]{:S(2)}, u32[]{:S(2)}) collective-permute-start(bf16[128,2048]{1,0:T(8,128)(2,1)S(1)} %fusion.1), channel_id=1, source_target_pairs={{0,16},{16,0},{1,17},{17,1},{2,18},{18,2},{3,19},{19,3},{4,20},{20... | collective-permute-start | bytes 1572872 | tf_op jit(solution)/shard_map/ppermute | solution.py:40
  141.4 22.6 %collective-permute-start.15 = (bf16[128,2048]{1,0:T(8,128)(2,1)S(1)}, bf16[128,2048]{1,0:T(8,128)(2,1)S(1)}, u32[]{:S(2)}, u32[]{:S(2)}) collective-permute-start(bf16[128,2048]{1,0:T(8,128)(2,1)S(1)} %get-tuple-element.34), channel_id=1, source_target_pairs={{0,96},{32,0},{64,32},{96,64},{1,97},{33,1},{65,33},{97,65},{2,98}... | collective-permute-start | bytes 1572872 | tf_op jit(solution)/shard_map/ppermute | solution.py:95
  152.8 14.3 %collective-permute-start.16 = (bf16[128,2048]{1,0:T(8,128)(2,1)S(1)}, bf16[128,2048]{1,0:T(8,128)(2,1)S(1)}, u32[]{:S(2)}, u32[]{:S(2)}) collective-permute-start(bf16[128,2048]{1,0:T(8,128)(2,1)S(1)} %get-tuple-element.35), channel_id=1, source_target_pairs={{0,32},{32,64},{64,96},{96,0},{1,33},{33,65},{65,97},{97,1},{2,34}... | collective-permute-start | bytes 1572872 | tf_op jit(solution)/shard_map/ppermute | solution.py:94
  154.7 13.7 %copy-start.4 = (bf16[512,2048]{1,0:T(8,128)(2,1)}, bf16[512,2048]{1,0:T(8,128)(2,1)S(1)}, u32[]{:S(2)}) copy-start(bf16[512,2048]{1,0:T(8,128)(2,1)S(1)} %convolution_convert_fusion) | copy-start | bytes 6291460
  167.1 3.8 %copy-start.9 = (bf16[128,2048]{1,0:T(8,128)(2,1)}, bf16[128,2048]{1,0:T(8,128)(2,1)S(1)}, u32[]{:S(2)}) copy-start(bf16[128,2048]{1,0:T(8,128)(2,1)S(1)} %collective-permute-done.16) | copy-start | bytes 1572868
  168.0 6.8 %collective-permute-start.18 = (bf16[64,2048]{1,0:T(8,128)(2,1)}, bf16[64,2048]{1,0:T(8,128)(2,1)}, u32[]{:S(2)}, u32[]{:S(2)}) collective-permute-start(bf16[64,2048]{1,0:T(8,128)(2,1)} %get-tuple-element.20), channel_id=1, source_target_pairs={{0,96},{32,0},{64,32},{96,64},{1,97},{33,1},{65,33},{97,65},{2,98}... | collective-permute-start | bytes 786440 | tf_op jit(solution)/shard_map/ppermute | solution.py:100
  169.4 16.7 %collective-permute-start.11 = (bf16[128,2048]{1,0:T(8,128)(2,1)}, bf16[128,2048]{1,0:T(8,128)(2,1)}, u32[]{:S(2)}, u32[]{:S(2)}) collective-permute-start(bf16[128,2048]{1,0:T(8,128)(2,1)} %get-tuple-element.38), channel_id=1, source_target_pairs={{0,96},{32,0},{64,32},{96,64},{1,97},{33,1},{65,33},{97,65},{2,98}... | collective-permute-start | bytes 1572872 | tf_op jit(solution)/shard_map/ppermute | solution.py:95
  169.4 16.7 %collective-permute-start.12 = (bf16[128,2048]{1,0:T(8,128)(2,1)}, bf16[128,2048]{1,0:T(8,128)(2,1)}, u32[]{:S(2)}, u32[]{:S(2)}) collective-permute-start(bf16[128,2048]{1,0:T(8,128)(2,1)} %get-tuple-element.39), channel_id=1, source_target_pairs={{0,32},{32,64},{64,96},{96,0},{1,33},{33,65},{65,97},{97,1},{2,34}... | collective-permute-start | bytes 1572872 | tf_op jit(solution)/shard_map/ppermute | solution.py:94
  171.3 39.0 %copy-start.8 = (f32[64,2048]{1,0:T(8,128)S(1)}, f32[64,2048]{1,0:T(8,128)}, u32[]{:S(2)}) copy-start(f32[64,2048]{1,0:T(8,128)} %param.16) | copy-start | bytes 1572868
  171.4 18.0 %collective-permute-start.17 = (bf16[64,2048]{1,0:T(8,128)(2,1)}, bf16[64,2048]{1,0:T(8,128)(2,1)S(1)}, u32[]{:S(2)}, u32[]{:S(2)}) collective-permute-start(bf16[64,2048]{1,0:T(8,128)(2,1)} %get-tuple-element.19), channel_id=1, source_target_pairs={{0,32},{32,64},{64,96},{96,0},{1,33},{33,65},{65,97},{97,1},{2,34}... | collective-permute-start | bytes 786440 | tf_op jit(solution)/shard_map/ppermute | solution.py:99
  176.0 15.8 %collective-permute-start.19 = (bf16[64,2048]{1,0:T(8,128)(2,1)S(1)}, bf16[64,2048]{1,0:T(8,128)(2,1)S(1)}, u32[]{:S(2)}, u32[]{:S(2)}) collective-permute-start(bf16[64,2048]{1,0:T(8,128)(2,1)S(1)} %add_convert_fusion.1), channel_id=1, source_target_pairs={{0,128},{128,0},{1,129},{129,1},{2,130},{130,2},{3,131},{131,3},{4... | collective-permute-start | bytes 786440 | tf_op jit(solution)/shard_map/ppermute | solution.py:40
  187.5 7.7 %collective-permute-start.14 = (bf16[64,2048]{1,0:T(8,128)(2,1)S(1)}, bf16[64,2048]{1,0:T(8,128)(2,1)S(1)}, u32[]{:S(2)}, u32[]{:S(2)}) collective-permute-start(bf16[64,2048]{1,0:T(8,128)(2,1)S(1)} %get-tuple-element.18), channel_id=1, source_target_pairs={{0,96},{32,0},{64,32},{96,64},{1,97},{33,1},{65,33},{97,65},{2,98}... | collective-permute-start | bytes 786440 | tf_op jit(solution)/shard_map/ppermute | solution.py:100
  189.4 7.8 %collective-permute-start.13 = (bf16[64,2048]{1,0:T(8,128)(2,1)S(1)}, bf16[64,2048]{1,0:T(8,128)(2,1)S(1)}, u32[]{:S(2)}, u32[]{:S(2)}) collective-permute-start(bf16[64,2048]{1,0:T(8,128)(2,1)S(1)} %get-tuple-element.17), channel_id=1, source_target_pairs={{0,32},{32,64},{64,96},{96,0},{1,33},{33,65},{65,97},{97,1},{2,34}... | collective-permute-start | bytes 786440 | tf_op jit(solution)/shard_map/ppermute | solution.py:99
  196.3 14.0 %collective-permute-start.20 = (bf16[64,2048]{1,0:T(8,128)(2,1)S(1)}, bf16[64,2048]{1,0:T(8,128)(2,1)S(1)}, u32[]{:S(2)}, u32[]{:S(2)}) collective-permute-start(bf16[64,2048]{1,0:T(8,128)(2,1)S(1)} %add_convert_fusion), channel_id=1, source_target_pairs={{0,128},{128,0},{1,129},{129,1},{2,130},{130,2},{3,131},{131,3},{4... | collective-permute-start | bytes 786440 | tf_op jit(solution)/shard_map/ppermute | solution.py:40

commit v7 on v6

--- a/solution.py
+++ b/solution.py
@@ -52,9 +52,11 @@
 def over_neighbours(sums):
     count = lax.axis_size(BLOCKS)
     sums = sums + from_partner(sums, "core")
-    before = lax.ppermute(sums, BLOCKS, [(i, i + 1) for i in range(count - 1)])
-    after = lax.ppermute(sums, BLOCKS, [(i + 1, i) for i in range(count - 1)])
-    return sums + before + after
+    swaps = []
+    for start in (1, 0):
+        pairs = [(i, i + 1) for i in range(start, count - 1, 2)]
+        swaps.append(lax.ppermute(sums, BLOCKS, pairs + [(j, i) for i, j in pairs]))
+    return sums + swaps[0] + swaps[1]
 
 
 LEAVING = ((0, 2), (1, 1), (1, 2), (0, 3), (0, 0), (1, 0), (0, 1), (1, 3))
@@ -114,8 +116,8 @@
 
 def summed_over_dp(partial, late_y, late_z):
     kept, other = over_y(partial, late_y)
-    sent = (other + late_z).astype(jnp.bfloat16)
-    return kept + from_partner(sent, "z_hi").astype(jnp.float32)
+    arrived = from_partner((other + late_z).astype(jnp.bfloat16), "z_hi")
+    return kept + arrived.astype(jnp.float32), nothing(arrived[0, 0])
 
 
 def shards(
@@ -188,8 +190,8 @@
             emb_bf = (emb + delta_whole * token_scale).astype(jnp.bfloat16)
     partial_in = partial_over_chip(lefts_in, rights_in)
     there = nothing(partial_in[0, 0])
-    summed_out = summed_over_dp(partial_out, there, there)
-    summed_in = summed_over_dp(partial_in, 0.0, nothing(summed_out[0, 0]))
+    summed_out, there = summed_over_dp(partial_out, there, there)
+    summed_in, _ = summed_over_dp(partial_in, 0.0, there)
     summed_out = summed_out.T
     dp_rows = moment_in.shape[0]
     offset = lax.axis_index(DP) * dp_rows

time: 216 us -> 212 us (0.981)
  waiting for transfers between devices: 64 us -> 56.2 us
  starting transfers between devices: 55.3 us -> 59.3 us
    ppermute x2, waiting for transfers between devices: 18 us -> 6.91 us  [over_y(): sunk = lax.ppermute(partial[2 * few:4 * few], 'y', down)]
    ppermute x11, waiting for transfers between devices: 16.5 us -> 9.83 us  [from_partner(): return lax.ppermute(array, axis, [(0, 1), (1, 0)])]
    ppermute x2, waiting for transfers between devices: 3.1 us -> 8.94 us  [over_y(): risen = lax.ppermute(partial[:2 * few], 'y', up)]
    ppermute x2, starting transfers between devices: 11.4 us -> 6.24 us  [over_y(): sunk = lax.ppermute(partial[2 * few:4 * few], 'y', down)]
    ppermute x11, starting transfers between devices: 12.4 us -> 17.5 us  [from_partner(): return lax.ppermute(array, axis, [(0, 1), (1, 0)])]
    ppermute x2, waiting for transfers between devices: 0.01 us -> 3.59 us  [over_y(): lax.ppermute(on_up, 'y', up)]
    ppermute x2, starting transfers between devices: 2.25 us -> 5.73 us  [over_y(): lax.ppermute(on_down, 'y', down)]
  transfers between devices with their start and end apart: 25 -> 25, of which waited for: 12 -> 13; matrix products, arithmetic and copies ran while one was open for 11% -> 11% of each run, Pallas kernels for 0% -> 0%
where the time goes in v7:
time: 212 us; the launch traced here: 208 us
  starting transfers between devices  59.3 us (28%)
  waiting for transfers between devices  56.2 us (27%)
  blocking collectives  42.8 us (20%)
  matrix products  26.9 us (13%)
  other arithmetic  11.9 us (6%)
  local copies, waits for them, and re-layouts  8.03 us (4%)
  between operations  3.07 us (1%)
    all_to_all x3, blocking collectives, to_peers(): return lax.all_to_all(blocks, axis, 0, 0, tiled=True)  42.8 us
    all_to_all x4, waiting for transfers between devices, to_peers(): return lax.all_to_all(blocks, axis, 0, 0, tiled=True)  23.2 us
    all_to_all x4, starting transfers between devices, to_peers(): return lax.all_to_all(blocks, axis, 0, 0, tiled=True)  22.1 us
    ppermute x11, starting transfers between devices, from_partner(): return lax.ppermute(array, axis, [(0, 1), (1, 0)])  17.5 us
    ppermute x11, waiting for transfers between devices, from_partner(): return lax.ppermute(array, axis, [(0, 1), (1, 0)])  9.83 us
    ppermute x2, waiting for transfers between devices, over_y(): risen = lax.ppermute(partial[:2 * few], 'y', up)  8.94 us
    dot_general x2, matrix products, shards(): preact = jnp.dot(normed, weight_in, preferred_element_type=jnp.float32)  8.55 us
    ppermute x2, waiting for transfers between devices, over_y(): sunk = lax.ppermute(partial[2 * few:4 * few], 'y', down)  6.91 us
  transfers between devices with their start and end apart: 25, of which 13 were waited for; matrix products, arithmetic and copies ran while one was open for 11% of the time, Pallas kernels for 0%

profile of v7, /device:TPU:33, one launch (start us, length us, event | category | flops | bytes accessed | tf_op | source)
XLA Modules:
  0.0 208.2 jit_solution(5954855757828260422)
XLA Ops:
  0.6 0.8 fusion.79
  1.5 15.8 %all_to_all.35 = bf16[16,128,64]{1,2,0:T(8,128)(2,1)S(1)} all-to-all(bf16[16,128,64]{1,2,0:T(8,128)(2,1)S(1)} %broadcast_in_dim.100), channel_id=1, replica_groups=mesh['z_hi'=2,'y'=4,'core'=2,'x'=4,'z_lo'=4] {'x','z_lo'}, dimensions={0} | all-to-all | bytes 524288 | tf_op jit(solution)/shard_map/all_to_all | solution.py:22
  17.6 3.8 %fusion.36 = (f32[128,2048]{1,0:T(8,128)S(1)}, bf16[128,2048]{1,0:T(8,128)(2,1)S(1)}) fusion(bf16[1024,2048]{1,0:T(8,128)(2,1)} %param.14, bf16[128,1024]{1,0:T(8,128)(2,1)S(1)} %copy.26, f32[1024]{0:T(1024)} %param.13, f32[128]{0:T(128)S(1)} %add_rsqrt_fusion.1), kind=kOutput, calls=%fused_computation.48 | convolution fusion | flops 542375936 | bytes 6033920 | tf_op jit(solution)/shard_map/dot_general | solution.py:144
  21.4 0.7 convolution_convert_fusion.3
  22.4 13.7 %all_to_all.36 = bf16[16,128,64]{1,2,0:T(8,128)(2,1)S(1)} all-to-all(bf16[16,128,64]{1,2,0:T(8,128)(2,1)S(1)} %bitcast.63), channel_id=1, replica_groups=mesh['z_hi'=2,'y'=4,'core'=2,'x'=4,'z_lo'=4] {'x','z_lo'}, dimensions={0} | all-to-all | bytes 524288 | tf_op jit(solution)/shard_map/all_to_all | solution.py:22
  36.3 13.3 %all_to_all.37 = bf16[16,128,64]{1,2,0:T(8,128)(2,1)S(1)} all-to-all(bf16[16,128,64]{1,2,0:T(8,128)(2,1)S(1)} %broadcast_in_dim.117), channel_id=1, replica_groups=mesh['z_hi'=2,'y'=4,'core'=2,'x'=4,'z_lo'=4] {'x','z_lo'}, dimensions={0} | all-to-all | bytes 524288 | tf_op jit(solution)/shard_map/all_to_all | solution.py:22
  49.5 3.7 %fusion = bf16[128,2048]{1,0:T(8,128)(2,1)S(1)} fusion(f32[128,2048]{1,0:T(8,128)S(1)} %get-tuple-element.14, bf16[128,1024]{0,1:T(8,128)(2,1)S(1)} %bitcast.55, bf16[2048,1024]{1,0:T(8,128)(2,1)} %param.15), kind=kOutput, calls=%fused_computation.4 | convolution fusion | flops 537395200 | bytes 6029312 | tf_op jit(solution)/shard_map/dot_general | solution.py:157
  53.3 1.6 fusion.109
  55.1 0.7 pad_maximum_fusion
  55.8 5.6 %all-to-all-start.3 = ((bf16[16,128,66]{1,2,0:T(8,128)(2,1)}), bf16[16,128,66]{1,2,0:T(8,128)(2,1)S(1)}, u32[]{:S(2)}, u32[]{:S(2)}) async-start(bf16[16,128,66]{1,2,0:T(8,128)(2,1)} %pad_maximum_fusion), calls=%async_computation.3 | async-start | bytes 589824 | tf_op jit(solution)/shard_map/all_to_all | solution.py:22
  61.5 8.0 %all-to-all-done.3 = bf16[16,128,66]{1,2,0:T(8,128)(2,1)S(1)} async-done(((bf16[16,128,66]{1,2,0:T(8,128)(2,1)}), bf16[16,128,66]{1,2,0:T(8,128)(2,1)S(1)}, u32[]{:S(2)}, u32[]{:S(2)}) %all-to-all-start.3) | async-done | bytes 270368 | tf_op jit(solution)/shard_map/all_to_all | solution.py:22
  69.6 0.8 broadcast_in_dim.119
  70.4 6.1 %all-to-all-start.4 = ((bf16[16,128,64]{1,2,0:T(8,128)(2,1)}), bf16[16,128,64]{1,2,0:T(8,128)(2,1)S(1)}, u32[]{:S(2)}, u32[]{:S(2)}) async-start(bf16[16,128,64]{1,2,0:T(8,128)(2,1)} %broadcast_in_dim.119), calls=%async_computation.4 | async-start | bytes 524288 | tf_op jit(solution)/shard_map/all_to_all | solution.py:22
  76.5 7.7 %all-to-all-done.4 = bf16[16,128,64]{1,2,0:T(8,128)(2,1)S(1)} async-done(((bf16[16,128,64]{1,2,0:T(8,128)(2,1)}), bf16[16,128,64]{1,2,0:T(8,128)(2,1)S(1)}, u32[]{:S(2)}, u32[]{:S(2)}) %all-to-all-start.4) | async-done | bytes 262176 | tf_op jit(solution)/shard_map/all_to_all | solution.py:22
  84.5 2.9 %collective-permute-start.1 = (f32[2,32]{1,0:T(2,128)S(1)}, f32[2,32]{1,0:T(2,128)S(1)}, u32[]{:S(2)}, u32[]{:S(2)}) collective-permute-start(f32[2,32]{1,0:T(2,128)S(1)} %pad_maximum_fusion.1), channel_id=1, source_target_pairs={{0,16},{16,0},{1,17},{17,1},{2,18},{18,2},{3,19},{19,3},{4,20},{20... | collective-permute-start | bytes 776 | tf_op jit(solution)/shard_map/ppermute | solution.py:40
  87.4 0.8 collective-permute-done.1
  88.2 0.7 collective-permute-start.2
  88.9 3.9 %collective-permute-start.3 = (f32[2,32]{1,0:T(2,128)S(1)}, f32[2,32]{1,0:T(2,128)S(1)}, u32[]{:S(2)}, u32[]{:S(2)}) collective-permute-start(f32[2,32]{1,0:T(2,128)S(1)} %fusion.97), channel_id=1, source_target_pairs={{0,32},{64,96},{128,160},{192,224},{32,0},{96,64},{160,128},{224,1... | collective-permute-start | bytes 776 | tf_op jit(solution)/shard_map/ppermute | solution.py:58
  93.1 0.7 collective-permute-done.3
  94.2 4.8 %fusion.41 = (f32[128,2048]{1,0:T(8,128)}, bf16[128,2048]{1,0:T(8,128)(2,1)S(1)}) fusion(bf16[1024,2048]{1,0:T(8,128)(2,1)} %param.14, bf16[128,1024]{1,0:T(8,128)(2,1)S(1)} %fusion.57, f32[128]{0:T(128)S(1)} %add_rsqrt_fusion, f32[1024]{0:T(1024)S(1)} %copy-done.15), kind=kOutput, calls=%fused_computation.53 | convolution fusion | flops 542375936 | bytes 6033920 | tf_op jit(solution)/shard_map/dot_general | solution.py:144
  98.9 0.7 convolution_convert_fusion.2
  99.7 0.8 copy.30
  100.5 4.8 %all-to-all-start.5 = ((bf16[16,128,64]{1,2,0:T(8,128)(2,1)}), bf16[16,128,64]{1,2,0:T(8,128)(2,1)S(1)}, u32[]{:S(2)}, u32[]{:S(2)}) async-start(bf16[16,128,64]{1,2,0:T(8,128)(2,1)} %bitcast.15), calls=%async_computation.5 | async-start | bytes 524288 | tf_op jit(solution)/shard_map/all_to_all | solution.py:22
  105.3 1.8 collective-permute-start.8
  107.1 0.5 fusion.28
  108.0 1.2 fusion.24
  109.1 4.1 %all-to-all-done.5 = bf16[16,128,64]{1,2,0:T(8,128)(2,1)S(1)} async-done(((bf16[16,128,64]{1,2,0:T(8,128)(2,1)}), bf16[16,128,64]{1,2,0:T(8,128)(2,1)S(1)}, u32[]{:S(2)}, u32[]{:S(2)}) %all-to-all-start.5) | async-done | bytes 262176 | tf_op jit(solution)/shard_map/all_to_all | solution.py:22
  113.3 0.7 fusion.75
  114.0 0.8 broadcast_in_dim.120
  114.8 5.6 %all-to-all-start.6 = ((bf16[16,128,64]{1,2,0:T(8,128)(2,1)}), bf16[16,128,64]{1,2,0:T(8,128)(2,1)S(1)}, u32[]{:S(2)}, u32[]{:S(2)}) async-start(bf16[16,128,64]{1,2,0:T(8,128)(2,1)} %broadcast_in_dim.120), calls=%async_computation.6 | async-start | bytes 524288 | tf_op jit(solution)/shard_map/all_to_all | solution.py:22
  120.4 0.5 fusion.30
  120.9 2.1 %collective-permute-start.6 = (bf16[128,512]{1,0:T(8,128)(2,1)S(1)}, bf16[128,512]{1,0:T(8,128)(2,1)S(1)}, u32[]{:S(2)}, u32[]{:S(2)}) collective-permute-start(bf16[128,512]{1,0:T(8,128)(2,1)S(1)} %fusion.30), channel_id=1, source_target_pairs={{0,16},{16,0},{1,17},{17,1},{2,18},{18,2},{3,19},{19,3},{4,20},{20... | collective-permute-start | bytes 393224 | tf_op jit(solution)/shard_map/ppermute | solution.py:40
  123.1 1.2 fusion.26
  124.8 3.3 %all-to-all-done.6 = bf16[16,128,64]{1,2,0:T(8,128)(2,1)S(1)} async-done(((bf16[16,128,64]{1,2,0:T(8,128)(2,1)}), bf16[16,128,64]{1,2,0:T(8,128)(2,1)S(1)}, u32[]{:S(2)}, u32[]{:S(2)}) %all-to-all-start.6) | async-done | bytes 262176 | tf_op jit(solution)/shard_map/all_to_all | solution.py:22
  128.1 0.5 fusion.31
  128.7 2.8 %collective-permute-start.7 = (bf16[128,512]{1,0:T(8,128)(2,1)S(1)}, bf16[128,512]{1,0:T(8,128)(2,1)S(1)}, u32[]{:S(2)}, u32[]{:S(2)}) collective-permute-start(bf16[128,512]{1,0:T(8,128)(2,1)S(1)} %fusion.31), channel_id=1, source_target_pairs={{0,16},{16,0},{1,17},{17,1},{2,18},{18,2},{3,19},{19,3},{4,20},{20... | collective-permute-start | bytes 393224 | tf_op jit(solution)/shard_map/ppermute | solution.py:40
  131.5 0.5 fusion.27
  132.8 0.8 copy-done.17
  133.6 3.1 %convolution_convert_fusion.1 = bf16[512,2048]{1,0:T(8,128)(2,1)S(1)} fusion(bf16[128,2048]{1,0:T(8,128)(2,1)} %copy-done.17, bf16[128,2048]{1,0:T(8,128)(2,1)} %copy-done.8, bf16[128,2048]{1,0:T(8,128)(2,1)} %collective-permute-done.8, bf16[128,2048]{1,0:T(8,128)(2,1)} %copy-done.7, bf16[128,512]{1,0:T(8,128)(2,1)S(1)} %collective-permute-done.7, ...), kind=kOutput, calls=%fused_computation.1 | convolution fusion | flops 1085276160 | bytes 4718592 | tf_op jit(solution)/shard_map/dot_general | solution.py:112
  138.0 1.5 fusion.1
  140.0 1.5 collective-permute-start.15
  141.5 6.2 %collective-permute-start.16 = (bf16[128,2048]{1,0:T(8,128)(2,1)S(1)}, bf16[128,2048]{1,0:T(8,128)(2,1)S(1)}, u32[]{:S(2)}, u32[]{:S(2)}) collective-permute-start(bf16[128,2048]{1,0:T(8,128)(2,1)S(1)} %get-tuple-element.33), channel_id=1, source_target_pairs={{0,96},{32,0},{64,32},{96,64},{1,97},{33,1},{65,33},{97,65},{2,98}... | collective-permute-start | bytes 1572872 | tf_op jit(solution)/shard_map/ppermute | solution.py:97
  147.6 0.5 fusion.25
  148.2 1.3 convolution_convert_fusion
  149.5 0.6 slice.118
  150.7 8.9 %collective-permute-done.15 = bf16[128,2048]{1,0:T(8,128)(2,1)S(1)} collective-permute-done((bf16[128,2048]{1,0:T(8,128)(2,1)S(1)}, bf16[128,2048]{1,0:T(8,128)(2,1)S(1)}, u32[]{:S(2)}, u32[]{:S(2)}) %collective-permute-start.15) | collective-permute-done | bytes 524320 | tf_op jit(solution)/shard_map/ppermute | solution.py:96
  159.7 0.9 add_convert_fusion.2
  160.6 2.4 %collective-permute-start.17 = (bf16[64,2048]{1,0:T(8,128)(2,1)S(1)}, bf16[64,2048]{1,0:T(8,128)(2,1)S(1)}, u32[]{:S(2)}, u32[]{:S(2)}) collective-permute-start(bf16[64,2048]{1,0:T(8,128)(2,1)S(1)} %get-tuple-element.19), channel_id=1, source_target_pairs={{0,96},{32,0},{64,32},{96,64},{1,97},{33,1},{65,33},{97,65},{2,98}... | collective-permute-start | bytes 786440 | tf_op jit(solution)/shard_map/ppermute | solution.py:102
  163.2 1.5 collective-permute-start.12
  164.7 3.1 %collective-permute-done.17 = bf16[64,2048]{1,0:T(8,128)(2,1)S(1)} collective-permute-done((bf16[64,2048]{1,0:T(8,128)(2,1)S(1)}, bf16[64,2048]{1,0:T(8,128)(2,1)S(1)}, u32[]{:S(2)}, u32[]{:S(2)}) %collective-permute-start.17) | collective-permute-done | bytes 262176 | tf_op jit(solution)/shard_map/ppermute | solution.py:102
  167.7 0.8 add_convert_fusion.1
  168.6 3.5 %collective-permute-start.18 = (bf16[64,2048]{1,0:T(8,128)(2,1)}, bf16[64,2048]{1,0:T(8,128)(2,1)}, u32[]{:S(2)}, u32[]{:S(2)}) collective-permute-start(bf16[64,2048]{1,0:T(8,128)(2,1)} %add_convert_fusion.1), channel_id=1, source_target_pairs={{0,128},{128,0},{1,129},{129,1},{2,130},{130,2},{3,131},{131,3},{4... | collective-permute-start | bytes 786440 | tf_op jit(solution)/shard_map/ppermute | solution.py:40
  172.0 6.9 %collective-permute-done.11 = bf16[128,2048]{1,0:T(8,128)(2,1)S(1)} collective-permute-done((bf16[128,2048]{1,0:T(8,128)(2,1)S(1)}, bf16[128,2048]{1,0:T(8,128)(2,1)S(1)}, u32[]{:S(2)}, u32[]{:S(2)}) %collective-permute-start.11) | collective-permute-done | bytes 524320 | tf_op jit(solution)/shard_map/ppermute | solution.py:97
  179.0 1.0 add_convert_fusion.4
  180.0 3.3 %collective-permute-start.14 = (bf16[64,2048]{1,0:T(8,128)(2,1)}, bf16[64,2048]{1,0:T(8,128)(2,1)}, u32[]{:S(2)}, u32[]{:S(2)}) collective-permute-start(bf16[64,2048]{1,0:T(8,128)(2,1)} %get-tuple-element.18), channel_id=1, source_target_pairs={{0,96},{32,0},{64,32},{96,64},{1,97},{33,1},{65,33},{97,65},{2,98}... | collective-permute-start | bytes 786440 | tf_op jit(solution)/shard_map/ppermute | solution.py:102
  183.3 1.2 constant_dynamic-slice_fusion
  184.9 0.7 collective-permute-done.18
  185.6 1.1 slice.122
  187.3 1.2 add_convert_fusion
  188.6 3.2 %collective-permute-start.19 = (bf16[64,2048]{1,0:T(8,128)(2,1)S(1)}, bf16[64,2048]{1,0:T(8,128)(2,1)S(1)}, u32[]{:S(2)}, u32[]{:S(2)}) collective-permute-start(bf16[64,2048]{1,0:T(8,128)(2,1)S(1)} %add_convert_fusion), channel_id=1, source_target_pairs={{0,128},{128,0},{1,129},{129,1},{2,130},{130,2},{3,131},{131,3},{4... | collective-permute-start | bytes 786440 | tf_op jit(solution)/shard_map/ppermute | solution.py:40
  191.8 2.1 %subtract_convert_fusion = (bf16[2048,64]{0,1:T(8,128)(2,1)}, f32[2048,64]{0,1:T(8,128)}) fusion(bf16[2048,64]{0,1:T(8,128)(2,1)S(1)} %copy.32, bf16[64,2048]{1,0:T(8,128)(2,1)} %collective-permute-done.18, bf16[64,2048]{1,0:T(8,128)(2,1)S(1)} %collective-permute-done.20, bf16[128,2048]{1,0:T(8,128)(2,1)} %copy-done.9, ...), kind=kLoop, calls=%fused_computation.94 | loop fusion | flops 1835008 | bytes 2621440 | tf_op jit(solution)/shard_map/convert_element_type | solution.py:203
  194.0 3.5 %collective-permute-done.13 = bf16[64,2048]{1,0:T(8,128)(2,1)S(1)} collective-permute-done((bf16[64,2048]{1,0:T(8,128)(2,1)}, bf16[64,2048]{1,0:T(8,128)(2,1)S(1)}, u32[]{:S(2)}, u32[]{:S(2)}) %collective-permute-start.13) | collective-permute-done | bytes 262176 | tf_op jit(solution)/shard_map/ppermute | solution.py:101
  197.4 8.3 %collective-permute-done.19 = bf16[64,2048]{1,0:T(8,128)(2,1)S(1)} collective-permute-done((bf16[64,2048]{1,0:T(8,128)(2,1)S(1)}, bf16[64,2048]{1,0:T(8,128)(2,1)S(1)}, u32[]{:S(2)}, u32[]{:S(2)}) %collective-permute-start.19) | collective-permute-done | bytes 262176 | tf_op jit(solution)/shard_map/ppermute | solution.py:40
  205.8 2.4 %subtract_convert_fusion.1 = (bf16[64,2048]{1,0:T(8,128)(2,1)}, f32[64,2048]{1,0:T(8,128)}) fusion(bf16[1024,2048]{1,0:T(8,128)(2,1)} %param.14, s32[]{:T(128)S(6)} %select_n.195, bf16[64,2048]{1,0:T(8,128)(2,1)S(1)} %collective-permute-done.19, bf16[64,2048]{1,0:T(8,128)(2,1)S(1)} %collective-permute-done.13, bf16[128,2048]{1,0:T(8,128)(2,1)} %copy-done.11, ...), kind=kLoop, calls=%fused_computation.95 | loop fusion | flops 1835008 | bytes 2621444 | tf_op jit(solution)/shard_map/convert_element_type | solution.py:202
  (97 shorter events, 5.3 us)
Async XLA Ops:
  17.6 3.8 %copy-start = (bf16[2048,1024]{1,0:T(8,128)(2,1)S(1)}, bf16[2048,1024]{1,0:T(8,128)(2,1)}, u32[]{:S(2)}) copy-start(bf16[2048,1024]{1,0:T(8,128)(2,1)} %param.15) | copy-start | bytes 12582916
  21.4 84.0 %copy-start.7 = (bf16[128,2048]{1,0:T(8,128)(2,1)}, bf16[128,2048]{1,0:T(8,128)(2,1)S(1)}, u32[]{:S(2)}) copy-start(bf16[128,2048]{1,0:T(8,128)(2,1)S(1)} %get-tuple-element.13) | copy-start | bytes 1572868
  21.4 14.8 %copy-start.12 = (f32[128,64]{0,1:T(8,128)S(1)}, f32[128,64]{0,1:T(8,128)}, u32[]{:S(2)}) copy-start(f32[128,64]{0,1:T(8,128)} %param.10) | copy-start | bytes 98308
  21.4 14.8 %copy-start.13 = (bf16[128,64]{0,1:T(8,128)(2,1)S(1)}, bf16[128,64]{0,1:T(8,128)(2,1)}, u32[]{:S(2)}) copy-start(bf16[128,64]{0,1:T(8,128)(2,1)} %param.9) | copy-start | bytes 49156
  21.4 14.8 %copy-start.14 = (f32[128,64]{0,1:T(8,128)S(1)}, f32[128,64]{0,1:T(8,128)}, u32[]{:S(2)}) copy-start(f32[128,64]{0,1:T(8,128)} %param.12) | copy-start | bytes 98308
  22.2 31.1 %copy-start.15 = (f32[1024]{0:T(1024)S(1)}, f32[1024]{0:T(1024)}, u32[]{:S(2)}) copy-start(f32[1024]{0:T(1024)} %param.13) | copy-start | bytes 12292
  22.4 30.9 %copy-start.3 = (bf16[1024,2048]{1,0:T(8,128)(2,1)S(1)}, bf16[1024,2048]{1,0:T(8,128)(2,1)}, u32[]{:S(2)}) copy-start(bf16[1024,2048]{1,0:T(8,128)(2,1)} %param.14) | copy-start | bytes 12582916
  53.3 31.1 %copy-start.16 = (s32[128]{0:T(128)S(1)}, s32[128]{0:T(128)}, u32[]{:S(2)}) copy-start(s32[128]{0:T(128)} %param.11) | copy-start | bytes 1540
  55.8 13.6 %all-to-all-start.3 = ((bf16[16,128,66]{1,2,0:T(8,128)(2,1)}), bf16[16,128,66]{1,2,0:T(8,128)(2,1)S(1)}, u32[]{:S(2)}, u32[]{:S(2)}) async-start(bf16[16,128,66]{1,2,0:T(8,128)(2,1)} %pad_maximum_fusion), calls=%async_computation.3 | async-start | bytes 589824 | tf_op jit(solution)/shard_map/all_to_all | solution.py:22
  70.4 13.9 %all-to-all-start.4 = ((bf16[16,128,64]{1,2,0:T(8,128)(2,1)}), bf16[16,128,64]{1,2,0:T(8,128)(2,1)S(1)}, u32[]{:S(2)}, u32[]{:S(2)}) async-start(bf16[16,128,64]{1,2,0:T(8,128)(2,1)} %broadcast_in_dim.119), calls=%async_computation.4 | async-start | bytes 524288 | tf_op jit(solution)/shard_map/all_to_all | solution.py:22
  84.5 3.7 %collective-permute-start.1 = (f32[2,32]{1,0:T(2,128)S(1)}, f32[2,32]{1,0:T(2,128)S(1)}, u32[]{:S(2)}, u32[]{:S(2)}) collective-permute-start(f32[2,32]{1,0:T(2,128)S(1)} %pad_maximum_fusion.1), channel_id=1, source_target_pairs={{0,16},{16,0},{1,17},{17,1},{2,18},{18,2},{3,19},{19,3},{4,20},{20... | collective-permute-start | bytes 776 | tf_op jit(solution)/shard_map/ppermute | solution.py:40
  88.2 4.8 %collective-permute-start.2 = (f32[2,32]{1,0:T(2,128)S(1)}, f32[2,32]{1,0:T(2,128)S(1)}, u32[]{:S(2)}, u32[]{:S(2)}) collective-permute-start(f32[2,32]{1,0:T(2,128)S(1)} %fusion.97), channel_id=1, source_target_pairs={{32,64},{96,128},{160,192},{64,32},{128,96},{192,160},{33,65},{97,... | collective-permute-start | bytes 776 | tf_op jit(solution)/shard_map/ppermute | solution.py:58
  88.9 4.9 %collective-permute-start.3 = (f32[2,32]{1,0:T(2,128)S(1)}, f32[2,32]{1,0:T(2,128)S(1)}, u32[]{:S(2)}, u32[]{:S(2)}) collective-permute-start(f32[2,32]{1,0:T(2,128)S(1)} %fusion.97), channel_id=1, source_target_pairs={{0,32},{64,96},{128,160},{192,224},{32,0},{96,64},{160,128},{224,1... | collective-permute-start | bytes 776 | tf_op jit(solution)/shard_map/ppermute | solution.py:58
  94.2 4.8 %copy-start.1 = (bf16[2048,1024]{1,0:T(8,128)(2,1)S(1)}, bf16[2048,1024]{1,0:T(8,128)(2,1)}, u32[]{:S(2)}) copy-start(bf16[2048,1024]{1,0:T(8,128)(2,1)} %param.15) | copy-start | bytes 12582916
  98.9 25.3 %copy-start.8 = (bf16[128,2048]{1,0:T(8,128)(2,1)}, bf16[128,2048]{1,0:T(8,128)(2,1)S(1)}, u32[]{:S(2)}) copy-start(bf16[128,2048]{1,0:T(8,128)(2,1)S(1)} %get-tuple-element.15) | copy-start | bytes 1572868
  100.5 12.7 %all-to-all-start.5 = ((bf16[16,128,64]{1,2,0:T(8,128)(2,1)}), bf16[16,128,64]{1,2,0:T(8,128)(2,1)S(1)}, u32[]{:S(2)}, u32[]{:S(2)}) async-start(bf16[16,128,64]{1,2,0:T(8,128)(2,1)} %bitcast.15), calls=%async_computation.5 | async-start | bytes 524288 | tf_op jit(solution)/shard_map/all_to_all | solution.py:22
  105.3 26.7 %collective-permute-start.8 = (bf16[128,2048]{1,0:T(8,128)(2,1)S(1)}, bf16[128,2048]{1,0:T(8,128)(2,1)}, u32[]{:S(2)}, u32[]{:S(2)}) collective-permute-start(bf16[128,2048]{1,0:T(8,128)(2,1)S(1)} %get-tuple-element.13), channel_id=1, source_target_pairs={{0,16},{16,0},{1,17},{17,1},{2,18},{18,2},{3,19},{19,3},{4,20},{20... | collective-permute-start | bytes 1572872 | tf_op jit(solution)/shard_map/ppermute | solution.py:40
  107.7 33.8 %collective-permute-start = (bf16[128,512]{1,0:T(8,128)(2,1)S(1)}, bf16[128,512]{1,0:T(8,128)(2,1)S(1)}, u32[]{:S(2)}, u32[]{:S(2)}) collective-permute-start(bf16[128,512]{1,0:T(8,128)(2,1)S(1)} %fusion.28), channel_id=1, source_target_pairs={{0,16},{16,0},{1,17},{17,1},{2,18},{18,2},{3,19},{19,3},{4,20},{20... | collective-permute-start | bytes 393224 | tf_op jit(solution)/shard_map/ppermute | solution.py:40
  114.8 13.4 %all-to-all-start.6 = ((bf16[16,128,64]{1,2,0:T(8,128)(2,1)}), bf16[16,128,64]{1,2,0:T(8,128)(2,1)S(1)}, u32[]{:S(2)}, u32[]{:S(2)}) async-start(bf16[16,128,64]{1,2,0:T(8,128)(2,1)} %broadcast_in_dim.120), calls=%async_computation.6 | async-start | bytes 524288 | tf_op jit(solution)/shard_map/all_to_all | solution.py:22
  120.9 11.2 %collective-permute-start.6 = (bf16[128,512]{1,0:T(8,128)(2,1)S(1)}, bf16[128,512]{1,0:T(8,128)(2,1)S(1)}, u32[]{:S(2)}, u32[]{:S(2)}) collective-permute-start(bf16[128,512]{1,0:T(8,128)(2,1)S(1)} %fusion.30), channel_id=1, source_target_pairs={{0,16},{16,0},{1,17},{17,1},{2,18},{18,2},{3,19},{19,3},{4,20},{20... | collective-permute-start | bytes 393224 | tf_op jit(solution)/shard_map/ppermute | solution.py:40
  124.3 8.4 %collective-permute-start.9 = (bf16[128,2048]{1,0:T(8,128)(2,1)S(1)}, bf16[128,2048]{1,0:T(8,128)(2,1)S(1)}, u32[]{:S(2)}, u32[]{:S(2)}) collective-permute-start(bf16[128,2048]{1,0:T(8,128)(2,1)S(1)} %get-tuple-element.15), channel_id=1, source_target_pairs={{0,16},{16,0},{1,17},{17,1},{2,18},{18,2},{3,19},{19,3},{4,20},{20... | collective-permute-start | bytes 1572872 | tf_op jit(solution)/shard_map/ppermute | solution.py:40
  128.7 5.0 %collective-permute-start.7 = (bf16[128,512]{1,0:T(8,128)(2,1)S(1)}, bf16[128,512]{1,0:T(8,128)(2,1)S(1)}, u32[]{:S(2)}, u32[]{:S(2)}) collective-permute-start(bf16[128,512]{1,0:T(8,128)(2,1)S(1)} %fusion.31), channel_id=1, source_target_pairs={{0,16},{16,0},{1,17},{17,1},{2,18},{18,2},{3,19},{19,3},{4,20},{20... | collective-permute-start | bytes 393224 | tf_op jit(solution)/shard_map/ppermute | solution.py:40
  132.0 5.9 %copy-start.2 = (bf16[2048,1024]{1,0:T(8,128)(2,1)S(1)}, bf16[2048,1024]{1,0:T(8,128)(2,1)}, u32[]{:S(2)}) copy-start(bf16[2048,1024]{1,0:T(8,128)(2,1)} %param.15) | copy-start | bytes 12582916
  132.0 5.9 %copy-start.5 = (f32[128,2048]{1,0:T(8,128)S(1)}, f32[128,2048]{1,0:T(8,128)}, u32[]{:S(2)}) copy-start(f32[128,2048]{1,0:T(8,128)} %get-tuple-element.16) | copy-start | bytes 3145732
  132.1 16.1 %collective-permute-start.5 = (bf16[128,2048]{1,0:T(8,128)(2,1)S(1)}, bf16[128,2048]{1,0:T(8,128)(2,1)S(1)}, u32[]{:S(2)}, u32[]{:S(2)}) collective-permute-start(bf16[128,2048]{1,0:T(8,128)(2,1)S(1)} %fusion), channel_id=1, source_target_pairs={{0,16},{16,0},{1,17},{17,1},{2,18},{18,2},{3,19},{19,3},{4,20},{20... | collective-permute-start | bytes 1572872 | tf_op jit(solution)/shard_map/ppermute | solution.py:40
  132.2 0.7 copy-start.18
  132.2 16.0 %collective-permute-start.4 = (bf16[128,512]{1,0:T(8,128)(2,1)S(1)}, bf16[128,512]{1,0:T(8,128)(2,1)S(1)}, u32[]{:S(2)}, u32[]{:S(2)}) collective-permute-start(bf16[128,512]{1,0:T(8,128)(2,1)S(1)} %fusion.29), channel_id=1, source_target_pairs={{0,16},{16,0},{1,17},{17,1},{2,18},{18,2},{3,19},{19,3},{4,20},{20... | collective-permute-start | bytes 393224 | tf_op jit(solution)/shard_map/ppermute | solution.py:40
  132.8 0.8 copy-start.17
  138.0 10.2 %copy-start.19 = (bf16[128,512]{1,0:T(8,128)(2,1)S(1)}, bf16[128,512]{1,0:T(8,128)(2,1)}, u32[]{:S(2)}) copy-start(bf16[128,512]{1,0:T(8,128)(2,1)} %fusion.24) | copy-start | bytes 393220
  139.5 8.7 %collective-permute-start.10 = (bf16[128,2048]{1,0:T(8,128)(2,1)S(1)}, bf16[128,2048]{1,0:T(8,128)(2,1)S(1)}, u32[]{:S(2)}, u32[]{:S(2)}) collective-permute-start(bf16[128,2048]{1,0:T(8,128)(2,1)S(1)} %fusion.1), channel_id=1, source_target_pairs={{0,16},{16,0},{1,17},{17,1},{2,18},{18,2},{3,19},{19,3},{4,20},{20... | collective-permute-start | bytes 1572872 | tf_op jit(solution)/shard_map/ppermute | solution.py:40
  140.0 19.7 %collective-permute-start.15 = (bf16[128,2048]{1,0:T(8,128)(2,1)S(1)}, bf16[128,2048]{1,0:T(8,128)(2,1)S(1)}, u32[]{:S(2)}, u32[]{:S(2)}) collective-permute-start(bf16[128,2048]{1,0:T(8,128)(2,1)S(1)} %get-tuple-element.34), channel_id=1, source_target_pairs={{0,32},{32,64},{64,96},{96,0},{1,33},{33,65},{65,97},{97,1},{2,34}... | collective-permute-start | bytes 1572872 | tf_op jit(solution)/shard_map/ppermute | solution.py:96
  141.5 18.2 %collective-permute-start.16 = (bf16[128,2048]{1,0:T(8,128)(2,1)S(1)}, bf16[128,2048]{1,0:T(8,128)(2,1)S(1)}, u32[]{:S(2)}, u32[]{:S(2)}) collective-permute-start(bf16[128,2048]{1,0:T(8,128)(2,1)S(1)} %get-tuple-element.33), channel_id=1, source_target_pairs={{0,96},{32,0},{64,32},{96,64},{1,97},{33,1},{65,33},{97,65},{2,98}... | collective-permute-start | bytes 1572872 | tf_op jit(solution)/shard_map/ppermute | solution.py:97
  149.5 29.5 %copy-start.4 = (bf16[512,2048]{1,0:T(8,128)(2,1)}, bf16[512,2048]{1,0:T(8,128)(2,1)S(1)}, u32[]{:S(2)}) copy-start(bf16[512,2048]{1,0:T(8,128)(2,1)S(1)} %convolution_convert_fusion) | copy-start | bytes 6291460
  159.7 20.3 %copy-start.9 = (bf16[128,2048]{1,0:T(8,128)(2,1)}, bf16[128,2048]{1,0:T(8,128)(2,1)S(1)}, u32[]{:S(2)}) copy-start(bf16[128,2048]{1,0:T(8,128)(2,1)S(1)} %collective-permute-done.16) | copy-start | bytes 1572868
  160.6 31.2 %copy-start.6 = (f32[2048,64]{0,1:T(8,128)S(1)}, f32[2048,64]{0,1:T(8,128)}, u32[]{:S(2)}) copy-start(f32[2048,64]{0,1:T(8,128)} %param.17) | copy-start | bytes 1572868
  160.6 7.1 %collective-permute-start.17 = (bf16[64,2048]{1,0:T(8,128)(2,1)S(1)}, bf16[64,2048]{1,0:T(8,128)(2,1)S(1)}, u32[]{:S(2)}, u32[]{:S(2)}) collective-permute-start(bf16[64,2048]{1,0:T(8,128)(2,1)S(1)} %get-tuple-element.19), channel_id=1, source_target_pairs={{0,96},{32,0},{64,32},{96,64},{1,97},{33,1},{65,33},{97,65},{2,98}... | collective-permute-start | bytes 786440 | tf_op jit(solution)/shard_map/ppermute | solution.py:102
  163.1 15.8 %collective-permute-start.11 = (bf16[128,2048]{1,0:T(8,128)(2,1)S(1)}, bf16[128,2048]{1,0:T(8,128)(2,1)S(1)}, u32[]{:S(2)}, u32[]{:S(2)}) collective-permute-start(bf16[128,2048]{1,0:T(8,128)(2,1)S(1)} %get-tuple-element.37), channel_id=1, source_target_pairs={{0,96},{32,0},{64,32},{96,64},{1,97},{33,1},{65,33},{97,65},{2,98}... | collective-permute-start | bytes 1572872 | tf_op jit(solution)/shard_map/ppermute | solution.py:97
  163.2 15.8 %collective-permute-start.12 = (bf16[128,2048]{1,0:T(8,128)(2,1)S(1)}, bf16[128,2048]{1,0:T(8,128)(2,1)S(1)}, u32[]{:S(2)}, u32[]{:S(2)}) collective-permute-start(bf16[128,2048]{1,0:T(8,128)(2,1)S(1)} %get-tuple-element.38), channel_id=1, source_target_pairs={{0,32},{32,64},{64,96},{96,0},{1,33},{33,65},{65,97},{97,1},{2,34}... | collective-permute-start | bytes 1572872 | tf_op jit(solution)/shard_map/ppermute | solution.py:96
  168.6 17.0 %collective-permute-start.18 = (bf16[64,2048]{1,0:T(8,128)(2,1)}, bf16[64,2048]{1,0:T(8,128)(2,1)}, u32[]{:S(2)}, u32[]{:S(2)}) collective-permute-start(bf16[64,2048]{1,0:T(8,128)(2,1)} %add_convert_fusion.1), channel_id=1, source_target_pairs={{0,128},{128,0},{1,129},{129,1},{2,130},{130,2},{3,131},{131,3},{4... | collective-permute-start | bytes 786440 | tf_op jit(solution)/shard_map/ppermute | solution.py:40
  179.0 1.1 copy-start.11
  179.0 4.3 %copy-start.10 = (bf16[128,2048]{1,0:T(8,128)(2,1)}, bf16[128,2048]{1,0:T(8,128)(2,1)S(1)}, u32[]{:S(2)}) copy-start(bf16[128,2048]{1,0:T(8,128)(2,1)S(1)} %collective-permute-done.12) | copy-start | bytes 1572868
  180.0 7.3 %collective-permute-start.14 = (bf16[64,2048]{1,0:T(8,128)(2,1)}, bf16[64,2048]{1,0:T(8,128)(2,1)}, u32[]{:S(2)}, u32[]{:S(2)}) collective-permute-start(bf16[64,2048]{1,0:T(8,128)(2,1)} %get-tuple-element.18), channel_id=1, source_target_pairs={{0,96},{32,0},{64,32},{96,64},{1,97},{33,1},{65,33},{97,65},{2,98}... | collective-permute-start | bytes 786440 | tf_op jit(solution)/shard_map/ppermute | solution.py:102
  184.8 7.1 %collective-permute-start.20 = (bf16[64,2048]{1,0:T(8,128)(2,1)}, bf16[64,2048]{1,0:T(8,128)(2,1)S(1)}, u32[]{:S(2)}, u32[]{:S(2)}) collective-permute-start(bf16[64,2048]{1,0:T(8,128)(2,1)} %get-tuple-element.20), channel_id=1, source_target_pairs={{0,32},{32,64},{64,96},{96,0},{1,33},{33,65},{65,97},{97,1},{2,34}... | collective-permute-start | bytes 786440 | tf_op jit(solution)/shard_map/ppermute | solution.py:101
  184.9 12.6 %collective-permute-start.13 = (bf16[64,2048]{1,0:T(8,128)(2,1)}, bf16[64,2048]{1,0:T(8,128)(2,1)S(1)}, u32[]{:S(2)}, u32[]{:S(2)}) collective-permute-start(bf16[64,2048]{1,0:T(8,128)(2,1)} %get-tuple-element.17), channel_id=1, source_target_pairs={{0,32},{32,64},{64,96},{96,0},{1,33},{33,65},{65,97},{97,1},{2,34}... | collective-permute-start | bytes 786440 | tf_op jit(solution)/shard_map/ppermute | solution.py:101
  188.6 17.2 %collective-permute-start.19 = (bf16[64,2048]{1,0:T(8,128)(2,1)S(1)}, bf16[64,2048]{1,0:T(8,128)(2,1)S(1)}, u32[]{:S(2)}, u32[]{:S(2)}) collective-permute-start(bf16[64,2048]{1,0:T(8,128)(2,1)S(1)} %add_convert_fusion), channel_id=1, source_target_pairs={{0,128},{128,0},{1,129},{129,1},{2,130},{130,2},{3,131},{131,3},{4... | collective-permute-start | bytes 786440 | tf_op jit(solution)/shard_map/ppermute | solution.py:40

commit v8 on v7

--- a/solution.py
+++ b/solution.py
@@ -41,11 +41,10 @@
 
 
 def gelu_and_slope(values):
-    tangent = jnp.tanh(coeff * (values + 0.044715 * values * values * values))
-    value = 0.5 * values * (1.0 + tangent)
-    slope = 0.5 * (1.0 + tangent) + 0.5 * values * (1.0 - tangent * tangent) * coeff * (
-        1.0 + 3.0 * 0.044715 * values * values
-    )
+    square = values * values
+    share = 0.5 * jnp.tanh(coeff * values * (1.0 + 0.044715 * square)) + 0.5
+    value = values * share
+    slope = share + 2.0 * share * (1.0 - share) * values * coeff * (1.0 + 3.0 * 0.044715 * square)
     return lax.optimization_barrier((value.astype(jnp.bfloat16), slope))
 
 
@@ -84,23 +83,37 @@
     return [own, from_partner(other, "core")]
 
 
-def over_y(partial, late):
+def along_y(message, step):
     n_y = lax.axis_size("y")
-    up = [(i, (i + 1) % n_y) for i in range(n_y)]
-    down = [(i, (i - 1) % n_y) for i in range(n_y)]
-    few = partial.shape[0] // len(LEAVING)
-
-    def wide(array, place):
-        return array[place * few : (place + 1) * few].astype(jnp.float32)
-
-    risen = lax.ppermute(partial[: 2 * few], "y", up)
-    sunk = lax.ppermute(partial[2 * few : 4 * few], "y", down)
-    on_up = (wide(partial, 6) + wide(risen, 0) + late).astype(jnp.bfloat16)
-    on_down = (wide(partial, 7) + wide(sunk, 0) + late).astype(jnp.bfloat16)
-    on_up, on_down = lax.optimization_barrier((on_up, on_down))
-    kept = wide(partial, 4) + wide(sunk, 1) + wide(lax.ppermute(on_up, "y", up), 0)
-    other = wide(partial, 5) + wide(risen, 1) + wide(lax.ppermute(on_down, "y", down), 0)
-    return kept, other
+    return lax.ppermute(message, "y", [(i, (i + step) % n_y) for i in range(n_y)])
+
+
+def runs(array, *places):
+    few = D // 2 // len(LEAVING)
+    return [array[place * few : (place + 1) * few].astype(jnp.float32) for place in places]
+
+
+def first_step(partial, wide):
+    few = D // 2 // len(LEAVING)
+    sizes = 2 * few if wide else few
+    return along_y(partial[:sizes], 1), along_y(partial[2 * few : 2 * few + sizes], -1)
+
+
+def second_step(partial, risen, sunk, late, wide):
+    up_later, up, down_later, down, kept, other, near_up, near_down = runs(partial, *range(8))
+    near_up = near_up + runs(risen, 0)[0] + late[0]
+    near_down = near_down + runs(sunk, 0)[0] + late[1]
+    if wide:
+        near_down = near_down + nothing(runs(risen, 0)[0])
+        up, down = runs(risen, 1)[0], runs(sunk, 1)[0]
+        near_up = runs(along_y(near_up.astype(jnp.bfloat16), 1), 0)[0]
+        near_down = runs(along_y(near_down.astype(jnp.bfloat16), -1), 0)[0]
+    else:
+        above = along_y(jnp.concatenate([near_up, up]).astype(jnp.bfloat16), 1)
+        below = along_y(jnp.concatenate([near_down, down]).astype(jnp.bfloat16), -1)
+        near_up, up = runs(above, 0, 1)
+        near_down, down = runs(below, 0, 1)
+    return kept + near_up + down, other + near_down + up
 
 
 def nothing(value):
@@ -114,10 +127,10 @@
     ).astype(jnp.bfloat16)
 
 
-def summed_over_dp(partial, late_y, late_z):
-    kept, other = over_y(partial, late_y)
-    arrived = from_partner((other + late_z).astype(jnp.bfloat16), "z_hi")
-    return kept + arrived.astype(jnp.float32), nothing(arrived[0, 0])
+def over_z(sums, late):
+    kept, other = sums
+    arrived = from_partner((other + late).astype(jnp.bfloat16), "z_hi")
+    return kept + arrived.astype(jnp.float32), nothing(arrived)
 
 
 def shards(
@@ -189,9 +202,12 @@
             embedded = tokens.astype(jnp.float32) + perturb
             emb_bf = (emb + delta_whole * token_scale).astype(jnp.bfloat16)
     partial_in = partial_over_chip(lefts_in, rights_in)
-    there = nothing(partial_in[0, 0])
-    summed_out, there = summed_over_dp(partial_out, there, there)
-    summed_in, _ = summed_over_dp(partial_in, 0.0, there)
+    sent_out, sent_in = first_step(partial_out, True), first_step(partial_in, False)
+    there = [nothing(message) for message in sent_in]
+    sums_out = second_step(partial_out, *sent_out, there, True)
+    sums_in = second_step(partial_in, *sent_in, (0.0, 0.0), False)
+    summed_out, there = over_z(sums_out, 0.0)
+    summed_in, _ = over_z(sums_in, there)
     summed_out = summed_out.T
     dp_rows = moment_in.shape[0]
     offset = lax.axis_index(DP) * dp_rows

time: 212 us -> 212 us (level); the launches traced: 208 us -> 210 us
    ppermute x11, waiting for transfers between devices: 9.83 us -> 15.6 us  [from_partner(): return lax.ppermute(array, axis, [(0, 1), (1, 0)])]
    ppermute x8, waiting for transfers between devices: 22.5 us -> 18.7 us  [along_y(): lax.ppermute(message, 'y', [(i, (i + step) % n_y) for i in range(n_y)])]
    ppermute x8, starting transfers between devices: 15.1 us -> 18.3 us  [along_y(): lax.ppermute(message, 'y', [(i, (i + step) % n_y) for i in range(n_y)])]
    ppermute x2, starting transfers between devices: 4.58 us -> 2.03 us  [over_neighbours(): swaps.append(lax.ppermute(sums, BLOCKS, pairs + [(j, i) for i, j in pairs]))]
  transfers between devices with their start and end apart: 25 -> 25, of which waited for: 13 -> 14; matrix products, arithmetic and copies ran while one was open for 11% -> 11% of each run, Pallas kernels for 0% -> 0%
where the time goes in v8:
time: 212 us; the launch traced here: 210 us
  starting transfers between devices  61.4 us (29%)
  waiting for transfers between devices  56.6 us (27%)
  blocking collectives  42.8 us (20%)
  matrix products  28.3 us (13%)
  other arithmetic  12.7 us (6%)
  local copies, waits for them, and re-layouts  6.85 us (3%)
    all_to_all x3, blocking collectives, to_peers(): return lax.all_to_all(blocks, axis, 0, 0, tiled=True)  42.8 us
    all_to_all x4, starting transfers between devices, to_peers(): return lax.all_to_all(blocks, axis, 0, 0, tiled=True)  22.1 us
    all_to_all x4, waiting for transfers between devices, to_peers(): return lax.all_to_all(blocks, axis, 0, 0, tiled=True)  22.1 us
    ppermute x11, starting transfers between devices, from_partner(): return lax.ppermute(array, axis, [(0, 1), (1, 0)])  18.9 us
    ppermute x8, waiting for transfers between devices, along_y(): lax.ppermute(message, 'y', [(i, (i + step) % n_y) for i in range(n_y)])  18.7 us
    ppermute x8, starting transfers between devices, along_y(): lax.ppermute(message, 'y', [(i, (i + step) % n_y) for i in range(n_y)])  18.3 us
    ppermute x11, waiting for transfers between devices, from_partner(): return lax.ppermute(array, axis, [(0, 1), (1, 0)])  15.6 us
    dot_general x2, matrix products, shards(): preact = jnp.dot(normed, weight_in, preferred_element_type=jnp.float32)  8.43 us
  transfers between devices with their start and end apart: 25, of which 14 were waited for; matrix products, arithmetic and copies ran while one was open for 11% of the time, Pallas kernels for 0%

profile of v8, /device:TPU:33, one launch (start us, length us, event | category | flops | bytes accessed | tf_op | source)
XLA Modules:
  0.0 210.5 jit_solution(3157545096807245195)
XLA Ops:
  0.6 0.8 fusion.85
  1.5 15.8 %all_to_all.35 = bf16[16,128,64]{1,2,0:T(8,128)(2,1)S(1)} all-to-all(bf16[16,128,64]{1,2,0:T(8,128)(2,1)S(1)} %broadcast_in_dim.100), channel_id=1, replica_groups=mesh['z_hi'=2,'y'=4,'core'=2,'x'=4,'z_lo'=4] {'x','z_lo'}, dimensions={0} | all-to-all | bytes 524288 | tf_op jit(solution)/shard_map/all_to_all | solution.py:22
  17.6 3.7 %multiply_add_fusion.2 = (f32[128,2048]{1,0:T(8,128)S(1)}, bf16[128,2048]{1,0:T(8,128)(2,1)S(1)}) fusion(bf16[1024,2048]{1,0:T(8,128)(2,1)} %param.14, bf16[128,1024]{1,0:T(8,128)(2,1)S(1)} %copy.26, f32[1024]{0:T(1024)} %param.13, f32[128]{0:T(128)S(1)} %add_rsqrt_fusion.1), kind=kOutput, calls=%fused_computation.43 | convolution fusion | flops 542113792 | bytes 6033920 | tf_op jit(solution)/shard_map/dot_general | solution.py:157
  21.4 0.7 convolution_convert_fusion.3
  22.3 13.8 %all_to_all.36 = bf16[16,128,64]{1,2,0:T(8,128)(2,1)S(1)} all-to-all(bf16[16,128,64]{1,2,0:T(8,128)(2,1)S(1)} %bitcast.63), channel_id=1, replica_groups=mesh['z_hi'=2,'y'=4,'core'=2,'x'=4,'z_lo'=4] {'x','z_lo'}, dimensions={0} | all-to-all | bytes 524288 | tf_op jit(solution)/shard_map/all_to_all | solution.py:22
  36.2 13.2 %all_to_all.37 = bf16[16,128,64]{1,2,0:T(8,128)(2,1)S(1)} all-to-all(bf16[16,128,64]{1,2,0:T(8,128)(2,1)S(1)} %broadcast_in_dim.117), channel_id=1, replica_groups=mesh['z_hi'=2,'y'=4,'core'=2,'x'=4,'z_lo'=4] {'x','z_lo'}, dimensions={0} | all-to-all | bytes 524288 | tf_op jit(solution)/shard_map/all_to_all | solution.py:22
  49.4 3.7 %fusion = bf16[128,2048]{1,0:T(8,128)(2,1)S(1)} fusion(f32[128,2048]{1,0:T(8,128)S(1)} %get-tuple-element.10, bf16[128,1024]{0,1:T(8,128)(2,1)S(1)} %bitcast.55, bf16[2048,1024]{1,0:T(8,128)(2,1)} %param.15), kind=kOutput, calls=%fused_computation.4 | convolution fusion | flops 537395200 | bytes 6029312 | tf_op jit(solution)/shard_map/dot_general | solution.py:170
  53.2 1.6 fusion.116
  55.0 0.7 pad_maximum_fusion.2
  55.8 5.6 %all-to-all-start.3 = ((bf16[16,128,66]{1,2,0:T(8,128)(2,1)}), bf16[16,128,66]{1,2,0:T(8,128)(2,1)S(1)}, u32[]{:S(2)}, u32[]{:S(2)}) async-start(bf16[16,128,66]{1,2,0:T(8,128)(2,1)} %pad_maximum_fusion.2), calls=%async_computation.3 | async-start | bytes 589824 | tf_op jit(solution)/shard_map/all_to_all | solution.py:22
  61.4 8.0 %all-to-all-done.3 = bf16[16,128,66]{1,2,0:T(8,128)(2,1)S(1)} async-done(((bf16[16,128,66]{1,2,0:T(8,128)(2,1)}), bf16[16,128,66]{1,2,0:T(8,128)(2,1)S(1)}, u32[]{:S(2)}, u32[]{:S(2)}) %all-to-all-start.3) | async-done | bytes 270368 | tf_op jit(solution)/shard_map/all_to_all | solution.py:22
  69.6 0.8 broadcast_in_dim.119
  70.3 6.1 %all-to-all-start.4 = ((bf16[16,128,64]{1,2,0:T(8,128)(2,1)}), bf16[16,128,64]{1,2,0:T(8,128)(2,1)S(1)}, u32[]{:S(2)}, u32[]{:S(2)}) async-start(bf16[16,128,64]{1,2,0:T(8,128)(2,1)} %broadcast_in_dim.119), calls=%async_computation.4 | async-start | bytes 524288 | tf_op jit(solution)/shard_map/all_to_all | solution.py:22
  76.4 0.6 select_add_fusion
  77.0 7.2 %all-to-all-done.4 = bf16[16,128,64]{1,2,0:T(8,128)(2,1)S(1)} async-done(((bf16[16,128,64]{1,2,0:T(8,128)(2,1)}), bf16[16,128,64]{1,2,0:T(8,128)(2,1)S(1)}, u32[]{:S(2)}, u32[]{:S(2)}) %all-to-all-start.4) | async-done | bytes 262176 | tf_op jit(solution)/shard_map/all_to_all | solution.py:22
  84.5 2.9 %collective-permute-start.1 = (f32[2,32]{1,0:T(2,128)S(1)}, f32[2,32]{1,0:T(2,128)S(1)}, u32[]{:S(2)}, u32[]{:S(2)}) collective-permute-start(f32[2,32]{1,0:T(2,128)S(1)} %pad_maximum_fusion.3), channel_id=1, source_target_pairs={{0,16},{16,0},{1,17},{17,1},{2,18},{18,2},{3,19},{19,3},{4,20},{20... | collective-permute-start | bytes 776 | tf_op jit(solution)/shard_map/ppermute | solution.py:40
  87.3 0.8 collective-permute-done.1
  88.2 1.4 collective-permute-start.3
  89.5 0.6 collective-permute-start.2
  91.1 4.7 %multiply_add_fusion = (f32[128,2048]{1,0:T(8,128)}, bf16[128,2048]{1,0:T(8,128)(2,1)S(1)}) fusion(bf16[1024,2048]{1,0:T(8,128)(2,1)} %param.14, bf16[128,1024]{1,0:T(8,128)(2,1)S(1)} %fusion.63, f32[128]{0:T(128)S(1)} %add_rsqrt_fusion, f32[1024]{0:T(1024)S(1)} %copy-done.14), kind=kOutput, calls=%fused_computation.40 | convolution fusion | flops 542113792 | bytes 6033920 | tf_op jit(solution)/shard_map/dot_general | solution.py:157
  95.8 0.7 convolution_convert_fusion.2
  96.6 0.8 copy.30
  97.4 4.7 %all-to-all-start.5 = ((bf16[16,128,64]{1,2,0:T(8,128)(2,1)}), bf16[16,128,64]{1,2,0:T(8,128)(2,1)S(1)}, u32[]{:S(2)}, u32[]{:S(2)}) async-start(bf16[16,128,64]{1,2,0:T(8,128)(2,1)} %bitcast.15), calls=%async_computation.5 | async-start | bytes 524288 | tf_op jit(solution)/shard_map/all_to_all | solution.py:22
  102.2 1.9 collective-permute-start.8
  104.0 1.2 fusion.28
  105.3 1.2 fusion.24
  106.4 3.6 %all-to-all-done.5 = bf16[16,128,64]{1,2,0:T(8,128)(2,1)S(1)} async-done(((bf16[16,128,64]{1,2,0:T(8,128)(2,1)}), bf16[16,128,64]{1,2,0:T(8,128)(2,1)S(1)}, u32[]{:S(2)}, u32[]{:S(2)}) %all-to-all-start.5) | async-done | bytes 262176 | tf_op jit(solution)/shard_map/all_to_all | solution.py:22
  110.1 0.7 fusion.81
  110.8 0.8 broadcast_in_dim.120
  111.6 5.7 %all-to-all-start.6 = ((bf16[16,128,64]{1,2,0:T(8,128)(2,1)}), bf16[16,128,64]{1,2,0:T(8,128)(2,1)S(1)}, u32[]{:S(2)}, u32[]{:S(2)}) async-start(bf16[16,128,64]{1,2,0:T(8,128)(2,1)} %broadcast_in_dim.120), calls=%async_computation.6 | async-start | bytes 524288 | tf_op jit(solution)/shard_map/all_to_all | solution.py:22
  117.2 0.5 fusion.30
  117.8 2.1 %collective-permute-start.6 = (bf16[128,512]{1,0:T(8,128)(2,1)S(1)}, bf16[128,512]{1,0:T(8,128)(2,1)S(1)}, u32[]{:S(2)}, u32[]{:S(2)}) collective-permute-start(bf16[128,512]{1,0:T(8,128)(2,1)S(1)} %fusion.30), channel_id=1, source_target_pairs={{0,16},{16,0},{1,17},{17,1},{2,18},{18,2},{3,19},{19,3},{4,20},{20... | collective-permute-start | bytes 393224 | tf_op jit(solution)/shard_map/ppermute | solution.py:40
  119.9 1.2 fusion.26
  121.1 0.5 fusion.29
  121.7 3.3 %all-to-all-done.6 = bf16[16,128,64]{1,2,0:T(8,128)(2,1)S(1)} async-done(((bf16[16,128,64]{1,2,0:T(8,128)(2,1)}), bf16[16,128,64]{1,2,0:T(8,128)(2,1)S(1)}, u32[]{:S(2)}, u32[]{:S(2)}) %all-to-all-start.6) | async-done | bytes 262176 | tf_op jit(solution)/shard_map/all_to_all | solution.py:22
  125.0 0.5 fusion.31
  125.5 2.8 %collective-permute-start.7 = (bf16[128,512]{1,0:T(8,128)(2,1)S(1)}, bf16[128,512]{1,0:T(8,128)(2,1)S(1)}, u32[]{:S(2)}, u32[]{:S(2)}) collective-permute-start(bf16[128,512]{1,0:T(8,128)(2,1)S(1)} %fusion.31), channel_id=1, source_target_pairs={{0,16},{16,0},{1,17},{17,1},{2,18},{18,2},{3,19},{19,3},{4,20},{20... | collective-permute-start | bytes 393224 | tf_op jit(solution)/shard_map/ppermute | solution.py:40
  128.3 0.5 fusion.27
  129.1 0.6 copy-done.22
  129.7 0.8 copy-done.21
  130.5 3.1 %convolution_convert_fusion.1 = bf16[512,2048]{1,0:T(8,128)(2,1)S(1)} fusion(bf16[128,2048]{1,0:T(8,128)(2,1)} %copy-done.21, bf16[128,2048]{1,0:T(8,128)(2,1)} %copy-done.8, bf16[128,2048]{1,0:T(8,128)(2,1)} %collective-permute-done.8, bf16[128,2048]{1,0:T(8,128)(2,1)} %copy-done.6, bf16[128,512]{1,0:T(8,128)(2,1)S(1)} %collective-permute-done.7, ...), kind=kOutput, calls=%fused_computation.1 | convolution fusion | flops 1085276160 | bytes 4718592 | tf_op jit(solution)/shard_map/dot_general | solution.py:125
  134.8 1.5 fusion.1
  137.7 4.1 %collective-permute-start.16 = (bf16[128,2048]{1,0:T(8,128)(2,1)S(1)}, bf16[128,2048]{1,0:T(8,128)(2,1)S(1)}, u32[]{:S(2)}, u32[]{:S(2)}) collective-permute-start(bf16[128,2048]{1,0:T(8,128)(2,1)S(1)} %get-tuple-element.31), channel_id=1, source_target_pairs={{0,32},{32,64},{64,96},{96,0},{1,33},{33,65},{65,97},{97,1},{2,34}... | collective-permute-start | bytes 1572872 | tf_op jit(solution)/shard_map/ppermute | solution.py:88
  141.8 7.2 %collective-permute-start.15 = (bf16[128,2048]{1,0:T(8,128)(2,1)S(1)}, bf16[128,2048]{1,0:T(8,128)(2,1)S(1)}, u32[]{:S(2)}, u32[]{:S(2)}) collective-permute-start(bf16[128,2048]{1,0:T(8,128)(2,1)S(1)} %get-tuple-element.32), channel_id=1, source_target_pairs={{0,96},{32,0},{64,32},{96,64},{1,97},{33,1},{65,33},{97,65},{2,98}... | collective-permute-start | bytes 1572872 | tf_op jit(solution)/shard_map/ppermute | solution.py:88
  149.0 2.2 %convolution_convert_fusion = bf16[512,2048]{1,0:T(8,128)(2,1)S(1)} fusion(bf16[128,2048]{1,0:T(8,128)(2,1)S(1)} %collective-permute-done.10, bf16[128,2048]{1,0:T(8,128)(2,1)S(1)} %fusion.1, bf16[128,2048]{1,0:T(8,128)(2,1)S(1)} %collective-permute-done.5, bf16[128,2048]{1,0:T(8,128)(2,1)S(1)} %fusion, bf16[128,512]{1,0:T(8,128)(2,1)S(1)} %collective-permute-done.4, ...), kind=kOutput, calls=%fused_computation | convolution fusion | flops 1085276160 | bytes 4718592 | tf_op jit(solution)/shard_map/dot_general | solution.py:125
  151.3 1.7 collective-permute-start.13
  153.1 7.9 %collective-permute-done.16 = bf16[128,2048]{1,0:T(8,128)(2,1)S(1)} collective-permute-done((bf16[128,2048]{1,0:T(8,128)(2,1)S(1)}, bf16[128,2048]{1,0:T(8,128)(2,1)S(1)}, u32[]{:S(2)}, u32[]{:S(2)}) %collective-permute-start.16) | collective-permute-done | bytes 524320 | tf_op jit(solution)/shard_map/ppermute | solution.py:88
  161.0 4.7 %collective-permute-done.13 = bf16[64,2048]{1,0:T(8,128)(2,1)S(1)} collective-permute-done((bf16[64,2048]{1,0:T(8,128)(2,1)S(1)}, bf16[64,2048]{1,0:T(8,128)(2,1)S(1)}, u32[]{:S(2)}, u32[]{:S(2)}) %collective-permute-start.13) | collective-permute-done | bytes 262176 | tf_op jit(solution)/shard_map/ppermute | solution.py:88
  165.6 1.0 collective-permute-done.11
  167.0 2.5 %collective-permute-start.17 = (bf16[64,2048]{1,0:T(8,128)(2,1)S(1)}, bf16[64,2048]{1,0:T(8,128)(2,1)S(1)}, u32[]{:S(2)}, u32[]{:S(2)}) collective-permute-start(bf16[64,2048]{1,0:T(8,128)(2,1)S(1)} %get-tuple-element.37), channel_id=1, source_target_pairs={{0,96},{32,0},{64,32},{96,64},{1,97},{33,1},{65,33},{97,65},{2,98}... | collective-permute-start | bytes 786440 | tf_op jit(solution)/shard_map/ppermute | solution.py:88
  169.5 0.8 pad_maximum_fusion
  170.4 0.8 pad_maximum_fusion.1
  171.2 2.7 %collective-permute-start.14 = (bf16[128,2048]{1,0:T(8,128)(2,1)}, bf16[128,2048]{1,0:T(8,128)(2,1)}, u32[]{:S(2)}, u32[]{:S(2)}) collective-permute-start(bf16[128,2048]{1,0:T(8,128)(2,1)} %pad_maximum_fusion.1), channel_id=1, source_target_pairs={{0,96},{32,0},{64,32},{96,64},{1,97},{33,1},{65,33},{97,65},{2,98}... | collective-permute-start | bytes 1572872 | tf_op jit(solution)/shard_map/ppermute | solution.py:88
  174.1 0.8 add_convert_fusion
  174.9 4.3 %collective-permute-start.18 = (bf16[64,2048]{1,0:T(8,128)(2,1)}, bf16[64,2048]{1,0:T(8,128)(2,1)S(1)}, u32[]{:S(2)}, u32[]{:S(2)}) collective-permute-start(bf16[64,2048]{1,0:T(8,128)(2,1)} %add_convert_fusion), channel_id=1, source_target_pairs={{0,128},{128,0},{1,129},{129,1},{2,130},{130,2},{3,131},{131,3},{4... | collective-permute-start | bytes 786440 | tf_op jit(solution)/shard_map/ppermute | solution.py:40
  179.2 1.2 constant_dynamic-slice_fusion
  180.8 3.1 %collective-permute-done.12 = bf16[128,2048]{1,0:T(8,128)(2,1)} collective-permute-done((bf16[128,2048]{1,0:T(8,128)(2,1)}, bf16[128,2048]{1,0:T(8,128)(2,1)}, u32[]{:S(2)}, u32[]{:S(2)}) %collective-permute-start.12) | collective-permute-done | bytes 524320 | tf_op jit(solution)/shard_map/ppermute | solution.py:88
  183.9 1.9 collective-permute-done.14
  185.8 6.5 %collective-permute-done.18 = bf16[64,2048]{1,0:T(8,128)(2,1)S(1)} collective-permute-done((bf16[64,2048]{1,0:T(8,128)(2,1)}, bf16[64,2048]{1,0:T(8,128)(2,1)S(1)}, u32[]{:S(2)}, u32[]{:S(2)}) %collective-permute-start.18) | collective-permute-done | bytes 262176 | tf_op jit(solution)/shard_map/ppermute | solution.py:40
  192.3 1.3 fusion.55
  193.6 4.1 %collective-permute-start.19 = (bf16[64,2048]{1,0:T(8,128)(2,1)S(1)}, bf16[64,2048]{1,0:T(8,128)(2,1)S(1)}, u32[]{:S(2)}, u32[]{:S(2)}) collective-permute-start(bf16[64,2048]{1,0:T(8,128)(2,1)S(1)} %fusion.55), channel_id=1, source_target_pairs={{0,128},{128,0},{1,129},{129,1},{2,130},{130,2},{3,131},{131,3},{4... | collective-permute-start | bytes 786440 | tf_op jit(solution)/shard_map/ppermute | solution.py:40
  197.7 2.2 %subtract_convert_fusion = (bf16[2048,64]{0,1:T(8,128)(2,1)}, f32[2048,64]{0,1:T(8,128)}) fusion(bf16[2048,64]{0,1:T(8,128)(2,1)S(1)} %copy.32, bf16[64,2048]{1,0:T(8,128)(2,1)S(1)} %collective-permute-done.18, bf16[128,2048]{1,0:T(8,128)(2,1)} %copy-done.7, bf16[64,2048]{1,0:T(8,128)(2,1)S(1)} %collective-permute-done.20, ...), kind=kLoop, calls=%fused_computation.109 | loop fusion | flops 1835008 | bytes 2621440 | tf_op jit(solution)/shard_map/convert_element_type | solution.py:219
  199.9 8.2 %collective-permute-done.19 = bf16[64,2048]{1,0:T(8,128)(2,1)S(1)} collective-permute-done((bf16[64,2048]{1,0:T(8,128)(2,1)S(1)}, bf16[64,2048]{1,0:T(8,128)(2,1)S(1)}, u32[]{:S(2)}, u32[]{:S(2)}) %collective-permute-start.19) | collective-permute-done | bytes 262176 | tf_op jit(solution)/shard_map/ppermute | solution.py:40
  208.2 2.3 %subtract_convert_fusion.1 = (bf16[64,2048]{1,0:T(8,128)(2,1)}, f32[64,2048]{1,0:T(8,128)}) fusion(bf16[1024,2048]{1,0:T(8,128)(2,1)} %param.14, s32[]{:T(128)S(6)} %select_n.195, bf16[64,2048]{1,0:T(8,128)(2,1)S(1)} %collective-permute-done.19, bf16[128,2048]{1,0:T(8,128)(2,1)} %collective-permute-done.14, bf16[128,2048]{1,0:T(8,128)(2,1)} %collective-permute-done.12, ...), kind=kLoop, calls=%fused_computation.110 | loop fusion | flops 1835008 | bytes 2621444 | tf_op jit(solution)/shard_map/convert_element_type | solution.py:218
  (108 shorter events, 5.4 us)
Async XLA Ops:
  17.6 3.8 %copy-start = (bf16[2048,1024]{1,0:T(8,128)(2,1)S(1)}, bf16[2048,1024]{1,0:T(8,128)(2,1)}, u32[]{:S(2)}) copy-start(bf16[2048,1024]{1,0:T(8,128)(2,1)} %param.15) | copy-start | bytes 12582916
  21.3 80.9 %copy-start.6 = (bf16[128,2048]{1,0:T(8,128)(2,1)}, bf16[128,2048]{1,0:T(8,128)(2,1)S(1)}, u32[]{:S(2)}) copy-start(bf16[128,2048]{1,0:T(8,128)(2,1)S(1)} %get-tuple-element.9) | copy-start | bytes 1572868
  21.3 14.8 %copy-start.10 = (f32[128,64]{0,1:T(8,128)S(1)}, f32[128,64]{0,1:T(8,128)}, u32[]{:S(2)}) copy-start(f32[128,64]{0,1:T(8,128)} %param.10) | copy-start | bytes 98308
  21.3 14.8 %copy-start.11 = (bf16[128,64]{0,1:T(8,128)(2,1)S(1)}, bf16[128,64]{0,1:T(8,128)(2,1)}, u32[]{:S(2)}) copy-start(bf16[128,64]{0,1:T(8,128)(2,1)} %param.9) | copy-start | bytes 49156
  21.3 14.8 %copy-start.12 = (f32[128,64]{0,1:T(8,128)S(1)}, f32[128,64]{0,1:T(8,128)}, u32[]{:S(2)}) copy-start(f32[128,64]{0,1:T(8,128)} %param.12) | copy-start | bytes 98308
  22.1 31.1 %copy-start.14 = (f32[1024]{0:T(1024)S(1)}, f32[1024]{0:T(1024)}, u32[]{:S(2)}) copy-start(f32[1024]{0:T(1024)} %param.13) | copy-start | bytes 12292
  22.3 30.9 %copy-start.3 = (bf16[1024,2048]{1,0:T(8,128)(2,1)S(1)}, bf16[1024,2048]{1,0:T(8,128)(2,1)}, u32[]{:S(2)}) copy-start(bf16[1024,2048]{1,0:T(8,128)(2,1)} %param.14) | copy-start | bytes 12582916
  53.2 31.2 %copy-start.20 = (s32[128]{0:T(128)S(1)}, s32[128]{0:T(128)}, u32[]{:S(2)}) copy-start(s32[128]{0:T(128)} %param.11) | copy-start | bytes 1540
  55.8 13.6 %all-to-all-start.3 = ((bf16[16,128,66]{1,2,0:T(8,128)(2,1)}), bf16[16,128,66]{1,2,0:T(8,128)(2,1)S(1)}, u32[]{:S(2)}, u32[]{:S(2)}) async-start(bf16[16,128,66]{1,2,0:T(8,128)(2,1)} %pad_maximum_fusion.2), calls=%async_computation.3 | async-start | bytes 589824 | tf_op jit(solution)/shard_map/all_to_all | solution.py:22
  69.5 21.6 %copy-start.15 = (f32[128]{0:T(128)}, f32[128]{0:T(128)S(1)}, u32[]{:S(2)}) copy-start(f32[128]{0:T(128)S(1)} %slice_reduce_fusion) | copy-start | bytes 1540
  70.3 13.9 %all-to-all-start.4 = ((bf16[16,128,64]{1,2,0:T(8,128)(2,1)}), bf16[16,128,64]{1,2,0:T(8,128)(2,1)S(1)}, u32[]{:S(2)}, u32[]{:S(2)}) async-start(bf16[16,128,64]{1,2,0:T(8,128)(2,1)} %broadcast_in_dim.119), calls=%async_computation.4 | async-start | bytes 524288 | tf_op jit(solution)/shard_map/all_to_all | solution.py:22
  84.5 3.7 %collective-permute-start.1 = (f32[2,32]{1,0:T(2,128)S(1)}, f32[2,32]{1,0:T(2,128)S(1)}, u32[]{:S(2)}, u32[]{:S(2)}) collective-permute-start(f32[2,32]{1,0:T(2,128)S(1)} %pad_maximum_fusion.3), channel_id=1, source_target_pairs={{0,16},{16,0},{1,17},{17,1},{2,18},{18,2},{3,19},{19,3},{4,20},{20... | collective-permute-start | bytes 776 | tf_op jit(solution)/shard_map/ppermute | solution.py:40
  88.2 2.5 %collective-permute-start.3 = (f32[2,32]{1,0:T(2,128)S(1)}, f32[2,32]{1,0:T(2,128)S(1)}, u32[]{:S(2)}, u32[]{:S(2)}) collective-permute-start(f32[2,32]{1,0:T(2,128)S(1)} %fusion.103), channel_id=1, source_target_pairs={{0,32},{64,96},{128,160},{192,224},{32,0},{96,64},{160,128},{224,1... | collective-permute-start | bytes 776 | tf_op jit(solution)/shard_map/ppermute | solution.py:57
  89.5 1.1 collective-permute-start.2
  91.1 30.1 %copy-start.23 = (f32[128]{0:T(128)}, f32[128]{0:T(128)S(1)}, u32[]{:S(2)}) copy-start(f32[128]{0:T(128)S(1)} %add_rsqrt_fusion) | copy-start | bytes 1540
  91.1 4.7 %copy-start.1 = (bf16[2048,1024]{1,0:T(8,128)(2,1)S(1)}, bf16[2048,1024]{1,0:T(8,128)(2,1)}, u32[]{:S(2)}) copy-start(bf16[2048,1024]{1,0:T(8,128)(2,1)} %param.15) | copy-start | bytes 12582916
  95.8 25.3 %copy-start.8 = (bf16[128,2048]{1,0:T(8,128)(2,1)}, bf16[128,2048]{1,0:T(8,128)(2,1)S(1)}, u32[]{:S(2)}) copy-start(bf16[128,2048]{1,0:T(8,128)(2,1)S(1)} %get-tuple-element.11) | copy-start | bytes 1572868
  95.8 8.2 %copy-start.17 = (s32[512]{0:T(512)S(1)}, s32[512]{0:T(512)}, u32[]{:S(2)}) copy-start(s32[512]{0:T(512)} %select_add_fusion) | copy-start | bytes 6148
  95.8 14.3 %copy-start.13 = (f32[128,64]{0,1:T(8,128)S(1)}, f32[128,64]{0,1:T(8,128)}, u32[]{:S(2)}) copy-start(f32[128,64]{0,1:T(8,128)} %param.12) | copy-start | bytes 98308
  95.8 14.3 %copy-start.16 = (f32[128]{0:T(128)S(1)}, f32[128]{0:T(128)}, u32[]{:S(2)}) copy-start(f32[128]{0:T(128)} %copy-done.15) | copy-start | bytes 1540
  97.4 12.6 %all-to-all-start.5 = ((bf16[16,128,64]{1,2,0:T(8,128)(2,1)}), bf16[16,128,64]{1,2,0:T(8,128)(2,1)S(1)}, u32[]{:S(2)}, u32[]{:S(2)}) async-start(bf16[16,128,64]{1,2,0:T(8,128)(2,1)} %bitcast.15), calls=%async_computation.5 | async-start | bytes 524288 | tf_op jit(solution)/shard_map/all_to_all | solution.py:22
  102.2 26.7 %copy-start.18 = (s32[512]{0:T(512)}, s32[512]{0:T(512)S(1)}, u32[]{:S(2)}) copy-start(s32[512]{0:T(512)S(1)} %select_add_fusion.1) | copy-start | bytes 6148
  102.2 26.8 %collective-permute-start.8 = (bf16[128,2048]{1,0:T(8,128)(2,1)S(1)}, bf16[128,2048]{1,0:T(8,128)(2,1)}, u32[]{:S(2)}, u32[]{:S(2)}) collective-permute-start(bf16[128,2048]{1,0:T(8,128)(2,1)S(1)} %get-tuple-element.9), channel_id=1, source_target_pairs={{0,16},{16,0},{1,17},{17,1},{2,18},{18,2},{3,19},{19,3},{4,20},{20... | collective-permute-start | bytes 1572872 | tf_op jit(solution)/shard_map/ppermute | solution.py:40
  105.2 36.6 %collective-permute-start = (bf16[128,512]{1,0:T(8,128)(2,1)}, bf16[128,512]{1,0:T(8,128)(2,1)}, u32[]{:S(2)}, u32[]{:S(2)}) collective-permute-start(bf16[128,512]{1,0:T(8,128)(2,1)} %fusion.28), channel_id=1, source_target_pairs={{0,16},{16,0},{1,17},{17,1},{2,18},{18,2},{3,19},{19,3},{4,20},{20... | collective-permute-start | bytes 393224 | tf_op jit(solution)/shard_map/ppermute | solution.py:40
  111.6 13.4 %all-to-all-start.6 = ((bf16[16,128,64]{1,2,0:T(8,128)(2,1)}), bf16[16,128,64]{1,2,0:T(8,128)(2,1)S(1)}, u32[]{:S(2)}, u32[]{:S(2)}) async-start(bf16[16,128,64]{1,2,0:T(8,128)(2,1)} %broadcast_in_dim.120), calls=%async_computation.6 | async-start | bytes 524288 | tf_op jit(solution)/shard_map/all_to_all | solution.py:22
  117.8 11.3 %collective-permute-start.6 = (bf16[128,512]{1,0:T(8,128)(2,1)S(1)}, bf16[128,512]{1,0:T(8,128)(2,1)S(1)}, u32[]{:S(2)}, u32[]{:S(2)}) collective-permute-start(bf16[128,512]{1,0:T(8,128)(2,1)S(1)} %fusion.30), channel_id=1, source_target_pairs={{0,16},{16,0},{1,17},{17,1},{2,18},{18,2},{3,19},{19,3},{4,20},{20... | collective-permute-start | bytes 393224 | tf_op jit(solution)/shard_map/ppermute | solution.py:40
  121.1 7.9 %collective-permute-start.9 = (bf16[128,2048]{1,0:T(8,128)(2,1)S(1)}, bf16[128,2048]{1,0:T(8,128)(2,1)S(1)}, u32[]{:S(2)}, u32[]{:S(2)}) collective-permute-start(bf16[128,2048]{1,0:T(8,128)(2,1)S(1)} %get-tuple-element.11), channel_id=1, source_target_pairs={{0,16},{16,0},{1,17},{17,1},{2,18},{18,2},{3,19},{19,3},{4,20},{20... | collective-permute-start | bytes 1572872 | tf_op jit(solution)/shard_map/ppermute | solution.py:40
  125.5 5.0 %collective-permute-start.7 = (bf16[128,512]{1,0:T(8,128)(2,1)S(1)}, bf16[128,512]{1,0:T(8,128)(2,1)S(1)}, u32[]{:S(2)}, u32[]{:S(2)}) collective-permute-start(bf16[128,512]{1,0:T(8,128)(2,1)S(1)} %fusion.31), channel_id=1, source_target_pairs={{0,16},{16,0},{1,17},{17,1},{2,18},{18,2},{3,19},{19,3},{4,20},{20... | collective-permute-start | bytes 393224 | tf_op jit(solution)/shard_map/ppermute | solution.py:40
  128.9 5.9 %copy-start.2 = (bf16[2048,1024]{1,0:T(8,128)(2,1)S(1)}, bf16[2048,1024]{1,0:T(8,128)(2,1)}, u32[]{:S(2)}) copy-start(bf16[2048,1024]{1,0:T(8,128)(2,1)} %param.15) | copy-start | bytes 12582916
  128.9 5.9 %copy-start.5 = (f32[128,2048]{1,0:T(8,128)S(1)}, f32[128,2048]{1,0:T(8,128)}, u32[]{:S(2)}) copy-start(f32[128,2048]{1,0:T(8,128)} %get-tuple-element.12) | copy-start | bytes 3145732
  128.9 20.1 %collective-permute-start.5 = (bf16[128,2048]{1,0:T(8,128)(2,1)S(1)}, bf16[128,2048]{1,0:T(8,128)(2,1)S(1)}, u32[]{:S(2)}, u32[]{:S(2)}) collective-permute-start(bf16[128,2048]{1,0:T(8,128)(2,1)S(1)} %fusion), channel_id=1, source_target_pairs={{0,16},{16,0},{1,17},{17,1},{2,18},{18,2},{3,19},{19,3},{4,20},{20... | collective-permute-start | bytes 1572872 | tf_op jit(solution)/shard_map/ppermute | solution.py:40
  129.0 0.7 copy-start.22
  129.7 0.8 copy-start.21
  133.6 3.1 %copy-start.19 = (s32[512]{0:T(512)S(1)}, s32[512]{0:T(512)}, u32[]{:S(2)}) copy-start(s32[512]{0:T(512)} %copy-done.18) | copy-start | bytes 6148
  133.6 3.1 %copy-start.24 = (f32[128]{0:T(128)S(1)}, f32[128]{0:T(128)}, u32[]{:S(2)}) copy-start(f32[128]{0:T(128)} %copy-done.23) | copy-start | bytes 1540
  134.8 14.2 %copy-start.25 = (bf16[128,512]{1,0:T(8,128)(2,1)S(1)}, bf16[128,512]{1,0:T(8,128)(2,1)}, u32[]{:S(2)}) copy-start(bf16[128,512]{1,0:T(8,128)(2,1)} %fusion.24) | copy-start | bytes 393220
  136.4 12.6 %collective-permute-start.10 = (bf16[128,2048]{1,0:T(8,128)(2,1)S(1)}, bf16[128,2048]{1,0:T(8,128)(2,1)S(1)}, u32[]{:S(2)}, u32[]{:S(2)}) collective-permute-start(bf16[128,2048]{1,0:T(8,128)(2,1)S(1)} %fusion.1), channel_id=1, source_target_pairs={{0,16},{16,0},{1,17},{17,1},{2,18},{18,2},{3,19},{19,3},{4,20},{20... | collective-permute-start | bytes 1572872 | tf_op jit(solution)/shard_map/ppermute | solution.py:40
  137.3 11.7 %collective-permute-start.4 = (bf16[128,512]{1,0:T(8,128)(2,1)S(1)}, bf16[128,512]{1,0:T(8,128)(2,1)S(1)}, u32[]{:S(2)}, u32[]{:S(2)}) collective-permute-start(bf16[128,512]{1,0:T(8,128)(2,1)S(1)} %fusion.29), channel_id=1, source_target_pairs={{0,16},{16,0},{1,17},{17,1},{2,18},{18,2},{3,19},{19,3},{4,20},{20... | collective-permute-start | bytes 393224 | tf_op jit(solution)/shard_map/ppermute | solution.py:40
  137.7 23.3 %collective-permute-start.16 = (bf16[128,2048]{1,0:T(8,128)(2,1)S(1)}, bf16[128,2048]{1,0:T(8,128)(2,1)S(1)}, u32[]{:S(2)}, u32[]{:S(2)}) collective-permute-start(bf16[128,2048]{1,0:T(8,128)(2,1)S(1)} %get-tuple-element.31), channel_id=1, source_target_pairs={{0,32},{32,64},{64,96},{96,0},{1,33},{33,65},{65,97},{97,1},{2,34}... | collective-permute-start | bytes 1572872 | tf_op jit(solution)/shard_map/ppermute | solution.py:88
  141.8 19.1 %collective-permute-start.15 = (bf16[128,2048]{1,0:T(8,128)(2,1)S(1)}, bf16[128,2048]{1,0:T(8,128)(2,1)S(1)}, u32[]{:S(2)}, u32[]{:S(2)}) collective-permute-start(bf16[128,2048]{1,0:T(8,128)(2,1)S(1)} %get-tuple-element.32), channel_id=1, source_target_pairs={{0,96},{32,0},{64,32},{96,64},{1,97},{33,1},{65,33},{97,65},{2,98}... | collective-permute-start | bytes 1572872 | tf_op jit(solution)/shard_map/ppermute | solution.py:88
  151.2 23.7 %copy-start.4 = (bf16[512,2048]{1,0:T(8,128)(2,1)}, bf16[512,2048]{1,0:T(8,128)(2,1)S(1)}, u32[]{:S(2)}) copy-start(bf16[512,2048]{1,0:T(8,128)(2,1)S(1)} %convolution_convert_fusion) | copy-start | bytes 6291460
  151.3 14.3 %collective-permute-start.13 = (bf16[64,2048]{1,0:T(8,128)(2,1)S(1)}, bf16[64,2048]{1,0:T(8,128)(2,1)S(1)}, u32[]{:S(2)}, u32[]{:S(2)}) collective-permute-start(bf16[64,2048]{1,0:T(8,128)(2,1)S(1)} %get-tuple-element.28), channel_id=1, source_target_pairs={{0,96},{32,0},{64,32},{96,64},{1,97},{33,1},{65,33},{97,65},{2,98}... | collective-permute-start | bytes 786440 | tf_op jit(solution)/shard_map/ppermute | solution.py:88
  153.0 13.6 %collective-permute-start.11 = (bf16[64,2048]{1,0:T(8,128)(2,1)S(1)}, bf16[64,2048]{1,0:T(8,128)(2,1)S(1)}, u32[]{:S(2)}, u32[]{:S(2)}) collective-permute-start(bf16[64,2048]{1,0:T(8,128)(2,1)S(1)} %get-tuple-element.30), channel_id=1, source_target_pairs={{0,32},{32,64},{64,96},{96,0},{1,33},{33,65},{65,97},{97,1},{2,34}... | collective-permute-start | bytes 786440 | tf_op jit(solution)/shard_map/ppermute | solution.py:88
  161.0 13.1 %copy-start.7 = (bf16[128,2048]{1,0:T(8,128)(2,1)}, bf16[128,2048]{1,0:T(8,128)(2,1)S(1)}, u32[]{:S(2)}) copy-start(bf16[128,2048]{1,0:T(8,128)(2,1)S(1)} %collective-permute-done.15) | copy-start | bytes 1572868
  167.0 7.1 %collective-permute-start.17 = (bf16[64,2048]{1,0:T(8,128)(2,1)S(1)}, bf16[64,2048]{1,0:T(8,128)(2,1)S(1)}, u32[]{:S(2)}, u32[]{:S(2)}) collective-permute-start(bf16[64,2048]{1,0:T(8,128)(2,1)S(1)} %get-tuple-element.37), channel_id=1, source_target_pairs={{0,96},{32,0},{64,32},{96,64},{1,97},{33,1},{65,33},{97,65},{2,98}... | collective-permute-start | bytes 786440 | tf_op jit(solution)/shard_map/ppermute | solution.py:88
  170.4 13.5 %collective-permute-start.12 = (bf16[128,2048]{1,0:T(8,128)(2,1)}, bf16[128,2048]{1,0:T(8,128)(2,1)}, u32[]{:S(2)}, u32[]{:S(2)}) collective-permute-start(bf16[128,2048]{1,0:T(8,128)(2,1)} %pad_maximum_fusion), channel_id=1, source_target_pairs={{0,32},{32,64},{64,96},{96,0},{1,33},{33,65},{65,97},{97,1},{2,34}... | collective-permute-start | bytes 1572872 | tf_op jit(solution)/shard_map/ppermute | solution.py:88
  171.2 14.6 %collective-permute-start.14 = (bf16[128,2048]{1,0:T(8,128)(2,1)}, bf16[128,2048]{1,0:T(8,128)(2,1)}, u32[]{:S(2)}, u32[]{:S(2)}) collective-permute-start(bf16[128,2048]{1,0:T(8,128)(2,1)} %pad_maximum_fusion.1), channel_id=1, source_target_pairs={{0,96},{32,0},{64,32},{96,64},{1,97},{33,1},{65,33},{97,65},{2,98}... | collective-permute-start | bytes 1572872 | tf_op jit(solution)/shard_map/ppermute | solution.py:88
  174.9 17.4 %collective-permute-start.18 = (bf16[64,2048]{1,0:T(8,128)(2,1)}, bf16[64,2048]{1,0:T(8,128)(2,1)S(1)}, u32[]{:S(2)}, u32[]{:S(2)}) collective-permute-start(bf16[64,2048]{1,0:T(8,128)(2,1)} %add_convert_fusion), channel_id=1, source_target_pairs={{0,128},{128,0},{1,129},{129,1},{2,130},{130,2},{3,131},{131,3},{4... | collective-permute-start | bytes 786440 | tf_op jit(solution)/shard_map/ppermute | solution.py:40
  180.7 27.5 %copy-start.9 = (f32[64,2048]{1,0:T(8,128)S(1)}, f32[64,2048]{1,0:T(8,128)}, u32[]{:S(2)}) copy-start(f32[64,2048]{1,0:T(8,128)} %param.16) | copy-start | bytes 1572868
  180.7 17.0 %collective-permute-start.20 = (bf16[64,2048]{1,0:T(8,128)(2,1)S(1)}, bf16[64,2048]{1,0:T(8,128)(2,1)S(1)}, u32[]{:S(2)}, u32[]{:S(2)}) collective-permute-start(bf16[64,2048]{1,0:T(8,128)(2,1)S(1)} %get-tuple-element.38), channel_id=1, source_target_pairs={{0,32},{32,64},{64,96},{96,0},{1,33},{33,65},{65,97},{97,1},{2,34}... | collective-permute-start | bytes 786440 | tf_op jit(solution)/shard_map/ppermute | solution.py:88
  193.6 14.6 %collective-permute-start.19 = (bf16[64,2048]{1,0:T(8,128)(2,1)S(1)}, bf16[64,2048]{1,0:T(8,128)(2,1)S(1)}, u32[]{:S(2)}, u32[]{:S(2)}) collective-permute-start(bf16[64,2048]{1,0:T(8,128)(2,1)S(1)} %fusion.55), channel_id=1, source_target_pairs={{0,128},{128,0},{1,129},{129,1},{2,130},{130,2},{3,131},{131,3},{4... | collective-permute-start | bytes 786440 | tf_op jit(solution)/shard_map/ppermute | solution.py:40

commit v9 on v8

--- a/solution.py
+++ b/solution.py
@@ -101,8 +101,8 @@
 
 def second_step(partial, risen, sunk, late, wide):
     up_later, up, down_later, down, kept, other, near_up, near_down = runs(partial, *range(8))
-    near_up = near_up + runs(risen, 0)[0] + late[0]
-    near_down = near_down + runs(sunk, 0)[0] + late[1]
+    near_up = near_up + runs(lax.optimization_barrier(risen), 0)[0] + late[0]
+    near_down = near_down + runs(sunk, 0)[0]
     if wide:
         near_down = near_down + nothing(runs(risen, 0)[0])
         up, down = runs(risen, 1)[0], runs(sunk, 1)[0]
@@ -165,7 +165,7 @@
         lefts_out += for_both_cores(grad, orders)
         if last:
             partial_out = partial_over_chip(lefts_out, rights_out)
-            slope = slope + nothing(partial_out[0, 0])
+            slope = slope + nothing(partial_out[:local_tokens])
         hidden_grad = (
             jnp.dot(grad, weight_out.T, preferred_element_type=jnp.float32) * slope
         ).astype(jnp.bfloat16)

time: 212 us -> 212 us (level)
  the two profiles are of different devices: /device:TPU:33 before, /device:TPU:1 now
where the time goes in v9:
time: 212 us; the launch traced here: 211 us
  waiting for transfers between devices  68.8 us (32%)
  starting transfers between devices  48 us (23%)
  blocking collectives  45.6 us (22%)
  matrix products  28.3 us (13%)
  other arithmetic  12.6 us (6%)
  local copies, waits for them, and re-layouts  6.36 us (3%)
    all_to_all x3, blocking collectives, to_peers(): return lax.all_to_all(blocks, axis, 0, 0, tiled=True)  45.6 us
    all_to_all x4, waiting for transfers between devices, to_peers(): return lax.all_to_all(blocks, axis, 0, 0, tiled=True)  27.6 us
    ppermute x8, waiting for transfers between devices, along_y(): lax.ppermute(message, 'y', [(i, (i + step) % n_y) for i in range(n_y)])  24.8 us
    ppermute x11, waiting for transfers between devices, from_partner(): return lax.ppermute(array, axis, [(0, 1), (1, 0)])  15.7 us
    ppermute x11, starting transfers between devices, from_partner(): return lax.ppermute(array, axis, [(0, 1), (1, 0)])  15.7 us
    all_to_all x4, starting transfers between devices, to_peers(): return lax.all_to_all(blocks, axis, 0, 0, tiled=True)  15.5 us
    ppermute x8, starting transfers between devices, along_y(): lax.ppermute(message, 'y', [(i, (i + step) % n_y) for i in range(n_y)])  12.2 us
    dot_general x2, matrix products, shards(): preact = jnp.dot(normed, weight_in, preferred_element_type=jnp.float32)  8.41 us
  transfers between devices with their start and end apart: 25, of which 12 were waited for; matrix products, arithmetic and copies ran while one was open for 11% of the time, Pallas kernels for 0%

profile of v9, /device:TPU:1, one launch (start us, length us, event | category | flops | bytes accessed | tf_op | source)
XLA Modules:
  0.0 211.0 jit_solution(10386310424778913068)
XLA Ops:
  0.6 0.8 fusion.75
  1.5 18.5 %all_to_all.35 = bf16[16,128,64]{1,2,0:T(8,128)(2,1)S(1)} all-to-all(bf16[16,128,64]{1,2,0:T(8,128)(2,1)S(1)} %broadcast_in_dim.100), channel_id=1, replica_groups=mesh['z_hi'=2,'y'=4,'core'=2,'x'=4,'z_lo'=4] {'x','z_lo'}, dimensions={0} | all-to-all | bytes 524288 | tf_op jit(solution)/shard_map/all_to_all | solution.py:22
  20.3 3.7 %multiply_add_fusion.2 = (f32[128,2048]{1,0:T(8,128)S(1)}, bf16[128,2048]{1,0:T(8,128)(2,1)S(1)}) fusion(bf16[1024,2048]{1,0:T(8,128)(2,1)} %param.14, bf16[128,1024]{1,0:T(8,128)(2,1)S(1)} %copy.26, f32[1024]{0:T(1024)} %param.13, f32[128]{0:T(128)S(1)} %add_rsqrt_fusion.1), kind=kOutput, calls=%fused_computation.43 | convolution fusion | flops 542113792 | bytes 6033920 | tf_op jit(solution)/shard_map/dot_general | solution.py:157
  24.0 0.7 convolution_convert_fusion.3
  25.0 13.8 %all_to_all.36 = bf16[16,128,64]{1,2,0:T(8,128)(2,1)S(1)} all-to-all(bf16[16,128,64]{1,2,0:T(8,128)(2,1)S(1)} %bitcast.62), channel_id=1, replica_groups=mesh['z_hi'=2,'y'=4,'core'=2,'x'=4,'z_lo'=4] {'x','z_lo'}, dimensions={0} | all-to-all | bytes 524288 | tf_op jit(solution)/shard_map/all_to_all | solution.py:22
  38.9 13.3 %all_to_all.37 = bf16[16,128,64]{1,2,0:T(8,128)(2,1)S(1)} all-to-all(bf16[16,128,64]{1,2,0:T(8,128)(2,1)S(1)} %broadcast_in_dim.117), channel_id=1, replica_groups=mesh['z_hi'=2,'y'=4,'core'=2,'x'=4,'z_lo'=4] {'x','z_lo'}, dimensions={0} | all-to-all | bytes 524288 | tf_op jit(solution)/shard_map/all_to_all | solution.py:22
  52.2 3.7 %fusion = bf16[128,2048]{1,0:T(8,128)(2,1)S(1)} fusion(f32[128,2048]{1,0:T(8,128)S(1)} %get-tuple-element.10, bf16[128,1024]{0,1:T(8,128)(2,1)S(1)} %bitcast.54, bf16[2048,1024]{1,0:T(8,128)(2,1)} %param.15), kind=kOutput, calls=%fused_computation.4 | convolution fusion | flops 537395200 | bytes 6029312 | tf_op jit(solution)/shard_map/dot_general | solution.py:170
  56.0 1.6 fusion.106
  57.8 0.7 pad_maximum_fusion.2
  58.5 3.9 %all-to-all-start.3 = ((bf16[16,128,66]{1,2,0:T(8,128)(2,1)}), bf16[16,128,66]{1,2,0:T(8,128)(2,1)S(1)}, u32[]{:S(2)}, u32[]{:S(2)}) async-start(bf16[16,128,66]{1,2,0:T(8,128)(2,1)} %pad_maximum_fusion.2), calls=%async_computation.3 | async-start | bytes 589824 | tf_op jit(solution)/shard_map/all_to_all | solution.py:22
  62.6 9.9 %all-to-all-done.3 = bf16[16,128,66]{1,2,0:T(8,128)(2,1)S(1)} async-done(((bf16[16,128,66]{1,2,0:T(8,128)(2,1)}), bf16[16,128,66]{1,2,0:T(8,128)(2,1)S(1)}, u32[]{:S(2)}, u32[]{:S(2)}) %all-to-all-start.3) | async-done | bytes 270368 | tf_op jit(solution)/shard_map/all_to_all | solution.py:22
  72.6 0.8 broadcast_in_dim.119
  73.4 4.1 %all-to-all-start.4 = ((bf16[16,128,64]{1,2,0:T(8,128)(2,1)}), bf16[16,128,64]{1,2,0:T(8,128)(2,1)S(1)}, u32[]{:S(2)}, u32[]{:S(2)}) async-start(bf16[16,128,64]{1,2,0:T(8,128)(2,1)} %broadcast_in_dim.119), calls=%async_computation.4 | async-start | bytes 524288 | tf_op jit(solution)/shard_map/all_to_all | solution.py:22
  77.6 0.6 select_add_fusion
  78.2 7.9 %all-to-all-done.4 = bf16[16,128,64]{1,2,0:T(8,128)(2,1)S(1)} async-done(((bf16[16,128,64]{1,2,0:T(8,128)(2,1)}), bf16[16,128,64]{1,2,0:T(8,128)(2,1)S(1)}, u32[]{:S(2)}, u32[]{:S(2)}) %all-to-all-start.4) | async-done | bytes 262176 | tf_op jit(solution)/shard_map/all_to_all | solution.py:22
  86.3 3.4 %collective-permute-start.1 = (f32[2,32]{1,0:T(2,128)S(1)}, f32[2,32]{1,0:T(2,128)S(1)}, u32[]{:S(2)}, u32[]{:S(2)}) collective-permute-start(f32[2,32]{1,0:T(2,128)S(1)} %pad_maximum_fusion.3), channel_id=1, source_target_pairs={{0,16},{16,0},{1,17},{17,1},{2,18},{18,2},{3,19},{19,3},{4,20},{20... | collective-permute-start | bytes 776 | tf_op jit(solution)/shard_map/ppermute | solution.py:40
  89.7 0.8 collective-permute-done.1
  90.6 0.7 collective-permute-start.2
  91.2 3.9 %collective-permute-start.3 = (f32[2,32]{1,0:T(2,128)S(1)}, f32[2,32]{1,0:T(2,128)S(1)}, u32[]{:S(2)}, u32[]{:S(2)}) collective-permute-start(f32[2,32]{1,0:T(2,128)S(1)} %fusion.93), channel_id=1, source_target_pairs={{0,32},{64,96},{128,160},{192,224},{32,0},{96,64},{160,128},{224,1... | collective-permute-start | bytes 776 | tf_op jit(solution)/shard_map/ppermute | solution.py:57
  95.4 0.7 collective-permute-done.3
  96.6 4.7 %multiply_add_fusion = (f32[128,2048]{1,0:T(8,128)}, bf16[128,2048]{1,0:T(8,128)(2,1)S(1)}) fusion(bf16[1024,2048]{1,0:T(8,128)(2,1)} %param.14, bf16[128,1024]{1,0:T(8,128)(2,1)S(1)} %fusion.53, f32[128]{0:T(128)S(1)} %add_rsqrt_fusion, f32[1024]{0:T(1024)S(1)} %copy-done.14), kind=kOutput, calls=%fused_computation.40 | convolution fusion | flops 542113792 | bytes 6033920 | tf_op jit(solution)/shard_map/dot_general | solution.py:157
  101.3 0.7 convolution_convert_fusion.2
  102.0 0.8 copy.30
  102.9 3.5 %all-to-all-start.5 = ((bf16[16,128,64]{1,2,0:T(8,128)(2,1)}), bf16[16,128,64]{1,2,0:T(8,128)(2,1)S(1)}, u32[]{:S(2)}, u32[]{:S(2)}) async-start(bf16[16,128,64]{1,2,0:T(8,128)(2,1)} %bitcast.15), calls=%async_computation.5 | async-start | bytes 524288 | tf_op jit(solution)/shard_map/all_to_all | solution.py:22
  106.5 1.6 collective-permute-start.8
  108.1 1.2 fusion.28
  109.3 1.2 fusion.24
  110.4 5.5 %all-to-all-done.5 = bf16[16,128,64]{1,2,0:T(8,128)(2,1)S(1)} async-done(((bf16[16,128,64]{1,2,0:T(8,128)(2,1)}), bf16[16,128,64]{1,2,0:T(8,128)(2,1)S(1)}, u32[]{:S(2)}, u32[]{:S(2)}) %all-to-all-start.5) | async-done | bytes 262176 | tf_op jit(solution)/shard_map/all_to_all | solution.py:22
  116.0 0.7 fusion.71
  116.7 0.8 broadcast_in_dim.120
  117.5 3.9 %all-to-all-start.6 = ((bf16[16,128,64]{1,2,0:T(8,128)(2,1)}), bf16[16,128,64]{1,2,0:T(8,128)(2,1)S(1)}, u32[]{:S(2)}, u32[]{:S(2)}) async-start(bf16[16,128,64]{1,2,0:T(8,128)(2,1)} %broadcast_in_dim.120), calls=%async_computation.6 | async-start | bytes 524288 | tf_op jit(solution)/shard_map/all_to_all | solution.py:22
  121.4 0.5 fusion.30
  121.9 2.0 collective-permute-start.6
  123.9 1.2 fusion.26
  125.1 0.5 fusion.29
  125.7 4.3 %all-to-all-done.6 = bf16[16,128,64]{1,2,0:T(8,128)(2,1)S(1)} async-done(((bf16[16,128,64]{1,2,0:T(8,128)(2,1)}), bf16[16,128,64]{1,2,0:T(8,128)(2,1)S(1)}, u32[]{:S(2)}, u32[]{:S(2)}) %all-to-all-start.6) | async-done | bytes 262176 | tf_op jit(solution)/shard_map/all_to_all | solution.py:22
  129.9 0.5 fusion.31
  130.5 3.4 %collective-permute-start.7 = (bf16[128,512]{1,0:T(8,128)(2,1)S(1)}, bf16[128,512]{1,0:T(8,128)(2,1)S(1)}, u32[]{:S(2)}, u32[]{:S(2)}) collective-permute-start(bf16[128,512]{1,0:T(8,128)(2,1)S(1)} %fusion.31), channel_id=1, source_target_pairs={{0,16},{16,0},{1,17},{17,1},{2,18},{18,2},{3,19},{19,3},{4,20},{20... | collective-permute-start | bytes 393224 | tf_op jit(solution)/shard_map/ppermute | solution.py:40
  133.9 0.5 fusion.27
  134.6 0.6 copy-done.22
  135.2 0.8 copy-done.21
  136.0 3.1 %convolution_convert_fusion.1 = bf16[512,2048]{1,0:T(8,128)(2,1)S(1)} fusion(bf16[128,2048]{1,0:T(8,128)(2,1)} %copy-done.21, bf16[128,2048]{1,0:T(8,128)(2,1)} %copy-done.7, bf16[128,2048]{1,0:T(8,128)(2,1)} %collective-permute-done.8, bf16[128,2048]{1,0:T(8,128)(2,1)} %copy-done.6, bf16[128,512]{1,0:T(8,128)(2,1)S(1)} %collective-permute-done.7, ...), kind=kOutput, calls=%fused_computation.1 | convolution fusion | flops 1085276160 | bytes 4718592 | tf_op jit(solution)/shard_map/dot_general | solution.py:125
  139.2 1.5 fusion.1
  140.8 0.4 collective-permute-start.10
  141.1 0.5 fusion.25
  142.0 7.6 %collective-permute-start.15 = (bf16[128,2048]{1,0:T(8,128)(2,1)S(1)}, bf16[128,2048]{1,0:T(8,128)(2,1)S(1)}, u32[]{:S(2)}, u32[]{:S(2)}) collective-permute-start(bf16[128,2048]{1,0:T(8,128)(2,1)S(1)} %get-tuple-element.31), channel_id=1, source_target_pairs={{0,96},{32,0},{64,32},{96,64},{1,97},{33,1},{65,33},{97,65},{2,98}... | collective-permute-start | bytes 1572872 | tf_op jit(solution)/shard_map/ppermute | solution.py:88
  149.7 2.2 %convolution_convert_fusion = bf16[512,2048]{1,0:T(8,128)(2,1)S(1)} fusion(bf16[128,2048]{1,0:T(8,128)(2,1)S(1)} %collective-permute-done.10, bf16[128,2048]{1,0:T(8,128)(2,1)S(1)} %fusion.1, bf16[128,2048]{1,0:T(8,128)(2,1)S(1)} %collective-permute-done.5, bf16[128,2048]{1,0:T(8,128)(2,1)S(1)} %fusion, bf16[128,512]{1,0:T(8,128)(2,1)S(1)} %collective-permute-done.4, ...), kind=kOutput, calls=%fused_computation | convolution fusion | flops 1085276160 | bytes 4718592 | tf_op jit(solution)/shard_map/dot_general | solution.py:125
  152.3 2.7 %collective-permute-start.13 = (bf16[64,2048]{1,0:T(8,128)(2,1)S(1)}, bf16[64,2048]{1,0:T(8,128)(2,1)S(1)}, u32[]{:S(2)}, u32[]{:S(2)}) collective-permute-start(bf16[64,2048]{1,0:T(8,128)(2,1)S(1)} %get-tuple-element.27), channel_id=1, source_target_pairs={{0,96},{32,0},{64,32},{96,64},{1,97},{33,1},{65,33},{97,65},{2,98}... | collective-permute-start | bytes 786440 | tf_op jit(solution)/shard_map/ppermute | solution.py:88
  155.0 8.7 %collective-permute-done.16 = bf16[128,2048]{1,0:T(8,128)(2,1)S(1)} collective-permute-done((bf16[128,2048]{1,0:T(8,128)(2,1)S(1)}, bf16[128,2048]{1,0:T(8,128)(2,1)S(1)}, u32[]{:S(2)}, u32[]{:S(2)}) %collective-permute-start.16) | collective-permute-done | bytes 524320 | tf_op jit(solution)/shard_map/ppermute | solution.py:88
  163.8 5.6 %collective-permute-done.11 = bf16[64,2048]{1,0:T(8,128)(2,1)S(1)} collective-permute-done((bf16[64,2048]{1,0:T(8,128)(2,1)S(1)}, bf16[64,2048]{1,0:T(8,128)(2,1)S(1)}, u32[]{:S(2)}, u32[]{:S(2)}) %collective-permute-start.11) | collective-permute-done | bytes 262176 | tf_op jit(solution)/shard_map/ppermute | solution.py:88
  169.4 0.9 add_convert_fusion
  170.5 0.8 pad_maximum_fusion.1
  171.3 0.8 pad_maximum_fusion
  172.1 1.5 collective-permute-start.12
  173.6 3.1 %collective-permute-done.17 = bf16[64,2048]{1,0:T(8,128)(2,1)S(1)} collective-permute-done((bf16[64,2048]{1,0:T(8,128)(2,1)S(1)}, bf16[64,2048]{1,0:T(8,128)(2,1)S(1)}, u32[]{:S(2)}, u32[]{:S(2)}) %collective-permute-start.17) | collective-permute-done | bytes 262176 | tf_op jit(solution)/shard_map/ppermute | solution.py:88
  176.8 2.3 %collective-permute-start.18 = (bf16[64,2048]{1,0:T(8,128)(2,1)S(1)}, bf16[64,2048]{1,0:T(8,128)(2,1)S(1)}, u32[]{:S(2)}, u32[]{:S(2)}) collective-permute-start(bf16[64,2048]{1,0:T(8,128)(2,1)S(1)} %add_convert_fusion.1), channel_id=1, source_target_pairs={{0,128},{128,0},{1,129},{129,1},{2,130},{130,2},{3,131},{131,3},{4... | collective-permute-start | bytes 786440 | tf_op jit(solution)/shard_map/ppermute | solution.py:40
  179.1 1.2 constant_dynamic-slice_fusion
  180.7 7.4 %collective-permute-done.14 = bf16[128,2048]{1,0:T(8,128)(2,1)} collective-permute-done((bf16[128,2048]{1,0:T(8,128)(2,1)}, bf16[128,2048]{1,0:T(8,128)(2,1)}, u32[]{:S(2)}, u32[]{:S(2)}) %collective-permute-start.14) | collective-permute-done | bytes 524320 | tf_op jit(solution)/shard_map/ppermute | solution.py:88
  188.0 5.2 %collective-permute-done.18 = bf16[64,2048]{1,0:T(8,128)(2,1)S(1)} collective-permute-done((bf16[64,2048]{1,0:T(8,128)(2,1)S(1)}, bf16[64,2048]{1,0:T(8,128)(2,1)S(1)}, u32[]{:S(2)}, u32[]{:S(2)}) %collective-permute-start.18) | collective-permute-done | bytes 262176 | tf_op jit(solution)/shard_map/ppermute | solution.py:40
  193.3 1.3 fusion.45
  194.5 2.2 %collective-permute-start.19 = (bf16[64,2048]{1,0:T(8,128)(2,1)S(1)}, bf16[64,2048]{1,0:T(8,128)(2,1)S(1)}, u32[]{:S(2)}, u32[]{:S(2)}) collective-permute-start(bf16[64,2048]{1,0:T(8,128)(2,1)S(1)} %fusion.45), channel_id=1, source_target_pairs={{0,128},{128,0},{1,129},{129,1},{2,130},{130,2},{3,131},{131,3},{4... | collective-permute-start | bytes 786440 | tf_op jit(solution)/shard_map/ppermute | solution.py:40
  196.7 2.2 %subtract_convert_fusion = (bf16[2048,64]{0,1:T(8,128)(2,1)}, f32[2048,64]{0,1:T(8,128)}) fusion(bf16[2048,64]{0,1:T(8,128)(2,1)S(1)} %copy.32, bf16[64,2048]{1,0:T(8,128)(2,1)S(1)} %collective-permute-done.18, bf16[128,2048]{1,0:T(8,128)(2,1)} %copy-done.9, bf16[64,2048]{1,0:T(8,128)(2,1)S(1)} %collective-permute-done.20, ...), kind=kLoop, calls=%fused_computation.93 | loop fusion | flops 1835008 | bytes 2621440 | tf_op jit(solution)/shard_map/convert_element_type | solution.py:219
  199.0 9.7 %collective-permute-done.19 = bf16[64,2048]{1,0:T(8,128)(2,1)S(1)} collective-permute-done((bf16[64,2048]{1,0:T(8,128)(2,1)S(1)}, bf16[64,2048]{1,0:T(8,128)(2,1)S(1)}, u32[]{:S(2)}, u32[]{:S(2)}) %collective-permute-start.19) | collective-permute-done | bytes 262176 | tf_op jit(solution)/shard_map/ppermute | solution.py:40
  208.7 2.3 %subtract_convert_fusion.1 = (bf16[64,2048]{1,0:T(8,128)(2,1)}, f32[64,2048]{1,0:T(8,128)}) fusion(bf16[1024,2048]{1,0:T(8,128)(2,1)} %param.14, s32[]{:T(128)S(6)} %select_n.195, bf16[64,2048]{1,0:T(8,128)(2,1)S(1)} %collective-permute-done.19, bf16[128,2048]{1,0:T(8,128)(2,1)} %collective-permute-done.14, bf16[128,2048]{1,0:T(8,128)(2,1)} %collective-permute-done.12, ...), kind=kLoop, calls=%fused_computation.95 | loop fusion | flops 1835008 | bytes 2621444 | tf_op jit(solution)/shard_map/convert_element_type | solution.py:218
  (108 shorter events, 3.6 us)
Async XLA Ops:
  20.3 3.8 %copy-start = (bf16[2048,1024]{1,0:T(8,128)(2,1)S(1)}, bf16[2048,1024]{1,0:T(8,128)(2,1)}, u32[]{:S(2)}) copy-start(bf16[2048,1024]{1,0:T(8,128)(2,1)} %param.15) | copy-start | bytes 12582916
  24.0 82.5 %copy-start.6 = (bf16[128,2048]{1,0:T(8,128)(2,1)}, bf16[128,2048]{1,0:T(8,128)(2,1)S(1)}, u32[]{:S(2)}) copy-start(bf16[128,2048]{1,0:T(8,128)(2,1)S(1)} %get-tuple-element.9) | copy-start | bytes 1572868
  24.0 14.8 %copy-start.10 = (f32[128,64]{0,1:T(8,128)S(1)}, f32[128,64]{0,1:T(8,128)}, u32[]{:S(2)}) copy-start(f32[128,64]{0,1:T(8,128)} %param.10) | copy-start | bytes 98308
  24.0 14.8 %copy-start.11 = (bf16[128,64]{0,1:T(8,128)(2,1)S(1)}, bf16[128,64]{0,1:T(8,128)(2,1)}, u32[]{:S(2)}) copy-start(bf16[128,64]{0,1:T(8,128)(2,1)} %param.9) | copy-start | bytes 49156
  24.0 14.8 %copy-start.12 = (f32[128,64]{0,1:T(8,128)S(1)}, f32[128,64]{0,1:T(8,128)}, u32[]{:S(2)}) copy-start(f32[128,64]{0,1:T(8,128)} %param.12) | copy-start | bytes 98308
  24.8 31.1 %copy-start.14 = (f32[1024]{0:T(1024)S(1)}, f32[1024]{0:T(1024)}, u32[]{:S(2)}) copy-start(f32[1024]{0:T(1024)} %param.13) | copy-start | bytes 12292
  25.0 31.0 %copy-start.3 = (bf16[1024,2048]{1,0:T(8,128)(2,1)S(1)}, bf16[1024,2048]{1,0:T(8,128)(2,1)}, u32[]{:S(2)}) copy-start(bf16[1024,2048]{1,0:T(8,128)(2,1)} %param.14) | copy-start | bytes 12582916
  56.0 30.2 %copy-start.20 = (s32[128]{0:T(128)S(1)}, s32[128]{0:T(128)}, u32[]{:S(2)}) copy-start(s32[128]{0:T(128)} %param.11) | copy-start | bytes 1540
  58.5 13.9 %all-to-all-start.3 = ((bf16[16,128,66]{1,2,0:T(8,128)(2,1)}), bf16[16,128,66]{1,2,0:T(8,128)(2,1)S(1)}, u32[]{:S(2)}, u32[]{:S(2)}) async-start(bf16[16,128,66]{1,2,0:T(8,128)(2,1)} %pad_maximum_fusion.2), calls=%async_computation.3 | async-start | bytes 589824 | tf_op jit(solution)/shard_map/all_to_all | solution.py:22
  72.5 24.0 %copy-start.15 = (f32[128]{0:T(128)}, f32[128]{0:T(128)S(1)}, u32[]{:S(2)}) copy-start(f32[128]{0:T(128)S(1)} %slice_reduce_fusion) | copy-start | bytes 1540
  73.4 12.6 %all-to-all-start.4 = ((bf16[16,128,64]{1,2,0:T(8,128)(2,1)}), bf16[16,128,64]{1,2,0:T(8,128)(2,1)S(1)}, u32[]{:S(2)}, u32[]{:S(2)}) async-start(bf16[16,128,64]{1,2,0:T(8,128)(2,1)} %broadcast_in_dim.119), calls=%async_computation.4 | async-start | bytes 524288 | tf_op jit(solution)/shard_map/all_to_all | solution.py:22
  86.3 4.2 %collective-permute-start.1 = (f32[2,32]{1,0:T(2,128)S(1)}, f32[2,32]{1,0:T(2,128)S(1)}, u32[]{:S(2)}, u32[]{:S(2)}) collective-permute-start(f32[2,32]{1,0:T(2,128)S(1)} %pad_maximum_fusion.3), channel_id=1, source_target_pairs={{0,16},{16,0},{1,17},{17,1},{2,18},{18,2},{3,19},{19,3},{4,20},{20... | collective-permute-start | bytes 776 | tf_op jit(solution)/shard_map/ppermute | solution.py:40
  90.6 4.8 %collective-permute-start.2 = (f32[2,32]{1,0:T(2,128)S(1)}, f32[2,32]{1,0:T(2,128)S(1)}, u32[]{:S(2)}, u32[]{:S(2)}) collective-permute-start(f32[2,32]{1,0:T(2,128)S(1)} %fusion.93), channel_id=1, source_target_pairs={{32,64},{96,128},{160,192},{64,32},{128,96},{192,160},{33,65},{97,... | collective-permute-start | bytes 776 | tf_op jit(solution)/shard_map/ppermute | solution.py:57
  91.2 4.9 %collective-permute-start.3 = (f32[2,32]{1,0:T(2,128)S(1)}, f32[2,32]{1,0:T(2,128)S(1)}, u32[]{:S(2)}, u32[]{:S(2)}) collective-permute-start(f32[2,32]{1,0:T(2,128)S(1)} %fusion.93), channel_id=1, source_target_pairs={{0,32},{64,96},{128,160},{192,224},{32,0},{96,64},{160,128},{224,1... | collective-permute-start | bytes 776 | tf_op jit(solution)/shard_map/ppermute | solution.py:57
  96.5 28.6 %copy-start.23 = (f32[128]{0:T(128)}, f32[128]{0:T(128)S(1)}, u32[]{:S(2)}) copy-start(f32[128]{0:T(128)S(1)} %add_rsqrt_fusion) | copy-start | bytes 1540
  96.6 4.7 %copy-start.1 = (bf16[2048,1024]{1,0:T(8,128)(2,1)S(1)}, bf16[2048,1024]{1,0:T(8,128)(2,1)}, u32[]{:S(2)}) copy-start(bf16[2048,1024]{1,0:T(8,128)(2,1)} %param.15) | copy-start | bytes 12582916
  101.3 23.9 %copy-start.7 = (bf16[128,2048]{1,0:T(8,128)(2,1)}, bf16[128,2048]{1,0:T(8,128)(2,1)S(1)}, u32[]{:S(2)}) copy-start(bf16[128,2048]{1,0:T(8,128)(2,1)S(1)} %get-tuple-element.11) | copy-start | bytes 1572868
  101.3 6.8 %copy-start.17 = (s32[512]{0:T(512)S(1)}, s32[512]{0:T(512)}, u32[]{:S(2)}) copy-start(s32[512]{0:T(512)} %select_add_fusion) | copy-start | bytes 6148
  101.3 14.7 %copy-start.13 = (f32[128,64]{0,1:T(8,128)S(1)}, f32[128,64]{0,1:T(8,128)}, u32[]{:S(2)}) copy-start(f32[128,64]{0,1:T(8,128)} %param.12) | copy-start | bytes 98308
  101.3 14.7 %copy-start.16 = (f32[128]{0:T(128)S(1)}, f32[128]{0:T(128)}, u32[]{:S(2)}) copy-start(f32[128]{0:T(128)} %copy-done.15) | copy-start | bytes 1540
  102.9 13.1 %all-to-all-start.5 = ((bf16[16,128,64]{1,2,0:T(8,128)(2,1)}), bf16[16,128,64]{1,2,0:T(8,128)(2,1)S(1)}, u32[]{:S(2)}, u32[]{:S(2)}) async-start(bf16[16,128,64]{1,2,0:T(8,128)(2,1)} %bitcast.15), calls=%async_computation.5 | async-start | bytes 524288 | tf_op jit(solution)/shard_map/all_to_all | solution.py:22
  106.4 28.0 %copy-start.18 = (s32[512]{0:T(512)}, s32[512]{0:T(512)S(1)}, u32[]{:S(2)}) copy-start(s32[512]{0:T(512)S(1)} %select_add_fusion.1) | copy-start | bytes 6148
  106.5 28.0 %collective-permute-start.8 = (bf16[128,2048]{1,0:T(8,128)(2,1)S(1)}, bf16[128,2048]{1,0:T(8,128)(2,1)}, u32[]{:S(2)}, u32[]{:S(2)}) collective-permute-start(bf16[128,2048]{1,0:T(8,128)(2,1)S(1)} %get-tuple-element.9), channel_id=1, source_target_pairs={{0,16},{16,0},{1,17},{17,1},{2,18},{18,2},{3,19},{19,3},{4,20},{20... | collective-permute-start | bytes 1572872 | tf_op jit(solution)/shard_map/ppermute | solution.py:40
  109.2 40.4 %collective-permute-start = (bf16[128,512]{1,0:T(8,128)(2,1)}, bf16[128,512]{1,0:T(8,128)(2,1)}, u32[]{:S(2)}, u32[]{:S(2)}) collective-permute-start(bf16[128,512]{1,0:T(8,128)(2,1)} %fusion.28), channel_id=1, source_target_pairs={{0,16},{16,0},{1,17},{17,1},{2,18},{18,2},{3,19},{19,3},{4,20},{20... | collective-permute-start | bytes 393224 | tf_op jit(solution)/shard_map/ppermute | solution.py:40
  117.5 12.5 %all-to-all-start.6 = ((bf16[16,128,64]{1,2,0:T(8,128)(2,1)}), bf16[16,128,64]{1,2,0:T(8,128)(2,1)S(1)}, u32[]{:S(2)}, u32[]{:S(2)}) async-start(bf16[16,128,64]{1,2,0:T(8,128)(2,1)} %broadcast_in_dim.120), calls=%async_computation.6 | async-start | bytes 524288 | tf_op jit(solution)/shard_map/all_to_all | solution.py:22
  121.9 12.6 %collective-permute-start.6 = (bf16[128,512]{1,0:T(8,128)(2,1)S(1)}, bf16[128,512]{1,0:T(8,128)(2,1)S(1)}, u32[]{:S(2)}, u32[]{:S(2)}) collective-permute-start(bf16[128,512]{1,0:T(8,128)(2,1)S(1)} %fusion.30), channel_id=1, source_target_pairs={{0,16},{16,0},{1,17},{17,1},{2,18},{18,2},{3,19},{19,3},{4,20},{20... | collective-permute-start | bytes 393224 | tf_op jit(solution)/shard_map/ppermute | solution.py:40
  125.1 9.5 %collective-permute-start.9 = (bf16[128,2048]{1,0:T(8,128)(2,1)S(1)}, bf16[128,2048]{1,0:T(8,128)(2,1)S(1)}, u32[]{:S(2)}, u32[]{:S(2)}) collective-permute-start(bf16[128,2048]{1,0:T(8,128)(2,1)S(1)} %get-tuple-element.11), channel_id=1, source_target_pairs={{0,16},{16,0},{1,17},{17,1},{2,18},{18,2},{3,19},{19,3},{4,20},{20... | collective-permute-start | bytes 1572872 | tf_op jit(solution)/shard_map/ppermute | solution.py:40
  130.5 5.5 %collective-permute-start.7 = (bf16[128,512]{1,0:T(8,128)(2,1)S(1)}, bf16[128,512]{1,0:T(8,128)(2,1)S(1)}, u32[]{:S(2)}, u32[]{:S(2)}) collective-permute-start(bf16[128,512]{1,0:T(8,128)(2,1)S(1)} %fusion.31), channel_id=1, source_target_pairs={{0,16},{16,0},{1,17},{17,1},{2,18},{18,2},{3,19},{19,3},{4,20},{20... | collective-permute-start | bytes 393224 | tf_op jit(solution)/shard_map/ppermute | solution.py:40
  134.4 4.7 %copy-start.2 = (bf16[2048,1024]{1,0:T(8,128)(2,1)S(1)}, bf16[2048,1024]{1,0:T(8,128)(2,1)}, u32[]{:S(2)}) copy-start(bf16[2048,1024]{1,0:T(8,128)(2,1)} %param.15) | copy-start | bytes 12582916
  134.4 4.7 %copy-start.5 = (f32[128,2048]{1,0:T(8,128)S(1)}, f32[128,2048]{1,0:T(8,128)}, u32[]{:S(2)}) copy-start(f32[128,2048]{1,0:T(8,128)} %get-tuple-element.12) | copy-start | bytes 3145732
  134.5 15.2 %collective-permute-start.5 = (bf16[128,2048]{1,0:T(8,128)(2,1)S(1)}, bf16[128,2048]{1,0:T(8,128)(2,1)S(1)}, u32[]{:S(2)}, u32[]{:S(2)}) collective-permute-start(bf16[128,2048]{1,0:T(8,128)(2,1)S(1)} %fusion), channel_id=1, source_target_pairs={{0,16},{16,0},{1,17},{17,1},{2,18},{18,2},{3,19},{19,3},{4,20},{20... | collective-permute-start | bytes 1572872 | tf_op jit(solution)/shard_map/ppermute | solution.py:40
  134.6 0.7 copy-start.22
  135.2 0.8 copy-start.21
  139.2 2.0 copy-start.19
  139.2 1.9 copy-start.24
  139.2 10.5 %copy-start.25 = (bf16[128,512]{1,0:T(8,128)(2,1)S(1)}, bf16[128,512]{1,0:T(8,128)(2,1)}, u32[]{:S(2)}) copy-start(bf16[128,512]{1,0:T(8,128)(2,1)} %fusion.24) | copy-start | bytes 393220
  140.8 8.9 %collective-permute-start.10 = (bf16[128,2048]{1,0:T(8,128)(2,1)S(1)}, bf16[128,2048]{1,0:T(8,128)(2,1)S(1)}, u32[]{:S(2)}, u32[]{:S(2)}) collective-permute-start(bf16[128,2048]{1,0:T(8,128)(2,1)S(1)} %fusion.1), channel_id=1, source_target_pairs={{0,16},{16,0},{1,17},{17,1},{2,18},{18,2},{3,19},{19,3},{4,20},{20... | collective-permute-start | bytes 1572872 | tf_op jit(solution)/shard_map/ppermute | solution.py:40
  141.7 8.0 %collective-permute-start.4 = (bf16[128,512]{1,0:T(8,128)(2,1)S(1)}, bf16[128,512]{1,0:T(8,128)(2,1)S(1)}, u32[]{:S(2)}, u32[]{:S(2)}) collective-permute-start(bf16[128,512]{1,0:T(8,128)(2,1)S(1)} %fusion.29), channel_id=1, source_target_pairs={{0,16},{16,0},{1,17},{17,1},{2,18},{18,2},{3,19},{19,3},{4,20},{20... | collective-permute-start | bytes 393224 | tf_op jit(solution)/shard_map/ppermute | solution.py:40
  142.0 21.7 %collective-permute-start.15 = (bf16[128,2048]{1,0:T(8,128)(2,1)S(1)}, bf16[128,2048]{1,0:T(8,128)(2,1)S(1)}, u32[]{:S(2)}, u32[]{:S(2)}) collective-permute-start(bf16[128,2048]{1,0:T(8,128)(2,1)S(1)} %get-tuple-element.31), channel_id=1, source_target_pairs={{0,96},{32,0},{64,32},{96,64},{1,97},{33,1},{65,33},{97,65},{2,98}... | collective-permute-start | bytes 1572872 | tf_op jit(solution)/shard_map/ppermute | solution.py:88
  149.6 14.1 %collective-permute-start.16 = (bf16[128,2048]{1,0:T(8,128)(2,1)S(1)}, bf16[128,2048]{1,0:T(8,128)(2,1)S(1)}, u32[]{:S(2)}, u32[]{:S(2)}) collective-permute-start(bf16[128,2048]{1,0:T(8,128)(2,1)S(1)} %get-tuple-element.32), channel_id=1, source_target_pairs={{0,32},{32,64},{64,96},{96,0},{1,33},{33,65},{65,97},{97,1},{2,34}... | collective-permute-start | bytes 1572872 | tf_op jit(solution)/shard_map/ppermute | solution.py:88
  151.9 24.9 %copy-start.4 = (bf16[512,2048]{1,0:T(8,128)(2,1)}, bf16[512,2048]{1,0:T(8,128)(2,1)S(1)}, u32[]{:S(2)}) copy-start(bf16[512,2048]{1,0:T(8,128)(2,1)S(1)} %convolution_convert_fusion) | copy-start | bytes 6291460
  152.0 17.4 %collective-permute-start.11 = (bf16[64,2048]{1,0:T(8,128)(2,1)S(1)}, bf16[64,2048]{1,0:T(8,128)(2,1)S(1)}, u32[]{:S(2)}, u32[]{:S(2)}) collective-permute-start(bf16[64,2048]{1,0:T(8,128)(2,1)S(1)} %get-tuple-element.30), channel_id=1, source_target_pairs={{0,32},{32,64},{64,96},{96,0},{1,33},{33,65},{65,97},{97,1},{2,34}... | collective-permute-start | bytes 786440 | tf_op jit(solution)/shard_map/ppermute | solution.py:88
  152.3 18.0 %collective-permute-start.13 = (bf16[64,2048]{1,0:T(8,128)(2,1)S(1)}, bf16[64,2048]{1,0:T(8,128)(2,1)S(1)}, u32[]{:S(2)}, u32[]{:S(2)}) collective-permute-start(bf16[64,2048]{1,0:T(8,128)(2,1)S(1)} %get-tuple-element.27), channel_id=1, source_target_pairs={{0,96},{32,0},{64,32},{96,64},{1,97},{33,1},{65,33},{97,65},{2,98}... | collective-permute-start | bytes 786440 | tf_op jit(solution)/shard_map/ppermute | solution.py:88
  163.8 13.0 %copy-start.9 = (bf16[128,2048]{1,0:T(8,128)(2,1)}, bf16[128,2048]{1,0:T(8,128)(2,1)S(1)}, u32[]{:S(2)}) copy-start(bf16[128,2048]{1,0:T(8,128)(2,1)S(1)} %collective-permute-done.15) | copy-start | bytes 1572868
  170.3 6.4 %collective-permute-start.17 = (bf16[64,2048]{1,0:T(8,128)(2,1)S(1)}, bf16[64,2048]{1,0:T(8,128)(2,1)S(1)}, u32[]{:S(2)}, u32[]{:S(2)}) collective-permute-start(bf16[64,2048]{1,0:T(8,128)(2,1)S(1)} %get-tuple-element.24), channel_id=1, source_target_pairs={{0,96},{32,0},{64,32},{96,64},{1,97},{33,1},{65,33},{97,65},{2,98}... | collective-permute-start | bytes 786440 | tf_op jit(solution)/shard_map/ppermute | solution.py:88
  171.3 16.7 %collective-permute-start.14 = (bf16[128,2048]{1,0:T(8,128)(2,1)}, bf16[128,2048]{1,0:T(8,128)(2,1)}, u32[]{:S(2)}, u32[]{:S(2)}) collective-permute-start(bf16[128,2048]{1,0:T(8,128)(2,1)} %pad_maximum_fusion.1), channel_id=1, source_target_pairs={{0,96},{32,0},{64,32},{96,64},{1,97},{33,1},{65,33},{97,65},{2,98}... | collective-permute-start | bytes 1572872 | tf_op jit(solution)/shard_map/ppermute | solution.py:88
  172.1 15.9 %collective-permute-start.12 = (bf16[128,2048]{1,0:T(8,128)(2,1)}, bf16[128,2048]{1,0:T(8,128)(2,1)}, u32[]{:S(2)}, u32[]{:S(2)}) collective-permute-start(bf16[128,2048]{1,0:T(8,128)(2,1)} %pad_maximum_fusion), channel_id=1, source_target_pairs={{0,32},{32,64},{64,96},{96,0},{1,33},{33,65},{65,97},{97,1},{2,34}... | collective-permute-start | bytes 1572872 | tf_op jit(solution)/shard_map/ppermute | solution.py:88
  176.8 16.4 %collective-permute-start.18 = (bf16[64,2048]{1,0:T(8,128)(2,1)S(1)}, bf16[64,2048]{1,0:T(8,128)(2,1)S(1)}, u32[]{:S(2)}, u32[]{:S(2)}) collective-permute-start(bf16[64,2048]{1,0:T(8,128)(2,1)S(1)} %add_convert_fusion.1), channel_id=1, source_target_pairs={{0,128},{128,0},{1,129},{129,1},{2,130},{130,2},{3,131},{131,3},{4... | collective-permute-start | bytes 786440 | tf_op jit(solution)/shard_map/ppermute | solution.py:40
  180.6 28.1 %copy-start.8 = (f32[64,2048]{1,0:T(8,128)S(1)}, f32[64,2048]{1,0:T(8,128)}, u32[]{:S(2)}) copy-start(f32[64,2048]{1,0:T(8,128)} %param.16) | copy-start | bytes 1572868
  180.6 16.2 %collective-permute-start.20 = (bf16[64,2048]{1,0:T(8,128)(2,1)}, bf16[64,2048]{1,0:T(8,128)(2,1)S(1)}, u32[]{:S(2)}, u32[]{:S(2)}) collective-permute-start(bf16[64,2048]{1,0:T(8,128)(2,1)} %get-tuple-element.23), channel_id=1, source_target_pairs={{0,32},{32,64},{64,96},{96,0},{1,33},{33,65},{65,97},{97,1},{2,34}... | collective-permute-start | bytes 786440 | tf_op jit(solution)/shard_map/ppermute | solution.py:88
  194.5 14.1 %collective-permute-start.19 = (bf16[64,2048]{1,0:T(8,128)(2,1)S(1)}, bf16[64,2048]{1,0:T(8,128)(2,1)S(1)}, u32[]{:S(2)}, u32[]{:S(2)}) collective-permute-start(bf16[64,2048]{1,0:T(8,128)(2,1)S(1)} %fusion.45), channel_id=1, source_target_pairs={{0,128},{128,0},{1,129},{129,1},{2,130},{130,2},{3,131},{131,3},{4... | collective-permute-start | bytes 786440 | tf_op jit(solution)/shard_map/ppermute | solution.py:40

commit v10 on v8

--- a/solution.py
+++ b/solution.py
@@ -106,13 +106,13 @@
     if wide:
         near_down = near_down + nothing(runs(risen, 0)[0])
         up, down = runs(risen, 1)[0], runs(sunk, 1)[0]
-        near_up = runs(along_y(near_up.astype(jnp.bfloat16), 1), 0)[0]
-        near_down = runs(along_y(near_down.astype(jnp.bfloat16), -1), 0)[0]
     else:
-        above = along_y(jnp.concatenate([near_up, up]).astype(jnp.bfloat16), 1)
-        below = along_y(jnp.concatenate([near_down, down]).astype(jnp.bfloat16), -1)
-        near_up, up = runs(above, 0, 1)
-        near_down, down = runs(below, 0, 1)
+        up, down = [
+            runs(along_y(array.astype(jnp.bfloat16), step), 0)[0]
+            for array, step in ((up, 1), (down, -1))
+        ]
+    near_up = runs(along_y(near_up.astype(jnp.bfloat16), 1), 0)[0]
+    near_down = runs(along_y(near_down.astype(jnp.bfloat16), -1), 0)[0]
     return kept + near_up + down, other + near_down + up
 
 
@@ -165,7 +165,7 @@
         lefts_out += for_both_cores(grad, orders)
         if last:
             partial_out = partial_over_chip(lefts_out, rights_out)
-            slope = slope + nothing(partial_out[0, 0])
+            slope = slope + nothing(partial_out[:local_tokens])
         hidden_grad = (
             jnp.dot(grad, weight_out.T, preferred_element_type=jnp.float32) * slope
         ).astype(jnp.bfloat16)

time: 212 us -> 211 us (level); the launches traced: 210 us -> 207 us
  waiting for transfers between devices: 56.6 us -> 50.6 us
  starting transfers between devices: 61.4 us -> 65.1 us
    ppermute x8 -> x10, waiting for transfers between devices: 18.7 us -> 13.6 us  [along_y(): lax.ppermute(message, 'y', [(i, (i + step) % n_y) for i in range(n_y)])]
    ppermute x8 -> x10, starting transfers between devices: 18.3 us -> 22.4 us  [along_y(): lax.ppermute(message, 'y', [(i, (i + step) % n_y) for i in range(n_y)])]
  transfers between devices with their start and end apart: 25 -> 27, of which waited for: 14 -> 11; matrix products, arithmetic and copies ran while one was open for 11% -> 11% of each run, Pallas kernels for 0% -> 0%
where the time goes in v10:
time: 211 us; the launch traced here: 207 us
  starting transfers between devices  65.1 us (31%)
  waiting for transfers between devices  50.6 us (24%)
  blocking collectives  42.8 us (20%)
  matrix products  28.3 us (13%)
  other arithmetic  11.6 us (5%)
  local copies, waits for them, and re-layouts  7.32 us (3%)
    all_to_all x3, blocking collectives, to_peers(): return lax.all_to_all(blocks, axis, 0, 0, tiled=True)  42.8 us
    ppermute x10, starting transfers between devices, along_y(): lax.ppermute(message, 'y', [(i, (i + step) % n_y) for i in range(n_y)])  22.4 us
    all_to_all x4, starting transfers between devices, to_peers(): return lax.all_to_all(blocks, axis, 0, 0, tiled=True)  22.1 us
    all_to_all x4, waiting for transfers between devices, to_peers(): return lax.all_to_all(blocks, axis, 0, 0, tiled=True)  22.1 us
    ppermute x11, starting transfers between devices, from_partner(): return lax.ppermute(array, axis, [(0, 1), (1, 0)])  18.5 us
    ppermute x11, waiting for transfers between devices, from_partner(): return lax.ppermute(array, axis, [(0, 1), (1, 0)])  14.8 us
    ppermute x10, waiting for transfers between devices, along_y(): lax.ppermute(message, 'y', [(i, (i + step) % n_y) for i in range(n_y)])  13.6 us
    dot_general x2, matrix products, shards(): preact = jnp.dot(normed, weight_in, preferred_element_type=jnp.float32)  8.44 us
  transfers between devices with their start and end apart: 27, of which 11 were waited for; matrix products, arithmetic and copies ran while one was open for 11% of the time, Pallas kernels for 0%

profile of v10, /device:TPU:33, one launch (start us, length us, event | category | flops | bytes accessed | tf_op | source)
XLA Modules:
  0.0 206.9 jit_solution(16230477991256387749)
XLA Ops:
  0.6 0.8 fusion.85
  1.5 15.8 %all_to_all.35 = bf16[16,128,64]{1,2,0:T(8,128)(2,1)S(1)} all-to-all(bf16[16,128,64]{1,2,0:T(8,128)(2,1)S(1)} %broadcast_in_dim.100), channel_id=1, replica_groups=mesh['z_hi'=2,'y'=4,'core'=2,'x'=4,'z_lo'=4] {'x','z_lo'}, dimensions={0} | all-to-all | bytes 524288 | tf_op jit(solution)/shard_map/all_to_all | solution.py:22
  17.6 3.7 %multiply_add_fusion.2 = (f32[128,2048]{1,0:T(8,128)S(1)}, bf16[128,2048]{1,0:T(8,128)(2,1)S(1)}) fusion(bf16[1024,2048]{1,0:T(8,128)(2,1)} %param.14, bf16[128,1024]{1,0:T(8,128)(2,1)S(1)} %copy.26, f32[1024]{0:T(1024)} %param.13, f32[128]{0:T(128)S(1)} %add_rsqrt_fusion.1), kind=kOutput, calls=%fused_computation.43 | convolution fusion | flops 542113792 | bytes 6033920 | tf_op jit(solution)/shard_map/dot_general | solution.py:157
  21.4 0.7 convolution_convert_fusion.3
  22.3 13.8 %all_to_all.36 = bf16[16,128,64]{1,2,0:T(8,128)(2,1)S(1)} all-to-all(bf16[16,128,64]{1,2,0:T(8,128)(2,1)S(1)} %bitcast.62), channel_id=1, replica_groups=mesh['z_hi'=2,'y'=4,'core'=2,'x'=4,'z_lo'=4] {'x','z_lo'}, dimensions={0} | all-to-all | bytes 524288 | tf_op jit(solution)/shard_map/all_to_all | solution.py:22
  36.2 13.2 %all_to_all.37 = bf16[16,128,64]{1,2,0:T(8,128)(2,1)S(1)} all-to-all(bf16[16,128,64]{1,2,0:T(8,128)(2,1)S(1)} %broadcast_in_dim.117), channel_id=1, replica_groups=mesh['z_hi'=2,'y'=4,'core'=2,'x'=4,'z_lo'=4] {'x','z_lo'}, dimensions={0} | all-to-all | bytes 524288 | tf_op jit(solution)/shard_map/all_to_all | solution.py:22
  49.4 3.7 %fusion = bf16[128,2048]{1,0:T(8,128)(2,1)S(1)} fusion(f32[128,2048]{1,0:T(8,128)S(1)} %get-tuple-element.10, bf16[128,1024]{0,1:T(8,128)(2,1)S(1)} %bitcast.54, bf16[2048,1024]{1,0:T(8,128)(2,1)} %param.15), kind=kOutput, calls=%fused_computation.4 | convolution fusion | flops 537395200 | bytes 6029312 | tf_op jit(solution)/shard_map/dot_general | solution.py:170
  53.2 1.6 fusion.116
  55.0 0.7 pad_maximum_fusion
  55.8 5.6 %all-to-all-start.3 = ((bf16[16,128,66]{1,2,0:T(8,128)(2,1)}), bf16[16,128,66]{1,2,0:T(8,128)(2,1)S(1)}, u32[]{:S(2)}, u32[]{:S(2)}) async-start(bf16[16,128,66]{1,2,0:T(8,128)(2,1)} %pad_maximum_fusion), calls=%async_computation.3 | async-start | bytes 589824 | tf_op jit(solution)/shard_map/all_to_all | solution.py:22
  61.4 8.0 %all-to-all-done.3 = bf16[16,128,66]{1,2,0:T(8,128)(2,1)S(1)} async-done(((bf16[16,128,66]{1,2,0:T(8,128)(2,1)}), bf16[16,128,66]{1,2,0:T(8,128)(2,1)S(1)}, u32[]{:S(2)}, u32[]{:S(2)}) %all-to-all-start.3) | async-done | bytes 270368 | tf_op jit(solution)/shard_map/all_to_all | solution.py:22
  69.6 0.8 broadcast_in_dim.119
  70.3 6.1 %all-to-all-start.4 = ((bf16[16,128,64]{1,2,0:T(8,128)(2,1)}), bf16[16,128,64]{1,2,0:T(8,128)(2,1)S(1)}, u32[]{:S(2)}, u32[]{:S(2)}) async-start(bf16[16,128,64]{1,2,0:T(8,128)(2,1)} %broadcast_in_dim.119), calls=%async_computation.4 | async-start | bytes 524288 | tf_op jit(solution)/shard_map/all_to_all | solution.py:22
  76.4 0.6 select_add_fusion
  77.0 7.2 %all-to-all-done.4 = bf16[16,128,64]{1,2,0:T(8,128)(2,1)S(1)} async-done(((bf16[16,128,64]{1,2,0:T(8,128)(2,1)}), bf16[16,128,64]{1,2,0:T(8,128)(2,1)S(1)}, u32[]{:S(2)}, u32[]{:S(2)}) %all-to-all-start.4) | async-done | bytes 262176 | tf_op jit(solution)/shard_map/all_to_all | solution.py:22
  84.5 2.9 %collective-permute-start.1 = (f32[2,32]{1,0:T(2,128)S(1)}, f32[2,32]{1,0:T(2,128)S(1)}, u32[]{:S(2)}, u32[]{:S(2)}) collective-permute-start(f32[2,32]{1,0:T(2,128)S(1)} %pad_maximum_fusion.1), channel_id=1, source_target_pairs={{0,16},{16,0},{1,17},{17,1},{2,18},{18,2},{3,19},{19,3},{4,20},{20... | collective-permute-start | bytes 776 | tf_op jit(solution)/shard_map/ppermute | solution.py:40
  87.3 0.8 collective-permute-done.1
  88.2 1.4 collective-permute-start.3
  89.5 0.6 collective-permute-start.2
  91.1 4.7 %multiply_add_fusion = (f32[128,2048]{1,0:T(8,128)}, bf16[128,2048]{1,0:T(8,128)(2,1)S(1)}) fusion(bf16[1024,2048]{1,0:T(8,128)(2,1)} %param.14, bf16[128,1024]{1,0:T(8,128)(2,1)S(1)} %fusion.63, f32[128]{0:T(128)S(1)} %add_rsqrt_fusion, f32[1024]{0:T(1024)S(1)} %copy-done.14), kind=kOutput, calls=%fused_computation.40 | convolution fusion | flops 542113792 | bytes 6033920 | tf_op jit(solution)/shard_map/dot_general | solution.py:157
  95.8 0.7 convolution_convert_fusion.2
  96.6 0.8 copy.30
  97.4 4.7 %all-to-all-start.5 = ((bf16[16,128,64]{1,2,0:T(8,128)(2,1)}), bf16[16,128,64]{1,2,0:T(8,128)(2,1)S(1)}, u32[]{:S(2)}, u32[]{:S(2)}) async-start(bf16[16,128,64]{1,2,0:T(8,128)(2,1)} %bitcast.15), calls=%async_computation.5 | async-start | bytes 524288 | tf_op jit(solution)/shard_map/all_to_all | solution.py:22
  102.2 1.9 collective-permute-start.8
  104.1 1.2 fusion.28
  105.3 1.2 fusion.24
  106.4 3.6 %all-to-all-done.5 = bf16[16,128,64]{1,2,0:T(8,128)(2,1)S(1)} async-done(((bf16[16,128,64]{1,2,0:T(8,128)(2,1)}), bf16[16,128,64]{1,2,0:T(8,128)(2,1)S(1)}, u32[]{:S(2)}, u32[]{:S(2)}) %all-to-all-start.5) | async-done | bytes 262176 | tf_op jit(solution)/shard_map/all_to_all | solution.py:22
  110.1 0.7 fusion.81
  110.8 0.8 broadcast_in_dim.120
  111.6 5.7 %all-to-all-start.6 = ((bf16[16,128,64]{1,2,0:T(8,128)(2,1)}), bf16[16,128,64]{1,2,0:T(8,128)(2,1)S(1)}, u32[]{:S(2)}, u32[]{:S(2)}) async-start(bf16[16,128,64]{1,2,0:T(8,128)(2,1)} %broadcast_in_dim.120), calls=%async_computation.6 | async-start | bytes 524288 | tf_op jit(solution)/shard_map/all_to_all | solution.py:22
  117.2 0.5 fusion.30
  117.8 2.1 %collective-permute-start.6 = (bf16[128,512]{1,0:T(8,128)(2,1)S(1)}, bf16[128,512]{1,0:T(8,128)(2,1)S(1)}, u32[]{:S(2)}, u32[]{:S(2)}) collective-permute-start(bf16[128,512]{1,0:T(8,128)(2,1)S(1)} %fusion.30), channel_id=1, source_target_pairs={{0,16},{16,0},{1,17},{17,1},{2,18},{18,2},{3,19},{19,3},{4,20},{20... | collective-permute-start | bytes 393224 | tf_op jit(solution)/shard_map/ppermute | solution.py:40
  119.9 1.2 fusion.26
  121.1 0.5 fusion.29
  121.7 3.3 %all-to-all-done.6 = bf16[16,128,64]{1,2,0:T(8,128)(2,1)S(1)} async-done(((bf16[16,128,64]{1,2,0:T(8,128)(2,1)}), bf16[16,128,64]{1,2,0:T(8,128)(2,1)S(1)}, u32[]{:S(2)}, u32[]{:S(2)}) %all-to-all-start.6) | async-done | bytes 262176 | tf_op jit(solution)/shard_map/all_to_all | solution.py:22
  125.0 0.5 fusion.31
  125.5 2.8 %collective-permute-start.7 = (bf16[128,512]{1,0:T(8,128)(2,1)S(1)}, bf16[128,512]{1,0:T(8,128)(2,1)S(1)}, u32[]{:S(2)}, u32[]{:S(2)}) collective-permute-start(bf16[128,512]{1,0:T(8,128)(2,1)S(1)} %fusion.31), channel_id=1, source_target_pairs={{0,16},{16,0},{1,17},{17,1},{2,18},{18,2},{3,19},{19,3},{4,20},{20... | collective-permute-start | bytes 393224 | tf_op jit(solution)/shard_map/ppermute | solution.py:40
  128.4 0.5 fusion.27
  129.1 0.6 copy-done.22
  129.7 0.8 copy-done.21
  130.5 3.1 %convolution_convert_fusion.1 = bf16[512,2048]{1,0:T(8,128)(2,1)S(1)} fusion(bf16[128,2048]{1,0:T(8,128)(2,1)} %copy-done.21, bf16[128,2048]{1,0:T(8,128)(2,1)} %copy-done.8, bf16[128,2048]{1,0:T(8,128)(2,1)} %collective-permute-done.8, bf16[128,2048]{1,0:T(8,128)(2,1)} %copy-done.6, bf16[128,512]{1,0:T(8,128)(2,1)S(1)} %collective-permute-done.7, ...), kind=kOutput, calls=%fused_computation.1 | convolution fusion | flops 1085276160 | bytes 4718592 | tf_op jit(solution)/shard_map/dot_general | solution.py:125
  133.7 1.5 fusion.1
  135.6 0.5 fusion.25
  136.5 4.1 %collective-permute-start.18 = (bf16[128,2048]{1,0:T(8,128)(2,1)S(1)}, bf16[128,2048]{1,0:T(8,128)(2,1)S(1)}, u32[]{:S(2)}, u32[]{:S(2)}) collective-permute-start(bf16[128,2048]{1,0:T(8,128)(2,1)S(1)} %get-tuple-element.31), channel_id=1, source_target_pairs={{0,32},{32,64},{64,96},{96,0},{1,33},{33,65},{65,97},{97,1},{2,34}... | collective-permute-start | bytes 1572872 | tf_op jit(solution)/shard_map/ppermute | solution.py:88
  140.7 7.2 %collective-permute-start.17 = (bf16[128,2048]{1,0:T(8,128)(2,1)S(1)}, bf16[128,2048]{1,0:T(8,128)(2,1)S(1)}, u32[]{:S(2)}, u32[]{:S(2)}) collective-permute-start(bf16[128,2048]{1,0:T(8,128)(2,1)S(1)} %get-tuple-element.32), channel_id=1, source_target_pairs={{0,96},{32,0},{64,32},{96,64},{1,97},{33,1},{65,33},{97,65},{2,98}... | collective-permute-start | bytes 1572872 | tf_op jit(solution)/shard_map/ppermute | solution.py:88
  147.9 2.2 %convolution_convert_fusion = bf16[512,2048]{1,0:T(8,128)(2,1)S(1)} fusion(bf16[128,2048]{1,0:T(8,128)(2,1)S(1)} %collective-permute-done.10, bf16[128,2048]{1,0:T(8,128)(2,1)S(1)} %fusion.1, bf16[128,2048]{1,0:T(8,128)(2,1)S(1)} %collective-permute-done.5, bf16[128,2048]{1,0:T(8,128)(2,1)S(1)} %fusion, bf16[128,512]{1,0:T(8,128)(2,1)S(1)} %collective-permute-done.4, ...), kind=kOutput, calls=%fused_computation | convolution fusion | flops 1085276160 | bytes 4718592 | tf_op jit(solution)/shard_map/dot_general | solution.py:125
  150.1 1.1 fusion.114
  151.1 2.7 %collective-permute-start.14 = (bf16[64,2048]{1,0:T(8,128)(2,1)S(1)}, bf16[64,2048]{1,0:T(8,128)(2,1)S(1)}, u32[]{:S(2)}, u32[]{:S(2)}) collective-permute-start(bf16[64,2048]{1,0:T(8,128)(2,1)S(1)} %get-tuple-element.29), channel_id=1, source_target_pairs={{0,96},{32,0},{64,32},{96,64},{1,97},{33,1},{65,33},{97,65},{2,98}... | collective-permute-start | bytes 786440 | tf_op jit(solution)/shard_map/ppermute | solution.py:88
  153.8 6.0 %collective-permute-done.18 = bf16[128,2048]{1,0:T(8,128)(2,1)S(1)} collective-permute-done((bf16[128,2048]{1,0:T(8,128)(2,1)S(1)}, bf16[128,2048]{1,0:T(8,128)(2,1)S(1)}, u32[]{:S(2)}, u32[]{:S(2)}) %collective-permute-start.18) | collective-permute-done | bytes 524320 | tf_op jit(solution)/shard_map/ppermute | solution.py:88
  159.8 5.6 %collective-permute-done.11 = bf16[64,2048]{1,0:T(8,128)(2,1)S(1)} collective-permute-done((bf16[64,2048]{1,0:T(8,128)(2,1)S(1)}, bf16[64,2048]{1,0:T(8,128)(2,1)S(1)}, u32[]{:S(2)}, u32[]{:S(2)}) %collective-permute-start.11) | collective-permute-done | bytes 262176 | tf_op jit(solution)/shard_map/ppermute | solution.py:88
  165.4 1.2 fusion.43
  166.6 2.4 %collective-permute-start.19 = (bf16[64,2048]{1,0:T(8,128)(2,1)S(1)}, bf16[64,2048]{1,0:T(8,128)(2,1)S(1)}, u32[]{:S(2)}, u32[]{:S(2)}) collective-permute-start(bf16[64,2048]{1,0:T(8,128)(2,1)S(1)} %get-tuple-element.37), channel_id=1, source_target_pairs={{0,96},{32,0},{64,32},{96,64},{1,97},{33,1},{65,33},{97,65},{2,98}... | collective-permute-start | bytes 786440 | tf_op jit(solution)/shard_map/ppermute | solution.py:88
  169.1 2.7 %collective-permute-start.15 = (bf16[64,2048]{1,0:T(8,128)(2,1)}, bf16[64,2048]{1,0:T(8,128)(2,1)}, u32[]{:S(2)}, u32[]{:S(2)}) collective-permute-start(bf16[64,2048]{1,0:T(8,128)(2,1)} %get-tuple-element.26), channel_id=1, source_target_pairs={{0,96},{32,0},{64,32},{96,64},{1,97},{33,1},{65,33},{97,65},{2,98}... | collective-permute-start | bytes 786440 | tf_op jit(solution)/shard_map/ppermute | solution.py:88
  171.8 1.9 collective-permute-done.19
  173.7 0.8 add_convert_fusion
  174.5 4.3 %collective-permute-start.20 = (bf16[64,2048]{1,0:T(8,128)(2,1)}, bf16[64,2048]{1,0:T(8,128)(2,1)S(1)}, u32[]{:S(2)}, u32[]{:S(2)}) collective-permute-start(bf16[64,2048]{1,0:T(8,128)(2,1)} %add_convert_fusion), channel_id=1, source_target_pairs={{0,128},{128,0},{1,129},{129,1},{2,130},{130,2},{3,131},{131,3},{4... | collective-permute-start | bytes 786440 | tf_op jit(solution)/shard_map/ppermute | solution.py:40
  178.7 1.2 constant_dynamic-slice_fusion
  180.2 3.3 %collective-permute-start.13 = (bf16[64,2048]{1,0:T(8,128)(2,1)}, bf16[64,2048]{1,0:T(8,128)(2,1)S(1)}, u32[]{:S(2)}, u32[]{:S(2)}) collective-permute-start(bf16[64,2048]{1,0:T(8,128)(2,1)} %get-tuple-element.30), channel_id=1, source_target_pairs={{0,96},{32,0},{64,32},{96,64},{1,97},{33,1},{65,33},{97,65},{2,98}... | collective-permute-start | bytes 786440 | tf_op jit(solution)/shard_map/ppermute | solution.py:88
  183.5 7.7 %collective-permute-done.20 = bf16[64,2048]{1,0:T(8,128)(2,1)S(1)} collective-permute-done((bf16[64,2048]{1,0:T(8,128)(2,1)}, bf16[64,2048]{1,0:T(8,128)(2,1)S(1)}, u32[]{:S(2)}, u32[]{:S(2)}) %collective-permute-start.20) | collective-permute-done | bytes 262176 | tf_op jit(solution)/shard_map/ppermute | solution.py:40
  191.2 1.3 fusion.55
  192.5 3.8 %collective-permute-start.21 = (bf16[64,2048]{1,0:T(8,128)(2,1)S(1)}, bf16[64,2048]{1,0:T(8,128)(2,1)S(1)}, u32[]{:S(2)}, u32[]{:S(2)}) collective-permute-start(bf16[64,2048]{1,0:T(8,128)(2,1)S(1)} %fusion.55), channel_id=1, source_target_pairs={{0,128},{128,0},{1,129},{129,1},{2,130},{130,2},{3,131},{131,3},{4... | collective-permute-start | bytes 786440 | tf_op jit(solution)/shard_map/ppermute | solution.py:40
  196.3 2.2 %subtract_convert_fusion = (bf16[2048,64]{0,1:T(8,128)(2,1)}, f32[2048,64]{0,1:T(8,128)}) fusion(bf16[2048,64]{0,1:T(8,128)(2,1)S(1)} %copy.32, bf16[64,2048]{1,0:T(8,128)(2,1)S(1)} %collective-permute-done.20, bf16[128,2048]{1,0:T(8,128)(2,1)} %copy-done.7, bf16[64,2048]{1,0:T(8,128)(2,1)S(1)} %collective-permute-done.22, ...), kind=kLoop, calls=%fused_computation.107 | loop fusion | flops 1835008 | bytes 2621440 | tf_op jit(solution)/shard_map/convert_element_type | solution.py:219
  198.5 6.3 %collective-permute-done.21 = bf16[64,2048]{1,0:T(8,128)(2,1)S(1)} collective-permute-done((bf16[64,2048]{1,0:T(8,128)(2,1)S(1)}, bf16[64,2048]{1,0:T(8,128)(2,1)S(1)}, u32[]{:S(2)}, u32[]{:S(2)}) %collective-permute-start.21) | collective-permute-done | bytes 262176 | tf_op jit(solution)/shard_map/ppermute | solution.py:40
  204.8 2.1 %subtract_convert_fusion.1 = (bf16[64,2048]{1,0:T(8,128)(2,1)}, f32[64,2048]{1,0:T(8,128)}) fusion(bf16[1024,2048]{1,0:T(8,128)(2,1)} %param.14, s32[]{:T(128)S(6)} %select_n.195, bf16[64,2048]{1,0:T(8,128)(2,1)S(1)} %collective-permute-done.21, bf16[64,2048]{1,0:T(8,128)(2,1)S(1)} %collective-permute-done.13, ...), kind=kLoop, calls=%fused_computation.108 | loop fusion | flops 1835008 | bytes 2621444 | tf_op jit(solution)/shard_map/convert_element_type | solution.py:218
  (109 shorter events, 3.5 us)
Async XLA Ops:
  17.6 3.8 %copy-start = (bf16[2048,1024]{1,0:T(8,128)(2,1)S(1)}, bf16[2048,1024]{1,0:T(8,128)(2,1)}, u32[]{:S(2)}) copy-start(bf16[2048,1024]{1,0:T(8,128)(2,1)} %param.15) | copy-start | bytes 12582916
  21.3 80.9 %copy-start.6 = (bf16[128,2048]{1,0:T(8,128)(2,1)}, bf16[128,2048]{1,0:T(8,128)(2,1)S(1)}, u32[]{:S(2)}) copy-start(bf16[128,2048]{1,0:T(8,128)(2,1)S(1)} %get-tuple-element.9) | copy-start | bytes 1572868
  21.3 14.8 %copy-start.10 = (f32[128,64]{0,1:T(8,128)S(1)}, f32[128,64]{0,1:T(8,128)}, u32[]{:S(2)}) copy-start(f32[128,64]{0,1:T(8,128)} %param.10) | copy-start | bytes 98308
  21.3 14.8 %copy-start.11 = (bf16[128,64]{0,1:T(8,128)(2,1)S(1)}, bf16[128,64]{0,1:T(8,128)(2,1)}, u32[]{:S(2)}) copy-start(bf16[128,64]{0,1:T(8,128)(2,1)} %param.9) | copy-start | bytes 49156
  21.3 14.8 %copy-start.12 = (f32[128,64]{0,1:T(8,128)S(1)}, f32[128,64]{0,1:T(8,128)}, u32[]{:S(2)}) copy-start(f32[128,64]{0,1:T(8,128)} %param.12) | copy-start | bytes 98308
  22.1 31.1 %copy-start.14 = (f32[1024]{0:T(1024)S(1)}, f32[1024]{0:T(1024)}, u32[]{:S(2)}) copy-start(f32[1024]{0:T(1024)} %param.13) | copy-start | bytes 12292
  22.3 30.9 %copy-start.3 = (bf16[1024,2048]{1,0:T(8,128)(2,1)S(1)}, bf16[1024,2048]{1,0:T(8,128)(2,1)}, u32[]{:S(2)}) copy-start(bf16[1024,2048]{1,0:T(8,128)(2,1)} %param.14) | copy-start | bytes 12582916
  53.2 31.2 %copy-start.20 = (s32[128]{0:T(128)S(1)}, s32[128]{0:T(128)}, u32[]{:S(2)}) copy-start(s32[128]{0:T(128)} %param.11) | copy-start | bytes 1540
  55.8 13.6 %all-to-all-start.3 = ((bf16[16,128,66]{1,2,0:T(8,128)(2,1)}), bf16[16,128,66]{1,2,0:T(8,128)(2,1)S(1)}, u32[]{:S(2)}, u32[]{:S(2)}) async-start(bf16[16,128,66]{1,2,0:T(8,128)(2,1)} %pad_maximum_fusion), calls=%async_computation.3 | async-start | bytes 589824 | tf_op jit(solution)/shard_map/all_to_all | solution.py:22
  69.5 21.6 %copy-start.15 = (f32[128]{0:T(128)}, f32[128]{0:T(128)S(1)}, u32[]{:S(2)}) copy-start(f32[128]{0:T(128)S(1)} %slice_reduce_fusion) | copy-start | bytes 1540
  70.3 13.9 %all-to-all-start.4 = ((bf16[16,128,64]{1,2,0:T(8,128)(2,1)}), bf16[16,128,64]{1,2,0:T(8,128)(2,1)S(1)}, u32[]{:S(2)}, u32[]{:S(2)}) async-start(bf16[16,128,64]{1,2,0:T(8,128)(2,1)} %broadcast_in_dim.119), calls=%async_computation.4 | async-start | bytes 524288 | tf_op jit(solution)/shard_map/all_to_all | solution.py:22
  84.5 3.7 %collective-permute-start.1 = (f32[2,32]{1,0:T(2,128)S(1)}, f32[2,32]{1,0:T(2,128)S(1)}, u32[]{:S(2)}, u32[]{:S(2)}) collective-permute-start(f32[2,32]{1,0:T(2,128)S(1)} %pad_maximum_fusion.1), channel_id=1, source_target_pairs={{0,16},{16,0},{1,17},{17,1},{2,18},{18,2},{3,19},{19,3},{4,20},{20... | collective-permute-start | bytes 776 | tf_op jit(solution)/shard_map/ppermute | solution.py:40
  88.2 2.5 %collective-permute-start.3 = (f32[2,32]{1,0:T(2,128)S(1)}, f32[2,32]{1,0:T(2,128)S(1)}, u32[]{:S(2)}, u32[]{:S(2)}) collective-permute-start(f32[2,32]{1,0:T(2,128)S(1)} %fusion.103), channel_id=1, source_target_pairs={{0,32},{64,96},{128,160},{192,224},{32,0},{96,64},{160,128},{224,1... | collective-permute-start | bytes 776 | tf_op jit(solution)/shard_map/ppermute | solution.py:57
  89.5 1.1 collective-permute-start.2
  91.1 30.1 %copy-start.23 = (f32[128]{0:T(128)}, f32[128]{0:T(128)S(1)}, u32[]{:S(2)}) copy-start(f32[128]{0:T(128)S(1)} %add_rsqrt_fusion) | copy-start | bytes 1540
  91.1 4.7 %copy-start.1 = (bf16[2048,1024]{1,0:T(8,128)(2,1)S(1)}, bf16[2048,1024]{1,0:T(8,128)(2,1)}, u32[]{:S(2)}) copy-start(bf16[2048,1024]{1,0:T(8,128)(2,1)} %param.15) | copy-start | bytes 12582916
  95.8 25.3 %copy-start.8 = (bf16[128,2048]{1,0:T(8,128)(2,1)}, bf16[128,2048]{1,0:T(8,128)(2,1)S(1)}, u32[]{:S(2)}) copy-start(bf16[128,2048]{1,0:T(8,128)(2,1)S(1)} %get-tuple-element.11) | copy-start | bytes 1572868
  95.8 8.2 %copy-start.17 = (s32[512]{0:T(512)S(1)}, s32[512]{0:T(512)}, u32[]{:S(2)}) copy-start(s32[512]{0:T(512)} %select_add_fusion) | copy-start | bytes 6148
  95.8 14.3 %copy-start.13 = (f32[128,64]{0,1:T(8,128)S(1)}, f32[128,64]{0,1:T(8,128)}, u32[]{:S(2)}) copy-start(f32[128,64]{0,1:T(8,128)} %param.12) | copy-start | bytes 98308
  95.8 14.3 %copy-start.16 = (f32[128]{0:T(128)S(1)}, f32[128]{0:T(128)}, u32[]{:S(2)}) copy-start(f32[128]{0:T(128)} %copy-done.15) | copy-start | bytes 1540
  97.4 12.6 %all-to-all-start.5 = ((bf16[16,128,64]{1,2,0:T(8,128)(2,1)}), bf16[16,128,64]{1,2,0:T(8,128)(2,1)S(1)}, u32[]{:S(2)}, u32[]{:S(2)}) async-start(bf16[16,128,64]{1,2,0:T(8,128)(2,1)} %bitcast.15), calls=%async_computation.5 | async-start | bytes 524288 | tf_op jit(solution)/shard_map/all_to_all | solution.py:22
  102.2 26.7 %copy-start.18 = (s32[512]{0:T(512)}, s32[512]{0:T(512)S(1)}, u32[]{:S(2)}) copy-start(s32[512]{0:T(512)S(1)} %select_add_fusion.1) | copy-start | bytes 6148
  102.2 26.8 %collective-permute-start.8 = (bf16[128,2048]{1,0:T(8,128)(2,1)S(1)}, bf16[128,2048]{1,0:T(8,128)(2,1)}, u32[]{:S(2)}, u32[]{:S(2)}) collective-permute-start(bf16[128,2048]{1,0:T(8,128)(2,1)S(1)} %get-tuple-element.9), channel_id=1, source_target_pairs={{0,16},{16,0},{1,17},{17,1},{2,18},{18,2},{3,19},{19,3},{4,20},{20... | collective-permute-start | bytes 1572872 | tf_op jit(solution)/shard_map/ppermute | solution.py:40
  105.2 35.4 %collective-permute-start = (bf16[128,512]{1,0:T(8,128)(2,1)}, bf16[128,512]{1,0:T(8,128)(2,1)}, u32[]{:S(2)}, u32[]{:S(2)}) collective-permute-start(bf16[128,512]{1,0:T(8,128)(2,1)} %fusion.28), channel_id=1, source_target_pairs={{0,16},{16,0},{1,17},{17,1},{2,18},{18,2},{3,19},{19,3},{4,20},{20... | collective-permute-start | bytes 393224 | tf_op jit(solution)/shard_map/ppermute | solution.py:40
  111.6 13.4 %all-to-all-start.6 = ((bf16[16,128,64]{1,2,0:T(8,128)(2,1)}), bf16[16,128,64]{1,2,0:T(8,128)(2,1)S(1)}, u32[]{:S(2)}, u32[]{:S(2)}) async-start(bf16[16,128,64]{1,2,0:T(8,128)(2,1)} %broadcast_in_dim.120), calls=%async_computation.6 | async-start | bytes 524288 | tf_op jit(solution)/shard_map/all_to_all | solution.py:22
  117.8 11.3 %collective-permute-start.6 = (bf16[128,512]{1,0:T(8,128)(2,1)S(1)}, bf16[128,512]{1,0:T(8,128)(2,1)S(1)}, u32[]{:S(2)}, u32[]{:S(2)}) collective-permute-start(bf16[128,512]{1,0:T(8,128)(2,1)S(1)} %fusion.30), channel_id=1, source_target_pairs={{0,16},{16,0},{1,17},{17,1},{2,18},{18,2},{3,19},{19,3},{4,20},{20... | collective-permute-start | bytes 393224 | tf_op jit(solution)/shard_map/ppermute | solution.py:40
  121.1 7.9 %collective-permute-start.9 = (bf16[128,2048]{1,0:T(8,128)(2,1)S(1)}, bf16[128,2048]{1,0:T(8,128)(2,1)S(1)}, u32[]{:S(2)}, u32[]{:S(2)}) collective-permute-start(bf16[128,2048]{1,0:T(8,128)(2,1)S(1)} %get-tuple-element.11), channel_id=1, source_target_pairs={{0,16},{16,0},{1,17},{17,1},{2,18},{18,2},{3,19},{19,3},{4,20},{20... | collective-permute-start | bytes 1572872 | tf_op jit(solution)/shard_map/ppermute | solution.py:40
  125.5 5.0 %collective-permute-start.7 = (bf16[128,512]{1,0:T(8,128)(2,1)S(1)}, bf16[128,512]{1,0:T(8,128)(2,1)S(1)}, u32[]{:S(2)}, u32[]{:S(2)}) collective-permute-start(bf16[128,512]{1,0:T(8,128)(2,1)S(1)} %fusion.31), channel_id=1, source_target_pairs={{0,16},{16,0},{1,17},{17,1},{2,18},{18,2},{3,19},{19,3},{4,20},{20... | collective-permute-start | bytes 393224 | tf_op jit(solution)/shard_map/ppermute | solution.py:40
  128.9 4.7 %copy-start.2 = (bf16[2048,1024]{1,0:T(8,128)(2,1)S(1)}, bf16[2048,1024]{1,0:T(8,128)(2,1)}, u32[]{:S(2)}) copy-start(bf16[2048,1024]{1,0:T(8,128)(2,1)} %param.15) | copy-start | bytes 12582916
  128.9 4.7 %copy-start.5 = (f32[128,2048]{1,0:T(8,128)S(1)}, f32[128,2048]{1,0:T(8,128)}, u32[]{:S(2)}) copy-start(f32[128,2048]{1,0:T(8,128)} %get-tuple-element.12) | copy-start | bytes 3145732
  128.9 18.9 %collective-permute-start.5 = (bf16[128,2048]{1,0:T(8,128)(2,1)S(1)}, bf16[128,2048]{1,0:T(8,128)(2,1)S(1)}, u32[]{:S(2)}, u32[]{:S(2)}) collective-permute-start(bf16[128,2048]{1,0:T(8,128)(2,1)S(1)} %fusion), channel_id=1, source_target_pairs={{0,16},{16,0},{1,17},{17,1},{2,18},{18,2},{3,19},{19,3},{4,20},{20... | collective-permute-start | bytes 1572872 | tf_op jit(solution)/shard_map/ppermute | solution.py:40
  129.1 0.7 copy-start.22
  129.7 0.8 copy-start.21
  133.7 2.0 copy-start.19
  133.7 1.9 copy-start.24
  133.7 14.2 %copy-start.25 = (bf16[128,512]{1,0:T(8,128)(2,1)S(1)}, bf16[128,512]{1,0:T(8,128)(2,1)}, u32[]{:S(2)}) copy-start(bf16[128,512]{1,0:T(8,128)(2,1)} %fusion.24) | copy-start | bytes 393220
  135.2 12.6 %collective-permute-start.10 = (bf16[128,2048]{1,0:T(8,128)(2,1)S(1)}, bf16[128,2048]{1,0:T(8,128)(2,1)S(1)}, u32[]{:S(2)}, u32[]{:S(2)}) collective-permute-start(bf16[128,2048]{1,0:T(8,128)(2,1)S(1)} %fusion.1), channel_id=1, source_target_pairs={{0,16},{16,0},{1,17},{17,1},{2,18},{18,2},{3,19},{19,3},{4,20},{20... | collective-permute-start | bytes 1572872 | tf_op jit(solution)/shard_map/ppermute | solution.py:40
  136.1 11.7 %collective-permute-start.4 = (bf16[128,512]{1,0:T(8,128)(2,1)S(1)}, bf16[128,512]{1,0:T(8,128)(2,1)S(1)}, u32[]{:S(2)}, u32[]{:S(2)}) collective-permute-start(bf16[128,512]{1,0:T(8,128)(2,1)S(1)} %fusion.29), channel_id=1, source_target_pairs={{0,16},{16,0},{1,17},{17,1},{2,18},{18,2},{3,19},{19,3},{4,20},{20... | collective-permute-start | bytes 393224 | tf_op jit(solution)/shard_map/ppermute | solution.py:40
  136.5 23.3 %collective-permute-start.18 = (bf16[128,2048]{1,0:T(8,128)(2,1)S(1)}, bf16[128,2048]{1,0:T(8,128)(2,1)S(1)}, u32[]{:S(2)}, u32[]{:S(2)}) collective-permute-start(bf16[128,2048]{1,0:T(8,128)(2,1)S(1)} %get-tuple-element.31), channel_id=1, source_target_pairs={{0,32},{32,64},{64,96},{96,0},{1,33},{33,65},{65,97},{97,1},{2,34}... | collective-permute-start | bytes 1572872 | tf_op jit(solution)/shard_map/ppermute | solution.py:88
  140.7 19.2 %collective-permute-start.17 = (bf16[128,2048]{1,0:T(8,128)(2,1)S(1)}, bf16[128,2048]{1,0:T(8,128)(2,1)S(1)}, u32[]{:S(2)}, u32[]{:S(2)}) collective-permute-start(bf16[128,2048]{1,0:T(8,128)(2,1)S(1)} %get-tuple-element.32), channel_id=1, source_target_pairs={{0,96},{32,0},{64,32},{96,64},{1,97},{33,1},{65,33},{97,65},{2,98}... | collective-permute-start | bytes 1572872 | tf_op jit(solution)/shard_map/ppermute | solution.py:88
  150.0 15.4 %copy-start.4 = (bf16[512,2048]{1,0:T(8,128)(2,1)}, bf16[512,2048]{1,0:T(8,128)(2,1)S(1)}, u32[]{:S(2)}) copy-start(bf16[512,2048]{1,0:T(8,128)(2,1)S(1)} %convolution_convert_fusion) | copy-start | bytes 6291460
  151.1 14.3 %collective-permute-start.11 = (bf16[64,2048]{1,0:T(8,128)(2,1)S(1)}, bf16[64,2048]{1,0:T(8,128)(2,1)S(1)}, u32[]{:S(2)}, u32[]{:S(2)}) collective-permute-start(bf16[64,2048]{1,0:T(8,128)(2,1)S(1)} %get-tuple-element.27), channel_id=1, source_target_pairs={{0,32},{32,64},{64,96},{96,0},{1,33},{33,65},{65,97},{97,1},{2,34}... | collective-permute-start | bytes 786440 | tf_op jit(solution)/shard_map/ppermute | solution.py:88
  151.1 14.3 %collective-permute-start.14 = (bf16[64,2048]{1,0:T(8,128)(2,1)S(1)}, bf16[64,2048]{1,0:T(8,128)(2,1)S(1)}, u32[]{:S(2)}, u32[]{:S(2)}) collective-permute-start(bf16[64,2048]{1,0:T(8,128)(2,1)S(1)} %get-tuple-element.29), channel_id=1, source_target_pairs={{0,96},{32,0},{64,32},{96,64},{1,97},{33,1},{65,33},{97,65},{2,98}... | collective-permute-start | bytes 786440 | tf_op jit(solution)/shard_map/ppermute | solution.py:88
  159.8 18.9 %copy-start.7 = (bf16[128,2048]{1,0:T(8,128)(2,1)}, bf16[128,2048]{1,0:T(8,128)(2,1)S(1)}, u32[]{:S(2)}) copy-start(bf16[128,2048]{1,0:T(8,128)(2,1)S(1)} %collective-permute-done.17) | copy-start | bytes 1572868
  166.6 7.0 %collective-permute-start.19 = (bf16[64,2048]{1,0:T(8,128)(2,1)S(1)}, bf16[64,2048]{1,0:T(8,128)(2,1)S(1)}, u32[]{:S(2)}, u32[]{:S(2)}) collective-permute-start(bf16[64,2048]{1,0:T(8,128)(2,1)S(1)} %get-tuple-element.37), channel_id=1, source_target_pairs={{0,96},{32,0},{64,32},{96,64},{1,97},{33,1},{65,33},{97,65},{2,98}... | collective-permute-start | bytes 786440 | tf_op jit(solution)/shard_map/ppermute | solution.py:88
  169.1 14.4 %collective-permute-start.16 = (bf16[64,2048]{1,0:T(8,128)(2,1)}, bf16[64,2048]{1,0:T(8,128)(2,1)}, u32[]{:S(2)}, u32[]{:S(2)}) collective-permute-start(bf16[64,2048]{1,0:T(8,128)(2,1)} %get-tuple-element.28), channel_id=1, source_target_pairs={{0,32},{32,64},{64,96},{96,0},{1,33},{33,65},{65,97},{97,1},{2,34}... | collective-permute-start | bytes 786440 | tf_op jit(solution)/shard_map/ppermute | solution.py:88
  169.1 14.5 %collective-permute-start.15 = (bf16[64,2048]{1,0:T(8,128)(2,1)}, bf16[64,2048]{1,0:T(8,128)(2,1)}, u32[]{:S(2)}, u32[]{:S(2)}) collective-permute-start(bf16[64,2048]{1,0:T(8,128)(2,1)} %get-tuple-element.26), channel_id=1, source_target_pairs={{0,96},{32,0},{64,32},{96,64},{1,97},{33,1},{65,33},{97,65},{2,98}... | collective-permute-start | bytes 786440 | tf_op jit(solution)/shard_map/ppermute | solution.py:88
  174.5 16.8 %collective-permute-start.20 = (bf16[64,2048]{1,0:T(8,128)(2,1)}, bf16[64,2048]{1,0:T(8,128)(2,1)S(1)}, u32[]{:S(2)}, u32[]{:S(2)}) collective-permute-start(bf16[64,2048]{1,0:T(8,128)(2,1)} %add_convert_fusion), channel_id=1, source_target_pairs={{0,128},{128,0},{1,129},{129,1},{2,130},{130,2},{3,131},{131,3},{4... | collective-permute-start | bytes 786440 | tf_op jit(solution)/shard_map/ppermute | solution.py:40
  180.2 24.6 %copy-start.9 = (f32[64,2048]{1,0:T(8,128)S(1)}, f32[64,2048]{1,0:T(8,128)}, u32[]{:S(2)}) copy-start(f32[64,2048]{1,0:T(8,128)} %param.16) | copy-start | bytes 1572868
  180.2 18.3 %collective-permute-start.13 = (bf16[64,2048]{1,0:T(8,128)(2,1)}, bf16[64,2048]{1,0:T(8,128)(2,1)S(1)}, u32[]{:S(2)}, u32[]{:S(2)}) collective-permute-start(bf16[64,2048]{1,0:T(8,128)(2,1)} %get-tuple-element.30), channel_id=1, source_target_pairs={{0,96},{32,0},{64,32},{96,64},{1,97},{33,1},{65,33},{97,65},{2,98}... | collective-permute-start | bytes 786440 | tf_op jit(solution)/shard_map/ppermute | solution.py:88
  183.5 15.0 %collective-permute-start.12 = (bf16[64,2048]{1,0:T(8,128)(2,1)S(1)}, bf16[64,2048]{1,0:T(8,128)(2,1)S(1)}, u32[]{:S(2)}, u32[]{:S(2)}) collective-permute-start(bf16[64,2048]{1,0:T(8,128)(2,1)S(1)} %get-tuple-element.25), channel_id=1, source_target_pairs={{0,32},{32,64},{64,96},{96,0},{1,33},{33,65},{65,97},{97,1},{2,34}... | collective-permute-start | bytes 786440 | tf_op jit(solution)/shard_map/ppermute | solution.py:88
  183.5 12.8 %collective-permute-start.22 = (bf16[64,2048]{1,0:T(8,128)(2,1)}, bf16[64,2048]{1,0:T(8,128)(2,1)S(1)}, u32[]{:S(2)}, u32[]{:S(2)}) collective-permute-start(bf16[64,2048]{1,0:T(8,128)(2,1)} %get-tuple-element.38), channel_id=1, source_target_pairs={{0,32},{32,64},{64,96},{96,0},{1,33},{33,65},{65,97},{97,1},{2,34}... | collective-permute-start | bytes 786440 | tf_op jit(solution)/shard_map/ppermute | solution.py:88
  192.5 12.3 %collective-permute-start.21 = (bf16[64,2048]{1,0:T(8,128)(2,1)S(1)}, bf16[64,2048]{1,0:T(8,128)(2,1)S(1)}, u32[]{:S(2)}, u32[]{:S(2)}) collective-permute-start(bf16[64,2048]{1,0:T(8,128)(2,1)S(1)} %fusion.55), channel_id=1, source_target_pairs={{0,128},{128,0},{1,129},{129,1},{2,130},{130,2},{3,131},{131,3},{4... | collective-permute-start | bytes 786440 | tf_op jit(solution)/shard_map/ppermute | solution.py:40
